TPU v7x, 32 devices: a whole 2x2x4 slice. The times are simulated.
32 devices in a mesh: role: 2 (over x), dp: 4 (over z), mp: 4 (over y, core).
Axes of the slice: x: 2, y: 2, z: 4, core: 2. Of those that a mesh axis runs over, the one named last changes fastest.
Arguments:
- state: float32 [2, 2, 8, 256, 512], P('role', None, None, 'dp', 'mp'), may hold values from 0 to 1
- embed: bfloat16 [2, 1024, 4096], P('role', 'dp', 'mp'), may hold values from -0.09375 to 0.09375
- mlp: bfloat16 [2, 2, 1024, 4096], P('role', None, 'dp', 'mp'), may hold values from -0.1875 to 0.1875
- mom_embed: float32 [2, 1024, 4096], P('role', 'dp', 'mp'), may hold values from -6 to 6
- mom_mlp: float32 [2, 2, 1024, 4096], P('role', None, 'dp', 'mp'), may hold values from -6 to 6
Outputs:
- state_out: float32 [2, 8, 256, 512], P(None, None, 'dp', 'mp')
- embed_out: bfloat16 [2, 1024, 4096], P('role', 'dp', 'mp')
- mlp_out: bfloat16 [2, 2, 1024, 4096], P('role', None, 'dp', 'mp')
- mom_embed_out: float32 [2, 1024, 4096], P('role', 'dp', 'mp')
- mom_mlp_out: float32 [2, 2, 1024, 4096], P('role', None, 'dp', 'mp')
All inputs are finite; a program needn't handle non-finite values.
Results may differ from a plain program's by a relative error of at most 0.0034.
Values may be sent and summed in bfloat16 or wider, within the bound.
No kernel may reach another device: no remote copies, remote signals or barrier semaphores. Data moves between devices by JAX's collectives and lax.ppermute only.
A program may use at most 128 MiB of HBM per device.

v0:
```python
import jax
import jax.numpy as jnp
from jax import lax
from jax.sharding import PartitionSpec as P

PATCH = 16
STEPS = 4


SUBSTRATE_DIFFUSION = 0.2
CATALYST_DIFFUSION = 0.1
FEED_RATE = 0.037
KILL_RATE = 0.06
TIME_STEP = 0.8
GELU_FACTOR = 0.7978845608028654
MOMENTUM_DECAY = 0.9
LEARNING_RATE = 0.003


def extended(cells, sides, width):
    for axis, dim in sides:
        count = lax.axis_size(axis)
        head = lax.slice_in_dim(cells, 0, width, axis=dim)
        tail = lax.slice_in_dim(cells, cells.shape[dim] - width, cells.shape[dim], axis=dim)
        cells = jnp.concatenate(
            [
                lax.ppermute(tail, axis, [(i, (i + 1) % count) for i in range(count)]),
                cells,
                lax.ppermute(head, axis, [((i + 1) % count, i) for i in range(count)]),
            ],
            axis=dim,
        )
    return cells


def from_behind(value, axis, steps):
    count = lax.axis_size(axis)
    leading, last = (max(0, -steps), min(count, count - steps))
    return lax.ppermute(value, axis, [(source, source + steps) for source in range(leading, last)])


def react(padded):
    center = padded[:, :, 1:-1, 1:-1]
    below_plane = jnp.concatenate([center[:, :1], center[:, :-1]], axis=1)
    above_plane = jnp.concatenate([center[:, 1:], center[:, -1:]], axis=1)
    beside = below_plane + above_plane + padded[:, :, :-2, 1:-1] + padded[:, :, 2:, 1:-1]
    beside = beside + padded[:, :, 1:-1, :-2] + padded[:, :, 1:-1, 2:]
    laplace = beside - 6.0 * center
    substrate = center[0]
    catalyst = center[1]
    growth = substrate * catalyst * catalyst
    new_substrate = substrate + TIME_STEP * (
        SUBSTRATE_DIFFUSION * laplace[0] - growth + FEED_RATE * (1.0 - substrate)
    )
    new_catalyst = catalyst + TIME_STEP * (
        CATALYST_DIFFUSION * laplace[1] + growth - (FEED_RATE + KILL_RATE) * catalyst
    )
    return jnp.stack([new_substrate, new_catalyst])


def gelu_slope(preact):
    cubic = 0.044715 * preact * preact * preact
    tangent = jnp.tanh(GELU_FACTOR * (preact + cubic))
    return 0.5 * (1.0 + tangent) + 0.5 * preact * (1.0 - tangent * tangent) * GELU_FACTOR * (
        1.0 + 3.0 * 0.044715 * preact * preact
    )


def to_patches(brick):
    extent = brick.shape
    blocks = brick.reshape(
        extent[0], extent[1], extent[2] // PATCH, PATCH, extent[3] // PATCH, PATCH
    )
    blocks = blocks.transpose(2, 4, 0, 1, 3, 5)
    return blocks.reshape(
        extent[2] // PATCH * (extent[3] // PATCH), extent[0] * extent[1] * PATCH * PATCH
    )


def advance(cells):
    padded = extended(cells, (("dp", 2), ("mp", 3)), STEPS)
    for iteration in range(STEPS):
        padded = react(padded)
    return padded


def shards(state, embed, mlp, mom_embed, mom_mlp):
    group_index = lax.axis_index("role")
    start_cells = state[0]
    start_half = start_cells.astype(jnp.bfloat16)
    initial = from_behind(start_half, "role", 1)
    stacked = jnp.concatenate([embed[0], mlp[0, 0], mlp[0, 1]], axis=1)
    whole = lax.all_gather(stacked, "dp", axis=0, tiled=True)
    cells = advance(start_cells)
    arrived = from_behind(cells, "role", 1)
    state_out = jnp.where(group_index == 0, cells, arrived)
    final_rows = to_patches(arrived.astype(jnp.bfloat16))
    inputs, targets = (
        lax.all_to_all(to_patches(initial), "mp", split_axis=1, concat_axis=0, tiled=True),
        lax.all_to_all(final_rows, "mp", split_axis=1, concat_axis=0, tiled=True),
    )
    feature_cols = embed.shape[2]
    hidden_cols = mlp.shape[3]
    embed_full = whole[:, :feature_cols]
    up_full = whole[:, feature_cols : feature_cols + hidden_cols]
    down_full = whole[:, feature_cols + hidden_cols :]
    patch_rows = inputs.shape[0]
    loss_scale = float(patch_rows * lax.axis_size("dp")) ** (-0.5)
    embedded = lax.psum_scatter(
        jnp.dot(inputs, embed_full.T, preferred_element_type=jnp.float32),
        "mp",
        scatter_dimension=0,
        tiled=True,
    )
    recip = lax.rsqrt(jnp.mean(embedded * embedded, axis=1, keepdims=True) + 1e-06)
    normed = lax.all_gather((embedded * recip).astype(jnp.bfloat16), "mp", axis=0, tiled=True)
    hidden_pre = jnp.dot(normed, up_full, preferred_element_type=jnp.float32)
    active = jax.nn.gelu(hidden_pre, approximate=True).astype(jnp.bfloat16)
    branch = lax.psum_scatter(
        jnp.dot(active, down_full.T, preferred_element_type=jnp.float32),
        "mp",
        scatter_dimension=0,
        tiled=True,
    )
    stream = lax.all_gather((embedded + branch).astype(jnp.bfloat16), "mp", axis=0, tiled=True)
    predicted = inputs.astype(jnp.float32) + jnp.dot(
        stream, embed_full, preferred_element_type=jnp.float32
    )
    residual_grad = ((predicted - targets.astype(jnp.float32)) * loss_scale).astype(jnp.bfloat16)
    stream_grad = lax.psum_scatter(
        jnp.dot(residual_grad, embed_full.T, preferred_element_type=jnp.float32),
        "mp",
        scatter_dimension=0,
        tiled=True,
    )
    stream_sent = lax.all_gather(stream_grad.astype(jnp.bfloat16), "mp", axis=0, tiled=True)
    hidden_grad = (
        jnp.dot(stream_sent, down_full, preferred_element_type=jnp.float32) * gelu_slope(hidden_pre)
    ).astype(jnp.bfloat16)
    normed_grad = lax.psum_scatter(
        jnp.dot(hidden_grad, up_full.T, preferred_element_type=jnp.float32),
        "mp",
        scatter_dimension=0,
        tiled=True,
    )
    embed_grad = (
        stream_grad
        + recip * normed_grad
        - embedded
        * (recip * recip * recip)
        * jnp.mean(normed_grad * embedded, axis=1, keepdims=True)
    )
    embed_sent = lax.all_gather(embed_grad.astype(jnp.bfloat16), "mp", axis=0, tiled=True)
    up_part = jnp.dot(normed.T, hidden_grad, preferred_element_type=jnp.float32)
    down_part = jnp.dot(stream_sent.T, active, preferred_element_type=jnp.float32)
    first = jnp.dot(stream.T, residual_grad, preferred_element_type=jnp.float32)
    grads = lax.psum_scatter(
        jnp.concatenate(
            [
                first + jnp.dot(embed_sent.T, inputs, preferred_element_type=jnp.float32),
                up_part,
                down_part,
            ],
            axis=1,
        ),
        "dp",
        scatter_dimension=0,
        tiled=True,
    )
    mirrored = from_behind(grads, "role", -1)
    grads = jnp.where(group_index == 0, mirrored, grads)
    grad_embed_rows = grads[:, :feature_cols]
    grad_mlp_rows = jnp.stack(
        [
            grads[:, feature_cols : feature_cols + hidden_cols],
            grads[:, feature_cols + hidden_cols :],
        ]
    )
    mom_embed_out = MOMENTUM_DECAY * mom_embed + grad_embed_rows[None]
    mom_mlp_out = MOMENTUM_DECAY * mom_mlp + grad_mlp_rows[None]
    embed_out = (embed.astype(jnp.float32) - LEARNING_RATE * mom_embed_out).astype(jnp.bfloat16)
    mlp_out = (mlp.astype(jnp.float32) - LEARNING_RATE * mom_mlp_out).astype(jnp.bfloat16)
    return (state_out, embed_out, mlp_out, mom_embed_out, mom_mlp_out)


def solution(mesh):
    placed = (
        P("role", None, None, "dp", "mp"),
        P("role", "dp", "mp"),
        P("role", None, "dp", "mp"),
        P("role", "dp", "mp"),
        P("role", None, "dp", "mp"),
    )
    return jax.shard_map(
        shards,
        mesh=mesh,
        in_specs=placed,
        out_specs=(
            P(None, None, "dp", "mp"),
            P("role", "dp", "mp"),
            P("role", None, "dp", "mp"),
            P("role", "dp", "mp"),
            P("role", None, "dp", "mp"),
        ),
        check_vma=False,
    )
```

profile of v0, /device:TPU:0, one launch (start us, length us, event | category | flops | bytes accessed | tf_op | source)
XLA Modules:
  0.0 591.7 jit_solution(593477143505401968)
XLA Ops:
  7.2 1.3 slice_bitcast_fusion.4
  11.2 3.1 collective-permute-start
  14.3 2.1 collective-permute-start.1
  16.4 1.9 collective-permute-done
  19.3 1.8 collective-permute-start.3
  21.4 3.4 collective-permute-start.5
  30.3 2.3 fusion.39
  32.6 1.4 reshape.46
  34.0 1.8 copy.118
  35.8 3.9 all_to_all.24
  40.5 4.0 all-to-all-start
  45.2 5.4 all-to-all-done
  50.7 77.4 %all-gather.2.cloned.1.call-done = bf16[1024,3072]{1,0:T(8,128)(2,1)} async-done(((bf16[256,3072]{1,0:T(8,128)(2,1)}), bf16[1024,3072]{1,0:T(8,128)(2,1)}) %all-gather.2.cloned.1.call-update) | async-done | bytes 6291472 | tf_op jit(solution)/shard_map/all_gather | solution.py:93
  128.1 2.3 fusion.15
  135.5 15.9 %reduce-scatter.16.cloned.1.call-done = f32[32,1024]{1,0:T(8,128)} async-done(((f32[128,1024]{1,0:T(8,128)}), f32[32,1024]{1,0:T(8,128)}) %reduce-scatter.16.cloned.1.call-update) | async-done | bytes 131088 | tf_op jit(solution)/shard_map/reduce_scatter | solution.py:109
  152.9 5.8 all_gather.16
  158.6 2.1 fusion.7
  160.8 3.4 fusion.3
  164.6 3.4 collective-permute-start.4
  168.0 11.6 %collective-permute-done.4 = f32[2,8,64,128]{3,2,1,0:T(8,128)S(1)} collective-permute-done((f32[2,8,64,128]{3,2,1,0:T(8,128)S(1)}, f32[2,8,64,128]{3,2,1,0:T(8,128)S(1)}, u32[]{:S(2)}, u32[]{:S(2)}) %collective-permute-start.4) | collective-permute-done | bytes 524320 | tf_op jit(solution)/shard_map/ppermute | solution.py:39
  180.5 1.4 reshape.47
  181.9 1.8 copy.124
  183.7 3.8 all_to_all.28
  187.6 8.4 %all_to_all.32 = bf16[32,4,1024]{2,0,1:T(8,128)(2,1)S(1)} all-to-all(bf16[32,4,1024]{2,0,1:T(8,128)(2,1)S(1)} %copy.125), channel_id=1, replica_groups=mesh['role'=2,'dp'=4,'mp'=4] {'mp'}, dimensions={1} | all-to-all | bytes 524288 | tf_op jit(solution)/shard_map/all_to_all | solution.py:100
  197.0 5.8 all_gather.17
  202.8 2.1 fusion.30
  204.9 3.3 fusion.9
  208.2 22.8 %reduce-scatter.20.cloned.1.call-done = f32[32,1024]{1,0:T(8,128)} async-done(((f32[128,1024]{1,0:T(8,128)}), f32[32,1024]{1,0:T(8,128)}) %reduce-scatter.20.cloned.1.call-update) | async-done | bytes 131088 | tf_op jit(solution)/shard_map/reduce_scatter | solution.py:130
  232.0 6.0 %all_gather.18 = bf16[128,1024]{1,0:T(8,128)(2,1)S(1)} all-gather(bf16[32,1024]{1,0:T(8,128)(2,1)S(1)} %convert_element_type.62), channel_id=1, replica_groups=mesh['role'=2,'dp'=4,'mp'=4] {'mp'}, dimensions={0}, use_global_device_ids=true | all-gather | bytes 327680 | tf_op jit(solution)/shard_map/all_gather | solution.py:136
  238.0 2.3 fusion.33
  240.3 3.2 fusion.5
  243.6 2.8 fusion.135
  246.4 2.7 fusion.136
  249.1 2.8 fusion.126
  251.9 13.5 %reduce-scatter.22.cloned.1.call-done = f32[32,1024]{1,0:T(8,128)} async-done(((f32[128,1024]{1,0:T(8,128)}), f32[32,1024]{1,0:T(8,128)}) %reduce-scatter.22.cloned.1.call-update) | async-done | bytes 131088 | tf_op jit(solution)/shard_map/reduce_scatter | solution.py:140
  266.8 5.8 all_gather.19
  272.6 3.2 convolution_add_fusion
  277.4 5.6 pad_maximum_fusion
  283.1 212.0 %reduce-scatter.14.cloned.1.call-done = f32[256,3072]{0,1:T(8,128)} async-done(((f32[1024,3072]{0,1:T(8,128)}), f32[256,3072]{0,1:T(8,128)}) %reduce-scatter.14.cloned.1.call-update) | async-done | bytes 3145744 | tf_op jit(solution)/shard_map/reduce_scatter | solution.py:157
  498.7 3.0 copy.133
  504.2 63.0 %collective-permute-done.6 = f32[256,3072]{0,1:T(8,128)} collective-permute-done((f32[256,3072]{0,1:T(8,128)}, f32[256,3072]{0,1:T(8,128)}, u32[]{:S(2)}, u32[]{:S(2)}) %collective-permute-start.6) | collective-permute-done | bytes 3145760 | tf_op jit(solution)/shard_map/ppermute | solution.py:39
  567.2 2.3 broadcast_select_fusion
  569.6 1.4 copy-done.2
  571.3 2.1 subtract_convert_fusion
  573.4 2.9 copy.138
  576.3 2.3 copy.136
  578.6 2.7 subtract_convert_fusion.1
  581.3 2.6 copy.137
  (109 shorter events, 31.4 us)
Async XLA Ops:
  7.2 1.4 copy-start.10
  7.2 120.9 %all-gather.2.cloned.1.call-start = ((), (), s32[]{:S(2)}) async-start(), calls=%async_computation.7 | async-start | bytes 7864320 | tf_op jit(solution)/shard_map/all_gather | solution.py:93
  9.8 1.0 copy-start.6
  11.2 7.1 %collective-permute-start = (f32[2,8,4,128]{3,1,2,0:T(8,128)S(1)}, f32[2,8,4,128]{3,1,2,0:T(8,128)S(1)}, u32[]{:S(2)}, u32[]{:S(2)}) collective-permute-start(f32[2,8,4,128]{3,1,2,0:T(8,128)S(1)} %get-tuple-element.67), channel_id=1, source_target_pairs={{0,4},{4,8},{8,12},{12,0},{1,5},{5,9},{9,13},{13,1},{2,6},{6,10},{... | collective-permute-start | bytes 98312 | tf_op jit(solution)/shard_map/ppermute | solution.py:27
  14.3 4.3 collective-permute-start.1
  19.1 5.8 collective-permute-start.2
  19.3 5.8 collective-permute-start.3
  21.4 11.2 %collective-permute-start.5 = (bf16[2,8,64,128]{3,1,2,0:T(8,128)(2,1)S(1)}, bf16[2,8,64,128]{3,1,2,0:T(8,128)(2,1)S(1)}, u32[]{:S(2)}, u32[]{:S(2)}) collective-permute-start(bf16[2,8,64,128]{3,1,2,0:T(8,128)(2,1)S(1)} %bitcast.67), channel_id=1, source_target_pairs={{0,16},{1,17},{2,18},{3,19},{4,20},{5,21},{6,22},{7,23},{8,24},{9,... | collective-permute-start | bytes 786440 | tf_op jit(solution)/shard_map/ppermute | solution.py:39
  35.8 9.0 %copy-start.3 = (f32[2,8,68,132]{3,1,2,0:T(8,128)S(1)}, f32[2,8,68,132]{3,1,2,0:T(8,128)}, u32[]{:S(2)}) copy-start(f32[2,8,68,132]{3,1,2,0:T(8,128)} %fusion.39) | copy-start | bytes 1723396
  40.5 10.2 %all-to-all-start = ((bf16[32,4,1024]{2,0,1:T(8,128)(2,1)}), bf16[32,4,1024]{2,0,1:T(8,128)(2,1)}, u32[]{:S(2)}, u32[]{:S(2)}) async-start(bf16[32,4,1024]{2,0,1:T(8,128)(2,1)} %copy.119), calls=%async_computation | async-start | bytes 524288 | tf_op jit(solution)/shard_map/all_to_all | solution.py:99
  44.6 106.9 %reduce-scatter.16.cloned.1.call-start = ((), (), s32[]{:S(2)}) async-start(), calls=%async_computation.9 | async-start | bytes 655360 | tf_op jit(solution)/shard_map/reduce_scatter | solution.py:109
  131.4 64.7 %reduce-scatter.18.cloned.1.call-start = ((), (), s32[]{:S(2)}) async-start(), calls=%async_computation.10 | async-start | bytes 655360 | tf_op jit(solution)/shard_map/reduce_scatter | solution.py:119
  151.4 1.3 copy-start.9
  158.6 2.1 copy-start.13
  160.8 3.4 copy-start.16
  164.2 66.9 %reduce-scatter.20.cloned.1.call-start = ((), (), s32[]{:S(2)}) async-start(), calls=%async_computation.11 | async-start | bytes 655360 | tf_op jit(solution)/shard_map/reduce_scatter | solution.py:130
  164.6 15.0 %collective-permute-start.4 = (f32[2,8,64,128]{3,2,1,0:T(8,128)S(1)}, f32[2,8,64,128]{3,2,1,0:T(8,128)S(1)}, u32[]{:S(2)}, u32[]{:S(2)}) collective-permute-start(f32[2,8,64,128]{3,2,1,0:T(8,128)S(1)} %copy.113), channel_id=1, source_target_pairs={{0,16},{1,17},{2,18},{3,19},{4,20},{5,21},{6,22},{7,23},{8,24},{9,... | collective-permute-start | bytes 1572872 | tf_op jit(solution)/shard_map/ppermute | solution.py:39
  179.7 0.8 copy-start.7
  204.9 33.1 %copy-start.17 = (f32[128,1024]{1,0:T(8,128)S(1)}, f32[128,1024]{1,0:T(8,128)}, u32[]{:S(2)}) copy-start(f32[128,1024]{1,0:T(8,128)} %copy-done.16) | copy-start | bytes 1572868
  208.2 57.1 %reduce-scatter.22.cloned.1.call-start = ((), (), s32[]{:S(2)}) async-start(), calls=%async_computation.12 | async-start | bytes 655360 | tf_op jit(solution)/shard_map/reduce_scatter | solution.py:140
  243.5 2.8 copy-start.14
  243.5 251.6 %reduce-scatter.14.cloned.1.call-start = ((), (), s32[]{:S(2)}) async-start(), calls=%async_computation.8 | async-start | bytes 15728640 | tf_op jit(solution)/shard_map/reduce_scatter | solution.py:157
  251.9 14.8 %copy-start.19 = (f32[32,1024]{1,0:T(8,128)S(1)}, f32[32,1024]{1,0:T(8,128)}, u32[]{:S(2)}) copy-start(f32[32,1024]{1,0:T(8,128)} %reduce-scatter.20.cloned.1.call-done) | copy-start | bytes 393220
  265.3 1.3 copy-start.18
  272.6 3.5 copy-start
  272.6 4.8 copy-start.1
  283.0 213.3 %copy-start.4 = (bf16[1,2,256,1024]{3,2,1,0:T(8,128)(2,1)S(1)}, bf16[1,2,256,1024]{3,2,1,0:T(8,128)(2,1)}, u32[]{:S(2)}) copy-start(bf16[1,2,256,1024]{3,2,1,0:T(8,128)(2,1)} %param.7) | copy-start | bytes 3145732
  283.0 214.6 %copy-start.11 = (bf16[1,256,1024]{2,1,0:T(8,128)(2,1)S(1)}, bf16[1,256,1024]{2,1,0:T(8,128)(2,1)}, u32[]{:S(2)}) copy-start(bf16[1,256,1024]{2,1,0:T(8,128)(2,1)} %param.6) | copy-start | bytes 1572868
  495.1 72.1 %collective-permute-start.6 = (f32[256,3072]{0,1:T(8,128)}, f32[256,3072]{0,1:T(8,128)}, u32[]{:S(2)}, u32[]{:S(2)}) collective-permute-start(f32[256,3072]{0,1:T(8,128)} %reduce-scatter.14.cloned.1.call-done), channel_id=1, source_target_pairs={{16,0},{17,1},{18,2},{19,3},{20,4},{21,5},{22,6},{23,7},{24,8},{25... | collective-permute-start | bytes 9437192 | tf_op jit(solution)/shard_map/ppermute | solution.py:39
  498.7 3.0 copy-start.15
  501.7 1.3 copy-start.8
  569.5 1.6 copy-start.2
  569.5 1.8 copy-start.5
  581.3 2.6 copy-start.12
Sparse Core Ops, SparseCore 0:
  10.0 118.0 all-gather.1
  131.5 19.8 reduce-scatter.15
  164.3 21.6 reduce-scatter.17
  208.3 22.7 reduce-scatter.19
  243.6 21.6 reduce-scatter.21
  283.2 211.8 reduce-scatter.13
where the time goes:
time: 593 us; the launch traced here: 592 us
  waiting for transfers between devices  424 us (72%)
  local copies, waits for them, and re-layouts  44.5 us (8%)
  blocking collectives  31.8 us (5%)
  matrix products  30.1 us (5%)
  other arithmetic  27.3 us (5%)
  starting transfers between devices  19.5 us (3%)
  between operations  14.6 us (2%)
    reduce_scatter x1, waiting for transfers between devices, shards(): lax.psum_scatter(jnp.concatenate([first + jnp.dot(embed_sent.T, inputs, p...  212 us
    all_gather x1, waiting for transfers between devices, shards(): whole = lax.all_gather(stacked, 'dp', axis=0, tiled=True)  77.4 us
    ppermute x3, waiting for transfers between devices, from_behind(): lax.ppermute(value, axis, [(source, source + steps) for source in range(l...  74.6 us
    unnamed x54, local copies, waits for them, and re-layouts  25.4 us
    reduce_scatter x1, waiting for transfers between devices, shards(): lax.psum_scatter(jnp.dot(residual_grad, embed_full.T, preferred_element_t...  22.8 us
    reduce_scatter x1, waiting for transfers between devices, shards(): lax.psum_scatter(jnp.dot(inputs, embed_full.T, preferred_element_type=jnp...  15.9 us
    reduce_scatter x1, waiting for transfers between devices, shards(): lax.psum_scatter(jnp.dot(hidden_grad, up_full.T, preferred_element_type=j...  13.5 us
  transfers between devices with their start and end apart: 14, of which 10 were waited for; matrix products, arithmetic and copies ran while one was open for 6% of the time, Pallas kernels for 0%

commit v1 on v0

v1 whole, which is shorter than its diff:
```python
import jax
import jax.numpy as jnp
from jax import lax
from jax.sharding import PartitionSpec as P

PATCH = 16
STEPS = 4


SUBSTRATE_DIFFUSION = 0.2
CATALYST_DIFFUSION = 0.1
FEED_RATE = 0.037
KILL_RATE = 0.06
TIME_STEP = 0.8
GELU_FACTOR = 0.7978845608028654
MOMENTUM_DECAY = 0.9
LEARNING_RATE = 0.003

SOLVER, TRAINER = 0, 1
BF16 = jnp.bfloat16
F32 = jnp.float32


class Digit:
    def __init__(self, axis, stride, size):
        self.axis, self.stride, self.size = axis, stride, size
        self.position = lax.axis_index(axis) // stride % size

    def shifted(self, value, step):
        pairs = []
        for index in range(lax.axis_size(self.axis)):
            digit = index // self.stride % self.size
            pairs.append((index, index + ((digit + step) % self.size - digit) * self.stride))
        return lax.ppermute(value, self.axis, pairs)

    def gathered(self, pick, axis):
        parts = [pick(0)] + [self.shifted(pick(k), k) for k in range(1, self.size)]
        return jnp.concatenate(parts, axis=axis) if self.size > 1 else parts[0]

    def ordered(self, pick):
        parts = [pick(0)] + [self.shifted(pick(k), k) for k in range(1, self.size)]
        slots = []
        for slot in range(self.size):
            value = parts[0]
            for k in range(1, self.size):
                value = jnp.where((self.position - slot) % self.size == k, parts[k], value)
            slots.append(value)
        return jnp.concatenate(slots, axis=0)

    def summed(self, value):
        sent = value.astype(BF16)
        for k in range(1, self.size):
            value = value + self.shifted(sent, k).astype(F32)
        return value


def extended(cells, sides, width):
    for axis, dim in sides:
        count = lax.axis_size(axis)
        head = lax.slice_in_dim(cells, 0, width, axis=dim)
        tail = lax.slice_in_dim(cells, cells.shape[dim] - width, cells.shape[dim], axis=dim)
        cells = jnp.concatenate(
            [
                lax.ppermute(tail, axis, [(i, (i + 1) % count) for i in range(count)]),
                cells,
                lax.ppermute(head, axis, [((i + 1) % count, i) for i in range(count)]),
            ],
            axis=dim,
        )
    return cells


def react(padded):
    center = padded[:, :, 1:-1, 1:-1]
    below_plane = jnp.concatenate([center[:, :1], center[:, :-1]], axis=1)
    above_plane = jnp.concatenate([center[:, 1:], center[:, -1:]], axis=1)
    beside = below_plane + above_plane + padded[:, :, :-2, 1:-1] + padded[:, :, 2:, 1:-1]
    beside = beside + padded[:, :, 1:-1, :-2] + padded[:, :, 1:-1, 2:]
    laplace = beside - 6.0 * center
    substrate = center[0]
    catalyst = center[1]
    growth = substrate * catalyst * catalyst
    new_substrate = substrate + TIME_STEP * (
        SUBSTRATE_DIFFUSION * laplace[0] - growth + FEED_RATE * (1.0 - substrate)
    )
    new_catalyst = catalyst + TIME_STEP * (
        CATALYST_DIFFUSION * laplace[1] + growth - (FEED_RATE + KILL_RATE) * catalyst
    )
    return jnp.stack([new_substrate, new_catalyst])


def advance(cells):
    padded = extended(cells, (("dp", 2), ("mp", 3)), STEPS)
    for iteration in range(STEPS):
        padded = react(padded)
    return padded


def gelu_slope(preact):
    cubic = 0.044715 * preact * preact * preact
    tangent = jnp.tanh(GELU_FACTOR * (preact + cubic))
    return 0.5 * (1.0 + tangent) + 0.5 * preact * (1.0 - tangent * tangent) * GELU_FACTOR * (
        1.0 + 3.0 * 0.044715 * preact * preact
    )


def to_patches(brick):
    extent = brick.shape
    blocks = brick.reshape(
        extent[0], extent[1], extent[2] // PATCH, PATCH, extent[3] // PATCH, PATCH
    )
    blocks = blocks.transpose(2, 4, 0, 1, 3, 5)
    return blocks.reshape(
        extent[2] // PATCH * (extent[3] // PATCH), extent[0] * extent[1] * PATCH * PATCH
    )


def rows_dot(left, right):
    return lax.dot_general(left, right, (((1,), (1,)), ((), ())), preferred_element_type=F32)


def cols_dot(left, right):
    return lax.dot_general(left, right, (((0,), (0,)), ((), ())), preferred_element_type=F32)


def dot(left, right):
    return jnp.dot(left, right, preferred_element_type=F32)


def shards(state, embed, mlp, mom_embed, mom_mlp):
    dp_count, mp_count = lax.axis_size("dp"), lax.axis_size("mp")
    halves = 2 if dp_count % 2 == 0 else 1
    pairs = 2 if mp_count % 2 == 0 else 1
    wide = Digit("dp", dp_count // halves, halves)
    band = Digit("dp", 1, dp_count // halves)
    part = Digit("mp", pairs, mp_count // pairs)
    core = Digit("mp", 1, pairs)
    role = Digit("role", 1, lax.axis_size("role"))
    solving = role.position == SOLVER
    width = embed.shape[1] * dp_count
    own_rows, own_cols = embed.shape[1], embed.shape[2]

    def weights(block):
        held = jnp.where(solving, lax.ppermute(block, "role", [(TRAINER, SOLVER)]), block)
        held = band.gathered(lambda k: held, 0)
        return core.gathered(lambda k: held, 1)

    def spread(patches):
        cut = patches.reshape(patches.shape[0], part.size, core.size, own_cols)

        def features(k):
            target = lax.dynamic_index_in_dim(
                cut, (part.position + k) % part.size, axis=1, keepdims=False
            )
            picked = [
                lax.dynamic_index_in_dim(
                    target, (core.position - t) % core.size, axis=1, keepdims=False
                )
                for t in range(core.size)
            ]
            return jnp.concatenate(picked, axis=1)

        rows = part.ordered(features)
        return wide.ordered(lambda k: rows)

    start_cells = state[0]
    start_patches = to_patches(start_cells.astype(BF16))
    half_rows = start_patches.shape[0] // 2
    arrived_half = lax.ppermute(start_patches[half_rows:], "role", [(SOLVER, TRAINER)])
    inputs = spread(jnp.where(solving, start_patches[:half_rows], arrived_half))

    embed_held = weights(embed[0])
    up_held = weights(mlp[0, 0])
    down_held = weights(mlp[0, 1])

    cells = advance(start_cells)
    arrived = lax.ppermute(cells, "role", [(SOLVER, TRAINER)])
    state_out = jnp.where(solving, cells, arrived)
    end_patches = to_patches(state_out.astype(BF16))
    targets = spread(jnp.where(solving, end_patches[:half_rows], end_patches[half_rows:]))

    def all_rows(feature_like, width_like):
        def to_core(k):
            slot = (-k) % core.size * own_cols
            cuts = [v[:, slot : slot + own_cols] for v in feature_like] + list(width_like)
            return jnp.concatenate(cuts, axis=1) if len(cuts) > 1 else cuts[0]

        both = core.gathered(to_core, 0)

        def to_band(k):
            slot = (-k) % band.size * own_rows
            base = len(feature_like) * own_cols
            cuts = [both[:, :base]] if base else []
            for index in range(len(width_like)):
                first = base + index * own_rows * band.size + slot
                cuts.append(both[:, first : first + own_rows])
            return jnp.concatenate(cuts, axis=1) if len(cuts) > 1 else cuts[0]

        banded = band.gathered(to_band, 0)
        whole = role.gathered(lambda k: banded, 0)
        pieces = []
        first = 0
        for size in [own_cols] * len(feature_like) + [own_rows] * len(width_like):
            pieces.append(whole[:, first : first + size])
            first += size
        return pieces

    total_rows = inputs.shape[0] * core.size * band.size * role.size
    loss_scale = float(total_rows) ** (-0.5)

    embedded = part.summed(rows_dot(inputs, embed_held))
    squares = jnp.sum(embedded * embedded, axis=1, keepdims=True)
    for k in range(1, wide.size):
        squares = squares + wide.shifted(squares, k)
    recip = lax.rsqrt(squares / width + 1e-06)
    hidden_pre = wide.summed(dot(embedded.astype(BF16), up_held)) * recip
    normed = (embedded * recip).astype(BF16)
    active = jax.nn.gelu(hidden_pre, approximate=True).astype(BF16)
    branch = part.summed(rows_dot(active, down_held))
    stream = (embedded + branch).astype(BF16)
    predicted = inputs.astype(F32) + wide.summed(dot(stream, embed_held))
    residual = ((predicted - targets.astype(F32)) * loss_scale).astype(BF16)
    stream_grad = part.summed(rows_dot(residual, embed_held))
    stream_sent = stream_grad.astype(BF16)
    hidden_grad = (wide.summed(dot(stream_sent, down_held)) * gelu_slope(hidden_pre)).astype(BF16)
    normed_grad = part.summed(rows_dot(hidden_grad, up_held))
    inner = jnp.sum(hidden_grad.astype(F32) * hidden_pre, axis=1, keepdims=True)
    for k in range(1, part.size):
        inner = inner + part.shifted(inner, k)
    embed_grad = stream_grad + recip * normed_grad - embedded * (recip * recip) * (inner / width)
    embed_sent = embed_grad.astype(BF16)

    (all_inputs,) = all_rows([inputs], [])
    all_active, all_normed, all_stream = all_rows([active], [normed, stream])
    all_residual, all_stream_sent = all_rows([residual], [stream_sent])
    (all_hidden_grad,) = all_rows([hidden_grad], [])
    (all_embed_sent,) = all_rows([], [embed_sent])

    grad_down = cols_dot(all_stream_sent, all_active)
    grad_up = cols_dot(all_normed, all_hidden_grad)
    grad_embed = cols_dot(all_stream, all_residual) + cols_dot(all_embed_sent, all_inputs)

    mom_embed_out = MOMENTUM_DECAY * mom_embed + grad_embed[None]
    mom_mlp_out = MOMENTUM_DECAY * mom_mlp + jnp.stack([grad_up, grad_down])[None]
    embed_out = (embed.astype(F32) - LEARNING_RATE * mom_embed_out).astype(BF16)
    mlp_out = (mlp.astype(F32) - LEARNING_RATE * mom_mlp_out).astype(BF16)
    return (state_out, embed_out, mlp_out, mom_embed_out, mom_mlp_out)


def solution(mesh):
    placed = (
        P("role", None, None, "dp", "mp"),
        P("role", "dp", "mp"),
        P("role", None, "dp", "mp"),
        P("role", "dp", "mp"),
        P("role", None, "dp", "mp"),
    )
    return jax.shard_map(
        shards,
        mesh=mesh,
        in_specs=placed,
        out_specs=(
            P(None, None, "dp", "mp"),
            P("role", "dp", "mp"),
            P("role", None, "dp", "mp"),
            P("role", "dp", "mp"),
            P("role", None, "dp", "mp"),
        ),
        check_vma=False,
    )
```

time: 593 us -> 224 us (0.38)
  waiting for transfers between devices: 424 us -> 118 us
  blocking collectives: 31.8 us -> 0 us
  local copies, waits for them, and re-layouts: 44.5 us -> 21.5 us
  starting transfers between devices: 19.5 us -> 42.1 us
  matrix products: 30.1 us -> 17 us
  between operations: 14.6 us -> 1.7 us
    reduce_scatter x5 -> x0, waiting for transfers between devices: 264 us -> none  [the longest x1 212 us: shards(): lax.psum_scatter(jnp.concatenate([first + jnp.dot(embed_sent.T, inputs, p...]
    all_gather x1 -> x0, waiting for transfers between devices: 77.4 us -> none  [shards(): whole = lax.all_gather(stacked, 'dp', axis=0, tiled=True)]
    ppermute x3 -> x39, waiting for transfers between devices: 74.6 us -> 118 us  [the longest x34 113 us: shifted(): return lax.ppermute(value, self.axis, pairs)]
    ppermute x3 -> x39, starting transfers between devices: 8.09 us -> 35.2 us  [the longest x34 20.3 us: shifted(): return lax.ppermute(value, self.axis, pairs)]
    all_gather x4 -> x0, blocking collectives: 23.4 us -> none  [the longest x1 6 us: shards(): lax.all_gather(stream_grad.astype(jnp.bfloat16), 'mp', axis=0, tiled=True)]
    unnamed x54 -> x24, local copies, waits for them, and re-layouts: 25.4 us -> 3.59 us
    unnamed x3 -> x0, matrix products: 9.89 us -> none
    all_to_all x4 -> x0, local copies, waits for them, and re-layouts: 8.51 us -> none  [the longest x2 4.65 us: shards(): lax.all_to_all(to_patches(initial), 'mp', split_axis=1, concat_axis=0, ti...]
  transfers between devices with their start and end apart: 14 -> 43, of which waited for: 10 -> 20; matrix products, arithmetic and copies ran while one was open for 6% -> 24% of each run, Pallas kernels for 0% -> 0%
where the time goes in v1:
time: 224 us; the launch traced here: 223 us
  waiting for transfers between devices  118 us (53%)
  starting transfers between devices  42.1 us (19%)
  other arithmetic  23.3 us (10%)
  local copies, waits for them, and re-layouts  21.5 us (10%)
  matrix products  17 us (8%)
    ppermute x34, waiting for transfers between devices, shifted(): return lax.ppermute(value, self.axis, pairs)  113 us
    ppermute x34, starting transfers between devices, shifted(): return lax.ppermute(value, self.axis, pairs)  20.3 us
    dot_general x4, matrix products, rows_dot(): lax.dot_general(left, right, (((1,), (1,)), ((), ())), preferred_element_...  7.86 us
    ppermute x1, starting transfers between devices, shards(): arrived = lax.ppermute(cells, 'role', [(SOLVER, TRAINER)])  6.6 us
    dot_general x3, matrix products, dot(): return jnp.dot(left, right, preferred_element_type=F32)  5.08 us
  transfers between devices with their start and end apart: 43, of which 20 were waited for; matrix products, arithmetic and copies ran while one was open for 24% of the time, Pallas kernels for 0%

profile of v1, /device:TPU:0, one launch (start us, length us, event | category | flops | bytes accessed | tf_op | source)
XLA Modules:
  0.0 223.5 jit_solution(5694366245565903099)
XLA Ops:
  0.6 1.4 copy.55
  2.1 3.1 %collective-permute-start = (f32[2,8,4,128]{3,1,2,0:T(8,128)S(1)}, f32[2,8,4,128]{3,1,2,0:T(8,128)S(1)}, u32[]{:S(2)}, u32[]{:S(2)}) collective-permute-start(f32[2,8,4,128]{3,1,2,0:T(8,128)S(1)} %get-tuple-element.58), channel_id=1, source_target_pairs={{0,4},{4,8},{8,12},{12,0},{1,5},{5,9},{9,13},{13,1},{2,6},{6,10},{... | collective-permute-start | bytes 98312 | tf_op jit(solution)/shard_map/ppermute | solution.py:64
  5.1 2.1 collective-permute-start.1
  7.3 1.4 convert_element_type.99
  9.6 1.8 slice.354
  11.3 4.2 %collective-permute-start.5 = (bf16[16,4096]{1,0:T(8,128)(2,1)S(1)}, bf16[16,4096]{1,0:T(8,128)(2,1)}, u32[]{:S(2)}, u32[]{:S(2)}) collective-permute-start(bf16[16,4096]{1,0:T(8,128)(2,1)S(1)} %slice.354), channel_id=1, source_target_pairs={{0,16},{1,17},{2,18},{3,19},{4,20},{5,21},{6,22},{7,23},{8,24},{9,... | collective-permute-start | bytes 393224 | tf_op jit(solution)/shard_map/ppermute | solution.py:169
  17.9 2.0 copy.24
  20.8 1.7 collective-permute-start.3
  25.1 1.8 slice.352
  26.9 1.5 collective-permute-start.17
  41.4 6.6 %collective-permute-start.4 = (f32[2,8,64,128]{3,2,1,0:T(8,128)S(1)}, f32[2,8,64,128]{3,2,1,0:T(8,128)S(1)}, u32[]{:S(2)}, u32[]{:S(2)}) collective-permute-start(f32[2,8,64,128]{3,2,1,0:T(8,128)S(1)} %copy.28), channel_id=1, source_target_pairs={{0,16},{1,17},{2,18},{3,19},{4,20},{5,21},{6,22},{7,23},{8,24},{9,... | collective-permute-start | bytes 1572872 | tf_op jit(solution)/shard_map/ppermute | solution.py:177
  48.1 2.1 broadcast_select_fusion.2
  50.2 3.0 %collective-permute-done.17 = bf16[256,1024]{1,0:T(8,128)(2,1)} collective-permute-done((bf16[256,1024]{1,0:T(8,128)(2,1)}, bf16[256,1024]{1,0:T(8,128)(2,1)}, u32[]{:S(2)}, u32[]{:S(2)}) %collective-permute-start.17) | collective-permute-done | bytes 524320 | tf_op jit(solution)/shard_map/ppermute | solution.py:144
  53.2 2.3 %broadcast_select_fusion = (bf16[256,1024]{1,0:T(8,128)(2,1)}, bf16[256,1024]{1,0:T(8,128)(2,1)}) fusion(bf16[256,1024]{1,0:T(8,128)(2,1)} %collective-permute-done.17, pred[]{:T(512)S(6)} %eq.44, bf16[1,2,256,1024]{3,2,1,0:T(8,128)(2,1)S(1)} %copy-done, bf16[256,1024]{1,0:T(8,128)(2,1)} %collective-permute-done.12), kind=kLoop, calls=%fused_computation.217 | loop fusion | flops 524288 | bytes 3145729 | tf_op jit(solution)/shard_map/jit(_where)/select_n | solution.py:144
  55.4 2.0 collective-permute-start.18
  57.5 1.7 collective-permute-done.4
  60.4 1.6 reshape.47
  64.7 1.5 collective-permute-start.25
  66.3 2.2 collective-permute-done.6
  70.7 8.7 %collective-permute-done.13 = bf16[256,1024]{1,0:T(8,128)(2,1)} collective-permute-done((bf16[256,1024]{1,0:T(8,128)(2,1)}, bf16[256,1024]{1,0:T(8,128)(2,1)}, u32[]{:S(2)}, u32[]{:S(2)}) %collective-permute-start.13) | collective-permute-done | bytes 524320 | tf_op jit(solution)/shard_map/ppermute | solution.py:34
  80.9 7.2 %collective-permute-done.7 = bf16[32,2048]{1,0:T(8,128)(2,1)S(1)} collective-permute-done((bf16[32,2048]{1,0:T(8,128)(2,1)S(1)}, bf16[32,2048]{1,0:T(8,128)(2,1)S(1)}, u32[]{:S(2)}, u32[]{:S(2)}) %collective-permute-start.7) | collective-permute-done | bytes 131104 | tf_op jit(solution)/shard_map/ppermute | solution.py:34
  88.1 2.0 fusion.185
  92.4 2.0 collective-permute-done.11
  94.4 1.7 fusion.186
  96.1 3.5 %collective-permute-start.15 = (bf16[64,2048]{1,0:T(8,128)(2,1)S(1)}, bf16[64,2048]{1,0:T(8,128)(2,1)S(1)}, u32[]{:S(2)}, u32[]{:S(2)}) collective-permute-start(bf16[64,2048]{1,0:T(8,128)(2,1)S(1)} %get-tuple-element.90), channel_id=1, source_target_pairs={{0,8},{4,12},{8,0},{12,4},{1,9},{5,13},{9,1},{13,5},{2,10},{6,14},... | collective-permute-start | bytes 786440 | tf_op jit(solution)/shard_map/ppermute | solution.py:34
  99.9 10.3 %collective-permute-done.16 = f32[64,1]{0,1:T(1,128)S(1)} collective-permute-done((f32[64,1]{0,1:T(1,128)S(1)}, f32[64,1]{0,1:T(1,128)S(1)}, u32[]{:S(2)}, u32[]{:S(2)}) %collective-permute-start.16) | collective-permute-done | bytes 288 | tf_op jit(solution)/shard_map/ppermute | solution.py:34
  110.5 2.0 fusion.187
  113.8 3.0 %collective-permute-done.20 = bf16[64,512]{1,0:T(8,128)(2,1)S(1)} collective-permute-done((bf16[64,512]{1,0:T(8,128)(2,1)S(1)}, bf16[64,512]{1,0:T(8,128)(2,1)S(1)}, u32[]{:S(2)}, u32[]{:S(2)}) %collective-permute-start.20) | collective-permute-done | bytes 65568 | tf_op jit(solution)/shard_map/ppermute | solution.py:34
  116.8 1.7 fusion.188
  118.7 2.6 %collective-permute-done.38 = bf16[128,1024]{1,0:T(8,128)(2,1)S(1)} collective-permute-done((bf16[128,1024]{1,0:T(8,128)(2,1)S(1)}, bf16[128,1024]{1,0:T(8,128)(2,1)S(1)}, u32[]{:S(2)}, u32[]{:S(2)}) %collective-permute-start.38) | collective-permute-done | bytes 262176 | tf_op jit(solution)/shard_map/ppermute | solution.py:34
  121.4 8.8 %collective-permute-done.24 = bf16[64,2048]{1,0:T(8,128)(2,1)S(1)} collective-permute-done((bf16[64,2048]{1,0:T(8,128)(2,1)S(1)}, bf16[64,2048]{1,0:T(8,128)(2,1)S(1)}, u32[]{:S(2)}, u32[]{:S(2)}) %collective-permute-start.24) | collective-permute-done | bytes 262176 | tf_op jit(solution)/shard_map/ppermute | solution.py:34
  130.3 2.0 fusion.189
  132.2 1.4 collective-permute-start.27
  133.7 2.9 %collective-permute-done.27 = bf16[64,512]{1,0:T(8,128)(2,1)S(1)} collective-permute-done((bf16[64,512]{1,0:T(8,128)(2,1)S(1)}, bf16[64,512]{1,0:T(8,128)(2,1)S(1)}, u32[]{:S(2)}, u32[]{:S(2)}) %collective-permute-start.27) | collective-permute-done | bytes 65568 | tf_op jit(solution)/shard_map/ppermute | solution.py:34
  136.6 1.7 fusion.190
  138.5 1.4 collective-permute-done.28
  140.0 10.5 %collective-permute-done.31 = bf16[64,2048]{1,0:T(8,128)(2,1)S(1)} collective-permute-done((bf16[64,2048]{1,0:T(8,128)(2,1)S(1)}, bf16[64,2048]{1,0:T(8,128)(2,1)S(1)}, u32[]{:S(2)}, u32[]{:S(2)}) %collective-permute-start.31) | collective-permute-done | bytes 262176 | tf_op jit(solution)/shard_map/ppermute | solution.py:34
  151.1 1.6 collective-permute-start.33
  152.8 2.0 fusion.191
  155.3 3.8 %collective-permute-done.32 = bf16[64,512]{1,0:T(8,128)(2,1)S(1)} collective-permute-done((bf16[64,512]{1,0:T(8,128)(2,1)S(1)}, bf16[64,512]{1,0:T(8,128)(2,1)S(1)}, u32[]{:S(2)}, u32[]{:S(2)}) %collective-permute-start.32) | collective-permute-done | bytes 65568 | tf_op jit(solution)/shard_map/ppermute | solution.py:34
  163.1 6.8 %collective-permute-done.29 = bf16[128,1280]{1,0:T(8,128)(2,1)S(1)} collective-permute-done((bf16[128,1280]{1,0:T(8,128)(2,1)S(1)}, bf16[128,1280]{1,0:T(8,128)(2,1)S(1)}, u32[]{:S(2)}, u32[]{:S(2)}) %collective-permute-start.29) | collective-permute-done | bytes 327712 | tf_op jit(solution)/shard_map/ppermute | solution.py:34
  170.1 8.2 %collective-permute-done.22 = bf16[128,1536]{1,0:T(8,128)(2,1)S(1)} collective-permute-done((bf16[128,1536]{1,0:T(8,128)(2,1)S(1)}, bf16[128,1536]{1,0:T(8,128)(2,1)S(1)}, u32[]{:S(2)}, u32[]{:S(2)}) %collective-permute-start.22) | collective-permute-done | bytes 393248 | tf_op jit(solution)/shard_map/ppermute | solution.py:34
  178.7 6.3 %collective-permute-done.35 = bf16[128,256]{1,0:T(8,128)(2,1)S(1)} collective-permute-done((bf16[128,256]{1,0:T(8,128)(2,1)S(1)}, bf16[128,256]{1,0:T(8,128)(2,1)S(1)}, u32[]{:S(2)}, u32[]{:S(2)}) %collective-permute-start.35) | collective-permute-done | bytes 65568 | tf_op jit(solution)/shard_map/ppermute | solution.py:34
  186.0 2.1 collective-permute-start.42
  188.1 19.3 %collective-permute-done.36 = bf16[256,256]{1,0:T(8,128)(2,1)S(1)} collective-permute-done((bf16[256,256]{1,0:T(8,128)(2,1)S(1)}, bf16[256,256]{1,0:T(8,128)(2,1)S(1)}, u32[]{:S(2)}, u32[]{:S(2)}) %collective-permute-start.36) | collective-permute-done | bytes 131104 | tf_op jit(solution)/shard_map/ppermute | solution.py:34
  208.4 8.5 %collective-permute-done.42 = bf16[256,1024]{1,0:T(8,128)(2,1)S(1)} collective-permute-done((bf16[256,1024]{1,0:T(8,128)(2,1)S(1)}, bf16[256,1024]{1,0:T(8,128)(2,1)S(1)}, u32[]{:S(2)}, u32[]{:S(2)}) %collective-permute-start.42) | collective-permute-done | bytes 524320 | tf_op jit(solution)/shard_map/ppermute | solution.py:34
  218.5 2.3 %subtract_convert_fusion = (bf16[1,2,256,1024]{3,2,1,0:T(8,128)(2,1)}, f32[1,2,256,1024]{3,2,1,0:T(8,128)}) fusion(bf16[1,2,256,1024]{3,2,1,0:T(8,128)(2,1)S(1)} %copy-done, f32[1,256,1024]{2,1,0:T(8,128)S(1)} %convolution_bitcast_fusion, f32[1,256,1024]{2,1,0:T(8,128)S(1)} %convolution_bitcast_fusion.1, f32[1,2,256,1024]{3,2,1,0:T(8,128)S(1)} %copy-done.5), kind=kLoop, calls=%fused_computation.52 | loop fusion | flops 3670016 | bytes 8388608 | tf_op jit(solution)/shard_map/convert_element_type | solution.py:246
  220.8 2.7 %subtract_convert_fusion.1 = (bf16[1,256,1024]{2,1,0:T(8,128)(2,1)}, f32[1,256,1024]{2,1,0:T(8,128)}) fusion(bf16[1,256,1024]{2,1,0:T(8,128)(2,1)} %param.6, f32[256,1024]{1,0:T(8,128)S(1)} %fusion.30, bf16[512,1280]{1,0:T(8,128)(2,1)S(1)} %pad_maximum_fusion.3, bf16[256,1536]{1,0:T(8,128)(2,1)S(1)} %collective-permute-done.23, ...), kind=kOutput, calls=%fused_computation.121 | convolution fusion | flops 271319040 | bytes 6815744 | tf_op jit(solution)/shard_map/dot_general | solution.py:123
  (163 shorter events, 41.2 us)
Async XLA Ops:
  0.6 6.6 %copy-start.3 = (f32[1,2,8,64,128]{4,3,2,1,0:T(8,128)S(1)}, f32[1,2,8,64,128]{4,3,2,1,0:T(8,128)}, u32[]{:S(2)}) copy-start(f32[1,2,8,64,128]{4,3,2,1,0:T(8,128)} %param.5) | copy-start | bytes 1572868
  2.1 14.8 %collective-permute-start = (f32[2,8,4,128]{3,1,2,0:T(8,128)S(1)}, f32[2,8,4,128]{3,1,2,0:T(8,128)S(1)}, u32[]{:S(2)}, u32[]{:S(2)}) collective-permute-start(f32[2,8,4,128]{3,1,2,0:T(8,128)S(1)} %get-tuple-element.58), channel_id=1, source_target_pairs={{0,4},{4,8},{8,12},{12,0},{1,5},{5,9},{9,13},{13,1},{2,6},{6,10},{... | collective-permute-start | bytes 98312 | tf_op jit(solution)/shard_map/ppermute | solution.py:64
  5.1 11.7 %collective-permute-start.1 = (f32[2,8,4,128]{3,1,2,0:T(8,128)S(1)}, f32[2,8,4,128]{3,1,2,0:T(8,128)S(1)}, u32[]{:S(2)}, u32[]{:S(2)}) collective-permute-start(f32[2,8,4,128]{3,1,2,0:T(8,128)S(1)} %get-tuple-element.59), channel_id=1, source_target_pairs={{4,0},{8,4},{12,8},{0,12},{5,1},{9,5},{13,9},{1,13},{6,2},{10,6},{... | collective-permute-start | bytes 98312 | tf_op jit(solution)/shard_map/ppermute | solution.py:66
  11.3 36.7 %collective-permute-start.5 = (bf16[16,4096]{1,0:T(8,128)(2,1)S(1)}, bf16[16,4096]{1,0:T(8,128)(2,1)}, u32[]{:S(2)}, u32[]{:S(2)}) collective-permute-start(bf16[16,4096]{1,0:T(8,128)(2,1)S(1)} %slice.354), channel_id=1, source_target_pairs={{0,16},{1,17},{2,18},{3,19},{4,20},{5,21},{6,22},{7,23},{8,24},{9,... | collective-permute-start | bytes 393224 | tf_op jit(solution)/shard_map/ppermute | solution.py:169
  15.6 32.6 %collective-permute-start.8 = (bf16[256,1024]{1,0:T(8,128)(2,1)}, bf16[256,1024]{1,0:T(8,128)(2,1)}, u32[]{:S(2)}, u32[]{:S(2)}) collective-permute-start(bf16[256,1024]{1,0:T(8,128)(2,1)} %bitcast.2), channel_id=1, source_target_pairs={{16,0},{17,1},{18,2},{19,3},{20,4},{21,5},{22,6},{23,7},{24,8},{25... | collective-permute-start | bytes 1572872 | tf_op jit(solution)/shard_map/ppermute | solution.py:144
  17.9 4.6 %copy-start = (bf16[1,2,256,1024]{3,2,1,0:T(8,128)(2,1)S(1)}, bf16[1,2,256,1024]{3,2,1,0:T(8,128)(2,1)}, u32[]{:S(2)}) copy-start(bf16[1,2,256,1024]{3,2,1,0:T(8,128)(2,1)} %param.7) | copy-start | bytes 3145732
  19.9 6.9 %collective-permute-start.2 = (f32[2,8,72,4]{2,1,3,0:T(8,128)}, f32[2,8,72,4]{2,1,3,0:T(8,128)}, u32[]{:S(2)}, u32[]{:S(2)}) collective-permute-start(f32[2,8,72,4]{2,1,3,0:T(8,128)} %copy.24), channel_id=1, source_target_pairs={{0,1},{1,2},{2,3},{3,0},{4,5},{5,6},{6,7},{7,4},{8,9},{9,10},{10,1... | collective-permute-start | bytes 55304 | tf_op jit(solution)/shard_map/ppermute | solution.py:64
  20.8 8.6 %collective-permute-start.3 = (f32[2,8,72,4]{2,1,3,0:T(8,128)}, f32[2,8,72,4]{2,1,3,0:T(8,128)}, u32[]{:S(2)}, u32[]{:S(2)}) collective-permute-start(f32[2,8,72,4]{2,1,3,0:T(8,128)} %copy.25), channel_id=1, source_target_pairs={{1,0},{2,1},{3,2},{0,3},{5,4},{6,5},{7,6},{4,7},{9,8},{10,9},{11,1... | collective-permute-start | bytes 55304 | tf_op jit(solution)/shard_map/ppermute | solution.py:66
  23.6 26.6 %collective-permute-start.12 = (bf16[256,1024]{1,0:T(8,128)(2,1)}, bf16[256,1024]{1,0:T(8,128)(2,1)}, u32[]{:S(2)}, u32[]{:S(2)}) collective-permute-start(bf16[256,1024]{1,0:T(8,128)(2,1)} %get-tuple-element.55), channel_id=1, source_target_pairs={{16,0},{17,1},{18,2},{19,3},{20,4},{21,5},{22,6},{23,7},{24,8},{25... | collective-permute-start | bytes 1572872 | tf_op jit(solution)/shard_map/ppermute | solution.py:144
  26.9 26.3 %collective-permute-start.17 = (bf16[256,1024]{1,0:T(8,128)(2,1)}, bf16[256,1024]{1,0:T(8,128)(2,1)}, u32[]{:S(2)}, u32[]{:S(2)}) collective-permute-start(bf16[256,1024]{1,0:T(8,128)(2,1)} %get-tuple-element.54), channel_id=1, source_target_pairs={{16,0},{17,1},{18,2},{19,3},{20,4},{21,5},{22,6},{23,7},{24,8},{25... | collective-permute-start | bytes 1572872 | tf_op jit(solution)/shard_map/ppermute | solution.py:144
  41.4 17.8 %collective-permute-start.4 = (f32[2,8,64,128]{3,2,1,0:T(8,128)S(1)}, f32[2,8,64,128]{3,2,1,0:T(8,128)S(1)}, u32[]{:S(2)}, u32[]{:S(2)}) collective-permute-start(f32[2,8,64,128]{3,2,1,0:T(8,128)S(1)} %copy.28), channel_id=1, source_target_pairs={{0,16},{1,17},{2,18},{3,19},{4,20},{5,21},{6,22},{7,23},{8,24},{9,... | collective-permute-start | bytes 1572872 | tf_op jit(solution)/shard_map/ppermute | solution.py:177
  50.2 19.2 %collective-permute-start.9 = (bf16[256,1024]{1,0:T(8,128)(2,1)}, bf16[256,1024]{1,0:T(8,128)(2,1)}, u32[]{:S(2)}, u32[]{:S(2)}) collective-permute-start(bf16[256,1024]{1,0:T(8,128)(2,1)} %broadcast_select_fusion.2), channel_id=1, source_target_pairs={{0,4},{4,0},{8,12},{12,8},{1,5},{5,1},{9,13},{13,9},{2,6},{6,2},{1... | collective-permute-start | bytes 1572872 | tf_op jit(solution)/shard_map/ppermute | solution.py:34
  55.4 23.9 %collective-permute-start.13 = (bf16[256,1024]{1,0:T(8,128)(2,1)}, bf16[256,1024]{1,0:T(8,128)(2,1)}, u32[]{:S(2)}, u32[]{:S(2)}) collective-permute-start(bf16[256,1024]{1,0:T(8,128)(2,1)} %get-tuple-element.53), channel_id=1, source_target_pairs={{0,4},{4,0},{8,12},{12,8},{1,5},{5,1},{9,13},{13,9},{2,6},{6,2},{1... | collective-permute-start | bytes 1572872 | tf_op jit(solution)/shard_map/ppermute | solution.py:34
  55.4 35.6 %collective-permute-start.18 = (bf16[256,1024]{1,0:T(8,128)(2,1)}, bf16[256,1024]{1,0:T(8,128)(2,1)}, u32[]{:S(2)}, u32[]{:S(2)}) collective-permute-start(bf16[256,1024]{1,0:T(8,128)(2,1)} %get-tuple-element.52), channel_id=1, source_target_pairs={{0,4},{4,0},{8,12},{12,8},{1,5},{5,1},{9,13},{13,9},{2,6},{6,2},{1... | collective-permute-start | bytes 1572872 | tf_op jit(solution)/shard_map/ppermute | solution.py:34
  64.1 4.3 %collective-permute-start.6 = (bf16[16,2048]{1,0:T(8,128)(2,1)S(1)}, bf16[16,2048]{1,0:T(8,128)(2,1)S(1)}, u32[]{:S(2)}, u32[]{:S(2)}) collective-permute-start(bf16[16,2048]{1,0:T(8,128)(2,1)S(1)} %pad_maximum_fusion.39), channel_id=1, source_target_pairs={{0,2},{1,3},{2,0},{3,1},{4,6},{5,7},{6,4},{7,5},{8,10},{9,11},{10,... | collective-permute-start | bytes 196616 | tf_op jit(solution)/shard_map/ppermute | solution.py:34
  64.7 16.1 %collective-permute-start.25 = (bf16[16,2048]{1,0:T(8,128)(2,1)S(1)}, bf16[16,2048]{1,0:T(8,128)(2,1)S(1)}, u32[]{:S(2)}, u32[]{:S(2)}) collective-permute-start(bf16[16,2048]{1,0:T(8,128)(2,1)S(1)} %pad_maximum_fusion.41), channel_id=1, source_target_pairs={{0,2},{1,3},{2,0},{3,1},{4,6},{5,7},{6,4},{7,5},{8,10},{9,11},{10,... | collective-permute-start | bytes 196616 | tf_op jit(solution)/shard_map/ppermute | solution.py:34
  68.5 19.6 %collective-permute-start.7 = (bf16[32,2048]{1,0:T(8,128)(2,1)S(1)}, bf16[32,2048]{1,0:T(8,128)(2,1)S(1)}, u32[]{:S(2)}, u32[]{:S(2)}) collective-permute-start(bf16[32,2048]{1,0:T(8,128)(2,1)S(1)} %pad_maximum_fusion.34), channel_id=1, source_target_pairs={{0,8},{4,12},{8,0},{12,4},{1,9},{5,13},{9,1},{13,5},{2,10},{6,14},... | collective-permute-start | bytes 393224 | tf_op jit(solution)/shard_map/ppermute | solution.py:34
  70.6 17.5 %collective-permute-start.10 = (bf16[512,1024]{1,0:T(8,128)(2,1)S(1)}, bf16[512,1024]{1,0:T(8,128)(2,1)S(1)}, u32[]{:S(2)}, u32[]{:S(2)}) collective-permute-start(bf16[512,1024]{1,0:T(8,128)(2,1)S(1)} %pad_maximum_fusion.13), channel_id=1, source_target_pairs={{0,1},{1,0},{2,3},{3,2},{4,5},{5,4},{6,7},{7,6},{8,9},{9,8},{10,11... | collective-permute-start | bytes 3145736 | tf_op jit(solution)/shard_map/ppermute | solution.py:34
  80.7 11.7 %collective-permute-start.14 = (bf16[512,1024]{1,0:T(8,128)(2,1)S(1)}, bf16[512,1024]{1,0:T(8,128)(2,1)S(1)}, u32[]{:S(2)}, u32[]{:S(2)}) collective-permute-start(bf16[512,1024]{1,0:T(8,128)(2,1)S(1)} %pad_maximum_fusion.14), channel_id=1, source_target_pairs={{0,1},{1,0},{2,3},{3,2},{4,5},{5,4},{6,7},{7,6},{8,9},{9,8},{10,11... | collective-permute-start | bytes 3145736 | tf_op jit(solution)/shard_map/ppermute | solution.py:34
  80.8 37.8 %collective-permute-start.26 = (bf16[32,2048]{1,0:T(8,128)(2,1)S(1)}, bf16[32,2048]{1,0:T(8,128)(2,1)S(1)}, u32[]{:S(2)}, u32[]{:S(2)}) collective-permute-start(bf16[32,2048]{1,0:T(8,128)(2,1)S(1)} %pad_maximum_fusion.35), channel_id=1, source_target_pairs={{0,8},{4,12},{8,0},{12,4},{1,9},{5,13},{9,1},{13,5},{2,10},{6,14},... | collective-permute-start | bytes 393224 | tf_op jit(solution)/shard_map/ppermute | solution.py:34
  90.1 4.3 %collective-permute-start.11 = (bf16[64,512]{1,0:T(8,128)(2,1)S(1)}, bf16[64,512]{1,0:T(8,128)(2,1)S(1)}, u32[]{:S(2)}, u32[]{:S(2)}) collective-permute-start(bf16[64,512]{1,0:T(8,128)(2,1)S(1)} %get-tuple-element.88), channel_id=1, source_target_pairs={{0,2},{1,3},{2,0},{3,1},{4,6},{5,7},{6,4},{7,5},{8,10},{9,11},{10,... | collective-permute-start | bytes 196616 | tf_op jit(solution)/shard_map/ppermute | solution.py:34
  92.3 18.2 %collective-permute-start.19 = (bf16[512,1024]{1,0:T(8,128)(2,1)S(1)}, bf16[512,1024]{1,0:T(8,128)(2,1)S(1)}, u32[]{:S(2)}, u32[]{:S(2)}) collective-permute-start(bf16[512,1024]{1,0:T(8,128)(2,1)S(1)} %pad_maximum_fusion.15), channel_id=1, source_target_pairs={{0,1},{1,0},{2,3},{3,2},{4,5},{5,4},{6,7},{7,6},{8,9},{9,8},{10,11... | collective-permute-start | bytes 3145736 | tf_op jit(solution)/shard_map/ppermute | solution.py:34
  96.1 14.1 %collective-permute-start.15 = (bf16[64,2048]{1,0:T(8,128)(2,1)S(1)}, bf16[64,2048]{1,0:T(8,128)(2,1)S(1)}, u32[]{:S(2)}, u32[]{:S(2)}) collective-permute-start(bf16[64,2048]{1,0:T(8,128)(2,1)S(1)} %get-tuple-element.90), channel_id=1, source_target_pairs={{0,8},{4,12},{8,0},{12,4},{1,9},{5,13},{9,1},{13,5},{2,10},{6,14},... | collective-permute-start | bytes 786440 | tf_op jit(solution)/shard_map/ppermute | solution.py:34
  99.7 10.5 %collective-permute-start.16 = (f32[64,1]{0,1:T(1,128)S(1)}, f32[64,1]{0,1:T(1,128)S(1)}, u32[]{:S(2)}, u32[]{:S(2)}) collective-permute-start(f32[64,1]{0,1:T(1,128)S(1)} %bitcast.95), channel_id=1, source_target_pairs={{0,8},{4,12},{8,0},{12,4},{1,9},{5,13},{9,1},{13,5},{2,10},{6,14},... | collective-permute-start | bytes 776 | tf_op jit(solution)/shard_map/ppermute | solution.py:34
  99.8 13.9 %collective-permute-start.37 = (bf16[64,1024]{1,0:T(8,128)(2,1)S(1)}, bf16[64,1024]{1,0:T(8,128)(2,1)S(1)}, u32[]{:S(2)}, u32[]{:S(2)}) collective-permute-start(bf16[64,1024]{1,0:T(8,128)(2,1)S(1)} %get-tuple-element.69), channel_id=1, source_target_pairs={{0,1},{1,0},{2,3},{3,2},{4,5},{5,4},{6,7},{7,6},{8,9},{9,8},{10,11... | collective-permute-start | bytes 393224 | tf_op jit(solution)/shard_map/ppermute | solution.py:34
  112.5 4.3 %collective-permute-start.20 = (bf16[64,512]{1,0:T(8,128)(2,1)S(1)}, bf16[64,512]{1,0:T(8,128)(2,1)S(1)}, u32[]{:S(2)}, u32[]{:S(2)}) collective-permute-start(bf16[64,512]{1,0:T(8,128)(2,1)S(1)} %get-tuple-element.92), channel_id=1, source_target_pairs={{0,2},{1,3},{2,0},{3,1},{4,6},{5,7},{6,4},{7,5},{8,10},{9,11},{10,... | collective-permute-start | bytes 196616 | tf_op jit(solution)/shard_map/ppermute | solution.py:34
  113.7 7.5 %collective-permute-start.38 = (bf16[128,1024]{1,0:T(8,128)(2,1)S(1)}, bf16[128,1024]{1,0:T(8,128)(2,1)S(1)}, u32[]{:S(2)}, u32[]{:S(2)}) collective-permute-start(bf16[128,1024]{1,0:T(8,128)(2,1)S(1)} %pad_maximum_fusion.30), channel_id=1, source_target_pairs={{0,4},{4,0},{8,12},{12,8},{1,5},{5,1},{9,13},{13,9},{2,6},{6,2},{1... | collective-permute-start | bytes 786440 | tf_op jit(solution)/shard_map/ppermute | solution.py:34
  118.5 11.6 %collective-permute-start.24 = (bf16[64,2048]{1,0:T(8,128)(2,1)S(1)}, bf16[64,2048]{1,0:T(8,128)(2,1)S(1)}, u32[]{:S(2)}, u32[]{:S(2)}) collective-permute-start(bf16[64,2048]{1,0:T(8,128)(2,1)S(1)} %get-tuple-element.94), channel_id=1, source_target_pairs={{0,8},{4,12},{8,0},{12,4},{1,9},{5,13},{9,1},{13,5},{2,10},{6,14},... | collective-permute-start | bytes 786440 | tf_op jit(solution)/shard_map/ppermute | solution.py:34
  121.3 66.8 %collective-permute-start.39 = (bf16[256,1024]{1,0:T(8,128)(2,1)S(1)}, bf16[256,1024]{1,0:T(8,128)(2,1)S(1)}, u32[]{:S(2)}, u32[]{:S(2)}) collective-permute-start(bf16[256,1024]{1,0:T(8,128)(2,1)S(1)} %pad_maximum_fusion.25), channel_id=1, source_target_pairs={{0,16},{16,0},{1,17},{17,1},{2,18},{18,2},{3,19},{19,3},{4,20},{20... | collective-permute-start | bytes 1572872 | tf_op jit(solution)/shard_map/ppermute | solution.py:34
  132.2 4.3 %collective-permute-start.27 = (bf16[64,512]{1,0:T(8,128)(2,1)S(1)}, bf16[64,512]{1,0:T(8,128)(2,1)S(1)}, u32[]{:S(2)}, u32[]{:S(2)}) collective-permute-start(bf16[64,512]{1,0:T(8,128)(2,1)S(1)} %get-tuple-element.96), channel_id=1, source_target_pairs={{0,2},{1,3},{2,0},{3,1},{4,6},{5,7},{6,4},{7,5},{8,10},{9,11},{10,... | collective-permute-start | bytes 196616 | tf_op jit(solution)/shard_map/ppermute | solution.py:34
  138.3 12.2 %collective-permute-start.31 = (bf16[64,2048]{1,0:T(8,128)(2,1)S(1)}, bf16[64,2048]{1,0:T(8,128)(2,1)S(1)}, u32[]{:S(2)}, u32[]{:S(2)}) collective-permute-start(bf16[64,2048]{1,0:T(8,128)(2,1)S(1)} %get-tuple-element.98), channel_id=1, source_target_pairs={{0,8},{4,12},{8,0},{12,4},{1,9},{5,13},{9,1},{13,5},{2,10},{6,14},... | collective-permute-start | bytes 786440 | tf_op jit(solution)/shard_map/ppermute | solution.py:34
  138.4 1.5 collective-permute-start.28
  139.9 11.2 %copy-start.1 = (bf16[128,1536]{1,0:T(8,128)(2,1)}, bf16[128,1536]{1,0:T(8,128)(2,1)S(1)}, u32[]{:S(2)}) copy-start(bf16[128,1536]{1,0:T(8,128)(2,1)S(1)} %pad_maximum_fusion.27) | copy-start | bytes 1179652
  151.1 4.1 %collective-permute-start.33 = (f32[64,1]{0,1:T(1,128)S(1)}, f32[64,1]{0,1:T(1,128)S(1)}, u32[]{:S(2)}, u32[]{:S(2)}) collective-permute-start(f32[64,1]{0,1:T(1,128)S(1)} %bitcast.96), channel_id=1, source_target_pairs={{0,2},{1,3},{2,0},{3,1},{4,6},{5,7},{6,4},{7,5},{8,10},{9,11},{10,... | collective-permute-start | bytes 776 | tf_op jit(solution)/shard_map/ppermute | solution.py:34
  154.7 4.6 %copy-start.2 = (bf16[128,1536]{1,0:T(8,128)(2,1)S(1)}, bf16[128,1536]{1,0:T(8,128)(2,1)}, u32[]{:S(2)}) copy-start(bf16[128,1536]{1,0:T(8,128)(2,1)} %copy-done.1) | copy-start | bytes 1179652
  154.7 4.3 %collective-permute-start.32 = (bf16[64,512]{1,0:T(8,128)(2,1)S(1)}, bf16[64,512]{1,0:T(8,128)(2,1)S(1)}, u32[]{:S(2)}, u32[]{:S(2)}) collective-permute-start(bf16[64,512]{1,0:T(8,128)(2,1)S(1)} %get-tuple-element.100), channel_id=1, source_target_pairs={{0,2},{1,3},{2,0},{3,1},{4,6},{5,7},{6,4},{7,5},{8,10},{9,11},{10,... | collective-permute-start | bytes 196616 | tf_op jit(solution)/shard_map/ppermute | solution.py:34
  159.2 1.6 collective-permute-start.21
  159.4 10.6 %collective-permute-start.29 = (bf16[128,1280]{1,0:T(8,128)(2,1)S(1)}, bf16[128,1280]{1,0:T(8,128)(2,1)S(1)}, u32[]{:S(2)}, u32[]{:S(2)}) collective-permute-start(bf16[128,1280]{1,0:T(8,128)(2,1)S(1)} %fusion.119), channel_id=1, source_target_pairs={{0,4},{4,0},{8,12},{12,8},{1,5},{5,1},{9,13},{13,9},{2,6},{6,2},{1... | collective-permute-start | bytes 983048 | tf_op jit(solution)/shard_map/ppermute | solution.py:34
  159.5 2.8 %collective-permute-start.40 = (bf16[64,1024]{1,0:T(8,128)(2,1)S(1)}, bf16[64,1024]{1,0:T(8,128)(2,1)S(1)}, u32[]{:S(2)}, u32[]{:S(2)}) collective-permute-start(bf16[64,1024]{1,0:T(8,128)(2,1)S(1)} %get-tuple-element.61), channel_id=1, source_target_pairs={{0,1},{1,0},{2,3},{3,2},{4,5},{5,4},{6,7},{7,6},{8,9},{9,8},{10,11... | collective-permute-start | bytes 393224 | tf_op jit(solution)/shard_map/ppermute | solution.py:34
  160.0 18.5 %collective-permute-start.34 = (bf16[64,512]{1,0:T(8,128)(2,1)S(1)}, bf16[64,512]{1,0:T(8,128)(2,1)S(1)}, u32[]{:S(2)}, u32[]{:S(2)}) collective-permute-start(bf16[64,512]{1,0:T(8,128)(2,1)S(1)} %get-tuple-element.73), channel_id=1, source_target_pairs={{0,1},{1,0},{2,3},{3,2},{4,5},{5,4},{6,7},{7,6},{8,9},{9,8},{10,11... | collective-permute-start | bytes 196616 | tf_op jit(solution)/shard_map/ppermute | solution.py:34
  160.9 17.4 %collective-permute-start.22 = (bf16[128,1536]{1,0:T(8,128)(2,1)S(1)}, bf16[128,1536]{1,0:T(8,128)(2,1)S(1)}, u32[]{:S(2)}, u32[]{:S(2)}) collective-permute-start(bf16[128,1536]{1,0:T(8,128)(2,1)S(1)} %fusion.112), channel_id=1, source_target_pairs={{0,4},{4,0},{8,12},{12,8},{1,5},{5,1},{9,13},{13,9},{2,6},{6,2},{1... | collective-permute-start | bytes 1179656 | tf_op jit(solution)/shard_map/ppermute | solution.py:34
  162.3 23.7 %collective-permute-start.41 = (bf16[128,1024]{1,0:T(8,128)(2,1)S(1)}, bf16[128,1024]{1,0:T(8,128)(2,1)S(1)}, u32[]{:S(2)}, u32[]{:S(2)}) collective-permute-start(bf16[128,1024]{1,0:T(8,128)(2,1)S(1)} %pad_maximum_fusion.31), channel_id=1, source_target_pairs={{0,4},{4,0},{8,12},{12,8},{1,5},{5,1},{9,13},{13,9},{2,6},{6,2},{1... | collective-permute-start | bytes 786440 | tf_op jit(solution)/shard_map/ppermute | solution.py:34
  170.0 37.9 %collective-permute-start.30 = (bf16[256,1280]{1,0:T(8,128)(2,1)S(1)}, bf16[256,1280]{1,0:T(8,128)(2,1)S(1)}, u32[]{:S(2)}, u32[]{:S(2)}) collective-permute-start(bf16[256,1280]{1,0:T(8,128)(2,1)S(1)} %pad_maximum_fusion.21), channel_id=1, source_target_pairs={{0,16},{16,0},{1,17},{17,1},{2,18},{18,2},{3,19},{19,3},{4,20},{20... | collective-permute-start | bytes 1966088 | tf_op jit(solution)/shard_map/ppermute | solution.py:34
  170.1 15.0 %copy-start.4 = (f32[2,8,64,128]{3,1,2,0:T(8,128)S(1)}, f32[2,8,64,128]{3,1,2,0:T(8,128)}, u32[]{:S(2)}) copy-start(f32[2,8,64,128]{3,1,2,0:T(8,128)} %get-tuple-element.27) | copy-start | bytes 1572868
  178.4 29.5 %collective-permute-start.23 = (bf16[256,1536]{1,0:T(8,128)(2,1)S(1)}, bf16[256,1536]{1,0:T(8,128)(2,1)S(1)}, u32[]{:S(2)}, u32[]{:S(2)}) collective-permute-start(bf16[256,1536]{1,0:T(8,128)(2,1)S(1)} %pad_maximum_fusion.20), channel_id=1, source_target_pairs={{0,16},{16,0},{1,17},{17,1},{2,18},{18,2},{3,19},{19,3},{4,20},{20... | collective-permute-start | bytes 2359304 | tf_op jit(solution)/shard_map/ppermute | solution.py:34
  178.5 6.5 %collective-permute-start.35 = (bf16[128,256]{1,0:T(8,128)(2,1)S(1)}, bf16[128,256]{1,0:T(8,128)(2,1)S(1)}, u32[]{:S(2)}, u32[]{:S(2)}) collective-permute-start(bf16[128,256]{1,0:T(8,128)(2,1)S(1)} %get-tuple-element.75), channel_id=1, source_target_pairs={{0,4},{4,0},{8,12},{12,8},{1,5},{5,1},{9,13},{13,9},{2,6},{6,2},{1... | collective-permute-start | bytes 196616 | tf_op jit(solution)/shard_map/ppermute | solution.py:34
  185.0 22.4 %collective-permute-start.36 = (bf16[256,256]{1,0:T(8,128)(2,1)S(1)}, bf16[256,256]{1,0:T(8,128)(2,1)S(1)}, u32[]{:S(2)}, u32[]{:S(2)}) collective-permute-start(bf16[256,256]{1,0:T(8,128)(2,1)S(1)} %pad_maximum_fusion.36), channel_id=1, source_target_pairs={{0,16},{16,0},{1,17},{17,1},{2,18},{18,2},{3,19},{19,3},{4,20},{20... | collective-permute-start | bytes 393224 | tf_op jit(solution)/shard_map/ppermute | solution.py:34
  186.0 30.9 %collective-permute-start.42 = (bf16[256,1024]{1,0:T(8,128)(2,1)S(1)}, bf16[256,1024]{1,0:T(8,128)(2,1)S(1)}, u32[]{:S(2)}, u32[]{:S(2)}) collective-permute-start(bf16[256,1024]{1,0:T(8,128)(2,1)S(1)} %pad_maximum_fusion.26), channel_id=1, source_target_pairs={{0,16},{16,0},{1,17},{17,1},{2,18},{18,2},{3,19},{19,3},{4,20},{20... | collective-permute-start | bytes 1572872 | tf_op jit(solution)/shard_map/ppermute | solution.py:34
  (3 other events, 8.5 us)

commit v2 on v0

v2 whole, which is shorter than its diff:
```python
import jax
import jax.numpy as jnp
from jax import lax
from jax.experimental import pallas as pl
from jax.experimental.pallas import tpu as pltpu
from jax.sharding import PartitionSpec as P

PATCH = 16
STEPS = 4


SUBSTRATE_DIFFUSION = 0.2
CATALYST_DIFFUSION = 0.1
FEED_RATE = 0.037
KILL_RATE = 0.06
TIME_STEP = 0.8
GELU_FACTOR = 0.7978845608028654
MOMENTUM_DECAY = 0.9
LEARNING_RATE = 0.003

SOLVER, TRAINER = 0, 1
BF16 = jnp.bfloat16
F32 = jnp.float32


class Digit:
    def __init__(self, axis, stride, size):
        self.axis, self.stride, self.size = axis, stride, size

    def shifted(self, value, step):
        pairs = []
        for index in range(lax.axis_size(self.axis)):
            digit = index // self.stride % self.size
            pairs.append((index, index + ((digit + step) % self.size - digit) * self.stride))
        return lax.ppermute(value, self.axis, pairs)

    def from_others(self, value):
        return [self.shifted(value, k) for k in range(1, self.size)]


def rows_dot(left, right):
    return lax.dot_general(left, right, (((1,), (1,)), ((), ())), preferred_element_type=F32)


def cols_dot(left, right):
    return lax.dot_general(left, right, (((0,), (0,)), ((), ())), preferred_element_type=F32)


def dot(left, right):
    return jnp.dot(left, right, preferred_element_type=F32)


def struct(shape, dtype):
    return jax.ShapeDtypeStruct(shape, dtype)


TOKEN = (8, 128)
CHEAP = pl.CostEstimate(flops=1, transcendentals=0, bytes_accessed=1)


class Work:
    def __init__(self, body, outs, args, in_hbm=(), scratch=(), aliases=None, extra=(), left=()):
        self.body, self.outs, self.args = body, list(outs), list(args)
        self.in_hbm, self.scratch, self.aliases = in_hbm, list(scratch), aliases or {}
        self.extra, self.left, self.results = list(extra), left, None


class Order:
    def __init__(self):
        self.token, self.pending, self.riders = None, [], []

    def wait_for(self, arrays):
        self.pending = self.pending + list(arrays)

    def ride(self, *args, **kwargs):
        self.riders.append(Work(*args, **kwargs))
        return self.riders[-1]

    def run(self, name):
        last = self.riders.pop()
        last.results = self.call(
            last.body,
            name,
            last.outs,
            last.args,
            in_hbm=last.in_hbm,
            scratch=last.scratch,
            left=last.left,
        )

    def call(self, body, name, outs, args, **kwargs):
        works = self.riders + [Work(body, outs, args, **kwargs)]
        after = ([] if self.token is None else [self.token]) + self.pending
        self.pending, self.riders = [], []
        vmem, anywhere = pl.BlockSpec(memory_space=pltpu.VMEM), pl.BlockSpec(memory_space=pl.ANY)
        args, in_specs, outs, out_specs, scratch, aliases, room = [], [], [], [], [], {}, 0
        spans = []
        for work in works:
            spans.append((len(args), len(outs), len(scratch)))
            for index, target in work.aliases.items():
                aliases[len(args) + index] = len(outs) + target
            for k, value in enumerate(work.args):
                in_specs.append(anywhere if k in work.left else vmem)
                room += 0 if k in work.left else value.size * value.dtype.itemsize
            for k, value in enumerate(work.outs):
                out_specs.append(anywhere if k in work.in_hbm else vmem)
                room += 0 if k in work.in_hbm else value.size * value.dtype.itemsize
            in_specs += [anywhere] * len(work.extra)
            args += work.args + work.extra
            outs += work.outs
            scratch += work.scratch
        in_count, out_count = len(args) + len(after), len(outs) + 1

        def kernel(*refs):
            ins, outs_refs, scratch_refs = (
                refs[:in_count],
                refs[in_count : in_count + out_count],
                refs[in_count + out_count :],
            )
            outs_refs[-1][...] = jnp.zeros(TOKEN, F32)
            for work, (first, out, extra) in zip(works, spans):
                work.body(
                    ins[first : first + len(work.args)],
                    outs_refs[out : out + len(work.outs)],
                    scratch_refs[extra : extra + len(work.scratch)],
                )

        *results, self.token = pl.pallas_call(
            kernel,
            name=name,
            out_shape=outs + [struct(TOKEN, F32)],
            in_specs=in_specs + [anywhere] * len(after),
            out_specs=out_specs + [vmem],
            scratch_shapes=scratch,
            input_output_aliases=aliases,
            compiler_params=pltpu.CompilerParams(
                vmem_limit_bytes=min(56 * 2**20, room + 12 * 2**20)
            ),
            cost_estimate=CHEAP,
        )(*args, *after)
        for work, (_, out, _) in zip(works, spans):
            work.results = results[out : out + len(work.outs)]
        return works[-1].results


class Matrix:
    def __init__(self, pieces):
        self.pieces = pieces
        self.row_count, self.col_count = len(pieces), len(pieces[0])
        self.flat = [piece for row in pieces for piece in row]
        self.rows = sum(row[0].shape[0] for row in pieces)
        self.cols = sum(piece.shape[1] for piece in pieces[0])

    def grid(self, refs):
        return [
            refs[index * self.col_count : (index + 1) * self.col_count]
            for index in range(self.row_count)
        ]

    def to_width(self, refs, value):
        done = []
        for row in self.grid(refs):
            total, first = None, 0
            for ref in row:
                term = rows_dot(value[:, first : first + ref.shape[1]], ref[...])
                total = term if total is None else total + term
                first += ref.shape[1]
            done.append(total)
        return jnp.concatenate(done, axis=1) if len(done) > 1 else done[0]

    def to_cols(self, refs, value):
        done = []
        for col in range(self.col_count):
            total, first = None, 0
            for row in self.grid(refs):
                ref = row[col]
                term = dot(value[:, first : first + ref.shape[0]], ref[...])
                total = term if total is None else total + term
                first += ref.shape[0]
            done.append(total)
        return jnp.concatenate(done, axis=1) if len(done) > 1 else done[0]


LANES = 128


def with_scalars(value, column):
    high = column.astype(BF16).astype(F32)
    low = column - high
    lane = lax.broadcasted_iota(jnp.int32, (value.shape[0], LANES), 1)
    extra = jnp.where(lane == 0, high, jnp.where(lane == 1, low, 0.0))
    return jnp.concatenate([value.astype(BF16), extra.astype(BF16)], axis=1)


def scalars_of(received):
    extra = received[:, received.shape[1] - LANES :].astype(F32)
    return jnp.sum(extra, axis=1, keepdims=True)


def swapped_tiles(cells):
    count = cells.shape[0]
    row = lax.broadcasted_iota(jnp.int32, cells.shape, 0)
    run = lax.broadcasted_iota(jnp.int32, cells.shape, 1) // PATCH
    for bit in (1, 2, 4):
        row_set, run_set = (row & bit) != 0, (run & bit) != 0
        moved = jnp.where(
            row_set, pltpu.roll(cells, bit, 0), pltpu.roll(cells, count - bit, 0)
        )
        shift = bit * PATCH
        moved = jnp.where(
            run_set, pltpu.roll(moved, shift, 1), pltpu.roll(moved, LANES - shift, 1)
        )
        cells = jnp.where(row_set == run_set, cells, moved)
    return cells


def write_patches(tile, outs):
    bands = len(outs)
    species, planes = tile.counts
    for s in range(species):
        for p in range(planes):
            plane = swapped_tiles(tile(s, p))
            octets = PATCH // 8
            groups = plane.shape[0] // PATCH
            each = groups // bands
            for o in range(octets):
                col = ((s * planes + p) * octets + o) * LANES
                for index, out in enumerate(outs):
                    rows = [
                        plane[(g * octets + o) * 8 : (g * octets + o + 1) * 8]
                        for g in range(index * each, (index + 1) * each)
                    ]
                    out[:, col : col + LANES] = jnp.concatenate(rows, axis=0).astype(BF16)


class Tile:
    def __init__(self, read, counts):
        self.read, self.counts = read, counts

    def __call__(self, s, p):
        return self.read(s, p)


def packed_edges(order, cells, head_rows, tail_rows, width):
    species, planes, rows, _ = cells.shape
    tall = rows + 2 * width

    def body(ins, outs, _):
        middle, head, tail = ins
        lane = lax.broadcasted_iota(jnp.int32, (tall, LANES), 1)
        total = jnp.zeros((tall, LANES), F32)
        for s in range(species):
            for p in range(planes):
                plane = jnp.concatenate([head[s, p], middle[s, p], tail[s, p]], axis=0)
                slot = (s * planes + p) * width
                first = plane if slot == 0 else pltpu.roll(plane, slot, 1)
                last = pltpu.roll(plane, (LANES // 2 + slot + width) % LANES, 1)
                total = jnp.where((lane >= slot) & (lane < slot + width), first, total)
                start = LANES // 2 + slot
                total = jnp.where((lane >= start) & (lane < start + width), last, total)
        outs[0][...] = total

    return order.ride(body, [struct((tall, LANES), F32)], [cells, head_rows, tail_rows])


def stepped(order, cells, head_rows, tail_rows, from_left, from_right, width, halves):
    species, planes, rows, cols = cells.shape
    tall = rows + 2 * width
    patch_rows = rows // PATCH * (cols // PATCH) // halves
    features = species * planes * PATCH * PATCH

    def body(ins, outs, scratch):
        middle, head, tail, left, right = ins
        (final, *patches), (now, later) = outs, scratch
        lane = lax.broadcasted_iota(jnp.int32, (tall, LANES), 1)
        from_l, from_r = left[...], right[...]
        for s in range(species):
            for p in range(planes):
                slot = (s * planes + p) * width
                now[0, s, p] = jnp.concatenate([head[s, p], middle[s, p], tail[s, p]], axis=0)
                ahead = from_r if slot == 0 else pltpu.roll(from_r, LANES - slot, 1)
                behind = pltpu.roll(from_l, LANES // 2 - slot - width, 1)
                halo = jnp.where(lane < width, ahead, 0.0)
                now[1, s, p] = jnp.where(lane >= LANES - width, behind, halo)

        def neighbours(field, halo):
            up_f, down_f = pltpu.roll(field, 1, 0), pltpu.roll(field, tall - 1, 0)
            up_h, down_h = pltpu.roll(halo, 1, 0), pltpu.roll(halo, tall - 1, 0)
            before_f, before_h = pltpu.roll(field, 1, 1), pltpu.roll(halo, 1, 1)
            after_f, after_h = pltpu.roll(field, LANES - 1, 1), pltpu.roll(halo, LANES - 1, 1)
            first, last = lane == 0, lane == LANES - 1
            sum_f = up_f + down_f + jnp.where(first, before_h, before_f)
            sum_f = sum_f + jnp.where(last, after_h, after_f)
            sum_h = up_h + down_h + jnp.where(first, before_f, before_h)
            sum_h = sum_h + jnp.where(last, after_f, after_h)
            return sum_f, sum_h

        for step in range(STEPS):
            source, target = (now, later) if step % 2 == 0 else (later, now)

            def one_plane(p, carry):
                below, above = jnp.maximum(p - 1, 0), jnp.minimum(p + 1, planes - 1)
                beside = [neighbours(source[0, s, p], source[1, s, p]) for s in range(2)]
                for layer in range(2):
                    u, v = source[layer, 0, p], source[layer, 1, p]
                    lap = []
                    for s, centre in ((0, u), (1, v)):
                        total = source[layer, s, below] + source[layer, s, above]
                        lap.append(total + beside[s][layer] - 6.0 * centre)
                    growth = u * v * v
                    target[layer, 0, p] = u + TIME_STEP * (
                        SUBSTRATE_DIFFUSION * lap[0] - growth + FEED_RATE * (1.0 - u)
                    )
                    target[layer, 1, p] = v + TIME_STEP * (
                        CATALYST_DIFFUSION * lap[1] + growth - (FEED_RATE + KILL_RATE) * v
                    )
                return carry

            lax.fori_loop(0, planes, one_plane, 0)
        source = now if STEPS % 2 == 0 else later
        for s in range(species):
            for p in range(planes):
                final[s, p] = source[0, s, p, width : width + rows]
        write_patches(Tile(lambda s, p: final[s, p], (species, planes)), patches)

    return order.call(
        body,
        "stencil",
        [struct(cells.shape, F32)] + [struct((patch_rows, features), BF16)] * halves,
        [cells, head_rows, tail_rows, from_left, from_right],
        scratch=[pltpu.VMEM((2, species, planes, tall, LANES), F32)] * 2,
    )


def gelu_parts(preact):
    squared = preact * preact
    tangent = jnp.tanh(GELU_FACTOR * (preact + 0.044715 * preact * squared))
    return squared, tangent


def shards(state, embed, mlp, mom_embed, mom_mlp):
    dp_count, mp_count = lax.axis_size("dp"), lax.axis_size("mp")
    halves = 2 if dp_count % 2 == 0 else 1
    pairs = 2 if mp_count % 2 == 0 else 1
    wide = Digit("dp", dp_count // halves, halves)
    band = Digit("dp", 1, dp_count // halves)
    part = Digit("mp", pairs, mp_count // pairs)
    core = Digit("mp", 1, pairs)
    role = Digit("role", 1, lax.axis_size("role"))
    width = embed.shape[1] * dp_count
    own_rows, own_cols = embed.shape[1], embed.shape[2]
    half_width, part_cols = own_rows * band.size, own_cols * core.size
    to_solver, to_trainer = [(TRAINER, SOLVER)], [(SOLVER, TRAINER)]
    order = Order()

    def keep_arrived(arrived, own, index, following, next_index):
        def body(ins, outs, scratch):
            (sems,) = scratch
            solving = lax.axis_index("role") == SOLVER
            ahead = pltpu.make_async_copy(ins[2].at[next_index], outs[1], sems.at[0])
            ahead.start()

            @pl.when(solving)
            def _():
                outs[0][...] = ins[0][...]

            @pl.when(jnp.logical_not(solving))
            def _():
                mine = pltpu.make_async_copy(ins[1].at[index], outs[0], sems.at[1])
                mine.start()
                mine.wait()

            ahead.wait()

        sent = following.shape[len(next_index) :]
        outs = [struct(arrived.shape, BF16), struct(sent, following.dtype)]
        return order.call(
            body,
            "held",
            outs,
            [arrived, own, following],
            left=(1, 2),
            scratch=[pltpu.SemaphoreType.DMA((2,))],
        )

    def relayed(blocks):
        def body(ins, outs, _):
            for source, target in zip(ins, outs):
                target[...] = source[...]

        return order.ride(body, [struct(v.shape, v.dtype) for v in blocks], blocks)

    def own_pieces(block):
        return [block] + core.from_others(block), band.from_others(block)

    def merged(parts):
        return [jnp.concatenate(parts, axis=0)] if len(parts) > 1 else parts

    def held_matrix(own, relay):
        return Matrix([own] + [[rows] + core.from_others(rows) for rows in relay.results])

    cells = state[0]
    rows_in = cells.shape[2]
    features = cells.shape[0] * cells.shape[1] * PATCH * PATCH
    half_rows = rows_in // PATCH * (cells.shape[3] // PATCH) // 2

    def around(axis, step):
        count = lax.axis_size(axis)
        return [(i, (i + step) % count) for i in range(count)]

    def patches_of(ins, outs, _):
        counts = (cells.shape[0], cells.shape[1])
        write_patches(Tile(lambda s, p: ins[0][s, p], counts), outs[:2])
        outs[2][...] = ins[0][:, :, :STEPS]
        outs[3][...] = ins[0][:, :, rows_in - STEPS :]

    def split_patches(own, arrived):
        def body(ins, outs, _):
            solving = lax.axis_index("role") == SOLVER
            position = lax.axis_index("mp")
            my_part, my_core = position // core.size, position % core.size
            for k in range(part.size):
                for t in range(core.size):
                    quarter = (my_part + k) % part.size * core.size
                    quarter = quarter + (my_core - t + core.size) % core.size
                    source = pl.ds(pl.multiple_of(quarter * own_cols, own_cols), own_cols)
                    cols = slice(t * own_cols, (t + 1) * own_cols)

                    @pl.when(solving)
                    def _():
                        outs[k][:, cols] = ins[0][:, source]

                    @pl.when(jnp.logical_not(solving))
                    def _():
                        outs[k][:, cols] = ins[1][:, source]

        return order.ride(
            body, [struct((half_rows, part_cols), BF16)] * part.size, [own, arrived]
        )

    def to_parts(cuts):
        return [cuts[0]] + [part.shifted(cuts[k], k) for k in range(1, part.size)]

    def slots(position, size, count):
        for k in range(size):
            slot = (position - k + size) % size
            yield k, pl.ds(pl.multiple_of(slot * count, count), count)

    def order_rows(pieces):
        def body(ins, outs, _):
            for k, rows in slots(lax.axis_index("mp") // core.size, part.size, half_rows):
                outs[0][rows, :] = ins[k][...]

        return order.ride(body, [struct((half_rows * part.size, part_cols), BF16)], pieces)

    def widened(rows):
        return [rows] + wide.from_others(rows)

    def pack(has_features, width_count):
        return struct((m, (own_cols if has_features else 0) + width_count * half_width), BF16)

    class Gather:
        def __init__(self, keep, sends, has_features, width_count):
            self.base = own_cols if has_features else 0
            self.width_count = width_count
            self.parts = [keep] + [core.shifted(sends[k - 1], k) for k in range(1, core.size)]

        def join(self):
            count = band.size if self.width_count else 1
            base = self.base

            def body(ins, outs, _):
                for c, ref in enumerate(ins):
                    rows = slice(c * m, (c + 1) * m)
                    for k in range(count):
                        if base:
                            outs[k][rows, :base] = ref[:, :base]
                        for index in range(self.width_count):
                            first = base + index * half_width + (-k) % band.size * own_rows
                            target = base + index * own_rows
                            outs[k][rows, target : target + own_rows] = ref[
                                :, first : first + own_rows
                            ]

            cols = base + self.width_count * own_rows
            self.joining = order.ride(
                body, [struct((m * core.size, cols), BF16)] * count, self.parts
            )

        def send(self):
            cuts = self.joining.results
            self.kept = cuts[0]
            self.banded = merged(
                [band.shifted(cuts[k % len(cuts)], k) for k in range(1, band.size)]
            )
            self.arrived = role.from_others(self.kept)

        def relay(self):
            self.relaying = relayed(self.banded)

        def forward(self, relayed_too=True):
            self.banded = self.relaying.results if relayed_too else self.banded
            for piece in self.banded:
                self.arrived = self.arrived + role.from_others(piece)

        def pieces(self):
            return [self.kept] + self.banded + self.arrived

    def selected_state(own, arrived):
        def body(ins, outs, scratch):
            solving = lax.axis_index("role") == SOLVER
            (sem,) = scratch
            for chosen, source in ((solving, ins[0]), (jnp.logical_not(solving), ins[1])):

                @pl.when(chosen)
                def _():
                    copy = pltpu.make_async_copy(source, outs[0], sem)
                    copy.start()
                    copy.wait()

        scratch = [pltpu.SemaphoreType.DMA]
        outs = [struct(own.shape, F32)]
        return order.call(body, "state", outs, [own, arrived], in_hbm=(0,), scratch=scratch)[0]

    m = half_rows * part.size * wide.size
    total_rows = m * core.size * band.size * role.size
    loss_scale = float(total_rows) ** (-0.5)

    arrived_embed = lax.ppermute(embed[0], "role", to_solver)
    edge_struct = struct(cells.shape[:2] + (STEPS, cells.shape[3]), F32)
    *start_halves, first_rows, last_rows = order.call(
        patches_of,
        "patches",
        [struct((half_rows, features), BF16)] * 2 + [edge_struct] * 2,
        [cells],
    )
    arrived_start = lax.ppermute(start_halves[1], "role", to_trainer)
    head_rows = lax.ppermute(last_rows, "dp", around("dp", 1))
    tail_rows = lax.ppermute(first_rows, "dp", around("dp", -1))
    splitting = split_patches(start_halves[0], arrived_start)
    order.run("split")
    ordering = order_rows(to_parts(splitting.results))
    edging = packed_edges(order, cells, head_rows, tail_rows, STEPS)
    embed_kept, up_block = keep_arrived(arrived_embed, embed, 0, mlp, (0, 0))
    embed_own, embed_bands = own_pieces(embed_kept)
    arrived_up = lax.ppermute(up_block, "role", to_solver)
    input_parts = widened(*ordering.results)
    (edges,) = edging.results
    from_left = lax.ppermute(edges, "mp", around("mp", 1))
    from_right = lax.ppermute(edges, "mp", around("mp", -1))
    relay = relayed(merged(embed_bands))
    order.wait_for([from_left, from_right] + input_parts[1:])
    up_kept, down_block = keep_arrived(arrived_up, mlp, (0, 0), mlp, (0, 1))
    up_own, up_bands = own_pieces(up_kept)
    arrived_down = lax.ppermute(down_block, "role", to_solver)
    embed_held = held_matrix(embed_own, relay)

    def embed_rows(ins, outs, _):
        parts, matrix = ins[: wide.size], ins[wide.size :]
        *inputs, mine, sent = outs
        position = lax.axis_index("dp") // band.size
        for k, rows in slots(position, wide.size, half_rows * part.size):
            for t in range(core.size):
                inputs[t][rows, :] = parts[k][:, t * own_cols : (t + 1) * own_cols]
        value = embed_held.to_width(matrix, jnp.concatenate([ref[...] for ref in inputs], axis=1))
        mine[...] = value
        sent[...] = value.astype(BF16)

    *inputs, embed_mine, embed_sum = order.call(
        embed_rows,
        "embed",
        [struct((m, own_cols), BF16)] * core.size
        + [struct((m, half_width), F32), struct((m, half_width), BF16)],
        input_parts + embed_held.flat,
    )
    embed_others = part.from_others(embed_sum)

    def core_slot(k):
        return slice((-k) % core.size * own_cols, ((-k) % core.size + 1) * own_cols)

    final_cells, *end_halves = stepped(
        order, cells, head_rows, tail_rows, from_left, from_right, STEPS, 2
    )
    arrived_end = lax.ppermute(end_halves[1], "role", to_trainer)
    relay = relayed(merged(up_bands))
    down_kept, cells_sent = keep_arrived(arrived_down, mlp, (0, 1), final_cells, ())
    down_own, down_bands = own_pieces(down_kept)
    arrived_cells = lax.ppermute(cells_sent, "role", to_trainer)
    up_held = held_matrix(up_own, relay)
    inputs_on = Gather(inputs[0], [inputs[(-k) % core.size] for k in range(1, core.size)], True, 0)

    def added(mine, refs, cols):
        total = mine[...]
        for ref in refs:
            total = total + ref[:, :cols].astype(F32)
        return total

    def up_rows(ins, outs, _):
        others, matrix = ins[1 : part.size], ins[part.size :]
        embedded, mine, sent = outs
        value = added(ins[0], others, half_width)
        embedded[...] = value
        hidden = up_held.to_cols(matrix, value.astype(BF16))
        mine[...] = hidden
        sent[...] = with_scalars(hidden, jnp.sum(value * value, axis=1, keepdims=True))

    embedded, up_mine, up_sum = order.call(
        up_rows,
        "up",
        [
            struct((m, half_width), F32),
            struct((m, part_cols), F32),
            struct((m, part_cols + LANES), BF16),
        ],
        [embed_mine] + embed_others + up_held.flat,
    )
    up_others = wide.from_others(up_sum)
    order.wait_for(up_others + [arrived_cells])
    inputs_on.join()
    splitting = split_patches(end_halves[0], arrived_end)
    relay = relayed(merged(down_bands))
    order.run("relay")
    down_held = held_matrix(down_own, relay)
    inputs_on.send()
    ordering = order_rows(to_parts(splitting.results))

    def down_rows(ins, outs, _):
        value, others, matrix = ins[0][...], ins[2 : 1 + wide.size], ins[1 + wide.size :]
        hidden, mine, sent, scale, *packs = outs
        squares = jnp.sum(value * value, axis=1, keepdims=True)
        for ref in others:
            squares = squares + scalars_of(ref)
        recip = lax.rsqrt(squares / width + 1e-06)
        preact = added(ins[1], others, part_cols) * recip
        hidden[...] = preact
        normed = (value * recip).astype(BF16)
        _, tangent = gelu_parts(preact)
        active = (0.5 * preact * (1.0 + tangent)).astype(BF16)
        branch = down_held.to_width(matrix, active)
        mine[...] = branch
        sent[...] = branch.astype(BF16)
        scale[...] = jnp.broadcast_to(recip, scale.shape)
        for k in range(core.size):
            packs[k][:, :own_cols] = active[:, core_slot(k)]
            packs[k][:, own_cols:] = normed

    hidden_pre, down_mine, down_sum, scale, *active_packs = order.call(
        down_rows,
        "down",
        [
            struct((m, part_cols), F32),
            struct((m, half_width), F32),
            struct((m, half_width), BF16),
            struct((m, LANES), F32),
        ]
        + [pack(True, 1)] * core.size,
        [embedded, up_mine] + up_others + down_held.flat,
    )
    down_others = part.from_others(down_sum)
    target_parts = widened(*ordering.results)
    active_on = Gather(active_packs[0], active_packs[1:], True, 1)
    inputs_on.relay()
    active_on.join()

    def predict_rows(ins, outs, _):
        others, matrix = ins[2 : 1 + part.size], ins[1 + part.size :]
        mine, sent, stream = outs
        value = (ins[0][...] + added(ins[1], others, half_width)).astype(BF16)
        stream[...] = value
        predicted = embed_held.to_cols(matrix, value)
        mine[...] = predicted
        sent[...] = predicted.astype(BF16)

    predict_mine, predict_sum, stream = order.call(
        predict_rows,
        "predict",
        [
            struct((m, part_cols), F32),
            struct((m, part_cols), BF16),
            struct((m, half_width), BF16),
        ],
        [embedded, down_mine] + down_others + embed_held.flat,
    )
    predict_others = wide.from_others(predict_sum)
    inputs_on.forward()
    active_on.send()
    active_on.relay()
    order.wait_for(inputs_on.arrived)

    def residual_rows(ins, outs, scratch):
        inputs, ins = ins[: core.size], ins[core.size :]
        mine_in, others, ins = ins[0], ins[1 : wide.size], ins[wide.size :]
        aims, stream, matrix = ins[: wide.size], ins[wide.size], ins[wide.size + 1 :]
        mine, sent, *packs = outs
        (aim,) = scratch
        position = lax.axis_index("dp") // band.size
        for k, rows in slots(position, wide.size, half_rows * part.size):
            aim[rows, :] = aims[k][...]
        known = jnp.concatenate([ref[...] for ref in inputs], axis=1).astype(F32)
        predicted = known + added(mine_in, others, part_cols)
        value = ((predicted - aim[...].astype(F32)) * loss_scale).astype(BF16)
        for k in range(core.size):
            packs[k][:, :own_cols] = value[:, core_slot(k)]
            packs[k][:, own_cols:] = stream[...]
        grad = embed_held.to_width(matrix, value)
        mine[...] = grad
        sent[...] = grad.astype(BF16)

    stream_mine, stream_sum, *residual_packs = order.call(
        residual_rows,
        "residual",
        [struct((m, half_width), F32), struct((m, half_width), BF16)]
        + [pack(True, 1)] * core.size,
        inputs + [predict_mine] + predict_others + target_parts + [stream] + embed_held.flat,
        scratch=[pltpu.VMEM((m, part_cols), BF16)],
    )
    stream_others = part.from_others(stream_sum)

    active_on.forward()
    residual_on = Gather(residual_packs[0], residual_packs[1:], True, 1)
    residual_on.join()

    def hidden_rows(ins, outs, _):
        others, matrix = ins[1 : part.size], ins[part.size :]
        grad, mine, sent, rounded_out = outs
        value = added(ins[0], others, half_width)
        grad[...] = value
        rounded = value.astype(BF16)
        back = down_held.to_cols(matrix, rounded)
        mine[...] = back
        sent[...] = back.astype(BF16)
        rounded_out[...] = rounded

    stream_grad, back_mine, back_sum, stream_sent = order.call(
        hidden_rows,
        "hidden",
        [
            struct((m, half_width), F32),
            struct((m, part_cols), F32),
            struct((m, part_cols), BF16),
            struct((m, half_width), BF16),
        ],
        [stream_mine] + stream_others + down_held.flat,
    )
    back_others = wide.from_others(back_sum)
    residual_on.send()
    residual_on.relay()
    order.wait_for(active_on.arrived)

    def normed_rows(ins, outs, _):
        stream_sent, others, matrix = ins[2], ins[3 : 2 + wide.size], ins[2 + wide.size :]
        mine, inner, sent, *packs = outs
        preact = ins[0][...]
        squared, tangent = gelu_parts(preact)
        slope = 0.5 * (1.0 + tangent) + 0.5 * preact * (1.0 - tangent * tangent) * GELU_FACTOR * (
            1.0 + 3.0 * 0.044715 * squared
        )
        value = (added(ins[1], others, part_cols) * slope).astype(BF16)
        for k in range(core.size):
            packs[k][:, :own_cols] = value[:, core_slot(k)]
            packs[k][:, own_cols:] = stream_sent[...]
        grad = up_held.to_width(matrix, value)
        mine[...] = grad
        both = jnp.sum(value.astype(F32) * preact, axis=1, keepdims=True)
        inner[...] = jnp.broadcast_to(both, inner.shape)
        sent[...] = with_scalars(grad, both)

    normed_mine, inner_mine, normed_sum, *hidden_packs = order.call(
        normed_rows,
        "normed",
        [
            struct((m, half_width), F32),
            struct((m, LANES), F32),
            struct((m, half_width + LANES), BF16),
        ]
        + [pack(True, 1)] * core.size,
        [hidden_pre, back_mine, stream_sent] + back_others + up_held.flat,
    )
    normed_others = part.from_others(normed_sum)
    residual_on.forward()
    hidden_on = Gather(hidden_packs[0], hidden_packs[1:], True, 1)
    hidden_on.join()

    def embed_grad_rows(ins, outs, _):
        value, grad, scale_ref, mine, inner_ref, *others = ins
        normed_grad = added(mine, others, half_width)
        inner = inner_ref[:, :1]
        for ref in others:
            inner = inner + scalars_of(ref)
        recip = scale_ref[:, :1]
        outs[0][...] = (
            grad[...] + recip * normed_grad - value[...] * (recip * recip) * (inner / width)
        ).astype(BF16)

    (embed_sent,) = order.call(
        embed_grad_rows,
        "embed_grad",
        [pack(False, 1)],
        [embedded, stream_grad, scale, normed_mine, inner_mine] + normed_others,
    )
    hidden_on.send()
    hidden_on.forward(False)
    embed_sent_on = Gather(embed_sent, [embed_sent] * (core.size - 1), False, 1)
    embed_sent_on.join()
    order.run("join")
    embed_sent_on.send()
    embed_sent_on.forward(False)
    state_out = selected_state(final_cells, arrived_cells)

    def updated(name, terms, momentum, weight, index, begun=()):
        pieces = {}
        for pair in terms:
            for arrays, _ in pair:
                for array in arrays:
                    pieces.setdefault(id(array), array)
        places = {key: place for place, key in enumerate(pieces)}
        arrays = list(pieces.values())
        cuts = 2
        step = own_rows // cuts

        def body(ins, outs, scratch):
            mom_new, weight_new, sems = scratch
            total = None
            for (lefts, left_col), (rights, right_col) in terms:
                for left, right in zip(lefts, rights):
                    left_ref, right_ref = ins[places[id(left)]], ins[places[id(right)]]
                    term = cols_dot(
                        left_ref[:, left_col : left_col + own_rows],
                        right_ref[:, right_col : right_col + own_cols],
                    )
                    total = term if total is None else total + term
            mom, old = ins[len(arrays)], ins[len(arrays) + 1]
            copies = []
            for cut in range(cuts):
                rows = slice(cut * step, (cut + 1) * step)
                fresh = MOMENTUM_DECAY * mom[index][rows] + total[rows]
                mom_new[rows, :] = fresh
                weight_new[rows, :] = (old[index][rows].astype(F32) - LEARNING_RATE * fresh).astype(
                    BF16
                )
                for number, source in enumerate((mom_new, weight_new)):
                    copies.append(
                        pltpu.make_async_copy(
                            source.at[pl.ds(cut * step, step)],
                            outs[number].at[index].at[pl.ds(cut * step, step)],
                            sems.at[2 * cut + number],
                        )
                    )
                    copies[-1].start()
            for copy in copies:
                copy.wait()

        count = len(arrays) + 2
        return order.call(
            body,
            name,
            [struct(momentum.shape, F32), struct(weight.shape, BF16)],
            arrays + [momentum, weight],
            in_hbm=(0, 1),
            scratch=[
                pltpu.VMEM((own_rows, own_cols), F32),
                pltpu.VMEM((own_rows, own_cols), BF16),
                pltpu.SemaphoreType.DMA((2 * cuts,)),
            ],
            aliases={count: 0, count + 1: 1} if begun else None,
            extra=begun,
        )

    all_inputs, all_active, all_residual = (
        inputs_on.pieces(),
        active_on.pieces(),
        residual_on.pieces(),
    )
    all_hidden, all_embed_sent = hidden_on.pieces(), embed_sent_on.pieces()
    begun = updated("update_down", [((all_hidden, own_cols), (all_active, 0))], mom_mlp, mlp, (0, 1))
    mom_mlp_out, mlp_out = updated(
        "update_up", [((all_active, own_cols), (all_hidden, 0))], mom_mlp, mlp, (0, 0), begun
    )
    mom_embed_out, embed_out = updated(
        "update_embed",
        [((all_residual, own_cols), (all_residual, 0)), ((all_embed_sent, 0), (all_inputs, 0))],
        mom_embed,
        embed,
        0,
    )
    return (state_out, embed_out, mlp_out, mom_embed_out, mom_mlp_out)


def solution(mesh):
    placed = (
        P("role", None, None, "dp", "mp"),
        P("role", "dp", "mp"),
        P("role", None, "dp", "mp"),
        P("role", "dp", "mp"),
        P("role", None, "dp", "mp"),
    )
    return jax.shard_map(
        shards,
        mesh=mesh,
        in_specs=placed,
        out_specs=(
            P(None, None, "dp", "mp"),
            P("role", "dp", "mp"),
            P("role", None, "dp", "mp"),
            P("role", "dp", "mp"),
            P("role", None, "dp", "mp"),
        ),
        check_vma=False,
    )
```

time: 593 us -> 176 us (0.30)
  waiting for transfers between devices: 424 us -> 92.9 us
  local copies, waits for them, and re-layouts: 44.5 us -> 4.37 us
  starting transfers between devices: 19.5 us -> 54 us
  blocking collectives: 31.8 us -> 0 us
  matrix products: 30.1 us -> 0 us
  other arithmetic: 27.3 us -> 0 us
  Pallas kernels: 0 us -> 23.4 us
  between operations: 14.6 us -> 1.13 us
    reduce_scatter x5 -> x0, waiting for transfers between devices: 264 us -> none  [the longest x1 212 us: shards(): lax.psum_scatter(jnp.concatenate([first + jnp.dot(embed_sent.T, inputs, p...]
    all_gather x1 -> x0, waiting for transfers between devices: 77.4 us -> none  [shards(): whole = lax.all_gather(stacked, 'dp', axis=0, tiled=True)]
    ppermute x7 -> x50, starting transfers between devices: 15 us -> 54 us  [the longest x40 36.9 us: shifted(): return lax.ppermute(value, self.axis, pairs)]
    pallas_call x0 -> x20, Pallas kernels: none -> 23.4 us  [call(): pl.pallas_call(kernel, name=name, out_shape=outs + [struct(TOKEN, F32)],...]
    all_gather x4 -> x0, blocking collectives: 23.4 us -> none  [the longest x1 6 us: shards(): lax.all_gather(stream_grad.astype(jnp.bfloat16), 'mp', axis=0, tiled=True)]
    unnamed x54 -> x18, local copies, waits for them, and re-layouts: 25.4 us -> 4.37 us
    dot_general x8 -> x0, matrix products: 20.2 us -> none  [the longest x1 3.17 us: shards(): jnp.dot(embed_sent.T, inputs, preferred_element_type=jnp.float32)]
    ppermute x7 -> x50, waiting for transfers between devices: 76.8 us -> 92.9 us  [the longest x40 77.3 us: shifted(): return lax.ppermute(value, self.axis, pairs)]
  transfers between devices with their start and end apart: 14 -> 50, of which waited for: 10 -> 28; matrix products, arithmetic and copies ran while one was open for 6% -> 0% of each run, Pallas kernels for 0% -> 10%
where the time goes in v2:
time: 176 us
  waiting for transfers between devices  92.9 us (53%)
  starting transfers between devices  54 us (31%)
  Pallas kernels  23.4 us (13%)
  local copies, waits for them, and re-layouts  4.37 us (2%)
    ppermute x40, waiting for transfers between devices, shifted(): return lax.ppermute(value, self.axis, pairs)  77.3 us
    ppermute x40, starting transfers between devices, shifted(): return lax.ppermute(value, self.axis, pairs)  36.9 us
    pallas_call x20, Pallas kernels, call(): pl.pallas_call(kernel, name=name, out_shape=outs + [struct(TOKEN, F32)],...  23.4 us
    ppermute x1, waiting for transfers between devices, shards(): arrived_end = lax.ppermute(end_halves[1], 'role', to_trainer)  5.7 us
    ppermute x1, starting transfers between devices, shards(): arrived_start = lax.ppermute(start_halves[1], 'role', to_trainer)  4.88 us
    unnamed x18, local copies, waits for them, and re-layouts  4.37 us
  transfers between devices with their start and end apart: 50, of which 28 were waited for; matrix products, arithmetic and copies ran while one was open for 0% of the time, Pallas kernels for 10%

profile of v2, /device:TPU:0, one launch (start us, length us, event | category | flops | bytes accessed | tf_op | source)
XLA Modules:
  0.0 175.8 jit_solution(2679056322732528128)
XLA Ops:
  0.6 1.3 collective-permute-start.4
  3.0 1.7 patches.1
  4.7 4.9 %collective-permute-start.2 = (bf16[16,4096]{1,0:T(8,128)(2,1)S(1)}, bf16[16,4096]{1,0:T(8,128)(2,1)S(1)}, u32[]{:S(2)}, u32[]{:S(2)}) collective-permute-start(bf16[16,4096]{1,0:T(8,128)(2,1)S(1)} %get-tuple-element.99), channel_id=1, source_target_pairs={{0,16},{1,17},{2,18},{3,19},{4,20},{5,21},{6,22},{7,23},{8,24},{9,... | collective-permute-start | bytes 393224 | tf_op jit(solution)/shard_map/ppermute | solution.py:537
  9.5 2.8 %collective-permute-done.2.refs_1_ = bf16[16,4096]{1,0:T(8,128)(2,1)S(1)} collective-permute-done((bf16[16,4096]{1,0:T(8,128)(2,1)S(1)}, bf16[16,4096]{1,0:T(8,128)(2,1)S(1)}, u32[]{:S(2)}, u32[]{:S(2)}) %collective-permute-start.2) | collective-permute-done | bytes 131104 | tf_op jit(solution)/shard_map/ppermute | solution.py:537
  12.3 2.5 %collective-permute-start.3 = (bf16[16,2048]{1,0:T(8,128)(2,1)S(1)}, bf16[16,2048]{1,0:T(8,128)(2,1)S(1)}, u32[]{:S(2)}, u32[]{:S(2)}) collective-permute-start(bf16[16,2048]{1,0:T(8,128)(2,1)S(1)} %get-tuple-element.102), channel_id=1, source_target_pairs={{0,2},{1,3},{2,0},{3,1},{4,6},{5,7},{6,4},{7,5},{8,10},{9,11},{10,... | collective-permute-start | bytes 196616 | tf_op jit(solution)/shard_map/ppermute | solution.py:35
  14.8 1.6 collective-permute-start
  16.4 2.2 %collective-permute-start.1 = (f32[2,8,4,128]{3,2,1,0:T(4,128)S(1)}, f32[2,8,4,128]{3,2,1,0:T(4,128)S(1)}, u32[]{:S(2)}, u32[]{:S(2)}) collective-permute-start(f32[2,8,4,128]{3,2,1,0:T(4,128)S(1)} %get-tuple-element.97), channel_id=1, source_target_pairs={{0,12},{4,0},{8,4},{12,8},{1,13},{5,1},{9,5},{13,9},{2,14},{6,2},{... | collective-permute-start | bytes 98312 | tf_op jit(solution)/shard_map/ppermute | solution.py:539
  18.6 2.0 %collective-permute-done.refs_3_.refs_1_ = f32[2,8,4,128]{3,2,1,0:T(4,128)S(1)} collective-permute-done((f32[2,8,4,128]{3,2,1,0:T(4,128)S(1)}, f32[2,8,4,128]{3,2,1,0:T(4,128)S(1)}, u32[]{:S(2)}, u32[]{:S(2)}) %collective-permute-start) | collective-permute-done | bytes 32800 | tf_op jit(solution)/shard_map/ppermute | solution.py:538
  24.4 1.3 collective-permute-start.9
  27.0 3.1 %collective-permute-start.7 = (bf16[32,2048]{1,0:T(8,128)(2,1)S(1)}, bf16[32,2048]{1,0:T(8,128)(2,1)S(1)}, u32[]{:S(2)}, u32[]{:S(2)}) collective-permute-start(bf16[32,2048]{1,0:T(8,128)(2,1)S(1)} %get-tuple-element.105.refs_0_), channel_id=1, source_target_pairs={{0,8},{4,12},{8,0},{12,4},{1,9},{5,13},{9,1},{13,5},{2,10},{6,14},... | collective-permute-start | bytes 393224 | tf_op jit(solution)/shard_map/ppermute | solution.py:35
  30.1 1.7 collective-permute-start.6
  31.8 1.6 collective-permute-done.5.refs_5_.refs_3_
  33.5 3.7 %collective-permute-done.7.refs_7_.refs_1_ = bf16[32,2048]{1,0:T(8,128)(2,1)S(1)} collective-permute-done((bf16[32,2048]{1,0:T(8,128)(2,1)S(1)}, bf16[32,2048]{1,0:T(8,128)(2,1)S(1)}, u32[]{:S(2)}, u32[]{:S(2)}) %collective-permute-start.7) | collective-permute-done | bytes 131104 | tf_op jit(solution)/shard_map/ppermute | solution.py:35
  38.7 2.4 %collective-permute-start.12 = (bf16[256,1024]{1,0:T(8,128)(2,1)S(1)}, bf16[256,1024]{1,0:T(8,128)(2,1)S(1)}, u32[]{:S(2)}, u32[]{:S(2)}) collective-permute-start(bf16[256,1024]{1,0:T(8,128)(2,1)S(1)} %get-tuple-element.113.refs_2_.refs_5_), channel_id=1, source_target_pairs={{0,4},{4,0},{8,12},{12,8},{1,5},{5,1},{9,13},{13,9},{2,6},{6,2},{1... | collective-permute-start | bytes 1572872 | tf_op jit(solution)/shard_map/ppermute | solution.py:35
  43.3 8.1 %stencil.1 = (f32[2,8,64,128]{3,2,1,0:T(8,128)S(1)}, bf16[16,4096]{1,0:T(8,128)(2,1)S(1)}, bf16[16,4096]{1,0:T(8,128)(2,1)S(1)}, f32[8,128]{1,0:T(8,128)S(1)}) custom-call(f32[2,8,64,128]{3,2,1,0:T(8,128)S(1)} %bitcast.4, f32[2,8,4,128]{3,2,1,0:T(4,128)S(1)} %collective-permute-done.refs_3_.refs_1_, ...), custom_call_target="tpu_custom_call" | custom-call | flops 1 | bytes 1 | tf_op jit(solution)/shard_map/stencil/pallas_call | solution.py:128
  51.4 2.1 %collective-permute-done.12.refs_0_ = bf16[256,1024]{1,0:T(8,128)(2,1)S(1)} collective-permute-done((bf16[256,1024]{1,0:T(8,128)(2,1)S(1)}, bf16[256,1024]{1,0:T(8,128)(2,1)S(1)}, u32[]{:S(2)}, u32[]{:S(2)}) %collective-permute-start.12) | collective-permute-done | bytes 524320 | tf_op jit(solution)/shard_map/ppermute | solution.py:35
  53.5 3.4 %collective-permute-done.13.refs_1_ = bf16[256,1024]{1,0:T(8,128)(2,1)S(1)} collective-permute-done((bf16[256,1024]{1,0:T(8,128)(2,1)S(1)}, bf16[256,1024]{1,0:T(8,128)(2,1)S(1)}, u32[]{:S(2)}, u32[]{:S(2)}) %collective-permute-start.13) | collective-permute-done | bytes 524320 | tf_op jit(solution)/shard_map/ppermute | solution.py:555
  57.1 1.5 collective-permute-start.14
  60.2 3.8 %collective-permute-done.18.refs_1_ = bf16[64,512]{1,0:T(8,128)(2,1)S(1)} collective-permute-done((bf16[64,512]{1,0:T(8,128)(2,1)S(1)}, bf16[64,512]{1,0:T(8,128)(2,1)S(1)}, u32[]{:S(2)}, u32[]{:S(2)}) %collective-permute-start.18) | collective-permute-done | bytes 65568 | tf_op jit(solution)/shard_map/ppermute | solution.py:35
  64.4 1.8 %collective-permute-start.21 = (bf16[64,2176]{1,0:T(8,128)(2,1)S(1)}, bf16[64,2176]{1,0:T(8,128)(2,1)S(1)}, u32[]{:S(2)}, u32[]{:S(2)}) collective-permute-start(bf16[64,2176]{1,0:T(8,128)(2,1)S(1)} %get-tuple-element.127), channel_id=1, source_target_pairs={{0,8},{4,12},{8,0},{12,4},{1,9},{5,13},{9,1},{13,5},{2,10},{6,14},... | collective-permute-start | bytes 835592 | tf_op jit(solution)/shard_map/ppermute | solution.py:35
  67.6 5.7 %collective-permute-done.16.refs_3_ = bf16[16,4096]{1,0:T(8,128)(2,1)S(1)} collective-permute-done((bf16[16,4096]{1,0:T(8,128)(2,1)S(1)}, bf16[16,4096]{1,0:T(8,128)(2,1)S(1)}, u32[]{:S(2)}, u32[]{:S(2)}) %collective-permute-start.16) | collective-permute-done | bytes 131104 | tf_op jit(solution)/shard_map/ppermute | solution.py:584
  73.3 5.5 %collective-permute-done.17.refs_4_ = bf16[256,1024]{1,0:T(8,128)(2,1)S(1)} collective-permute-done((bf16[256,1024]{1,0:T(8,128)(2,1)S(1)}, bf16[256,1024]{1,0:T(8,128)(2,1)S(1)}, u32[]{:S(2)}, u32[]{:S(2)}) %collective-permute-start.17) | collective-permute-done | bytes 524320 | tf_op jit(solution)/shard_map/ppermute | solution.py:35
  79.9 1.6 collective-permute-start.22
  81.5 2.2 %collective-permute-done.23.refs_1_ = bf16[16,2048]{1,0:T(8,128)(2,1)S(1)} collective-permute-done((bf16[16,2048]{1,0:T(8,128)(2,1)S(1)}, bf16[16,2048]{1,0:T(8,128)(2,1)S(1)}, u32[]{:S(2)}, u32[]{:S(2)}) %collective-permute-start.23) | collective-permute-done | bytes 65568 | tf_op jit(solution)/shard_map/ppermute | solution.py:35
  85.3 3.0 %collective-permute-done.22.refs_0_ = bf16[128,1024]{1,0:T(8,128)(2,1)S(1)} collective-permute-done((bf16[128,1024]{1,0:T(8,128)(2,1)S(1)}, bf16[128,1024]{1,0:T(8,128)(2,1)S(1)}, u32[]{:S(2)}, u32[]{:S(2)}) %collective-permute-start.22) | collective-permute-done | bytes 262176 | tf_op jit(solution)/shard_map/ppermute | solution.py:35
  89.6 1.8 %collective-permute-start.28 = (bf16[128,1280]{1,0:T(8,128)(2,1)S(1)}, bf16[128,1280]{1,0:T(8,128)(2,1)S(1)}, u32[]{:S(2)}, u32[]{:S(2)}) collective-permute-start(bf16[128,1280]{1,0:T(8,128)(2,1)S(1)} %get-tuple-element.140), channel_id=1, source_target_pairs={{0,4},{4,0},{8,12},{12,8},{1,5},{5,1},{9,13},{13,9},{2,6},{6,2},{1... | collective-permute-start | bytes 983048 | tf_op jit(solution)/shard_map/ppermute | solution.py:35
  92.3 2.0 %collective-permute-start.32 = (bf16[128,1024]{1,0:T(8,128)(2,1)S(1)}, bf16[128,1024]{1,0:T(8,128)(2,1)S(1)}, u32[]{:S(2)}, u32[]{:S(2)}) collective-permute-start(bf16[128,1024]{1,0:T(8,128)(2,1)S(1)} %get-tuple-element.146.refs_9_), channel_id=1, source_target_pairs={{0,16},{16,0},{1,17},{17,1},{2,18},{18,2},{3,19},{19,3},{4,20},{20... | collective-permute-start | bytes 786440 | tf_op jit(solution)/shard_map/ppermute | solution.py:35
  94.3 2.0 %collective-permute-start.30 = (bf16[32,2048]{1,0:T(8,128)(2,1)S(1)}, bf16[32,2048]{1,0:T(8,128)(2,1)S(1)}, u32[]{:S(2)}, u32[]{:S(2)}) collective-permute-start(bf16[32,2048]{1,0:T(8,128)(2,1)S(1)} %get-tuple-element.143.refs_5_), channel_id=1, source_target_pairs={{0,8},{4,12},{8,0},{12,4},{1,9},{5,13},{9,1},{13,5},{2,10},{6,14},... | collective-permute-start | bytes 393224 | tf_op jit(solution)/shard_map/ppermute | solution.py:35
  96.4 4.3 %collective-permute-done.31.refs_13_.refs_10_ = bf16[128,1024]{1,0:T(8,128)(2,1)S(1)} collective-permute-done((bf16[128,1024]{1,0:T(8,128)(2,1)S(1)}, bf16[128,1024]{1,0:T(8,128)(2,1)S(1)}, u32[]{:S(2)}, u32[]{:S(2)}) %collective-permute-start.31) | collective-permute-done | bytes 262176 | tf_op jit(solution)/shard_map/ppermute | solution.py:35
  100.7 10.5 %collective-permute-done.30.refs_6_ = bf16[32,2048]{1,0:T(8,128)(2,1)S(1)} collective-permute-done((bf16[32,2048]{1,0:T(8,128)(2,1)S(1)}, bf16[32,2048]{1,0:T(8,128)(2,1)S(1)}, u32[]{:S(2)}, u32[]{:S(2)}) %collective-permute-start.30) | collective-permute-done | bytes 131104 | tf_op jit(solution)/shard_map/ppermute | solution.py:35
  112.7 1.7 collective-permute-start.37
  114.7 1.9 %collective-permute-done.34.refs_3_ = bf16[64,512]{1,0:T(8,128)(2,1)S(1)} collective-permute-done((bf16[64,512]{1,0:T(8,128)(2,1)S(1)}, bf16[64,512]{1,0:T(8,128)(2,1)S(1)}, u32[]{:S(2)}, u32[]{:S(2)}) %collective-permute-start.34) | collective-permute-done | bytes 65568 | tf_op jit(solution)/shard_map/ppermute | solution.py:35
  117.2 2.1 %collective-permute-start.36 = (bf16[64,2048]{1,0:T(8,128)(2,1)S(1)}, bf16[64,2048]{1,0:T(8,128)(2,1)S(1)}, u32[]{:S(2)}, u32[]{:S(2)}) collective-permute-start(bf16[64,2048]{1,0:T(8,128)(2,1)S(1)} %get-tuple-element.156), channel_id=1, source_target_pairs={{0,8},{4,12},{8,0},{12,4},{1,9},{5,13},{9,1},{13,5},{2,10},{6,14},... | collective-permute-start | bytes 786440 | tf_op jit(solution)/shard_map/ppermute | solution.py:35
  119.3 3.9 %collective-permute-done.37.refs_10_.refs_6_.refs_2_ = bf16[128,1280]{1,0:T(8,128)(2,1)S(1)} collective-permute-done((bf16[128,1280]{1,0:T(8,128)(2,1)S(1)}, bf16[128,1280]{1,0:T(8,128)(2,1)S(1)}, u32[]{:S(2)}, u32[]{:S(2)}) %collective-permute-start.37) | collective-permute-done | bytes 327712 | tf_op jit(solution)/shard_map/ppermute | solution.py:35
  123.2 6.2 %collective-permute-done.38.refs_11_.refs_7_.refs_3_ = bf16[128,1280]{1,0:T(8,128)(2,1)S(1)} collective-permute-done((bf16[128,1280]{1,0:T(8,128)(2,1)S(1)}, bf16[128,1280]{1,0:T(8,128)(2,1)S(1)}, u32[]{:S(2)}, u32[]{:S(2)}) %collective-permute-start.38) | collective-permute-done | bytes 327712 | tf_op jit(solution)/shard_map/ppermute | solution.py:35
  129.9 2.2 %collective-permute-done.35.refs_0_ = bf16[128,1280]{1,0:T(8,128)(2,1)S(1)} collective-permute-done((bf16[128,1280]{1,0:T(8,128)(2,1)S(1)}, bf16[128,1280]{1,0:T(8,128)(2,1)S(1)}, u32[]{:S(2)}, u32[]{:S(2)}) %collective-permute-start.35) | collective-permute-done | bytes 327712 | tf_op jit(solution)/shard_map/ppermute | solution.py:35
  133.6 4.3 %collective-permute-done.40.refs_7_ = bf16[64,640]{1,0:T(8,128)(2,1)S(1)} collective-permute-done((bf16[64,640]{1,0:T(8,128)(2,1)S(1)}, bf16[64,640]{1,0:T(8,128)(2,1)S(1)}, u32[]{:S(2)}, u32[]{:S(2)}) %collective-permute-start.40) | collective-permute-done | bytes 81952 | tf_op jit(solution)/shard_map/ppermute | solution.py:35
  138.5 1.7 collective-permute-start.48
  140.2 7.2 %collective-permute-done.47.refs_1_.refs_5_ = bf16[128,1280]{1,0:T(8,128)(2,1)S(1)} collective-permute-done((bf16[128,1280]{1,0:T(8,128)(2,1)S(1)}, bf16[128,1280]{1,0:T(8,128)(2,1)S(1)}, u32[]{:S(2)}, u32[]{:S(2)}) %collective-permute-start.47) | collective-permute-done | bytes 327712 | tf_op jit(solution)/shard_map/ppermute | solution.py:35
  147.4 1.7 collective-permute-start.49
  149.4 1.7 collective-permute-start.43
  152.9 3.9 %collective-permute-done.44.refs_5_ = bf16[128,256]{1,0:T(8,128)(2,1)S(1)} collective-permute-done((bf16[128,256]{1,0:T(8,128)(2,1)S(1)}, bf16[128,256]{1,0:T(8,128)(2,1)S(1)}, u32[]{:S(2)}, u32[]{:S(2)}) %collective-permute-start.44) | collective-permute-done | bytes 65568 | tf_op jit(solution)/shard_map/ppermute | solution.py:35
  157.0 1.7 collective-permute-start.46
  159.6 1.9 %update_down.1 = (f32[1,2,256,1024]{3,2,1,0:T(8,128)}, bf16[1,2,256,1024]{3,2,1,0:T(8,128)(2,1)}, f32[8,128]{1,0:T(8,128)S(1)}) custom-call(bf16[128,1280]{1,0:T(8,128)(2,1)S(1)} %get-tuple-element.176.refs_0_.refs_4_, bf16[128,1280]{1,0:T(8,128)(2,1)S(1)} %collective-permute-done.47.refs_1_.refs_5_, ...), custom_call_target="tpu_custom_call" | custom-call | flops 1 | bytes 1 | tf_op jit(solution)/shard_map/update_down/pallas_call | solution.py:128
  161.6 1.9 %update_up.1 = (f32[1,2,256,1024]{3,2,1,0:T(8,128)}, bf16[1,2,256,1024]{3,2,1,0:T(8,128)(2,1)}, f32[8,128]{1,0:T(8,128)S(1)}) custom-call(bf16[128,1280]{1,0:T(8,128)(2,1)S(1)} %get-tuple-element.158.refs_4_.refs_0_, bf16[128,1280]{1,0:T(8,128)(2,1)S(1)} %get-tuple-element.159.refs_5_.refs_1_, ...), custom_call_target="tpu_custom_call", output_to_operand_aliasing={{0}: (10, {}), {1}: (11, {})} | custom-call | flops 1 | bytes 1 | tf_op jit(solution)/shard_map/update_up/pallas_call | solution.py:128
  163.5 1.6 collective-permute-done.42.refs_2_
  165.1 6.9 %collective-permute-done.45.refs_6_ = bf16[128,256]{1,0:T(8,128)(2,1)S(1)} collective-permute-done((bf16[128,256]{1,0:T(8,128)(2,1)S(1)}, bf16[128,256]{1,0:T(8,128)(2,1)S(1)}, u32[]{:S(2)}, u32[]{:S(2)}) %collective-permute-start.45) | collective-permute-done | bytes 65568 | tf_op jit(solution)/shard_map/ppermute | solution.py:35
  172.6 3.1 %update_embed.1 = (f32[1,256,1024]{2,1,0:T(8,128)}, bf16[1,256,1024]{2,1,0:T(8,128)(2,1)}, f32[8,128]{1,0:T(8,128)}) custom-call(bf16[128,1280]{1,0:T(8,128)(2,1)S(1)} %get-tuple-element.172.refs_0_, bf16[128,1280]{1,0:T(8,128)(2,1)S(1)} %get-tuple-element.173.refs_1_, bf16[128,1280]{1,0:T(8,128)(2,1)S(1)} %collective-permute-done.42.refs_2_, ...), custom_call_target="tpu_custom_call" | custom-call | flops 1 | bytes 1 | tf_op jit(solution)/shard_map/update_embed/pallas_call | solution.py:128
  (90 shorter events, 27.2 us)
Async XLA Ops:
  0.6 20.0 %collective-permute-start.4 = (bf16[256,1024]{1,0:T(8,128)(2,1)}, bf16[256,1024]{1,0:T(8,128)(2,1)S(1)}, u32[]{:S(2)}, u32[]{:S(2)}) collective-permute-start(bf16[256,1024]{1,0:T(8,128)(2,1)} %bitcast.5), channel_id=1, source_target_pairs={{16,0},{17,1},{18,2},{19,3},{20,4},{21,5},{22,6},{23,7},{24,8},{25... | collective-permute-start | bytes 1572872 | tf_op jit(solution)/shard_map/ppermute | solution.py:529
  4.7 7.7 %collective-permute-start.2 = (bf16[16,4096]{1,0:T(8,128)(2,1)S(1)}, bf16[16,4096]{1,0:T(8,128)(2,1)S(1)}, u32[]{:S(2)}, u32[]{:S(2)}) collective-permute-start(bf16[16,4096]{1,0:T(8,128)(2,1)S(1)} %get-tuple-element.99), channel_id=1, source_target_pairs={{0,16},{1,17},{2,18},{3,19},{4,20},{5,21},{6,22},{7,23},{8,24},{9,... | collective-permute-start | bytes 393224 | tf_op jit(solution)/shard_map/ppermute | solution.py:537
  12.3 8.3 %collective-permute-start.3 = (bf16[16,2048]{1,0:T(8,128)(2,1)S(1)}, bf16[16,2048]{1,0:T(8,128)(2,1)S(1)}, u32[]{:S(2)}, u32[]{:S(2)}) collective-permute-start(bf16[16,2048]{1,0:T(8,128)(2,1)S(1)} %get-tuple-element.102), channel_id=1, source_target_pairs={{0,2},{1,3},{2,0},{3,1},{4,6},{5,7},{6,4},{7,5},{8,10},{9,11},{10,... | collective-permute-start | bytes 196616 | tf_op jit(solution)/shard_map/ppermute | solution.py:35
  14.8 5.8 %collective-permute-start = (f32[2,8,4,128]{3,2,1,0:T(4,128)S(1)}, f32[2,8,4,128]{3,2,1,0:T(4,128)S(1)}, u32[]{:S(2)}, u32[]{:S(2)}) collective-permute-start(f32[2,8,4,128]{3,2,1,0:T(4,128)S(1)} %get-tuple-element.96), channel_id=1, source_target_pairs={{0,4},{4,8},{8,12},{12,0},{1,5},{5,9},{9,13},{13,1},{2,6},{6,10},{... | collective-permute-start | bytes 98312 | tf_op jit(solution)/shard_map/ppermute | solution.py:538
  16.4 4.3 %collective-permute-start.1 = (f32[2,8,4,128]{3,2,1,0:T(4,128)S(1)}, f32[2,8,4,128]{3,2,1,0:T(4,128)S(1)}, u32[]{:S(2)}, u32[]{:S(2)}) collective-permute-start(f32[2,8,4,128]{3,2,1,0:T(4,128)S(1)} %get-tuple-element.97), channel_id=1, source_target_pairs={{0,12},{4,0},{8,4},{12,8},{1,13},{5,1},{9,5},{13,9},{2,14},{6,2},{... | collective-permute-start | bytes 98312 | tf_op jit(solution)/shard_map/ppermute | solution.py:539
  24.4 13.9 %collective-permute-start.9 = (bf16[256,1024]{1,0:T(8,128)(2,1)S(1)}, bf16[256,1024]{1,0:T(8,128)(2,1)S(1)}, u32[]{:S(2)}, u32[]{:S(2)}) collective-permute-start(bf16[256,1024]{1,0:T(8,128)(2,1)S(1)} %get-tuple-element.106.refs_2_.refs_6_.refs_8_), channel_id=1, source_target_pairs={{0,4},{4,0},{8,12},{12,8},{1,5},{5,1},{9,13},{13,9},{2,6},{6,2},{1... | collective-permute-start | bytes 1572872 | tf_op jit(solution)/shard_map/ppermute | solution.py:35
  25.7 12.7 %collective-permute-start.10 = (bf16[256,1024]{1,0:T(8,128)(2,1)S(1)}, bf16[256,1024]{1,0:T(8,128)(2,1)S(1)}, u32[]{:S(2)}, u32[]{:S(2)}) collective-permute-start(bf16[256,1024]{1,0:T(8,128)(2,1)S(1)} %get-tuple-element.107), channel_id=1, source_target_pairs={{16,0},{17,1},{18,2},{19,3},{20,4},{21,5},{22,6},{23,7},{24,8},{25... | collective-permute-start | bytes 1572872 | tf_op jit(solution)/shard_map/ppermute | solution.py:546
  27.0 10.2 %collective-permute-start.7 = (bf16[32,2048]{1,0:T(8,128)(2,1)S(1)}, bf16[32,2048]{1,0:T(8,128)(2,1)S(1)}, u32[]{:S(2)}, u32[]{:S(2)}) collective-permute-start(bf16[32,2048]{1,0:T(8,128)(2,1)S(1)} %get-tuple-element.105.refs_0_), channel_id=1, source_target_pairs={{0,8},{4,12},{8,0},{12,4},{1,9},{5,13},{9,1},{13,5},{2,10},{6,14},... | collective-permute-start | bytes 393224 | tf_op jit(solution)/shard_map/ppermute | solution.py:35
  30.1 3.4 %collective-permute-start.6 = (f32[72,128]{1,0:T(8,128)S(1)}, f32[72,128]{1,0:T(8,128)S(1)}, u32[]{:S(2)}, u32[]{:S(2)}) collective-permute-start(f32[72,128]{1,0:T(8,128)S(1)} %get-tuple-element.104), channel_id=1, source_target_pairs={{0,3},{1,0},{2,1},{3,2},{4,7},{5,4},{6,5},{7,6},{8,11},{9,8},{10,9... | collective-permute-start | bytes 110600 | tf_op jit(solution)/shard_map/ppermute | solution.py:550
  33.5 9.0 %collective-permute-start.8 = (bf16[256,1024]{1,0:T(8,128)(2,1)S(1)}, bf16[256,1024]{1,0:T(8,128)(2,1)S(1)}, u32[]{:S(2)}, u32[]{:S(2)}) collective-permute-start(bf16[256,1024]{1,0:T(8,128)(2,1)S(1)} %get-tuple-element.106.refs_2_.refs_6_.refs_8_), channel_id=1, source_target_pairs={{0,1},{1,0},{2,3},{3,2},{4,5},{5,4},{6,7},{7,6},{8,9},{9,8},{10,11... | collective-permute-start | bytes 1572872 | tf_op jit(solution)/shard_map/ppermute | solution.py:35
  38.6 4.0 %collective-permute-start.11 = (bf16[256,1024]{1,0:T(8,128)(2,1)S(1)}, bf16[256,1024]{1,0:T(8,128)(2,1)S(1)}, u32[]{:S(2)}, u32[]{:S(2)}) collective-permute-start(bf16[256,1024]{1,0:T(8,128)(2,1)S(1)} %get-tuple-element.109.refs_4_.refs_8_.refs_10_), channel_id=1, source_target_pairs={{0,1},{1,0},{2,3},{3,2},{4,5},{5,4},{6,7},{7,6},{8,9},{9,8},{10,11... | collective-permute-start | bytes 1572872 | tf_op jit(solution)/shard_map/ppermute | solution.py:35
  38.7 14.9 %collective-permute-start.12 = (bf16[256,1024]{1,0:T(8,128)(2,1)S(1)}, bf16[256,1024]{1,0:T(8,128)(2,1)S(1)}, u32[]{:S(2)}, u32[]{:S(2)}) collective-permute-start(bf16[256,1024]{1,0:T(8,128)(2,1)S(1)} %get-tuple-element.113.refs_2_.refs_5_), channel_id=1, source_target_pairs={{0,4},{4,0},{8,12},{12,8},{1,5},{5,1},{9,13},{13,9},{2,6},{6,2},{1... | collective-permute-start | bytes 1572872 | tf_op jit(solution)/shard_map/ppermute | solution.py:35
  41.0 15.9 %collective-permute-start.13 = (bf16[256,1024]{1,0:T(8,128)(2,1)S(1)}, bf16[256,1024]{1,0:T(8,128)(2,1)S(1)}, u32[]{:S(2)}, u32[]{:S(2)}) collective-permute-start(bf16[256,1024]{1,0:T(8,128)(2,1)S(1)} %get-tuple-element.114), channel_id=1, source_target_pairs={{16,0},{17,1},{18,2},{19,3},{20,4},{21,5},{22,6},{23,7},{24,8},{25... | collective-permute-start | bytes 1572872 | tf_op jit(solution)/shard_map/ppermute | solution.py:555
  42.3 17.9 %collective-permute-start.19 = (bf16[256,1024]{1,0:T(8,128)(2,1)S(1)}, bf16[256,1024]{1,0:T(8,128)(2,1)S(1)}, u32[]{:S(2)}, u32[]{:S(2)}) collective-permute-start(bf16[256,1024]{1,0:T(8,128)(2,1)S(1)} %get-tuple-element.113.refs_2_.refs_5_), channel_id=1, source_target_pairs={{0,1},{1,0},{2,3},{3,2},{4,5},{5,4},{6,7},{7,6},{8,9},{9,8},{10,11... | collective-permute-start | bytes 1572872 | tf_op jit(solution)/shard_map/ppermute | solution.py:35
  57.0 6.9 %collective-permute-start.20 = (bf16[256,1024]{1,0:T(8,128)(2,1)S(1)}, bf16[256,1024]{1,0:T(8,128)(2,1)S(1)}, u32[]{:S(2)}, u32[]{:S(2)}) collective-permute-start(bf16[256,1024]{1,0:T(8,128)(2,1)S(1)} %get-tuple-element.124.refs_4_.refs_7_), channel_id=1, source_target_pairs={{0,1},{1,0},{2,3},{3,2},{4,5},{5,4},{6,7},{7,6},{8,9},{9,8},{10,11... | collective-permute-start | bytes 1572872 | tf_op jit(solution)/shard_map/ppermute | solution.py:35
  57.1 16.2 %collective-permute-start.14 = (f32[2,8,64,128]{3,2,1,0:T(8,128)S(1)}, f32[2,8,64,128]{3,2,1,0:T(8,128)S(1)}, u32[]{:S(2)}, u32[]{:S(2)}) collective-permute-start(f32[2,8,64,128]{3,2,1,0:T(8,128)S(1)} %get-tuple-element.116), channel_id=1, source_target_pairs={{0,16},{1,17},{2,18},{3,19},{4,20},{5,21},{6,22},{7,23},{8,24},{9,... | collective-permute-start | bytes 1572872 | tf_op jit(solution)/shard_map/ppermute | solution.py:588
  58.6 20.2 %collective-permute-start.17 = (bf16[256,1024]{1,0:T(8,128)(2,1)S(1)}, bf16[256,1024]{1,0:T(8,128)(2,1)S(1)}, u32[]{:S(2)}, u32[]{:S(2)}) collective-permute-start(bf16[256,1024]{1,0:T(8,128)(2,1)S(1)} %get-tuple-element.121.refs_5_.refs_4_), channel_id=1, source_target_pairs={{0,4},{4,0},{8,12},{12,8},{1,5},{5,1},{9,13},{13,9},{2,6},{6,2},{1... | collective-permute-start | bytes 1572872 | tf_op jit(solution)/shard_map/ppermute | solution.py:35
  59.7 4.3 %collective-permute-start.18 = (bf16[64,512]{1,0:T(8,128)(2,1)S(1)}, bf16[64,512]{1,0:T(8,128)(2,1)S(1)}, u32[]{:S(2)}, u32[]{:S(2)}) collective-permute-start(bf16[64,512]{1,0:T(8,128)(2,1)S(1)} %get-tuple-element.123), channel_id=1, source_target_pairs={{0,2},{1,3},{2,0},{3,1},{4,6},{5,7},{6,4},{7,5},{8,10},{9,11},{10,... | collective-permute-start | bytes 196616 | tf_op jit(solution)/shard_map/ppermute | solution.py:35
  64.4 14.3 %collective-permute-start.21 = (bf16[64,2176]{1,0:T(8,128)(2,1)S(1)}, bf16[64,2176]{1,0:T(8,128)(2,1)S(1)}, u32[]{:S(2)}, u32[]{:S(2)}) collective-permute-start(bf16[64,2176]{1,0:T(8,128)(2,1)S(1)} %get-tuple-element.127), channel_id=1, source_target_pairs={{0,8},{4,12},{8,0},{12,4},{1,9},{5,13},{9,1},{13,5},{2,10},{6,14},... | collective-permute-start | bytes 835592 | tf_op jit(solution)/shard_map/ppermute | solution.py:35
  66.2 7.1 %collective-permute-start.16 = (bf16[16,4096]{1,0:T(8,128)(2,1)S(1)}, bf16[16,4096]{1,0:T(8,128)(2,1)S(1)}, u32[]{:S(2)}, u32[]{:S(2)}) collective-permute-start(bf16[16,4096]{1,0:T(8,128)(2,1)S(1)} %get-tuple-element.120), channel_id=1, source_target_pairs={{0,16},{1,17},{2,18},{3,19},{4,20},{5,21},{6,22},{7,23},{8,24},{9,... | collective-permute-start | bytes 393224 | tf_op jit(solution)/shard_map/ppermute | solution.py:584
  67.5 5.8 %collective-permute-start.15 = (bf16[64,1024]{1,0:T(8,128)(2,1)S(1)}, bf16[64,1024]{1,0:T(8,128)(2,1)S(1)}, u32[]{:S(2)}, u32[]{:S(2)}) collective-permute-start(bf16[64,1024]{1,0:T(8,128)(2,1)S(1)} %get-tuple-element.118.refs_2_), channel_id=1, source_target_pairs={{0,1},{1,0},{2,3},{3,2},{4,5},{5,4},{6,7},{7,6},{8,9},{9,8},{10,11... | collective-permute-start | bytes 393224 | tf_op jit(solution)/shard_map/ppermute | solution.py:35
  73.3 8.2 %collective-permute-start.24 = (bf16[256,1024]{1,0:T(8,128)(2,1)S(1)}, bf16[256,1024]{1,0:T(8,128)(2,1)S(1)}, u32[]{:S(2)}, u32[]{:S(2)}) collective-permute-start(bf16[256,1024]{1,0:T(8,128)(2,1)S(1)} %get-tuple-element.121.refs_5_.refs_4_), channel_id=1, source_target_pairs={{0,1},{1,0},{2,3},{3,2},{4,5},{5,4},{6,7},{7,6},{8,9},{9,8},{10,11... | collective-permute-start | bytes 1572872 | tf_op jit(solution)/shard_map/ppermute | solution.py:35
  79.1 4.6 %collective-permute-start.25 = (bf16[256,1024]{1,0:T(8,128)(2,1)S(1)}, bf16[256,1024]{1,0:T(8,128)(2,1)S(1)}, u32[]{:S(2)}, u32[]{:S(2)}) collective-permute-start(bf16[256,1024]{1,0:T(8,128)(2,1)S(1)} %get-tuple-element.133.refs_7_.refs_6_), channel_id=1, source_target_pairs={{0,1},{1,0},{2,3},{3,2},{4,5},{5,4},{6,7},{7,6},{8,9},{9,8},{10,11... | collective-permute-start | bytes 1572872 | tf_op jit(solution)/shard_map/ppermute | solution.py:35
  79.1 4.5 %collective-permute-start.23 = (bf16[16,2048]{1,0:T(8,128)(2,1)S(1)}, bf16[16,2048]{1,0:T(8,128)(2,1)S(1)}, u32[]{:S(2)}, u32[]{:S(2)}) collective-permute-start(bf16[16,2048]{1,0:T(8,128)(2,1)S(1)} %get-tuple-element.130), channel_id=1, source_target_pairs={{0,2},{1,3},{2,0},{3,1},{4,6},{5,7},{6,4},{7,5},{8,10},{9,11},{10,... | collective-permute-start | bytes 196616 | tf_op jit(solution)/shard_map/ppermute | solution.py:35
  79.9 8.4 %collective-permute-start.22 = (bf16[128,1024]{1,0:T(8,128)(2,1)S(1)}, bf16[128,1024]{1,0:T(8,128)(2,1)S(1)}, u32[]{:S(2)}, u32[]{:S(2)}) collective-permute-start(bf16[128,1024]{1,0:T(8,128)(2,1)S(1)} %get-tuple-element.128.refs_8_), channel_id=1, source_target_pairs={{0,4},{4,0},{8,12},{12,8},{1,5},{5,1},{9,13},{13,9},{2,6},{6,2},{1... | collective-permute-start | bytes 786440 | tf_op jit(solution)/shard_map/ppermute | solution.py:35
  84.5 4.6 %collective-permute-start.26 = (bf16[64,1536]{1,0:T(8,128)(2,1)S(1)}, bf16[64,1536]{1,0:T(8,128)(2,1)S(1)}, u32[]{:S(2)}, u32[]{:S(2)}) collective-permute-start(bf16[64,1536]{1,0:T(8,128)(2,1)S(1)} %get-tuple-element.136), channel_id=1, source_target_pairs={{0,1},{1,0},{2,3},{3,2},{4,5},{5,4},{6,7},{7,6},{8,9},{9,8},{10,11... | collective-permute-start | bytes 589832 | tf_op jit(solution)/shard_map/ppermute | solution.py:35
  84.6 4.5 %collective-permute-start.27 = (bf16[64,512]{1,0:T(8,128)(2,1)S(1)}, bf16[64,512]{1,0:T(8,128)(2,1)S(1)}, u32[]{:S(2)}, u32[]{:S(2)}) collective-permute-start(bf16[64,512]{1,0:T(8,128)(2,1)S(1)} %get-tuple-element.138), channel_id=1, source_target_pairs={{0,2},{1,3},{2,0},{3,1},{4,6},{5,7},{6,4},{7,5},{8,10},{9,11},{10,... | collective-permute-start | bytes 196616 | tf_op jit(solution)/shard_map/ppermute | solution.py:35
  89.6 21.6 %collective-permute-start.28 = (bf16[128,1280]{1,0:T(8,128)(2,1)S(1)}, bf16[128,1280]{1,0:T(8,128)(2,1)S(1)}, u32[]{:S(2)}, u32[]{:S(2)}) collective-permute-start(bf16[128,1280]{1,0:T(8,128)(2,1)S(1)} %get-tuple-element.140), channel_id=1, source_target_pairs={{0,4},{4,0},{8,12},{12,8},{1,5},{5,1},{9,13},{13,9},{2,6},{6,2},{1... | collective-permute-start | bytes 983048 | tf_op jit(solution)/shard_map/ppermute | solution.py:35
  91.4 9.2 %collective-permute-start.31 = (bf16[128,1024]{1,0:T(8,128)(2,1)S(1)}, bf16[128,1024]{1,0:T(8,128)(2,1)S(1)}, u32[]{:S(2)}, u32[]{:S(2)}) collective-permute-start(bf16[128,1024]{1,0:T(8,128)(2,1)S(1)} %get-tuple-element.128.refs_8_), channel_id=1, source_target_pairs={{0,16},{16,0},{1,17},{17,1},{2,18},{18,2},{3,19},{19,3},{4,20},{20... | collective-permute-start | bytes 786440 | tf_op jit(solution)/shard_map/ppermute | solution.py:35
  91.4 19.8 %collective-permute-start.29 = (bf16[64,2048]{1,0:T(8,128)(2,1)S(1)}, bf16[64,2048]{1,0:T(8,128)(2,1)S(1)}, u32[]{:S(2)}, u32[]{:S(2)}) collective-permute-start(bf16[64,2048]{1,0:T(8,128)(2,1)S(1)} %get-tuple-element.142), channel_id=1, source_target_pairs={{0,8},{4,12},{8,0},{12,4},{1,9},{5,13},{9,1},{13,5},{2,10},{6,14},... | collective-permute-start | bytes 786440 | tf_op jit(solution)/shard_map/ppermute | solution.py:35
  92.3 18.9 %collective-permute-start.32 = (bf16[128,1024]{1,0:T(8,128)(2,1)S(1)}, bf16[128,1024]{1,0:T(8,128)(2,1)S(1)}, u32[]{:S(2)}, u32[]{:S(2)}) collective-permute-start(bf16[128,1024]{1,0:T(8,128)(2,1)S(1)} %get-tuple-element.146.refs_9_), channel_id=1, source_target_pairs={{0,16},{16,0},{1,17},{17,1},{2,18},{18,2},{3,19},{19,3},{4,20},{20... | collective-permute-start | bytes 786440 | tf_op jit(solution)/shard_map/ppermute | solution.py:35
  94.3 16.8 %collective-permute-start.30 = (bf16[32,2048]{1,0:T(8,128)(2,1)S(1)}, bf16[32,2048]{1,0:T(8,128)(2,1)S(1)}, u32[]{:S(2)}, u32[]{:S(2)}) collective-permute-start(bf16[32,2048]{1,0:T(8,128)(2,1)S(1)} %get-tuple-element.143.refs_5_), channel_id=1, source_target_pairs={{0,8},{4,12},{8,0},{12,4},{1,9},{5,13},{9,1},{13,5},{2,10},{6,14},... | collective-permute-start | bytes 393224 | tf_op jit(solution)/shard_map/ppermute | solution.py:35
  112.0 4.6 %collective-permute-start.33 = (bf16[64,1536]{1,0:T(8,128)(2,1)S(1)}, bf16[64,1536]{1,0:T(8,128)(2,1)S(1)}, u32[]{:S(2)}, u32[]{:S(2)}) collective-permute-start(bf16[64,1536]{1,0:T(8,128)(2,1)S(1)} %get-tuple-element.148), channel_id=1, source_target_pairs={{0,1},{1,0},{2,3},{3,2},{4,5},{5,4},{6,7},{7,6},{8,9},{9,8},{10,11... | collective-permute-start | bytes 589832 | tf_op jit(solution)/shard_map/ppermute | solution.py:35
  112.1 4.5 %collective-permute-start.34 = (bf16[64,512]{1,0:T(8,128)(2,1)S(1)}, bf16[64,512]{1,0:T(8,128)(2,1)S(1)}, u32[]{:S(2)}, u32[]{:S(2)}) collective-permute-start(bf16[64,512]{1,0:T(8,128)(2,1)S(1)} %get-tuple-element.150), channel_id=1, source_target_pairs={{0,2},{1,3},{2,0},{3,1},{4,6},{5,7},{6,4},{7,5},{8,10},{9,11},{10,... | collective-permute-start | bytes 196616 | tf_op jit(solution)/shard_map/ppermute | solution.py:35
  112.7 10.6 %collective-permute-start.37 = (bf16[128,1280]{1,0:T(8,128)(2,1)S(1)}, bf16[128,1280]{1,0:T(8,128)(2,1)S(1)}, u32[]{:S(2)}, u32[]{:S(2)}) collective-permute-start(bf16[128,1280]{1,0:T(8,128)(2,1)S(1)} %get-tuple-element.158.refs_4_.refs_0_), channel_id=1, source_target_pairs={{0,16},{16,0},{1,17},{17,1},{2,18},{18,2},{3,19},{19,3},{4,20},{20... | collective-permute-start | bytes 983048 | tf_op jit(solution)/shard_map/ppermute | solution.py:35
  114.4 15.1 %collective-permute-start.38 = (bf16[128,1280]{1,0:T(8,128)(2,1)S(1)}, bf16[128,1280]{1,0:T(8,128)(2,1)S(1)}, u32[]{:S(2)}, u32[]{:S(2)}) collective-permute-start(bf16[128,1280]{1,0:T(8,128)(2,1)S(1)} %get-tuple-element.159.refs_5_.refs_1_), channel_id=1, source_target_pairs={{0,16},{16,0},{1,17},{17,1},{2,18},{18,2},{3,19},{19,3},{4,20},{20... | collective-permute-start | bytes 983048 | tf_op jit(solution)/shard_map/ppermute | solution.py:35
  117.1 15.0 %collective-permute-start.35 = (bf16[128,1280]{1,0:T(8,128)(2,1)S(1)}, bf16[128,1280]{1,0:T(8,128)(2,1)S(1)}, u32[]{:S(2)}, u32[]{:S(2)}) collective-permute-start(bf16[128,1280]{1,0:T(8,128)(2,1)S(1)} %get-tuple-element.152), channel_id=1, source_target_pairs={{0,4},{4,0},{8,12},{12,8},{1,5},{5,1},{9,13},{13,9},{2,6},{6,2},{1... | collective-permute-start | bytes 983048 | tf_op jit(solution)/shard_map/ppermute | solution.py:35
  117.2 12.7 %collective-permute-start.36 = (bf16[64,2048]{1,0:T(8,128)(2,1)S(1)}, bf16[64,2048]{1,0:T(8,128)(2,1)S(1)}, u32[]{:S(2)}, u32[]{:S(2)}) collective-permute-start(bf16[64,2048]{1,0:T(8,128)(2,1)S(1)} %get-tuple-element.156), channel_id=1, source_target_pairs={{0,8},{4,12},{8,0},{12,4},{1,9},{5,13},{9,1},{13,5},{2,10},{6,14},... | collective-permute-start | bytes 786440 | tf_op jit(solution)/shard_map/ppermute | solution.py:35
  132.9 4.9 %collective-permute-start.39 = (bf16[64,1536]{1,0:T(8,128)(2,1)S(1)}, bf16[64,1536]{1,0:T(8,128)(2,1)S(1)}, u32[]{:S(2)}, u32[]{:S(2)}) collective-permute-start(bf16[64,1536]{1,0:T(8,128)(2,1)S(1)} %get-tuple-element.161), channel_id=1, source_target_pairs={{0,1},{1,0},{2,3},{3,2},{4,5},{5,4},{6,7},{7,6},{8,9},{9,8},{10,11... | collective-permute-start | bytes 589832 | tf_op jit(solution)/shard_map/ppermute | solution.py:35
  133.0 4.9 %collective-permute-start.40 = (bf16[64,640]{1,0:T(8,128)(2,1)S(1)}, bf16[64,640]{1,0:T(8,128)(2,1)S(1)}, u32[]{:S(2)}, u32[]{:S(2)}) collective-permute-start(bf16[64,640]{1,0:T(8,128)(2,1)S(1)} %get-tuple-element.166), channel_id=1, source_target_pairs={{0,2},{1,3},{2,0},{3,1},{4,6},{5,7},{6,4},{7,5},{8,10},{9,11},{10,... | collective-permute-start | bytes 245768 | tf_op jit(solution)/shard_map/ppermute | solution.py:35
  138.0 9.3 %collective-permute-start.47 = (bf16[128,1280]{1,0:T(8,128)(2,1)S(1)}, bf16[128,1280]{1,0:T(8,128)(2,1)S(1)}, u32[]{:S(2)}, u32[]{:S(2)}) collective-permute-start(bf16[128,1280]{1,0:T(8,128)(2,1)S(1)} %get-tuple-element.177), channel_id=1, source_target_pairs={{0,4},{4,0},{8,12},{12,8},{1,5},{5,1},{9,13},{13,9},{2,6},{6,2},{1... | collective-permute-start | bytes 983048 | tf_op jit(solution)/shard_map/ppermute | solution.py:35
  138.5 18.6 %collective-permute-start.48 = (bf16[128,1280]{1,0:T(8,128)(2,1)S(1)}, bf16[128,1280]{1,0:T(8,128)(2,1)S(1)}, u32[]{:S(2)}, u32[]{:S(2)}) collective-permute-start(bf16[128,1280]{1,0:T(8,128)(2,1)S(1)} %get-tuple-element.176.refs_0_.refs_4_), channel_id=1, source_target_pairs={{0,16},{16,0},{1,17},{17,1},{2,18},{18,2},{3,19},{19,3},{4,20},{20... | collective-permute-start | bytes 983048 | tf_op jit(solution)/shard_map/ppermute | solution.py:35
  147.4 12.2 %collective-permute-start.49 = (bf16[128,1280]{1,0:T(8,128)(2,1)S(1)}, bf16[128,1280]{1,0:T(8,128)(2,1)S(1)}, u32[]{:S(2)}, u32[]{:S(2)}) collective-permute-start(bf16[128,1280]{1,0:T(8,128)(2,1)S(1)} %collective-permute-done.47.refs_1_.refs_5_), channel_id=1, source_target_pairs={{0,16},{16,0},{1,17},{17,1},{2,18},{18,2},{3,19},{19,3},{4,20},{20... | collective-permute-start | bytes 983048 | tf_op jit(solution)/shard_map/ppermute | solution.py:35
  149.1 15.9 %collective-permute-start.42 = (bf16[128,1280]{1,0:T(8,128)(2,1)S(1)}, bf16[128,1280]{1,0:T(8,128)(2,1)S(1)}, u32[]{:S(2)}, u32[]{:S(2)}) collective-permute-start(bf16[128,1280]{1,0:T(8,128)(2,1)S(1)} %get-tuple-element.172.refs_0_), channel_id=1, source_target_pairs={{0,16},{16,0},{1,17},{17,1},{2,18},{18,2},{3,19},{19,3},{4,20},{20... | collective-permute-start | bytes 983048 | tf_op jit(solution)/shard_map/ppermute | solution.py:35
  149.4 22.5 %collective-permute-start.43 = (bf16[128,1280]{1,0:T(8,128)(2,1)S(1)}, bf16[128,1280]{1,0:T(8,128)(2,1)S(1)}, u32[]{:S(2)}, u32[]{:S(2)}) collective-permute-start(bf16[128,1280]{1,0:T(8,128)(2,1)S(1)} %get-tuple-element.173.refs_1_), channel_id=1, source_target_pairs={{0,16},{16,0},{1,17},{17,1},{2,18},{18,2},{3,19},{19,3},{4,20},{20... | collective-permute-start | bytes 983048 | tf_op jit(solution)/shard_map/ppermute | solution.py:35
  152.4 4.3 %collective-permute-start.44 = (bf16[128,256]{1,0:T(8,128)(2,1)S(1)}, bf16[128,256]{1,0:T(8,128)(2,1)S(1)}, u32[]{:S(2)}, u32[]{:S(2)}) collective-permute-start(bf16[128,256]{1,0:T(8,128)(2,1)S(1)} %get-tuple-element.175), channel_id=1, source_target_pairs={{0,4},{4,0},{8,12},{12,8},{1,5},{5,1},{9,13},{13,9},{2,6},{6,2},{1... | collective-permute-start | bytes 196616 | tf_op jit(solution)/shard_map/ppermute | solution.py:35
  156.8 15.2 %collective-permute-start.45 = (bf16[128,256]{1,0:T(8,128)(2,1)S(1)}, bf16[128,256]{1,0:T(8,128)(2,1)S(1)}, u32[]{:S(2)}, u32[]{:S(2)}) collective-permute-start(bf16[128,256]{1,0:T(8,128)(2,1)S(1)} %get-tuple-element.174.refs_4_), channel_id=1, source_target_pairs={{0,16},{16,0},{1,17},{17,1},{2,18},{18,2},{3,19},{19,3},{4,20},{20... | collective-permute-start | bytes 196616 | tf_op jit(solution)/shard_map/ppermute | solution.py:35
  157.0 15.6 %collective-permute-start.46 = (bf16[128,256]{1,0:T(8,128)(2,1)S(1)}, bf16[128,256]{1,0:T(8,128)(2,1)S(1)}, u32[]{:S(2)}, u32[]{:S(2)}) collective-permute-start(bf16[128,256]{1,0:T(8,128)(2,1)S(1)} %collective-permute-done.44.refs_5_), channel_id=1, source_target_pairs={{0,16},{16,0},{1,17},{17,1},{2,18},{18,2},{3,19},{19,3},{4,20},{20... | collective-permute-start | bytes 196616 | tf_op jit(solution)/shard_map/ppermute | solution.py:35
  (11 other events, 77.2 us)

commit v3 on v2

--- a/solution.py
+++ b/solution.py
@@ -93,6 +93,7 @@
         after = ([] if self.token is None else [self.token]) + self.pending
         self.pending, self.riders = [], []
         vmem, anywhere = pl.BlockSpec(memory_space=pltpu.VMEM), pl.BlockSpec(memory_space=pl.ANY)
+        hbm = pl.BlockSpec(memory_space=pltpu.HBM)
         args, in_specs, outs, out_specs, scratch, aliases, room = [], [], [], [], [], {}, 0
         spans = []
         for work in works:
@@ -100,12 +101,14 @@
             for index, target in work.aliases.items():
                 aliases[len(args) + index] = len(outs) + target
             for k, value in enumerate(work.args):
-                in_specs.append(anywhere if k in work.left else vmem)
+                in_specs.append(hbm if k in work.left else vmem)
+                if k in work.left:
+                    work.args[k] = pltpu.with_memory_space_constraint(value, pltpu.HBM)
                 room += 0 if k in work.left else value.size * value.dtype.itemsize
             for k, value in enumerate(work.outs):
-                out_specs.append(anywhere if k in work.in_hbm else vmem)
+                out_specs.append(hbm if k in work.in_hbm else vmem)
                 room += 0 if k in work.in_hbm else value.size * value.dtype.itemsize
-            in_specs += [anywhere] * len(work.extra)
+            in_specs += [hbm] * len(work.extra)
             args += work.args + work.extra
             outs += work.outs
             scratch += work.scratch
@@ -357,8 +360,9 @@
         def body(ins, outs, scratch):
             (sems,) = scratch
             solving = lax.axis_index("role") == SOLVER
-            ahead = pltpu.make_async_copy(ins[2].at[next_index], outs[1], sems.at[0])
-            ahead.start()
+            if following is not None:
+                ahead = pltpu.make_async_copy(ins[2].at[next_index], outs[1], sems.at[0])
+                ahead.start()
 
             @pl.when(solving)
             def _():
@@ -370,15 +374,15 @@
                 mine.start()
                 mine.wait()
 
-            ahead.wait()
-
-        sent = following.shape[len(next_index) :]
-        outs = [struct(arrived.shape, BF16), struct(sent, following.dtype)]
+            if following is not None:
+                ahead.wait()
+
+        more = [] if following is None else [following]
         return order.call(
             body,
             "held",
-            outs,
-            [arrived, own, following],
+            [struct(arrived.shape, BF16)] * (1 + len(more)),
+            [arrived, own] + more,
             left=(1, 2),
             scratch=[pltpu.SemaphoreType.DMA((2,))],
         )
@@ -413,6 +417,7 @@
         write_patches(Tile(lambda s, p: ins[0][s, p], counts), outs[:2])
         outs[2][...] = ins[0][:, :, :STEPS]
         outs[3][...] = ins[0][:, :, rows_in - STEPS :]
+        outs[4][...] = ins[0][...]
 
     def split_patches(own, arrived):
         def body(ins, outs, _):
@@ -487,6 +492,54 @@
                 body, [struct((m * core.size, cols), BF16)] * count, self.parts
             )
 
+        def join_for_role(self):
+            self.join()
+
+            def body(ins, outs, _):
+                for c, ref in enumerate(ins):
+                    outs[0][c * m : (c + 1) * m, :] = ref[...]
+
+            cols = self.base + self.width_count * half_width
+            self.whole = order.ride(body, [struct((m * core.size, cols), BF16)], self.parts)
+
+        def send_role_first(self):
+            (whole,) = self.whole.results
+            cuts = self.joining.results
+            self.kept = cuts[0]
+            self.banded = merged(
+                [band.shifted(cuts[k % len(cuts)], k) for k in range(1, band.size)]
+            )
+            self.crossed = role.from_others(whole)
+
+        def cut_crossed(self):
+            base = self.base
+
+            def body(ins, outs, _):
+                for number, ref in enumerate(ins):
+                    for k in range(band.size):
+                        out = outs[number * band.size + k]
+                        out[:, :base] = ref[:, :base]
+                        for index in range(self.width_count):
+                            first = base + index * half_width + (-k) % band.size * own_rows
+                            target = base + index * own_rows
+                            out[:, target : target + own_rows] = ref[:, first : first + own_rows]
+
+            cols = base + self.width_count * own_rows
+            self.cutting = order.ride(
+                body,
+                [struct((m * core.size, cols), BF16)] * (band.size * len(self.crossed)),
+                self.crossed,
+            )
+
+        def band_crossed(self):
+            self.arrived = []
+            cuts = self.cutting.results
+            for number in range(len(self.crossed)):
+                own = cuts[number * band.size : (number + 1) * band.size]
+                self.arrived += [own[0]] + merged(
+                    [band.shifted(own[k], k) for k in range(1, band.size)]
+                )
+
         def send(self):
             cuts = self.joining.results
             self.kept = cuts[0]
@@ -506,6 +559,23 @@
         def pieces(self):
             return [self.kept] + self.banded + self.arrived
 
+    def product(lefts, left_col, rights, right_col):
+        total = None
+        for left, right in zip(lefts, rights):
+            term = cols_dot(
+                left[:, left_col : left_col + own_rows], right[:, right_col : right_col + own_cols]
+            )
+            total = term if total is None else total + term
+        return total
+
+    def begun_gradient(lefts, left_col, rights, right_col):
+        count = len(lefts)
+
+        def body(ins, outs, _):
+            outs[0][...] = product(ins[:count], left_col, ins[count:], right_col)
+
+        return order.ride(body, [struct((own_rows, own_cols), F32)], lefts + rights)
+
     def selected_state(own, arrived):
         def body(ins, outs, scratch):
             solving = lax.axis_index("role") == SOLVER
@@ -528,22 +598,24 @@
 
     arrived_embed = lax.ppermute(embed[0], "role", to_solver)
     edge_struct = struct(cells.shape[:2] + (STEPS, cells.shape[3]), F32)
-    *start_halves, first_rows, last_rows = order.call(
+    *start_halves, first_rows, last_rows, cells = order.call(
         patches_of,
         "patches",
-        [struct((half_rows, features), BF16)] * 2 + [edge_struct] * 2,
+        [struct((half_rows, features), BF16)] * 2 + [edge_struct] * 2 + [struct(cells.shape, F32)],
         [cells],
     )
     arrived_start = lax.ppermute(start_halves[1], "role", to_trainer)
     head_rows = lax.ppermute(last_rows, "dp", around("dp", 1))
     tail_rows = lax.ppermute(first_rows, "dp", around("dp", -1))
     splitting = split_patches(start_halves[0], arrived_start)
+    order.wait_for([head_rows, tail_rows])
     order.run("split")
-    ordering = order_rows(to_parts(splitting.results))
-    edging = packed_edges(order, cells, head_rows, tail_rows, STEPS)
     embed_kept, up_block = keep_arrived(arrived_embed, embed, 0, mlp, (0, 0))
     embed_own, embed_bands = own_pieces(embed_kept)
     arrived_up = lax.ppermute(up_block, "role", to_solver)
+    ordering = order_rows(to_parts(splitting.results))
+    edging = packed_edges(order, cells, head_rows, tail_rows, STEPS)
+    order.run("order")
     input_parts = widened(*ordering.results)
     (edges,) = edging.results
     from_left = lax.ppermute(edges, "mp", around("mp", 1))
@@ -581,13 +653,13 @@
     final_cells, *end_halves = stepped(
         order, cells, head_rows, tail_rows, from_left, from_right, STEPS, 2
     )
-    arrived_end = lax.ppermute(end_halves[1], "role", to_trainer)
+    (arrived_end,) = role.from_others(end_halves[1])
     relay = relayed(merged(up_bands))
-    down_kept, cells_sent = keep_arrived(arrived_down, mlp, (0, 1), final_cells, ())
+    order.wait_for(embed_others)
+    (down_kept,) = keep_arrived(arrived_down, mlp, (0, 1), None, ())
     down_own, down_bands = own_pieces(down_kept)
-    arrived_cells = lax.ppermute(cells_sent, "role", to_trainer)
     up_held = held_matrix(up_own, relay)
-    inputs_on = Gather(inputs[0], [inputs[(-k) % core.size] for k in range(1, core.size)], True, 0)
+    copying = relayed([final_cells])
 
     def added(mine, refs, cols):
         total = mine[...]
@@ -615,14 +687,16 @@
         [embed_mine] + embed_others + up_held.flat,
     )
     up_others = wide.from_others(up_sum)
+    (arrived_cells,) = role.from_others(copying.results[0])
     order.wait_for(up_others + [arrived_cells])
+    splitting = split_patches(end_halves[0], arrived_end)
+    inputs_on = Gather(inputs[0], [inputs[(-k) % core.size] for k in range(1, core.size)], True, 0)
     inputs_on.join()
-    splitting = split_patches(end_halves[0], arrived_end)
     relay = relayed(merged(down_bands))
     order.run("relay")
     down_held = held_matrix(down_own, relay)
+    target_cuts = to_parts(splitting.results)
     inputs_on.send()
-    ordering = order_rows(to_parts(splitting.results))
 
     def down_rows(ins, outs, _):
         value, others, matrix = ins[0][...], ins[2 : 1 + wide.size], ins[1 + wide.size :]
@@ -657,19 +731,24 @@
         [embedded, up_mine] + up_others + down_held.flat,
     )
     down_others = part.from_others(down_sum)
-    target_parts = widened(*ordering.results)
     active_on = Gather(active_packs[0], active_packs[1:], True, 1)
+    active_on.join()
     inputs_on.relay()
-    active_on.join()
+    order.wait_for(inputs_on.arrived)
 
     def predict_rows(ins, outs, _):
+        aims, ins = ins[: part.size], ins[part.size :]
         others, matrix = ins[2 : 1 + part.size], ins[1 + part.size :]
         mine, sent, stream = outs
         value = (ins[0][...] + added(ins[1], others, half_width)).astype(BF16)
         stream[...] = value
-        predicted = embed_held.to_cols(matrix, value)
-        mine[...] = predicted
-        sent[...] = predicted.astype(BF16)
+        mine[...] = embed_held.to_cols(matrix, value)
+        position = lax.axis_index("dp") // band.size * part.size
+        for k, ref in enumerate(aims):
+            slot = (lax.axis_index("mp") // core.size - k + part.size) % part.size
+            rows = pl.ds(pl.multiple_of((position + slot) * half_rows, half_rows), half_rows)
+            mine[rows, :] = mine[rows, :] - ref[...].astype(F32)
+        sent[...] = mine[...].astype(BF16)
 
     predict_mine, predict_sum, stream = order.call(
         predict_rows,
@@ -679,26 +758,21 @@
             struct((m, part_cols), BF16),
             struct((m, half_width), BF16),
         ],
-        [embedded, down_mine] + down_others + embed_held.flat,
+        target_cuts + [embedded, down_mine] + down_others + embed_held.flat,
     )
     predict_others = wide.from_others(predict_sum)
     inputs_on.forward()
     active_on.send()
     active_on.relay()
-    order.wait_for(inputs_on.arrived)
-
-    def residual_rows(ins, outs, scratch):
+    order.wait_for(inputs_on.arrived + active_on.arrived)
+
+    def residual_rows(ins, outs, _):
         inputs, ins = ins[: core.size], ins[core.size :]
         mine_in, others, ins = ins[0], ins[1 : wide.size], ins[wide.size :]
-        aims, stream, matrix = ins[: wide.size], ins[wide.size], ins[wide.size + 1 :]
+        stream, matrix = ins[0], ins[1:]
         mine, sent, *packs = outs
-        (aim,) = scratch
-        position = lax.axis_index("dp") // band.size
-        for k, rows in slots(position, wide.size, half_rows * part.size):
-            aim[rows, :] = aims[k][...]
         known = jnp.concatenate([ref[...] for ref in inputs], axis=1).astype(F32)
-        predicted = known + added(mine_in, others, part_cols)
-        value = ((predicted - aim[...].astype(F32)) * loss_scale).astype(BF16)
+        value = ((known + added(mine_in, others, part_cols)) * loss_scale).astype(BF16)
         for k in range(core.size):
             packs[k][:, :own_cols] = value[:, core_slot(k)]
             packs[k][:, own_cols:] = stream[...]
@@ -711,14 +785,13 @@
         "residual",
         [struct((m, half_width), F32), struct((m, half_width), BF16)]
         + [pack(True, 1)] * core.size,
-        inputs + [predict_mine] + predict_others + target_parts + [stream] + embed_held.flat,
-        scratch=[pltpu.VMEM((m, part_cols), BF16)],
+        inputs + [predict_mine] + predict_others + [stream] + embed_held.flat,
     )
     stream_others = part.from_others(stream_sum)
 
     active_on.forward()
     residual_on = Gather(residual_packs[0], residual_packs[1:], True, 1)
-    residual_on.join()
+    residual_on.join_for_role()
 
     def hidden_rows(ins, outs, _):
         others, matrix = ins[1 : part.size], ins[part.size :]
@@ -743,9 +816,8 @@
         [stream_mine] + stream_others + down_held.flat,
     )
     back_others = wide.from_others(back_sum)
-    residual_on.send()
-    residual_on.relay()
-    order.wait_for(active_on.arrived)
+    residual_on.send_role_first()
+    order.wait_for(active_on.arrived + residual_on.banded + residual_on.crossed)
 
     def normed_rows(ins, outs, _):
         stream_sent, others, matrix = ins[2], ins[3 : 2 + wide.size], ins[2 + wide.size :]
@@ -777,9 +849,12 @@
         [hidden_pre, back_mine, stream_sent] + back_others + up_held.flat,
     )
     normed_others = part.from_others(normed_sum)
-    residual_on.forward()
     hidden_on = Gather(hidden_packs[0], hidden_packs[1:], True, 1)
     hidden_on.join()
+    order.run("join")
+    hidden_on.send()
+    hidden_on.forward(False)
+    residual_on.cut_crossed()
 
     def embed_grad_rows(ins, outs, _):
         value, grad, scale_ref, mine, inner_ref, *others = ins
@@ -798,37 +873,27 @@
         [pack(False, 1)],
         [embedded, stream_grad, scale, normed_mine, inner_mine] + normed_others,
     )
-    hidden_on.send()
-    hidden_on.forward(False)
     embed_sent_on = Gather(embed_sent, [embed_sent] * (core.size - 1), False, 1)
     embed_sent_on.join()
     order.run("join")
     embed_sent_on.send()
     embed_sent_on.forward(False)
+    residual_on.band_crossed()
+    all_residual = residual_on.pieces()
+    embed_term = begun_gradient(all_residual, own_cols, all_residual, 0)
     state_out = selected_state(final_cells, arrived_cells)
 
-    def updated(name, terms, momentum, weight, index, begun=()):
-        pieces = {}
-        for pair in terms:
-            for arrays, _ in pair:
-                for array in arrays:
-                    pieces.setdefault(id(array), array)
-        places = {key: place for place, key in enumerate(pieces)}
-        arrays = list(pieces.values())
+    def updated(name, lefts, left_col, rights, right_col, momentum, weight, index, term=(), begun=()):
+        arrays = lefts + rights + list(term)
+        count = len(lefts)
         cuts = 2
         step = own_rows // cuts
 
         def body(ins, outs, scratch):
             mom_new, weight_new, sems = scratch
-            total = None
-            for (lefts, left_col), (rights, right_col) in terms:
-                for left, right in zip(lefts, rights):
-                    left_ref, right_ref = ins[places[id(left)]], ins[places[id(right)]]
-                    term = cols_dot(
-                        left_ref[:, left_col : left_col + own_rows],
-                        right_ref[:, right_col : right_col + own_cols],
-                    )
-                    total = term if total is None else total + term
+            total = product(ins[:count], left_col, ins[count : 2 * count], right_col)
+            for ref in ins[2 * count : len(arrays)]:
+                total = total + ref[...]
             mom, old = ins[len(arrays)], ins[len(arrays) + 1]
             copies = []
             for cut in range(cuts):
@@ -850,7 +915,6 @@
             for copy in copies:
                 copy.wait()
 
-        count = len(arrays) + 2
         return order.call(
             body,
             name,
@@ -862,26 +926,18 @@
                 pltpu.VMEM((own_rows, own_cols), BF16),
                 pltpu.SemaphoreType.DMA((2 * cuts,)),
             ],
-            aliases={count: 0, count + 1: 1} if begun else None,
+            aliases={len(arrays) + 2: 0, len(arrays) + 3: 1} if begun else None,
             extra=begun,
         )
 
-    all_inputs, all_active, all_residual = (
-        inputs_on.pieces(),
-        active_on.pieces(),
-        residual_on.pieces(),
-    )
+    all_inputs, all_active = inputs_on.pieces(), active_on.pieces()
     all_hidden, all_embed_sent = hidden_on.pieces(), embed_sent_on.pieces()
-    begun = updated("update_down", [((all_hidden, own_cols), (all_active, 0))], mom_mlp, mlp, (0, 1))
+    begun = updated("update_down", all_hidden, own_cols, all_active, 0, mom_mlp, mlp, (0, 1))
     mom_mlp_out, mlp_out = updated(
-        "update_up", [((all_active, own_cols), (all_hidden, 0))], mom_mlp, mlp, (0, 0), begun
+        "update_up", all_active, own_cols, all_hidden, 0, mom_mlp, mlp, (0, 0), begun=begun
     )
     mom_embed_out, embed_out = updated(
-        "update_embed",
-        [((all_residual, own_cols), (all_residual, 0)), ((all_embed_sent, 0), (all_inputs, 0))],
-        mom_embed,
-        embed,
-        0,
+        "update_embed", all_embed_sent, 0, all_inputs, 0, mom_embed, embed, 0, embed_term.results
     )
     return (state_out, embed_out, mlp_out, mom_embed_out, mom_mlp_out)
 

time: 176 us -> 160 us (0.909)
  waiting for transfers between devices: 92.9 us -> 69.9 us
  starting transfers between devices: 54 us -> 62.1 us
  local copies, waits for them, and re-layouts: 4.37 us -> 1.06 us
  Pallas kernels: 23.4 us -> 25.2 us
    ppermute x40 -> x41, waiting for transfers between devices: 77.3 us -> 64.3 us  [shifted(): return lax.ppermute(value, self.axis, pairs)]
    ppermute x40 -> x41, starting transfers between devices: 36.9 us -> 47.9 us  [shifted(): return lax.ppermute(value, self.axis, pairs)]
    ppermute x2 -> x0, waiting for transfers between devices: 5.7 us -> none  [the longest x1 5.7 us: shards(): arrived_end = lax.ppermute(end_halves[1], 'role', to_trainer)]
    unnamed x18 -> x10, local copies, waits for them, and re-layouts: 4.37 us -> 1.06 us
    ppermute x2 -> x0, starting transfers between devices: 2.77 us -> none  [the longest x1 1.49 us: shards(): arrived_cells = lax.ppermute(cells_sent, 'role', to_trainer)]
    ppermute x1, waiting for transfers between devices: 2.77 us -> 0.01 us  [shards(): arrived_start = lax.ppermute(start_halves[1], 'role', to_trainer)]
    pallas_call x20 -> x22, Pallas kernels: 23.4 us -> 25.2 us  [call(): pl.pallas_call(kernel, name=name, out_shape=outs + [struct(TOKEN, F32)],...]
  transfers between devices with their start and end apart: 50 -> 49, of which waited for: 28 -> 22; matrix products, arithmetic and copies ran while one was open for 0% -> 0% of each run, Pallas kernels for 10% -> 12%
where the time goes in v3:
time: 160 us; the launch traced here: 159 us
  waiting for transfers between devices  69.9 us (44%)
  starting transfers between devices  62.1 us (39%)
  Pallas kernels  25.2 us (16%)
    ppermute x41, waiting for transfers between devices, shifted(): return lax.ppermute(value, self.axis, pairs)  64.3 us
    ppermute x41, starting transfers between devices, shifted(): return lax.ppermute(value, self.axis, pairs)  47.9 us
    pallas_call x22, Pallas kernels, call(): pl.pallas_call(kernel, name=name, out_shape=outs + [struct(TOKEN, F32)],...  25.2 us
    ppermute x1, starting transfers between devices, shards(): arrived_start = lax.ppermute(start_halves[1], 'role', to_trainer)  4.88 us
  transfers between devices with their start and end apart: 49, of which 22 were waited for; matrix products, arithmetic and copies ran while one was open for 0% of the time, Pallas kernels for 12%

profile of v3, /device:TPU:0, one launch (start us, length us, event | category | flops | bytes accessed | tf_op | source)
XLA Modules:
  0.0 159.3 jit_solution(16175222325888773709)
XLA Ops:
  0.6 1.3 collective-permute-start.4
  3.0 1.7 %patches.1 = (bf16[16,4096]{1,0:T(8,128)(2,1)S(1)}, bf16[16,4096]{1,0:T(8,128)(2,1)S(1)}, f32[2,8,4,128]{3,2,1,0:T(4,128)S(1)}, f32[2,8,4,128]{3,2,1,0:T(4,128)S...) custom-call(f32[2,8,64,128]{3,2,1,0:T(8,128)S(1)} %bitcast.3), custom_call_target="tpu_custom_call" | custom-call | flops 1 | bytes 1 | tf_op jit(solution)/shard_map/patches/pallas_call | solution.py:131
  4.7 4.9 %collective-permute-start.2 = (bf16[16,4096]{1,0:T(8,128)(2,1)S(1)}, bf16[16,4096]{1,0:T(8,128)(2,1)S(1)}, u32[]{:S(2)}, u32[]{:S(2)}) collective-permute-start(bf16[16,4096]{1,0:T(8,128)(2,1)S(1)} %get-tuple-element.105), channel_id=1, source_target_pairs={{0,16},{1,17},{2,18},{3,19},{4,20},{5,21},{6,22},{7,23},{8,24},{9,... | collective-permute-start | bytes 393224 | tf_op jit(solution)/shard_map/ppermute | solution.py:607
  9.5 2.8 %collective-permute-start = (f32[2,8,4,128]{3,2,1,0:T(4,128)S(1)}, f32[2,8,4,128]{3,2,1,0:T(4,128)S(1)}, u32[]{:S(2)}, u32[]{:S(2)}) collective-permute-start(f32[2,8,4,128]{3,2,1,0:T(4,128)S(1)} %get-tuple-element.102), channel_id=1, source_target_pairs={{0,4},{4,8},{8,12},{12,0},{1,5},{5,9},{9,13},{13,1},{2,6},{6,10},{... | collective-permute-start | bytes 98312 | tf_op jit(solution)/shard_map/ppermute | solution.py:608
  12.3 2.1 %collective-permute-start.1 = (f32[2,8,4,128]{3,2,1,0:T(4,128)S(1)}, f32[2,8,4,128]{3,2,1,0:T(4,128)S(1)}, u32[]{:S(2)}, u32[]{:S(2)}) collective-permute-start(f32[2,8,4,128]{3,2,1,0:T(4,128)S(1)} %get-tuple-element.103), channel_id=1, source_target_pairs={{0,12},{4,0},{8,4},{12,8},{1,13},{5,1},{9,5},{13,9},{2,14},{6,2},{... | collective-permute-start | bytes 98312 | tf_op jit(solution)/shard_map/ppermute | solution.py:609
  14.4 2.1 %collective-permute-done.refs_3_.refs_1_ = f32[2,8,4,128]{3,2,1,0:T(4,128)S(1)} collective-permute-done((f32[2,8,4,128]{3,2,1,0:T(4,128)S(1)}, f32[2,8,4,128]{3,2,1,0:T(4,128)S(1)}, u32[]{:S(2)}, u32[]{:S(2)}) %collective-permute-start) | collective-permute-done | bytes 32800 | tf_op jit(solution)/shard_map/ppermute | solution.py:608
  19.4 2.5 %collective-permute-start.9 = (bf16[256,1024]{1,0:T(8,128)(2,1)S(1)}, bf16[256,1024]{1,0:T(8,128)(2,1)S(1)}, u32[]{:S(2)}, u32[]{:S(2)}) collective-permute-start(bf16[256,1024]{1,0:T(8,128)(2,1)S(1)} %get-tuple-element.113.refs_2_.refs_8_.refs_6_), channel_id=1, source_target_pairs={{0,4},{4,0},{8,12},{12,8},{1,5},{5,1},{9,13},{13,9},{2,6},{6,2},{1... | collective-permute-start | bytes 1572872 | tf_op jit(solution)/shard_map/ppermute | solution.py:35
  21.9 1.5 collective-permute-start.3
  23.4 2.7 %collective-permute-done.3.refs_1_ = bf16[16,2048]{1,0:T(8,128)(2,1)S(1)} collective-permute-done((bf16[16,2048]{1,0:T(8,128)(2,1)S(1)}, bf16[16,2048]{1,0:T(8,128)(2,1)S(1)}, u32[]{:S(2)}, u32[]{:S(2)}) %collective-permute-start.3) | collective-permute-done | bytes 65568 | tf_op jit(solution)/shard_map/ppermute | solution.py:35
  26.5 2.7 %collective-permute-start.7 = (bf16[32,2048]{1,0:T(8,128)(2,1)S(1)}, bf16[32,2048]{1,0:T(8,128)(2,1)S(1)}, u32[]{:S(2)}, u32[]{:S(2)}) collective-permute-start(bf16[32,2048]{1,0:T(8,128)(2,1)S(1)} %get-tuple-element.112.refs_0_), channel_id=1, source_target_pairs={{0,8},{4,12},{8,0},{12,4},{1,9},{5,13},{9,1},{13,5},{2,10},{6,14},... | collective-permute-start | bytes 393224 | tf_op jit(solution)/shard_map/ppermute | solution.py:35
  30.8 2.3 %collective-permute-start.8 = (bf16[256,1024]{1,0:T(8,128)(2,1)S(1)}, bf16[256,1024]{1,0:T(8,128)(2,1)S(1)}, u32[]{:S(2)}, u32[]{:S(2)}) collective-permute-start(bf16[256,1024]{1,0:T(8,128)(2,1)S(1)} %get-tuple-element.113.refs_2_.refs_8_.refs_6_), channel_id=1, source_target_pairs={{0,1},{1,0},{2,3},{3,2},{4,5},{5,4},{6,7},{7,6},{8,9},{9,8},{10,11... | collective-permute-start | bytes 1572872 | tf_op jit(solution)/shard_map/ppermute | solution.py:35
  33.0 1.9 %collective-permute-done.7.refs_7_.refs_1_ = bf16[32,2048]{1,0:T(8,128)(2,1)S(1)} collective-permute-done((bf16[32,2048]{1,0:T(8,128)(2,1)S(1)}, bf16[32,2048]{1,0:T(8,128)(2,1)S(1)}, u32[]{:S(2)}, u32[]{:S(2)}) %collective-permute-start.7) | collective-permute-done | bytes 131104 | tf_op jit(solution)/shard_map/ppermute | solution.py:35
  36.9 1.3 collective-permute-start.15
  38.2 2.8 %collective-permute-start.14 = (bf16[256,1024]{1,0:T(8,128)(2,1)S(1)}, bf16[256,1024]{1,0:T(8,128)(2,1)S(1)}, u32[]{:S(2)}, u32[]{:S(2)}) collective-permute-start(bf16[256,1024]{1,0:T(8,128)(2,1)S(1)} %get-tuple-element.122.refs_3_.refs_4_), channel_id=1, source_target_pairs={{0,4},{4,0},{8,12},{12,8},{1,5},{5,1},{9,13},{13,9},{2,6},{6,2},{1... | collective-permute-start | bytes 1572872 | tf_op jit(solution)/shard_map/ppermute | solution.py:35
  41.8 1.6 collective-permute-start.12
  43.3 8.1 %stencil.1 = (f32[2,8,64,128]{3,2,1,0:T(8,128)S(1)}, bf16[16,4096]{1,0:T(8,128)(2,1)S(1)}, bf16[16,4096]{1,0:T(8,128)(2,1)S(1)}, f32[8,128]{1,0:T(8,128)S(1)}) custom-call(f32[2,8,64,128]{3,2,1,0:T(8,128)S(1)} %get-tuple-element.101.refs_2_.refs_0_, f32[2,8,4,128]{3,2,1,0:T(4,128)S(1)} %collective-permute-done.refs_3_.refs_1_, ...), custom_call_target="tpu_custom_call" | custom-call | flops 1 | bytes 1 | tf_op jit(solution)/shard_map/stencil/pallas_call | solution.py:131
  51.4 1.8 %collective-permute-done.15.refs_1_ = bf16[256,1024]{1,0:T(8,128)(2,1)S(1)} collective-permute-done((bf16[256,1024]{1,0:T(8,128)(2,1)S(1)}, bf16[256,1024]{1,0:T(8,128)(2,1)S(1)}, u32[]{:S(2)}, u32[]{:S(2)}) %collective-permute-start.15) | collective-permute-done | bytes 524320 | tf_op jit(solution)/shard_map/ppermute | solution.py:627
  53.7 2.5 %collective-permute-start.21 = (bf16[256,1024]{1,0:T(8,128)(2,1)S(1)}, bf16[256,1024]{1,0:T(8,128)(2,1)S(1)}, u32[]{:S(2)}, u32[]{:S(2)}) collective-permute-start(bf16[256,1024]{1,0:T(8,128)(2,1)S(1)} %get-tuple-element.130.refs_3_.refs_6_), channel_id=1, source_target_pairs={{0,4},{4,0},{8,12},{12,8},{1,5},{5,1},{9,13},{13,9},{2,6},{6,2},{1... | collective-permute-start | bytes 1572872 | tf_op jit(solution)/shard_map/ppermute | solution.py:35
  56.8 3.0 %collective-permute-start.22 = (f32[2,8,64,128]{3,2,1,0:T(8,128)S(1)}, f32[2,8,64,128]{3,2,1,0:T(8,128)S(1)}, u32[]{:S(2)}, u32[]{:S(2)}) collective-permute-start(f32[2,8,64,128]{3,2,1,0:T(8,128)S(1)} %get-tuple-element.136), channel_id=1, source_target_pairs={{0,16},{16,0},{1,17},{17,1},{2,18},{18,2},{3,19},{19,3},{4,20},{20... | collective-permute-start | bytes 1572872 | tf_op jit(solution)/shard_map/ppermute | solution.py:35
  59.8 1.7 %collective-permute-start.17 = (bf16[64,2176]{1,0:T(8,128)(2,1)S(1)}, bf16[64,2176]{1,0:T(8,128)(2,1)S(1)}, u32[]{:S(2)}, u32[]{:S(2)}) collective-permute-start(bf16[64,2176]{1,0:T(8,128)(2,1)S(1)} %get-tuple-element.129), channel_id=1, source_target_pairs={{0,8},{4,12},{8,0},{12,4},{1,9},{5,13},{9,1},{13,5},{2,10},{6,14},... | collective-permute-start | bytes 835592 | tf_op jit(solution)/shard_map/ppermute | solution.py:35
  61.6 13.3 %collective-permute-done.19.refs_1_ = bf16[16,4096]{1,0:T(8,128)(2,1)S(1)} collective-permute-done((bf16[16,4096]{1,0:T(8,128)(2,1)S(1)}, bf16[16,4096]{1,0:T(8,128)(2,1)S(1)}, u32[]{:S(2)}, u32[]{:S(2)}) %collective-permute-start.19) | collective-permute-done | bytes 131104 | tf_op jit(solution)/shard_map/ppermute | solution.py:35
  75.8 2.3 %collective-permute-start.28 = (bf16[128,1024]{1,0:T(8,128)(2,1)S(1)}, bf16[128,1024]{1,0:T(8,128)(2,1)S(1)}, u32[]{:S(2)}, u32[]{:S(2)}) collective-permute-start(bf16[128,1024]{1,0:T(8,128)(2,1)S(1)} %get-tuple-element.141.refs_4_), channel_id=1, source_target_pairs={{0,16},{16,0},{1,17},{17,1},{2,18},{18,2},{3,19},{19,3},{4,20},{20... | collective-permute-start | bytes 786440 | tf_op jit(solution)/shard_map/ppermute | solution.py:35
  78.1 1.6 %collective-permute-start.25 = (bf16[128,1024]{1,0:T(8,128)(2,1)S(1)}, bf16[128,1024]{1,0:T(8,128)(2,1)S(1)}, u32[]{:S(2)}, u32[]{:S(2)}) collective-permute-start(bf16[128,1024]{1,0:T(8,128)(2,1)S(1)} %get-tuple-element.141.refs_4_), channel_id=1, source_target_pairs={{0,4},{4,0},{8,12},{12,8},{1,5},{5,1},{9,13},{13,9},{2,6},{6,2},{1... | collective-permute-start | bytes 786440 | tf_op jit(solution)/shard_map/ppermute | solution.py:35
  80.6 1.6 collective-permute-start.26
  82.7 2.6 %collective-permute-done.26.refs_4_ = bf16[16,2048]{1,0:T(8,128)(2,1)S(1)} collective-permute-done((bf16[16,2048]{1,0:T(8,128)(2,1)S(1)}, bf16[16,2048]{1,0:T(8,128)(2,1)S(1)}, u32[]{:S(2)}, u32[]{:S(2)}) %collective-permute-start.26) | collective-permute-done | bytes 65568 | tf_op jit(solution)/shard_map/ppermute | solution.py:35
  87.1 1.6 %collective-permute-start.29 = (bf16[128,1280]{1,0:T(8,128)(2,1)S(1)}, bf16[128,1280]{1,0:T(8,128)(2,1)S(1)}, u32[]{:S(2)}, u32[]{:S(2)}) collective-permute-start(bf16[128,1280]{1,0:T(8,128)(2,1)S(1)} %get-tuple-element.147), channel_id=1, source_target_pairs={{0,4},{4,0},{8,12},{12,8},{1,5},{5,1},{9,13},{13,9},{2,6},{6,2},{1... | collective-permute-start | bytes 983048 | tf_op jit(solution)/shard_map/ppermute | solution.py:35
  89.0 1.7 %collective-permute-start.30 = (bf16[64,2048]{1,0:T(8,128)(2,1)S(1)}, bf16[64,2048]{1,0:T(8,128)(2,1)S(1)}, u32[]{:S(2)}, u32[]{:S(2)}) collective-permute-start(bf16[64,2048]{1,0:T(8,128)(2,1)S(1)} %get-tuple-element.149), channel_id=1, source_target_pairs={{0,8},{4,12},{8,0},{12,4},{1,9},{5,13},{9,1},{13,5},{2,10},{6,14},... | collective-permute-start | bytes 786440 | tf_op jit(solution)/shard_map/ppermute | solution.py:35
  90.8 1.7 %collective-permute-start.31 = (bf16[128,1024]{1,0:T(8,128)(2,1)S(1)}, bf16[128,1024]{1,0:T(8,128)(2,1)S(1)}, u32[]{:S(2)}, u32[]{:S(2)}) collective-permute-start(bf16[128,1024]{1,0:T(8,128)(2,1)S(1)} %get-tuple-element.152.refs_5_), channel_id=1, source_target_pairs={{0,16},{16,0},{1,17},{17,1},{2,18},{18,2},{3,19},{19,3},{4,20},{20... | collective-permute-start | bytes 786440 | tf_op jit(solution)/shard_map/ppermute | solution.py:35
  92.5 8.4 %collective-permute-done.30.refs_4_ = bf16[64,2048]{1,0:T(8,128)(2,1)S(1)} collective-permute-done((bf16[64,2048]{1,0:T(8,128)(2,1)S(1)}, bf16[64,2048]{1,0:T(8,128)(2,1)S(1)}, u32[]{:S(2)}, u32[]{:S(2)}) %collective-permute-start.30) | collective-permute-done | bytes 262176 | tf_op jit(solution)/shard_map/ppermute | solution.py:35
  100.9 2.2 %collective-permute-done.31.refs_12_.refs_7_ = bf16[128,1024]{1,0:T(8,128)(2,1)S(1)} collective-permute-done((bf16[128,1024]{1,0:T(8,128)(2,1)S(1)}, bf16[128,1024]{1,0:T(8,128)(2,1)S(1)}, u32[]{:S(2)}, u32[]{:S(2)}) %collective-permute-start.31) | collective-permute-done | bytes 262176 | tf_op jit(solution)/shard_map/ppermute | solution.py:35
  103.9 1.6 collective-permute-start.34
  105.5 2.9 %collective-permute-done.34.refs_5_ = bf16[64,512]{1,0:T(8,128)(2,1)S(1)} collective-permute-done((bf16[64,512]{1,0:T(8,128)(2,1)S(1)}, bf16[64,512]{1,0:T(8,128)(2,1)S(1)}, u32[]{:S(2)}, u32[]{:S(2)}) %collective-permute-start.34) | collective-permute-done | bytes 65568 | tf_op jit(solution)/shard_map/ppermute | solution.py:35
  109.7 1.4 collective-permute-start.38
  111.1 1.3 collective-permute-start.35
  112.4 1.7 %collective-permute-start.37 = (bf16[64,2048]{1,0:T(8,128)(2,1)S(1)}, bf16[64,2048]{1,0:T(8,128)(2,1)S(1)}, u32[]{:S(2)}, u32[]{:S(2)}) collective-permute-start(bf16[64,2048]{1,0:T(8,128)(2,1)S(1)} %get-tuple-element.167), channel_id=1, source_target_pairs={{0,8},{4,12},{8,0},{12,4},{1,9},{5,13},{9,1},{13,5},{2,10},{6,14},... | collective-permute-start | bytes 786440 | tf_op jit(solution)/shard_map/ppermute | solution.py:35
  114.1 12.6 %collective-permute-done.38.refs_10_.refs_7_.refs_3_ = bf16[128,1280]{1,0:T(8,128)(2,1)S(1)} collective-permute-done((bf16[128,1280]{1,0:T(8,128)(2,1)S(1)}, bf16[128,1280]{1,0:T(8,128)(2,1)S(1)}, u32[]{:S(2)}, u32[]{:S(2)}) %collective-permute-start.38) | collective-permute-done | bytes 327712 | tf_op jit(solution)/shard_map/ppermute | solution.py:35
  127.7 1.4 collective-permute-done.40.refs_1_
  129.1 1.4 collective-permute-start.46
  130.5 1.5 collective-permute-start.39
  132.0 2.9 %collective-permute-done.39.refs_6_ = bf16[64,640]{1,0:T(8,128)(2,1)S(1)} collective-permute-done((bf16[64,640]{1,0:T(8,128)(2,1)S(1)}, bf16[64,640]{1,0:T(8,128)(2,1)S(1)}, u32[]{:S(2)}, u32[]{:S(2)}) %collective-permute-start.39) | collective-permute-done | bytes 81952 | tf_op jit(solution)/shard_map/ppermute | solution.py:35
  136.5 3.2 %collective-permute-done.46.refs_1_.refs_5_ = bf16[128,1280]{1,0:T(8,128)(2,1)S(1)} collective-permute-done((bf16[128,1280]{1,0:T(8,128)(2,1)S(1)}, bf16[128,1280]{1,0:T(8,128)(2,1)S(1)}, u32[]{:S(2)}, u32[]{:S(2)}) %collective-permute-start.46) | collective-permute-done | bytes 327712 | tf_op jit(solution)/shard_map/ppermute | solution.py:35
  141.6 1.4 collective-permute-start.43
  143.0 1.4 collective-permute-start.44
  144.4 3.0 %collective-permute-done.43.refs_1_ = bf16[128,256]{1,0:T(8,128)(2,1)S(1)} collective-permute-done((bf16[128,256]{1,0:T(8,128)(2,1)S(1)}, bf16[128,256]{1,0:T(8,128)(2,1)S(1)}, u32[]{:S(2)}, u32[]{:S(2)}) %collective-permute-start.43) | collective-permute-done | bytes 65568 | tf_op jit(solution)/shard_map/ppermute | solution.py:35
  149.1 3.6 %collective-permute-done.48.refs_3_.refs_7_ = bf16[128,1280]{1,0:T(8,128)(2,1)S(1)} collective-permute-done((bf16[128,1280]{1,0:T(8,128)(2,1)S(1)}, bf16[128,1280]{1,0:T(8,128)(2,1)S(1)}, u32[]{:S(2)}, u32[]{:S(2)}) %collective-permute-start.48) | collective-permute-done | bytes 327712 | tf_op jit(solution)/shard_map/ppermute | solution.py:35
  152.7 1.9 %update_down.1 = (f32[1,2,256,1024]{3,2,1,0:T(8,128)}, bf16[1,2,256,1024]{3,2,1,0:T(8,128)(2,1)}, f32[8,128]{1,0:T(8,128)S(1)}) custom-call(bf16[128,1280]{1,0:T(8,128)(2,1)S(1)} %get-tuple-element.186.refs_0_.refs_4_, bf16[128,1280]{1,0:T(8,128)(2,1)S(1)} %collective-permute-done.46.refs_1_.refs_5_, ...), custom_call_target="tpu_custom_call" | custom-call | flops 1 | bytes 1 | tf_op jit(solution)/shard_map/update_down/pallas_call | solution.py:131
  154.7 1.9 %update_up.1 = (f32[1,2,256,1024]{3,2,1,0:T(8,128)}, bf16[1,2,256,1024]{3,2,1,0:T(8,128)(2,1)}, f32[8,128]{1,0:T(8,128)S(1)}) custom-call(bf16[128,1280]{1,0:T(8,128)(2,1)S(1)} %get-tuple-element.153.refs_4_.refs_0_, bf16[128,1280]{1,0:T(8,128)(2,1)S(1)} %get-tuple-element.169.refs_5_.refs_1_, ...), custom_call_target="tpu_custom_call", output_to_operand_aliasing={{0}: (10, {}), {1}: (11, {})} | custom-call | flops 1 | bytes 1 | tf_op jit(solution)/shard_map/update_up/pallas_call | solution.py:131
  156.6 2.5 %update_embed.1 = (f32[1,256,1024]{2,1,0:T(8,128)}, bf16[1,256,1024]{2,1,0:T(8,128)(2,1)}, f32[8,128]{1,0:T(8,128)}) custom-call(bf16[128,256]{1,0:T(8,128)(2,1)S(1)} %get-tuple-element.183.refs_0_, bf16[128,256]{1,0:T(8,128)(2,1)S(1)} %collective-permute-done.43.refs_1_, bf16[128,256]{1,0:T(8,128)(2,1)S(1)} %collective-permute-done.44.refs_2_, ...), custom_call_target="tpu_custom_call" | custom-call | flops 1 | bytes 1 | tf_op jit(solution)/shard_map/update_embed/pallas_call | solution.py:131
  (82 shorter events, 22.1 us)
Async XLA Ops:
  0.6 16.4 %collective-permute-start.4 = (bf16[256,1024]{1,0:T(8,128)(2,1)}, bf16[256,1024]{1,0:T(8,128)(2,1)S(1)}, u32[]{:S(2)}, u32[]{:S(2)}) collective-permute-start(bf16[256,1024]{1,0:T(8,128)(2,1)} %bitcast.2), channel_id=1, source_target_pairs={{16,0},{17,1},{18,2},{19,3},{20,4},{21,5},{22,6},{23,7},{24,8},{25... | collective-permute-start | bytes 1572872 | tf_op jit(solution)/shard_map/ppermute | solution.py:599
  4.7 11.9 %collective-permute-start.2 = (bf16[16,4096]{1,0:T(8,128)(2,1)S(1)}, bf16[16,4096]{1,0:T(8,128)(2,1)S(1)}, u32[]{:S(2)}, u32[]{:S(2)}) collective-permute-start(bf16[16,4096]{1,0:T(8,128)(2,1)S(1)} %get-tuple-element.105), channel_id=1, source_target_pairs={{0,16},{1,17},{2,18},{3,19},{4,20},{5,21},{6,22},{7,23},{8,24},{9,... | collective-permute-start | bytes 393224 | tf_op jit(solution)/shard_map/ppermute | solution.py:607
  9.5 7.0 %collective-permute-start = (f32[2,8,4,128]{3,2,1,0:T(4,128)S(1)}, f32[2,8,4,128]{3,2,1,0:T(4,128)S(1)}, u32[]{:S(2)}, u32[]{:S(2)}) collective-permute-start(f32[2,8,4,128]{3,2,1,0:T(4,128)S(1)} %get-tuple-element.102), channel_id=1, source_target_pairs={{0,4},{4,8},{8,12},{12,0},{1,5},{5,9},{9,13},{13,1},{2,6},{6,10},{... | collective-permute-start | bytes 98312 | tf_op jit(solution)/shard_map/ppermute | solution.py:608
  12.3 4.3 %collective-permute-start.1 = (f32[2,8,4,128]{3,2,1,0:T(4,128)S(1)}, f32[2,8,4,128]{3,2,1,0:T(4,128)S(1)}, u32[]{:S(2)}, u32[]{:S(2)}) collective-permute-start(f32[2,8,4,128]{3,2,1,0:T(4,128)S(1)} %get-tuple-element.103), channel_id=1, source_target_pairs={{0,12},{4,0},{8,4},{12,8},{1,13},{5,1},{9,5},{13,9},{2,14},{6,2},{... | collective-permute-start | bytes 98312 | tf_op jit(solution)/shard_map/ppermute | solution.py:609
  18.1 16.9 %collective-permute-start.10 = (bf16[256,1024]{1,0:T(8,128)(2,1)S(1)}, bf16[256,1024]{1,0:T(8,128)(2,1)S(1)}, u32[]{:S(2)}, u32[]{:S(2)}) collective-permute-start(bf16[256,1024]{1,0:T(8,128)(2,1)S(1)} %get-tuple-element.114), channel_id=1, source_target_pairs={{16,0},{17,1},{18,2},{19,3},{20,4},{21,5},{22,6},{23,7},{24,8},{25... | collective-permute-start | bytes 1572872 | tf_op jit(solution)/shard_map/ppermute | solution.py:615
  19.4 16.3 %collective-permute-start.9 = (bf16[256,1024]{1,0:T(8,128)(2,1)S(1)}, bf16[256,1024]{1,0:T(8,128)(2,1)S(1)}, u32[]{:S(2)}, u32[]{:S(2)}) collective-permute-start(bf16[256,1024]{1,0:T(8,128)(2,1)S(1)} %get-tuple-element.113.refs_2_.refs_8_.refs_6_), channel_id=1, source_target_pairs={{0,4},{4,0},{8,12},{12,8},{1,5},{5,1},{9,13},{13,9},{2,6},{6,2},{1... | collective-permute-start | bytes 1572872 | tf_op jit(solution)/shard_map/ppermute | solution.py:35
  21.9 4.3 %collective-permute-start.3 = (bf16[16,2048]{1,0:T(8,128)(2,1)S(1)}, bf16[16,2048]{1,0:T(8,128)(2,1)S(1)}, u32[]{:S(2)}, u32[]{:S(2)}) collective-permute-start(bf16[16,2048]{1,0:T(8,128)(2,1)S(1)} %get-tuple-element.108), channel_id=1, source_target_pairs={{0,2},{1,3},{2,0},{3,1},{4,6},{5,7},{6,4},{7,5},{8,10},{9,11},{10,... | collective-permute-start | bytes 196616 | tf_op jit(solution)/shard_map/ppermute | solution.py:35
  26.5 8.5 %collective-permute-start.7 = (bf16[32,2048]{1,0:T(8,128)(2,1)S(1)}, bf16[32,2048]{1,0:T(8,128)(2,1)S(1)}, u32[]{:S(2)}, u32[]{:S(2)}) collective-permute-start(bf16[32,2048]{1,0:T(8,128)(2,1)S(1)} %get-tuple-element.112.refs_0_), channel_id=1, source_target_pairs={{0,8},{4,12},{8,0},{12,4},{1,9},{5,13},{9,1},{13,5},{2,10},{6,14},... | collective-permute-start | bytes 393224 | tf_op jit(solution)/shard_map/ppermute | solution.py:35
  29.1 1.6 %collective-permute-start.6 = (f32[72,128]{1,0:T(8,128)S(1)}, f32[72,128]{1,0:T(8,128)S(1)}, u32[]{:S(2)}, u32[]{:S(2)}) collective-permute-start(f32[72,128]{1,0:T(8,128)S(1)} %get-tuple-element.111), channel_id=1, source_target_pairs={{0,3},{1,0},{2,1},{3,2},{4,7},{5,4},{6,5},{7,6},{8,11},{9,8},{10,9... | collective-permute-start | bytes 110600 | tf_op jit(solution)/shard_map/ppermute | solution.py:622
  29.1 3.9 %collective-permute-start.5 = (f32[72,128]{1,0:T(8,128)S(1)}, f32[72,128]{1,0:T(8,128)S(1)}, u32[]{:S(2)}, u32[]{:S(2)}) collective-permute-start(f32[72,128]{1,0:T(8,128)S(1)} %get-tuple-element.111), channel_id=1, source_target_pairs={{0,1},{1,2},{2,3},{3,0},{4,5},{5,6},{6,7},{7,4},{8,9},{9,10},{10,1... | collective-permute-start | bytes 110600 | tf_op jit(solution)/shard_map/ppermute | solution.py:621
  30.8 10.2 %collective-permute-start.8 = (bf16[256,1024]{1,0:T(8,128)(2,1)S(1)}, bf16[256,1024]{1,0:T(8,128)(2,1)S(1)}, u32[]{:S(2)}, u32[]{:S(2)}) collective-permute-start(bf16[256,1024]{1,0:T(8,128)(2,1)S(1)} %get-tuple-element.113.refs_2_.refs_8_.refs_6_), channel_id=1, source_target_pairs={{0,1},{1,0},{2,3},{3,2},{4,5},{5,4},{6,7},{7,6},{8,9},{9,8},{10,11... | collective-permute-start | bytes 1572872 | tf_op jit(solution)/shard_map/ppermute | solution.py:35
  36.8 4.2 %collective-permute-start.11 = (bf16[256,1024]{1,0:T(8,128)(2,1)S(1)}, bf16[256,1024]{1,0:T(8,128)(2,1)S(1)}, u32[]{:S(2)}, u32[]{:S(2)}) collective-permute-start(bf16[256,1024]{1,0:T(8,128)(2,1)S(1)} %get-tuple-element.116.refs_4_.refs_10_.refs_8_), channel_id=1, source_target_pairs={{0,1},{1,0},{2,3},{3,2},{4,5},{5,4},{6,7},{7,6},{8,9},{9,8},{10,11... | collective-permute-start | bytes 1572872 | tf_op jit(solution)/shard_map/ppermute | solution.py:35
  36.9 16.4 %collective-permute-start.15 = (bf16[256,1024]{1,0:T(8,128)(2,1)S(1)}, bf16[256,1024]{1,0:T(8,128)(2,1)S(1)}, u32[]{:S(2)}, u32[]{:S(2)}) collective-permute-start(bf16[256,1024]{1,0:T(8,128)(2,1)S(1)} %get-tuple-element.123), channel_id=1, source_target_pairs={{16,0},{17,1},{18,2},{19,3},{20,4},{21,5},{22,6},{23,7},{24,8},{25... | collective-permute-start | bytes 1572872 | tf_op jit(solution)/shard_map/ppermute | solution.py:627
  38.2 15.4 %collective-permute-start.14 = (bf16[256,1024]{1,0:T(8,128)(2,1)S(1)}, bf16[256,1024]{1,0:T(8,128)(2,1)S(1)}, u32[]{:S(2)}, u32[]{:S(2)}) collective-permute-start(bf16[256,1024]{1,0:T(8,128)(2,1)S(1)} %get-tuple-element.122.refs_3_.refs_4_), channel_id=1, source_target_pairs={{0,4},{4,0},{8,12},{12,8},{1,5},{5,1},{9,13},{13,9},{2,6},{6,2},{1... | collective-permute-start | bytes 1572872 | tf_op jit(solution)/shard_map/ppermute | solution.py:35
  41.8 11.8 %collective-permute-start.12 = (bf16[64,512]{1,0:T(8,128)(2,1)S(1)}, bf16[64,512]{1,0:T(8,128)(2,1)S(1)}, u32[]{:S(2)}, u32[]{:S(2)}) collective-permute-start(bf16[64,512]{1,0:T(8,128)(2,1)S(1)} %get-tuple-element.121), channel_id=1, source_target_pairs={{0,2},{1,3},{2,0},{3,1},{4,6},{5,7},{6,4},{7,5},{8,10},{9,11},{10,... | collective-permute-start | bytes 196616 | tf_op jit(solution)/shard_map/ppermute | solution.py:35
  43.3 12.9 %collective-permute-start.13 = (bf16[256,1024]{1,0:T(8,128)(2,1)S(1)}, bf16[256,1024]{1,0:T(8,128)(2,1)S(1)}, u32[]{:S(2)}, u32[]{:S(2)}) collective-permute-start(bf16[256,1024]{1,0:T(8,128)(2,1)S(1)} %get-tuple-element.122.refs_3_.refs_4_), channel_id=1, source_target_pairs={{0,1},{1,0},{2,3},{3,2},{4,5},{5,4},{6,7},{7,6},{8,9},{9,8},{10,11... | collective-permute-start | bytes 1572872 | tf_op jit(solution)/shard_map/ppermute | solution.py:35
  53.7 2.6 %collective-permute-start.16 = (bf16[256,1024]{1,0:T(8,128)(2,1)S(1)}, bf16[256,1024]{1,0:T(8,128)(2,1)S(1)}, u32[]{:S(2)}, u32[]{:S(2)}) collective-permute-start(bf16[256,1024]{1,0:T(8,128)(2,1)S(1)} %get-tuple-element.125.refs_5_.refs_6_), channel_id=1, source_target_pairs={{0,1},{1,0},{2,3},{3,2},{4,5},{5,4},{6,7},{7,6},{8,9},{9,8},{10,11... | collective-permute-start | bytes 1572872 | tf_op jit(solution)/shard_map/ppermute | solution.py:35
  53.7 21.1 %collective-permute-start.21 = (bf16[256,1024]{1,0:T(8,128)(2,1)S(1)}, bf16[256,1024]{1,0:T(8,128)(2,1)S(1)}, u32[]{:S(2)}, u32[]{:S(2)}) collective-permute-start(bf16[256,1024]{1,0:T(8,128)(2,1)S(1)} %get-tuple-element.130.refs_3_.refs_6_), channel_id=1, source_target_pairs={{0,4},{4,0},{8,12},{12,8},{1,5},{5,1},{9,13},{13,9},{2,6},{6,2},{1... | collective-permute-start | bytes 1572872 | tf_op jit(solution)/shard_map/ppermute | solution.py:35
  56.8 18.1 %collective-permute-start.22 = (f32[2,8,64,128]{3,2,1,0:T(8,128)S(1)}, f32[2,8,64,128]{3,2,1,0:T(8,128)S(1)}, u32[]{:S(2)}, u32[]{:S(2)}) collective-permute-start(f32[2,8,64,128]{3,2,1,0:T(8,128)S(1)} %get-tuple-element.136), channel_id=1, source_target_pairs={{0,16},{16,0},{1,17},{17,1},{2,18},{18,2},{3,19},{19,3},{4,20},{20... | collective-permute-start | bytes 1572872 | tf_op jit(solution)/shard_map/ppermute | solution.py:35
  59.8 15.1 %collective-permute-start.17 = (bf16[64,2176]{1,0:T(8,128)(2,1)S(1)}, bf16[64,2176]{1,0:T(8,128)(2,1)S(1)}, u32[]{:S(2)}, u32[]{:S(2)}) collective-permute-start(bf16[64,2176]{1,0:T(8,128)(2,1)S(1)} %get-tuple-element.129), channel_id=1, source_target_pairs={{0,8},{4,12},{8,0},{12,4},{1,9},{5,13},{9,1},{13,5},{2,10},{6,14},... | collective-permute-start | bytes 835592 | tf_op jit(solution)/shard_map/ppermute | solution.py:35
  61.5 13.4 %collective-permute-start.19 = (bf16[16,4096]{1,0:T(8,128)(2,1)S(1)}, bf16[16,4096]{1,0:T(8,128)(2,1)S(1)}, u32[]{:S(2)}, u32[]{:S(2)}) collective-permute-start(bf16[16,4096]{1,0:T(8,128)(2,1)S(1)} %get-tuple-element.132), channel_id=1, source_target_pairs={{0,16},{16,0},{1,17},{17,1},{2,18},{18,2},{3,19},{19,3},{4,20},{20... | collective-permute-start | bytes 393224 | tf_op jit(solution)/shard_map/ppermute | solution.py:35
  61.6 13.3 %collective-permute-start.20 = (bf16[64,1024]{1,0:T(8,128)(2,1)S(1)}, bf16[64,1024]{1,0:T(8,128)(2,1)S(1)}, u32[]{:S(2)}, u32[]{:S(2)}) collective-permute-start(bf16[64,1024]{1,0:T(8,128)(2,1)S(1)} %get-tuple-element.134.refs_2_), channel_id=1, source_target_pairs={{0,1},{1,0},{2,3},{3,2},{4,5},{5,4},{6,7},{7,6},{8,9},{9,8},{10,11... | collective-permute-start | bytes 393224 | tf_op jit(solution)/shard_map/ppermute | solution.py:35
  74.9 4.8 %collective-permute-start.18 = (bf16[256,1024]{1,0:T(8,128)(2,1)S(1)}, bf16[256,1024]{1,0:T(8,128)(2,1)S(1)}, u32[]{:S(2)}, u32[]{:S(2)}) collective-permute-start(bf16[256,1024]{1,0:T(8,128)(2,1)S(1)} %get-tuple-element.130.refs_3_.refs_6_), channel_id=1, source_target_pairs={{0,1},{1,0},{2,3},{3,2},{4,5},{5,4},{6,7},{7,6},{8,9},{9,8},{10,11... | collective-permute-start | bytes 1572872 | tf_op jit(solution)/shard_map/ppermute | solution.py:35
  75.2 4.5 %collective-permute-start.23 = (bf16[256,1024]{1,0:T(8,128)(2,1)S(1)}, bf16[256,1024]{1,0:T(8,128)(2,1)S(1)}, u32[]{:S(2)}, u32[]{:S(2)}) collective-permute-start(bf16[256,1024]{1,0:T(8,128)(2,1)S(1)} %get-tuple-element.137.refs_5_.refs_8_), channel_id=1, source_target_pairs={{0,1},{1,0},{2,3},{3,2},{4,5},{5,4},{6,7},{7,6},{8,9},{9,8},{10,11... | collective-permute-start | bytes 1572872 | tf_op jit(solution)/shard_map/ppermute | solution.py:35
  75.8 9.6 %collective-permute-start.28 = (bf16[128,1024]{1,0:T(8,128)(2,1)S(1)}, bf16[128,1024]{1,0:T(8,128)(2,1)S(1)}, u32[]{:S(2)}, u32[]{:S(2)}) collective-permute-start(bf16[128,1024]{1,0:T(8,128)(2,1)S(1)} %get-tuple-element.141.refs_4_), channel_id=1, source_target_pairs={{0,16},{16,0},{1,17},{17,1},{2,18},{18,2},{3,19},{19,3},{4,20},{20... | collective-permute-start | bytes 786440 | tf_op jit(solution)/shard_map/ppermute | solution.py:35
  78.1 8.4 %collective-permute-start.25 = (bf16[128,1024]{1,0:T(8,128)(2,1)S(1)}, bf16[128,1024]{1,0:T(8,128)(2,1)S(1)}, u32[]{:S(2)}, u32[]{:S(2)}) collective-permute-start(bf16[128,1024]{1,0:T(8,128)(2,1)S(1)} %get-tuple-element.141.refs_4_), channel_id=1, source_target_pairs={{0,4},{4,0},{8,12},{12,8},{1,5},{5,1},{9,13},{13,9},{2,6},{6,2},{1... | collective-permute-start | bytes 786440 | tf_op jit(solution)/shard_map/ppermute | solution.py:35
  80.5 6.0 %collective-permute-start.24 = (bf16[64,1536]{1,0:T(8,128)(2,1)S(1)}, bf16[64,1536]{1,0:T(8,128)(2,1)S(1)}, u32[]{:S(2)}, u32[]{:S(2)}) collective-permute-start(bf16[64,1536]{1,0:T(8,128)(2,1)S(1)} %get-tuple-element.140), channel_id=1, source_target_pairs={{0,1},{1,0},{2,3},{3,2},{4,5},{5,4},{6,7},{7,6},{8,9},{9,8},{10,11... | collective-permute-start | bytes 589832 | tf_op jit(solution)/shard_map/ppermute | solution.py:35
  80.6 4.7 %collective-permute-start.26 = (bf16[16,2048]{1,0:T(8,128)(2,1)S(1)}, bf16[16,2048]{1,0:T(8,128)(2,1)S(1)}, u32[]{:S(2)}, u32[]{:S(2)}) collective-permute-start(bf16[16,2048]{1,0:T(8,128)(2,1)S(1)} %get-tuple-element.143), channel_id=1, source_target_pairs={{0,2},{1,3},{2,0},{3,1},{4,6},{5,7},{6,4},{7,5},{8,10},{9,11},{10,... | collective-permute-start | bytes 196616 | tf_op jit(solution)/shard_map/ppermute | solution.py:35
  82.2 4.3 %collective-permute-start.27 = (bf16[64,512]{1,0:T(8,128)(2,1)S(1)}, bf16[64,512]{1,0:T(8,128)(2,1)S(1)}, u32[]{:S(2)}, u32[]{:S(2)}) collective-permute-start(bf16[64,512]{1,0:T(8,128)(2,1)S(1)} %get-tuple-element.145), channel_id=1, source_target_pairs={{0,2},{1,3},{2,0},{3,1},{4,6},{5,7},{6,4},{7,5},{8,10},{9,11},{10,... | collective-permute-start | bytes 196616 | tf_op jit(solution)/shard_map/ppermute | solution.py:35
  87.1 15.9 %collective-permute-start.29 = (bf16[128,1280]{1,0:T(8,128)(2,1)S(1)}, bf16[128,1280]{1,0:T(8,128)(2,1)S(1)}, u32[]{:S(2)}, u32[]{:S(2)}) collective-permute-start(bf16[128,1280]{1,0:T(8,128)(2,1)S(1)} %get-tuple-element.147), channel_id=1, source_target_pairs={{0,4},{4,0},{8,12},{12,8},{1,5},{5,1},{9,13},{13,9},{2,6},{6,2},{1... | collective-permute-start | bytes 983048 | tf_op jit(solution)/shard_map/ppermute | solution.py:35
  88.8 14.3 %collective-permute-start.32 = (bf16[128,1280]{1,0:T(8,128)(2,1)S(1)}, bf16[128,1280]{1,0:T(8,128)(2,1)S(1)}, u32[]{:S(2)}, u32[]{:S(2)}) collective-permute-start(bf16[128,1280]{1,0:T(8,128)(2,1)S(1)} %get-tuple-element.153.refs_4_.refs_0_), channel_id=1, source_target_pairs={{0,16},{16,0},{1,17},{17,1},{2,18},{18,2},{3,19},{19,3},{4,20},{20... | collective-permute-start | bytes 983048 | tf_op jit(solution)/shard_map/ppermute | solution.py:35
  89.0 11.8 %collective-permute-start.30 = (bf16[64,2048]{1,0:T(8,128)(2,1)S(1)}, bf16[64,2048]{1,0:T(8,128)(2,1)S(1)}, u32[]{:S(2)}, u32[]{:S(2)}) collective-permute-start(bf16[64,2048]{1,0:T(8,128)(2,1)S(1)} %get-tuple-element.149), channel_id=1, source_target_pairs={{0,8},{4,12},{8,0},{12,4},{1,9},{5,13},{9,1},{13,5},{2,10},{6,14},... | collective-permute-start | bytes 786440 | tf_op jit(solution)/shard_map/ppermute | solution.py:35
  90.8 12.3 %collective-permute-start.31 = (bf16[128,1024]{1,0:T(8,128)(2,1)S(1)}, bf16[128,1024]{1,0:T(8,128)(2,1)S(1)}, u32[]{:S(2)}, u32[]{:S(2)}) collective-permute-start(bf16[128,1024]{1,0:T(8,128)(2,1)S(1)} %get-tuple-element.152.refs_5_), channel_id=1, source_target_pairs={{0,16},{16,0},{1,17},{17,1},{2,18},{18,2},{3,19},{19,3},{4,20},{20... | collective-permute-start | bytes 786440 | tf_op jit(solution)/shard_map/ppermute | solution.py:35
  103.8 4.6 %collective-permute-start.33 = (bf16[64,1536]{1,0:T(8,128)(2,1)S(1)}, bf16[64,1536]{1,0:T(8,128)(2,1)S(1)}, u32[]{:S(2)}, u32[]{:S(2)}) collective-permute-start(bf16[64,1536]{1,0:T(8,128)(2,1)S(1)} %get-tuple-element.155), channel_id=1, source_target_pairs={{0,1},{1,0},{2,3},{3,2},{4,5},{5,4},{6,7},{7,6},{8,9},{9,8},{10,11... | collective-permute-start | bytes 589832 | tf_op jit(solution)/shard_map/ppermute | solution.py:35
  103.9 4.5 %collective-permute-start.34 = (bf16[64,512]{1,0:T(8,128)(2,1)S(1)}, bf16[64,512]{1,0:T(8,128)(2,1)S(1)}, u32[]{:S(2)}, u32[]{:S(2)}) collective-permute-start(bf16[64,512]{1,0:T(8,128)(2,1)S(1)} %get-tuple-element.157), channel_id=1, source_target_pairs={{0,2},{1,3},{2,0},{3,1},{4,6},{5,7},{6,4},{7,5},{8,10},{9,11},{10,... | collective-permute-start | bytes 196616 | tf_op jit(solution)/shard_map/ppermute | solution.py:35
  109.0 17.8 %collective-permute-start.36 = (bf16[128,1536]{1,0:T(8,128)(2,1)S(1)}, bf16[128,1536]{1,0:T(8,128)(2,1)S(1)}, u32[]{:S(2)}, u32[]{:S(2)}) collective-permute-start(bf16[128,1536]{1,0:T(8,128)(2,1)S(1)} %get-tuple-element.161), channel_id=1, source_target_pairs={{0,16},{16,0},{1,17},{17,1},{2,18},{18,2},{3,19},{19,3},{4,20},{20... | collective-permute-start | bytes 1179656 | tf_op jit(solution)/shard_map/ppermute | solution.py:35
  109.7 17.1 %collective-permute-start.38 = (bf16[128,1280]{1,0:T(8,128)(2,1)S(1)}, bf16[128,1280]{1,0:T(8,128)(2,1)S(1)}, u32[]{:S(2)}, u32[]{:S(2)}) collective-permute-start(bf16[128,1280]{1,0:T(8,128)(2,1)S(1)} %get-tuple-element.169.refs_5_.refs_1_), channel_id=1, source_target_pairs={{0,16},{16,0},{1,17},{17,1},{2,18},{18,2},{3,19},{19,3},{4,20},{20... | collective-permute-start | bytes 983048 | tf_op jit(solution)/shard_map/ppermute | solution.py:35
  111.1 15.7 %collective-permute-start.35 = (bf16[128,1280]{1,0:T(8,128)(2,1)S(1)}, bf16[128,1280]{1,0:T(8,128)(2,1)S(1)}, u32[]{:S(2)}, u32[]{:S(2)}) collective-permute-start(bf16[128,1280]{1,0:T(8,128)(2,1)S(1)} %get-tuple-element.160), channel_id=1, source_target_pairs={{0,4},{4,0},{8,12},{12,8},{1,5},{5,1},{9,13},{13,9},{2,6},{6,2},{1... | collective-permute-start | bytes 983048 | tf_op jit(solution)/shard_map/ppermute | solution.py:35
  112.4 14.4 %collective-permute-start.37 = (bf16[64,2048]{1,0:T(8,128)(2,1)S(1)}, bf16[64,2048]{1,0:T(8,128)(2,1)S(1)}, u32[]{:S(2)}, u32[]{:S(2)}) collective-permute-start(bf16[64,2048]{1,0:T(8,128)(2,1)S(1)} %get-tuple-element.167), channel_id=1, source_target_pairs={{0,8},{4,12},{8,0},{12,4},{1,9},{5,13},{9,1},{13,5},{2,10},{6,14},... | collective-permute-start | bytes 786440 | tf_op jit(solution)/shard_map/ppermute | solution.py:35
  127.6 1.5 collective-permute-start.40
  129.1 10.6 %collective-permute-start.46 = (bf16[128,1280]{1,0:T(8,128)(2,1)S(1)}, bf16[128,1280]{1,0:T(8,128)(2,1)S(1)}, u32[]{:S(2)}, u32[]{:S(2)}) collective-permute-start(bf16[128,1280]{1,0:T(8,128)(2,1)S(1)} %get-tuple-element.187), channel_id=1, source_target_pairs={{0,4},{4,0},{8,12},{12,8},{1,5},{5,1},{9,13},{13,9},{2,6},{6,2},{1... | collective-permute-start | bytes 983048 | tf_op jit(solution)/shard_map/ppermute | solution.py:35
  130.5 4.4 %collective-permute-start.39 = (bf16[64,640]{1,0:T(8,128)(2,1)S(1)}, bf16[64,640]{1,0:T(8,128)(2,1)S(1)}, u32[]{:S(2)}, u32[]{:S(2)}) collective-permute-start(bf16[64,640]{1,0:T(8,128)(2,1)S(1)} %get-tuple-element.172), channel_id=1, source_target_pairs={{0,2},{1,3},{2,0},{3,1},{4,6},{5,7},{6,4},{7,5},{8,10},{9,11},{10,... | collective-permute-start | bytes 245768 | tf_op jit(solution)/shard_map/ppermute | solution.py:35
  135.1 12.8 %collective-permute-start.41 = (bf16[128,1280]{1,0:T(8,128)(2,1)S(1)}, bf16[128,1280]{1,0:T(8,128)(2,1)S(1)}, u32[]{:S(2)}, u32[]{:S(2)}) collective-permute-start(bf16[128,1280]{1,0:T(8,128)(2,1)S(1)} %get-tuple-element.178), channel_id=1, source_target_pairs={{0,4},{4,0},{8,12},{12,8},{1,5},{5,1},{9,13},{13,9},{2,6},{6,2},{1... | collective-permute-start | bytes 983048 | tf_op jit(solution)/shard_map/ppermute | solution.py:35
  135.9 13.2 %collective-permute-start.47 = (bf16[128,1280]{1,0:T(8,128)(2,1)S(1)}, bf16[128,1280]{1,0:T(8,128)(2,1)S(1)}, u32[]{:S(2)}, u32[]{:S(2)}) collective-permute-start(bf16[128,1280]{1,0:T(8,128)(2,1)S(1)} %get-tuple-element.186.refs_0_.refs_4_), channel_id=1, source_target_pairs={{0,16},{16,0},{1,17},{17,1},{2,18},{18,2},{3,19},{19,3},{4,20},{20... | collective-permute-start | bytes 983048 | tf_op jit(solution)/shard_map/ppermute | solution.py:35
  139.7 12.9 %collective-permute-start.48 = (bf16[128,1280]{1,0:T(8,128)(2,1)S(1)}, bf16[128,1280]{1,0:T(8,128)(2,1)S(1)}, u32[]{:S(2)}, u32[]{:S(2)}) collective-permute-start(bf16[128,1280]{1,0:T(8,128)(2,1)S(1)} %collective-permute-done.46.refs_1_.refs_5_), channel_id=1, source_target_pairs={{0,16},{16,0},{1,17},{17,1},{2,18},{18,2},{3,19},{19,3},{4,20},{20... | collective-permute-start | bytes 983048 | tf_op jit(solution)/shard_map/ppermute | solution.py:35
  141.6 5.7 %collective-permute-start.43 = (bf16[128,256]{1,0:T(8,128)(2,1)S(1)}, bf16[128,256]{1,0:T(8,128)(2,1)S(1)}, u32[]{:S(2)}, u32[]{:S(2)}) collective-permute-start(bf16[128,256]{1,0:T(8,128)(2,1)S(1)} %get-tuple-element.184), channel_id=1, source_target_pairs={{0,4},{4,0},{8,12},{12,8},{1,5},{5,1},{9,13},{13,9},{2,6},{6,2},{1... | collective-permute-start | bytes 196616 | tf_op jit(solution)/shard_map/ppermute | solution.py:35
  143.0 13.6 %collective-permute-start.44 = (bf16[128,256]{1,0:T(8,128)(2,1)S(1)}, bf16[128,256]{1,0:T(8,128)(2,1)S(1)}, u32[]{:S(2)}, u32[]{:S(2)}) collective-permute-start(bf16[128,256]{1,0:T(8,128)(2,1)S(1)} %get-tuple-element.183.refs_0_), channel_id=1, source_target_pairs={{0,16},{16,0},{1,17},{17,1},{2,18},{18,2},{3,19},{19,3},{4,20},{20... | collective-permute-start | bytes 196616 | tf_op jit(solution)/shard_map/ppermute | solution.py:35
  147.4 9.2 %collective-permute-start.45 = (bf16[128,256]{1,0:T(8,128)(2,1)S(1)}, bf16[128,256]{1,0:T(8,128)(2,1)S(1)}, u32[]{:S(2)}, u32[]{:S(2)}) collective-permute-start(bf16[128,256]{1,0:T(8,128)(2,1)S(1)} %collective-permute-done.43.refs_1_), channel_id=1, source_target_pairs={{0,16},{16,0},{1,17},{17,1},{2,18},{18,2},{3,19},{19,3},{4,20},{20... | collective-permute-start | bytes 196616 | tf_op jit(solution)/shard_map/ppermute | solution.py:35
  (6 other events, 41.4 us)

commit v4 on v3

--- a/solution.py
+++ b/solution.py
@@ -560,13 +560,9 @@
             return [self.kept] + self.banded + self.arrived
 
     def product(lefts, left_col, rights, right_col):
-        total = None
-        for left, right in zip(lefts, rights):
-            term = cols_dot(
-                left[:, left_col : left_col + own_rows], right[:, right_col : right_col + own_cols]
-            )
-            total = term if total is None else total + term
-        return total
+        left = [ref[:, left_col : left_col + own_rows] for ref in lefts]
+        right = [ref[:, right_col : right_col + own_cols] for ref in rights]
+        return cols_dot(jnp.concatenate(left, axis=0), jnp.concatenate(right, axis=0))
 
     def begun_gradient(lefts, left_col, rights, right_col):
         count = len(lefts)
@@ -620,11 +616,12 @@
     (edges,) = edging.results
     from_left = lax.ppermute(edges, "mp", around("mp", 1))
     from_right = lax.ppermute(edges, "mp", around("mp", -1))
-    relay = relayed(merged(embed_bands))
-    order.wait_for([from_left, from_right] + input_parts[1:])
     up_kept, down_block = keep_arrived(arrived_up, mlp, (0, 0), mlp, (0, 1))
     up_own, up_bands = own_pieces(up_kept)
     arrived_down = lax.ppermute(down_block, "role", to_solver)
+    relay = relayed(merged(embed_bands))
+    order.wait_for([from_left, from_right] + input_parts[1:])
+    order.run("relay")
     embed_held = held_matrix(embed_own, relay)
 
     def embed_rows(ins, outs, _):
@@ -853,6 +850,7 @@
     hidden_on.join()
     order.run("join")
     hidden_on.send()
+    order.wait_for(hidden_on.arrived)
     hidden_on.forward(False)
     residual_on.cut_crossed()
 
@@ -883,35 +881,38 @@
     embed_term = begun_gradient(all_residual, own_cols, all_residual, 0)
     state_out = selected_state(final_cells, arrived_cells)
 
-    def updated(name, lefts, left_col, rights, right_col, momentum, weight, index, term=(), begun=()):
-        arrays = lefts + rights + list(term)
-        count = len(lefts)
+    def updated(name, products, momentum, weight, term=()):
+        arrays = [v for _, lefts, _, rights, _ in products for v in lefts + rights] + list(term)
         cuts = 2
         step = own_rows // cuts
+        blocks = len(products)
 
         def body(ins, outs, scratch):
             mom_new, weight_new, sems = scratch
-            total = product(ins[:count], left_col, ins[count : 2 * count], right_col)
-            for ref in ins[2 * count : len(arrays)]:
-                total = total + ref[...]
             mom, old = ins[len(arrays)], ins[len(arrays) + 1]
-            copies = []
-            for cut in range(cuts):
-                rows = slice(cut * step, (cut + 1) * step)
-                fresh = MOMENTUM_DECAY * mom[index][rows] + total[rows]
-                mom_new[rows, :] = fresh
-                weight_new[rows, :] = (old[index][rows].astype(F32) - LEARNING_RATE * fresh).astype(
-                    BF16
-                )
-                for number, source in enumerate((mom_new, weight_new)):
-                    copies.append(
-                        pltpu.make_async_copy(
-                            source.at[pl.ds(cut * step, step)],
-                            outs[number].at[index].at[pl.ds(cut * step, step)],
-                            sems.at[2 * cut + number],
+            copies, first = [], 0
+            for block, (index, lefts, left_col, rights, right_col) in enumerate(products):
+                middle, last = first + len(lefts), first + len(lefts) + len(rights)
+                total = product(ins[first:middle], left_col, ins[middle:last], right_col)
+                first = last
+                for ref in ins[first : first + len(term)]:
+                    total = total + ref[...]
+                for cut in range(cuts):
+                    rows = slice(cut * step, (cut + 1) * step)
+                    fresh = MOMENTUM_DECAY * mom[index][rows] + total[rows]
+                    mom_new[block, rows, :] = fresh
+                    weight_new[block, rows, :] = (
+                        old[index][rows].astype(F32) - LEARNING_RATE * fresh
+                    ).astype(BF16)
+                    for number, source in enumerate((mom_new, weight_new)):
+                        copies.append(
+                            pltpu.make_async_copy(
+                                source.at[block, pl.ds(cut * step, step)],
+                                outs[number].at[index].at[pl.ds(cut * step, step)],
+                                sems.at[(block * cuts + cut) * 2 + number],
+                            )
                         )
-                    )
-                    copies[-1].start()
+                        copies[-1].start()
             for copy in copies:
                 copy.wait()
 
@@ -922,22 +923,29 @@
             arrays + [momentum, weight],
             in_hbm=(0, 1),
             scratch=[
-                pltpu.VMEM((own_rows, own_cols), F32),
-                pltpu.VMEM((own_rows, own_cols), BF16),
-                pltpu.SemaphoreType.DMA((2 * cuts,)),
+                pltpu.VMEM((blocks, own_rows, own_cols), F32),
+                pltpu.VMEM((blocks, own_rows, own_cols), BF16),
+                pltpu.SemaphoreType.DMA((2 * cuts * blocks,)),
             ],
-            aliases={len(arrays) + 2: 0, len(arrays) + 3: 1} if begun else None,
-            extra=begun,
         )
 
     all_inputs, all_active = inputs_on.pieces(), active_on.pieces()
     all_hidden, all_embed_sent = hidden_on.pieces(), embed_sent_on.pieces()
-    begun = updated("update_down", all_hidden, own_cols, all_active, 0, mom_mlp, mlp, (0, 1))
     mom_mlp_out, mlp_out = updated(
-        "update_up", all_active, own_cols, all_hidden, 0, mom_mlp, mlp, (0, 0), begun=begun
+        "update_mlp",
+        [
+            ((0, 0), all_active, own_cols, all_hidden, 0),
+            ((0, 1), all_hidden, own_cols, all_active, 0),
+        ],
+        mom_mlp,
+        mlp,
     )
     mom_embed_out, embed_out = updated(
-        "update_embed", all_embed_sent, 0, all_inputs, 0, mom_embed, embed, 0, embed_term.results
+        "update_embed",
+        [(0, all_embed_sent, 0, all_inputs, 0)],
+        mom_embed,
+        embed,
+        embed_term.results,
     )
     return (state_out, embed_out, mlp_out, mom_embed_out, mom_mlp_out)
 

time: 160 us -> 155 us (0.969)
  starting transfers between devices: 62.1 us -> 59.6 us
  Pallas kernels: 25.2 us -> 23.3 us
    ppermute x1, waiting for transfers between devices: 0.01 us -> 3.48 us  [shards(): arrived_up = lax.ppermute(up_block, 'role', to_solver)]
    ppermute x41, starting transfers between devices: 47.9 us -> 45.4 us  [shifted(): return lax.ppermute(value, self.axis, pairs)]
    ppermute x41, waiting for transfers between devices: 64.3 us -> 62.2 us  [shifted(): return lax.ppermute(value, self.axis, pairs)]
    pallas_call x22, Pallas kernels: 25.2 us -> 23.3 us  [call(): pl.pallas_call(kernel, name=name, out_shape=outs + [struct(TOKEN, F32)],...]
  transfers between devices with their start and end apart: 49 -> 49, of which waited for: 22 -> 21; matrix products, arithmetic and copies ran while one was open for 0% -> 0% of each run, Pallas kernels for 12% -> 11%
where the time goes in v4:
time: 155 us
  waiting for transfers between devices  69.9 us (45%)
  starting transfers between devices  59.6 us (38%)
  Pallas kernels  23.3 us (15%)
    ppermute x41, waiting for transfers between devices, shifted(): return lax.ppermute(value, self.axis, pairs)  62.2 us
    ppermute x41, starting transfers between devices, shifted(): return lax.ppermute(value, self.axis, pairs)  45.4 us
    pallas_call x22, Pallas kernels, call(): pl.pallas_call(kernel, name=name, out_shape=outs + [struct(TOKEN, F32)],...  23.3 us
    ppermute x1, starting transfers between devices, shards(): arrived_start = lax.ppermute(start_halves[1], 'role', to_trainer)  4.88 us
    ppermute x1, waiting for transfers between devices, shards(): arrived_up = lax.ppermute(up_block, 'role', to_solver)  3.48 us
  transfers between devices with their start and end apart: 49, of which 21 were waited for; matrix products, arithmetic and copies ran while one was open for 0% of the time, Pallas kernels for 11%

profile of v4, /device:TPU:0, one launch (start us, length us, event | category | flops | bytes accessed | tf_op | source)
XLA Modules:
  0.0 155.0 jit_solution(8776050592457801674)
XLA Ops:
  0.6 1.3 collective-permute-start.4
  3.0 1.7 %patches.1 = (bf16[16,4096]{1,0:T(8,128)(2,1)S(1)}, bf16[16,4096]{1,0:T(8,128)(2,1)S(1)}, f32[2,8,4,128]{3,2,1,0:T(4,128)S(1)}, f32[2,8,4,128]{3,2,1,0:T(4,128)S...) custom-call(f32[2,8,64,128]{3,2,1,0:T(8,128)S(1)} %bitcast.3), custom_call_target="tpu_custom_call" | custom-call | flops 1 | bytes 1 | tf_op jit(solution)/shard_map/patches/pallas_call | solution.py:131
  4.7 4.9 %collective-permute-start.2 = (bf16[16,4096]{1,0:T(8,128)(2,1)S(1)}, bf16[16,4096]{1,0:T(8,128)(2,1)S(1)}, u32[]{:S(2)}, u32[]{:S(2)}) collective-permute-start(bf16[16,4096]{1,0:T(8,128)(2,1)S(1)} %get-tuple-element.103), channel_id=1, source_target_pairs={{0,16},{1,17},{2,18},{3,19},{4,20},{5,21},{6,22},{7,23},{8,24},{9,... | collective-permute-start | bytes 393224 | tf_op jit(solution)/shard_map/ppermute | solution.py:603
  9.5 2.8 %collective-permute-start = (f32[2,8,4,128]{3,2,1,0:T(4,128)S(1)}, f32[2,8,4,128]{3,2,1,0:T(4,128)S(1)}, u32[]{:S(2)}, u32[]{:S(2)}) collective-permute-start(f32[2,8,4,128]{3,2,1,0:T(4,128)S(1)} %get-tuple-element.100), channel_id=1, source_target_pairs={{0,4},{4,8},{8,12},{12,0},{1,5},{5,9},{9,13},{13,1},{2,6},{6,10},{... | collective-permute-start | bytes 98312 | tf_op jit(solution)/shard_map/ppermute | solution.py:604
  12.3 2.1 %collective-permute-start.1 = (f32[2,8,4,128]{3,2,1,0:T(4,128)S(1)}, f32[2,8,4,128]{3,2,1,0:T(4,128)S(1)}, u32[]{:S(2)}, u32[]{:S(2)}) collective-permute-start(f32[2,8,4,128]{3,2,1,0:T(4,128)S(1)} %get-tuple-element.101), channel_id=1, source_target_pairs={{0,12},{4,0},{8,4},{12,8},{1,13},{5,1},{9,5},{13,9},{2,14},{6,2},{... | collective-permute-start | bytes 98312 | tf_op jit(solution)/shard_map/ppermute | solution.py:605
  14.4 2.1 %collective-permute-done.refs_3_.refs_1_ = f32[2,8,4,128]{3,2,1,0:T(4,128)S(1)} collective-permute-done((f32[2,8,4,128]{3,2,1,0:T(4,128)S(1)}, f32[2,8,4,128]{3,2,1,0:T(4,128)S(1)}, u32[]{:S(2)}, u32[]{:S(2)}) %collective-permute-start) | collective-permute-done | bytes 32800 | tf_op jit(solution)/shard_map/ppermute | solution.py:604
  18.1 1.3 collective-permute-start.10
  19.4 2.5 %collective-permute-start.9 = (bf16[256,1024]{1,0:T(8,128)(2,1)S(1)}, bf16[256,1024]{1,0:T(8,128)(2,1)S(1)}, u32[]{:S(2)}, u32[]{:S(2)}) collective-permute-start(bf16[256,1024]{1,0:T(8,128)(2,1)S(1)} %get-tuple-element.111.refs_2_.refs_8_.refs_6_), channel_id=1, source_target_pairs={{0,4},{4,0},{8,12},{12,8},{1,5},{5,1},{9,13},{13,9},{2,6},{6,2},{1... | collective-permute-start | bytes 1572872 | tf_op jit(solution)/shard_map/ppermute | solution.py:35
  21.9 1.5 collective-permute-start.3
  23.4 2.7 %collective-permute-done.3.refs_1_ = bf16[16,2048]{1,0:T(8,128)(2,1)S(1)} collective-permute-done((bf16[16,2048]{1,0:T(8,128)(2,1)S(1)}, bf16[16,2048]{1,0:T(8,128)(2,1)S(1)}, u32[]{:S(2)}, u32[]{:S(2)}) %collective-permute-start.3) | collective-permute-done | bytes 65568 | tf_op jit(solution)/shard_map/ppermute | solution.py:35
  26.5 2.7 %collective-permute-start.7 = (bf16[32,2048]{1,0:T(8,128)(2,1)S(1)}, bf16[32,2048]{1,0:T(8,128)(2,1)S(1)}, u32[]{:S(2)}, u32[]{:S(2)}) collective-permute-start(bf16[32,2048]{1,0:T(8,128)(2,1)S(1)} %get-tuple-element.110.refs_0_), channel_id=1, source_target_pairs={{0,8},{4,12},{8,0},{12,4},{1,9},{5,13},{9,1},{13,5},{2,10},{6,14},... | collective-permute-start | bytes 393224 | tf_op jit(solution)/shard_map/ppermute | solution.py:35
  29.7 3.5 %collective-permute-done.10.refs_0_ = bf16[256,1024]{1,0:T(8,128)(2,1)S(1)} collective-permute-done((bf16[256,1024]{1,0:T(8,128)(2,1)S(1)}, bf16[256,1024]{1,0:T(8,128)(2,1)S(1)}, u32[]{:S(2)}, u32[]{:S(2)}) %collective-permute-start.10) | collective-permute-done | bytes 524320 | tf_op jit(solution)/shard_map/ppermute | solution.py:611
  35.8 1.3 collective-permute-start.15
  37.1 2.8 %collective-permute-start.14 = (bf16[256,1024]{1,0:T(8,128)(2,1)S(1)}, bf16[256,1024]{1,0:T(8,128)(2,1)S(1)}, u32[]{:S(2)}, u32[]{:S(2)}) collective-permute-start(bf16[256,1024]{1,0:T(8,128)(2,1)S(1)} %get-tuple-element.121.refs_3_.refs_4_), channel_id=1, source_target_pairs={{0,4},{4,0},{8,12},{12,8},{1,5},{5,1},{9,13},{13,9},{2,6},{6,2},{1... | collective-permute-start | bytes 1572872 | tf_op jit(solution)/shard_map/ppermute | solution.py:35
  40.7 1.6 %collective-permute-start.12 = (bf16[64,512]{1,0:T(8,128)(2,1)S(1)}, bf16[64,512]{1,0:T(8,128)(2,1)S(1)}, u32[]{:S(2)}, u32[]{:S(2)}) collective-permute-start(bf16[64,512]{1,0:T(8,128)(2,1)S(1)} %get-tuple-element.120), channel_id=1, source_target_pairs={{0,2},{1,3},{2,0},{3,1},{4,6},{5,7},{6,4},{7,5},{8,10},{9,11},{10,... | collective-permute-start | bytes 196616 | tf_op jit(solution)/shard_map/ppermute | solution.py:35
  42.3 8.1 %stencil.1 = (f32[2,8,64,128]{3,2,1,0:T(8,128)S(1)}, bf16[16,4096]{1,0:T(8,128)(2,1)S(1)}, bf16[16,4096]{1,0:T(8,128)(2,1)S(1)}, f32[8,128]{1,0:T(8,128)S(1)}) custom-call(f32[2,8,64,128]{3,2,1,0:T(8,128)S(1)} %get-tuple-element.99.refs_2_.refs_0_, f32[2,8,4,128]{3,2,1,0:T(4,128)S(1)} %collective-permute-done.refs_3_.refs_1_, ...), custom_call_target="tpu_custom_call" | custom-call | flops 1 | bytes 1 | tf_op jit(solution)/shard_map/stencil/pallas_call | solution.py:131
  50.4 1.7 %collective-permute-done.15.refs_1_ = bf16[256,1024]{1,0:T(8,128)(2,1)S(1)} collective-permute-done((bf16[256,1024]{1,0:T(8,128)(2,1)S(1)}, bf16[256,1024]{1,0:T(8,128)(2,1)S(1)}, u32[]{:S(2)}, u32[]{:S(2)}) %collective-permute-start.15) | collective-permute-done | bytes 524320 | tf_op jit(solution)/shard_map/ppermute | solution.py:621
  52.7 2.4 %collective-permute-start.21 = (bf16[256,1024]{1,0:T(8,128)(2,1)S(1)}, bf16[256,1024]{1,0:T(8,128)(2,1)S(1)}, u32[]{:S(2)}, u32[]{:S(2)}) collective-permute-start(bf16[256,1024]{1,0:T(8,128)(2,1)S(1)} %get-tuple-element.129.refs_3_.refs_6_), channel_id=1, source_target_pairs={{0,4},{4,0},{8,12},{12,8},{1,5},{5,1},{9,13},{13,9},{2,6},{6,2},{1... | collective-permute-start | bytes 1572872 | tf_op jit(solution)/shard_map/ppermute | solution.py:35
  55.6 3.0 %collective-permute-start.22 = (f32[2,8,64,128]{3,2,1,0:T(8,128)S(1)}, f32[2,8,64,128]{3,2,1,0:T(8,128)S(1)}, u32[]{:S(2)}, u32[]{:S(2)}) collective-permute-start(f32[2,8,64,128]{3,2,1,0:T(8,128)S(1)} %get-tuple-element.135), channel_id=1, source_target_pairs={{0,16},{16,0},{1,17},{17,1},{2,18},{18,2},{3,19},{19,3},{4,20},{20... | collective-permute-start | bytes 1572872 | tf_op jit(solution)/shard_map/ppermute | solution.py:35
  58.6 1.6 %collective-permute-start.17 = (bf16[64,2176]{1,0:T(8,128)(2,1)S(1)}, bf16[64,2176]{1,0:T(8,128)(2,1)S(1)}, u32[]{:S(2)}, u32[]{:S(2)}) collective-permute-start(bf16[64,2176]{1,0:T(8,128)(2,1)S(1)} %get-tuple-element.128), channel_id=1, source_target_pairs={{0,8},{4,12},{8,0},{12,4},{1,9},{5,13},{9,1},{13,5},{2,10},{6,14},... | collective-permute-start | bytes 835592 | tf_op jit(solution)/shard_map/ppermute | solution.py:35
  60.3 13.3 %collective-permute-done.19.refs_1_ = bf16[16,4096]{1,0:T(8,128)(2,1)S(1)} collective-permute-done((bf16[16,4096]{1,0:T(8,128)(2,1)S(1)}, bf16[16,4096]{1,0:T(8,128)(2,1)S(1)}, u32[]{:S(2)}, u32[]{:S(2)}) %collective-permute-start.19) | collective-permute-done | bytes 131104 | tf_op jit(solution)/shard_map/ppermute | solution.py:35
  74.6 2.3 %collective-permute-start.28 = (bf16[128,1024]{1,0:T(8,128)(2,1)S(1)}, bf16[128,1024]{1,0:T(8,128)(2,1)S(1)}, u32[]{:S(2)}, u32[]{:S(2)}) collective-permute-start(bf16[128,1024]{1,0:T(8,128)(2,1)S(1)} %get-tuple-element.140.refs_4_), channel_id=1, source_target_pairs={{0,16},{16,0},{1,17},{17,1},{2,18},{18,2},{3,19},{19,3},{4,20},{20... | collective-permute-start | bytes 786440 | tf_op jit(solution)/shard_map/ppermute | solution.py:35
  76.9 1.6 %collective-permute-start.25 = (bf16[128,1024]{1,0:T(8,128)(2,1)S(1)}, bf16[128,1024]{1,0:T(8,128)(2,1)S(1)}, u32[]{:S(2)}, u32[]{:S(2)}) collective-permute-start(bf16[128,1024]{1,0:T(8,128)(2,1)S(1)} %get-tuple-element.140.refs_4_), channel_id=1, source_target_pairs={{0,4},{4,0},{8,12},{12,8},{1,5},{5,1},{9,13},{13,9},{2,6},{6,2},{1... | collective-permute-start | bytes 786440 | tf_op jit(solution)/shard_map/ppermute | solution.py:35
  79.4 1.6 %collective-permute-start.26 = (bf16[16,2048]{1,0:T(8,128)(2,1)S(1)}, bf16[16,2048]{1,0:T(8,128)(2,1)S(1)}, u32[]{:S(2)}, u32[]{:S(2)}) collective-permute-start(bf16[16,2048]{1,0:T(8,128)(2,1)S(1)} %get-tuple-element.142), channel_id=1, source_target_pairs={{0,2},{1,3},{2,0},{3,1},{4,6},{5,7},{6,4},{7,5},{8,10},{9,11},{10,... | collective-permute-start | bytes 196616 | tf_op jit(solution)/shard_map/ppermute | solution.py:35
  81.5 2.6 %collective-permute-done.26.refs_4_ = bf16[16,2048]{1,0:T(8,128)(2,1)S(1)} collective-permute-done((bf16[16,2048]{1,0:T(8,128)(2,1)S(1)}, bf16[16,2048]{1,0:T(8,128)(2,1)S(1)}, u32[]{:S(2)}, u32[]{:S(2)}) %collective-permute-start.26) | collective-permute-done | bytes 65568 | tf_op jit(solution)/shard_map/ppermute | solution.py:35
  84.1 1.2 collective-permute-done.25.refs_2_
  85.9 1.6 %collective-permute-start.29 = (bf16[128,1280]{1,0:T(8,128)(2,1)S(1)}, bf16[128,1280]{1,0:T(8,128)(2,1)S(1)}, u32[]{:S(2)}, u32[]{:S(2)}) collective-permute-start(bf16[128,1280]{1,0:T(8,128)(2,1)S(1)} %get-tuple-element.146), channel_id=1, source_target_pairs={{0,4},{4,0},{8,12},{12,8},{1,5},{5,1},{9,13},{13,9},{2,6},{6,2},{1... | collective-permute-start | bytes 983048 | tf_op jit(solution)/shard_map/ppermute | solution.py:35
  87.8 1.7 %collective-permute-start.30 = (bf16[64,2048]{1,0:T(8,128)(2,1)S(1)}, bf16[64,2048]{1,0:T(8,128)(2,1)S(1)}, u32[]{:S(2)}, u32[]{:S(2)}) collective-permute-start(bf16[64,2048]{1,0:T(8,128)(2,1)S(1)} %get-tuple-element.148), channel_id=1, source_target_pairs={{0,8},{4,12},{8,0},{12,4},{1,9},{5,13},{9,1},{13,5},{2,10},{6,14},... | collective-permute-start | bytes 786440 | tf_op jit(solution)/shard_map/ppermute | solution.py:35
  89.5 1.7 %collective-permute-start.31 = (bf16[128,1024]{1,0:T(8,128)(2,1)S(1)}, bf16[128,1024]{1,0:T(8,128)(2,1)S(1)}, u32[]{:S(2)}, u32[]{:S(2)}) collective-permute-start(bf16[128,1024]{1,0:T(8,128)(2,1)S(1)} %get-tuple-element.151.refs_5_), channel_id=1, source_target_pairs={{0,16},{16,0},{1,17},{17,1},{2,18},{18,2},{3,19},{19,3},{4,20},{20... | collective-permute-start | bytes 786440 | tf_op jit(solution)/shard_map/ppermute | solution.py:35
  91.3 8.4 %collective-permute-done.30.refs_4_ = bf16[64,2048]{1,0:T(8,128)(2,1)S(1)} collective-permute-done((bf16[64,2048]{1,0:T(8,128)(2,1)S(1)}, bf16[64,2048]{1,0:T(8,128)(2,1)S(1)}, u32[]{:S(2)}, u32[]{:S(2)}) %collective-permute-start.30) | collective-permute-done | bytes 262176 | tf_op jit(solution)/shard_map/ppermute | solution.py:35
  99.7 2.2 %collective-permute-done.31.refs_12_.refs_7_ = bf16[128,1024]{1,0:T(8,128)(2,1)S(1)} collective-permute-done((bf16[128,1024]{1,0:T(8,128)(2,1)S(1)}, bf16[128,1024]{1,0:T(8,128)(2,1)S(1)}, u32[]{:S(2)}, u32[]{:S(2)}) %collective-permute-start.31) | collective-permute-done | bytes 262176 | tf_op jit(solution)/shard_map/ppermute | solution.py:35
  102.7 1.6 %collective-permute-start.34 = (bf16[64,512]{1,0:T(8,128)(2,1)S(1)}, bf16[64,512]{1,0:T(8,128)(2,1)S(1)}, u32[]{:S(2)}, u32[]{:S(2)}) collective-permute-start(bf16[64,512]{1,0:T(8,128)(2,1)S(1)} %get-tuple-element.156), channel_id=1, source_target_pairs={{0,2},{1,3},{2,0},{3,1},{4,6},{5,7},{6,4},{7,5},{8,10},{9,11},{10,... | collective-permute-start | bytes 196616 | tf_op jit(solution)/shard_map/ppermute | solution.py:35
  104.3 2.9 %collective-permute-done.34.refs_5_ = bf16[64,512]{1,0:T(8,128)(2,1)S(1)} collective-permute-done((bf16[64,512]{1,0:T(8,128)(2,1)S(1)}, bf16[64,512]{1,0:T(8,128)(2,1)S(1)}, u32[]{:S(2)}, u32[]{:S(2)}) %collective-permute-start.34) | collective-permute-done | bytes 65568 | tf_op jit(solution)/shard_map/ppermute | solution.py:35
  108.4 1.4 collective-permute-start.38
  109.8 1.3 collective-permute-start.35
  111.1 1.7 %collective-permute-start.37 = (bf16[64,2048]{1,0:T(8,128)(2,1)S(1)}, bf16[64,2048]{1,0:T(8,128)(2,1)S(1)}, u32[]{:S(2)}, u32[]{:S(2)}) collective-permute-start(bf16[64,2048]{1,0:T(8,128)(2,1)S(1)} %get-tuple-element.166), channel_id=1, source_target_pairs={{0,8},{4,12},{8,0},{12,4},{1,9},{5,13},{9,1},{13,5},{2,10},{6,14},... | collective-permute-start | bytes 786440 | tf_op jit(solution)/shard_map/ppermute | solution.py:35
  112.9 12.6 %collective-permute-done.38.refs_10_.refs_3_.refs_15_ = bf16[128,1280]{1,0:T(8,128)(2,1)S(1)} collective-permute-done((bf16[128,1280]{1,0:T(8,128)(2,1)S(1)}, bf16[128,1280]{1,0:T(8,128)(2,1)S(1)}, u32[]{:S(2)}, u32[]{:S(2)}) %collective-permute-start.38) | collective-permute-done | bytes 327712 | tf_op jit(solution)/shard_map/ppermute | solution.py:35
  126.4 1.4 collective-permute-done.40.refs_1_
  128.6 1.3 collective-permute-start.47
  129.9 1.5 collective-permute-start.39
  131.4 2.9 %collective-permute-done.39.refs_6_ = bf16[64,640]{1,0:T(8,128)(2,1)S(1)} collective-permute-done((bf16[64,640]{1,0:T(8,128)(2,1)S(1)}, bf16[64,640]{1,0:T(8,128)(2,1)S(1)}, u32[]{:S(2)}, u32[]{:S(2)}) %collective-permute-start.39) | collective-permute-done | bytes 81952 | tf_op jit(solution)/shard_map/ppermute | solution.py:35
  134.3 3.4 %collective-permute-done.41.refs_8_.refs_6_.refs_10_ = bf16[128,1280]{1,0:T(8,128)(2,1)S(1)} collective-permute-done((bf16[128,1280]{1,0:T(8,128)(2,1)S(1)}, bf16[128,1280]{1,0:T(8,128)(2,1)S(1)}, u32[]{:S(2)}, u32[]{:S(2)}) %collective-permute-start.41) | collective-permute-done | bytes 327712 | tf_op jit(solution)/shard_map/ppermute | solution.py:35
  137.9 1.4 collective-permute-start.42
  139.9 1.3 collective-permute-done.43.refs_1_
  142.1 1.3 collective-permute-start.45
  143.4 4.9 %collective-permute-done.44.refs_1_ = bf16[128,256]{1,0:T(8,128)(2,1)S(1)} collective-permute-done((bf16[128,256]{1,0:T(8,128)(2,1)S(1)}, bf16[128,256]{1,0:T(8,128)(2,1)S(1)}, u32[]{:S(2)}, u32[]{:S(2)}) %collective-permute-start.44) | collective-permute-done | bytes 65568 | tf_op jit(solution)/shard_map/ppermute | solution.py:35
  150.0 2.3 %update_mlp.1 = (f32[1,2,256,1024]{3,2,1,0:T(8,128)}, bf16[1,2,256,1024]{3,2,1,0:T(8,128)(2,1)}, f32[8,128]{1,0:T(8,128)S(1)}) custom-call(bf16[128,1280]{1,0:T(8,128)(2,1)S(1)} %get-tuple-element.152.refs_0_.refs_12_, bf16[128,1280]{1,0:T(8,128)(2,1)S(1)} %get-tuple-element.168.refs_1_.refs_13_, ...), custom_call_target="tpu_custom_call" | custom-call | flops 1 | bytes 1 | tf_op jit(solution)/shard_map/update_mlp/pallas_call | solution.py:131
  152.6 2.3 %update_embed.1 = (f32[1,256,1024]{2,1,0:T(8,128)}, bf16[1,256,1024]{2,1,0:T(8,128)(2,1)}, f32[8,128]{1,0:T(8,128)}) custom-call(bf16[128,256]{1,0:T(8,128)(2,1)S(1)} %get-tuple-element.183.refs_0_, bf16[128,256]{1,0:T(8,128)(2,1)S(1)} %collective-permute-done.44.refs_1_, bf16[128,256]{1,0:T(8,128)(2,1)S(1)} %collective-permute-done.45.refs_2_, ...), custom_call_target="tpu_custom_call" | custom-call | flops 1 | bytes 1 | tf_op jit(solution)/shard_map/update_embed/pallas_call | solution.py:131
  (82 shorter events, 18.6 us)
Async XLA Ops:
  0.6 16.4 %collective-permute-start.4 = (bf16[256,1024]{1,0:T(8,128)(2,1)}, bf16[256,1024]{1,0:T(8,128)(2,1)S(1)}, u32[]{:S(2)}, u32[]{:S(2)}) collective-permute-start(bf16[256,1024]{1,0:T(8,128)(2,1)} %bitcast.2), channel_id=1, source_target_pairs={{16,0},{17,1},{18,2},{19,3},{20,4},{21,5},{22,6},{23,7},{24,8},{25... | collective-permute-start | bytes 1572872 | tf_op jit(solution)/shard_map/ppermute | solution.py:595
  4.7 11.9 %collective-permute-start.2 = (bf16[16,4096]{1,0:T(8,128)(2,1)S(1)}, bf16[16,4096]{1,0:T(8,128)(2,1)S(1)}, u32[]{:S(2)}, u32[]{:S(2)}) collective-permute-start(bf16[16,4096]{1,0:T(8,128)(2,1)S(1)} %get-tuple-element.103), channel_id=1, source_target_pairs={{0,16},{1,17},{2,18},{3,19},{4,20},{5,21},{6,22},{7,23},{8,24},{9,... | collective-permute-start | bytes 393224 | tf_op jit(solution)/shard_map/ppermute | solution.py:603
  9.5 7.0 %collective-permute-start = (f32[2,8,4,128]{3,2,1,0:T(4,128)S(1)}, f32[2,8,4,128]{3,2,1,0:T(4,128)S(1)}, u32[]{:S(2)}, u32[]{:S(2)}) collective-permute-start(f32[2,8,4,128]{3,2,1,0:T(4,128)S(1)} %get-tuple-element.100), channel_id=1, source_target_pairs={{0,4},{4,8},{8,12},{12,0},{1,5},{5,9},{9,13},{13,1},{2,6},{6,10},{... | collective-permute-start | bytes 98312 | tf_op jit(solution)/shard_map/ppermute | solution.py:604
  12.3 4.3 %collective-permute-start.1 = (f32[2,8,4,128]{3,2,1,0:T(4,128)S(1)}, f32[2,8,4,128]{3,2,1,0:T(4,128)S(1)}, u32[]{:S(2)}, u32[]{:S(2)}) collective-permute-start(f32[2,8,4,128]{3,2,1,0:T(4,128)S(1)} %get-tuple-element.101), channel_id=1, source_target_pairs={{0,12},{4,0},{8,4},{12,8},{1,13},{5,1},{9,5},{13,9},{2,14},{6,2},{... | collective-permute-start | bytes 98312 | tf_op jit(solution)/shard_map/ppermute | solution.py:605
  18.1 15.0 %collective-permute-start.10 = (bf16[256,1024]{1,0:T(8,128)(2,1)S(1)}, bf16[256,1024]{1,0:T(8,128)(2,1)S(1)}, u32[]{:S(2)}, u32[]{:S(2)}) collective-permute-start(bf16[256,1024]{1,0:T(8,128)(2,1)S(1)} %get-tuple-element.112), channel_id=1, source_target_pairs={{16,0},{17,1},{18,2},{19,3},{20,4},{21,5},{22,6},{23,7},{24,8},{25... | collective-permute-start | bytes 1572872 | tf_op jit(solution)/shard_map/ppermute | solution.py:611
  19.4 16.3 %collective-permute-start.9 = (bf16[256,1024]{1,0:T(8,128)(2,1)S(1)}, bf16[256,1024]{1,0:T(8,128)(2,1)S(1)}, u32[]{:S(2)}, u32[]{:S(2)}) collective-permute-start(bf16[256,1024]{1,0:T(8,128)(2,1)S(1)} %get-tuple-element.111.refs_2_.refs_8_.refs_6_), channel_id=1, source_target_pairs={{0,4},{4,0},{8,12},{12,8},{1,5},{5,1},{9,13},{13,9},{2,6},{6,2},{1... | collective-permute-start | bytes 1572872 | tf_op jit(solution)/shard_map/ppermute | solution.py:35
  21.9 4.3 %collective-permute-start.3 = (bf16[16,2048]{1,0:T(8,128)(2,1)S(1)}, bf16[16,2048]{1,0:T(8,128)(2,1)S(1)}, u32[]{:S(2)}, u32[]{:S(2)}) collective-permute-start(bf16[16,2048]{1,0:T(8,128)(2,1)S(1)} %get-tuple-element.106), channel_id=1, source_target_pairs={{0,2},{1,3},{2,0},{3,1},{4,6},{5,7},{6,4},{7,5},{8,10},{9,11},{10,... | collective-permute-start | bytes 196616 | tf_op jit(solution)/shard_map/ppermute | solution.py:35
  26.5 8.5 %collective-permute-start.7 = (bf16[32,2048]{1,0:T(8,128)(2,1)S(1)}, bf16[32,2048]{1,0:T(8,128)(2,1)S(1)}, u32[]{:S(2)}, u32[]{:S(2)}) collective-permute-start(bf16[32,2048]{1,0:T(8,128)(2,1)S(1)} %get-tuple-element.110.refs_0_), channel_id=1, source_target_pairs={{0,8},{4,12},{8,0},{12,4},{1,9},{5,13},{9,1},{13,5},{2,10},{6,14},... | collective-permute-start | bytes 393224 | tf_op jit(solution)/shard_map/ppermute | solution.py:35
  29.1 5.1 %collective-permute-start.6 = (f32[72,128]{1,0:T(8,128)S(1)}, f32[72,128]{1,0:T(8,128)S(1)}, u32[]{:S(2)}, u32[]{:S(2)}) collective-permute-start(f32[72,128]{1,0:T(8,128)S(1)} %get-tuple-element.109), channel_id=1, source_target_pairs={{0,3},{1,0},{2,1},{3,2},{4,7},{5,4},{6,5},{7,6},{8,11},{9,8},{10,9... | collective-permute-start | bytes 110600 | tf_op jit(solution)/shard_map/ppermute | solution.py:618
  29.1 5.1 %collective-permute-start.5 = (f32[72,128]{1,0:T(8,128)S(1)}, f32[72,128]{1,0:T(8,128)S(1)}, u32[]{:S(2)}, u32[]{:S(2)}) collective-permute-start(f32[72,128]{1,0:T(8,128)S(1)} %get-tuple-element.109), channel_id=1, source_target_pairs={{0,1},{1,2},{2,3},{3,0},{4,5},{5,6},{6,7},{7,4},{8,9},{9,10},{10,1... | collective-permute-start | bytes 110600 | tf_op jit(solution)/shard_map/ppermute | solution.py:617
  33.1 6.8 %collective-permute-start.8 = (bf16[256,1024]{1,0:T(8,128)(2,1)S(1)}, bf16[256,1024]{1,0:T(8,128)(2,1)S(1)}, u32[]{:S(2)}, u32[]{:S(2)}) collective-permute-start(bf16[256,1024]{1,0:T(8,128)(2,1)S(1)} %get-tuple-element.111.refs_2_.refs_8_.refs_6_), channel_id=1, source_target_pairs={{0,1},{1,0},{2,3},{3,2},{4,5},{5,4},{6,7},{7,6},{8,9},{9,8},{10,11... | collective-permute-start | bytes 1572872 | tf_op jit(solution)/shard_map/ppermute | solution.py:35
  35.8 4.2 %collective-permute-start.11 = (bf16[256,1024]{1,0:T(8,128)(2,1)S(1)}, bf16[256,1024]{1,0:T(8,128)(2,1)S(1)}, u32[]{:S(2)}, u32[]{:S(2)}) collective-permute-start(bf16[256,1024]{1,0:T(8,128)(2,1)S(1)} %get-tuple-element.115.refs_4_.refs_10_.refs_8_), channel_id=1, source_target_pairs={{0,1},{1,0},{2,3},{3,2},{4,5},{5,4},{6,7},{7,6},{8,9},{9,8},{10,11... | collective-permute-start | bytes 1572872 | tf_op jit(solution)/shard_map/ppermute | solution.py:35
  35.8 16.2 %collective-permute-start.15 = (bf16[256,1024]{1,0:T(8,128)(2,1)S(1)}, bf16[256,1024]{1,0:T(8,128)(2,1)S(1)}, u32[]{:S(2)}, u32[]{:S(2)}) collective-permute-start(bf16[256,1024]{1,0:T(8,128)(2,1)S(1)} %get-tuple-element.122), channel_id=1, source_target_pairs={{16,0},{17,1},{18,2},{19,3},{20,4},{21,5},{22,6},{23,7},{24,8},{25... | collective-permute-start | bytes 1572872 | tf_op jit(solution)/shard_map/ppermute | solution.py:621
  37.1 15.4 %collective-permute-start.14 = (bf16[256,1024]{1,0:T(8,128)(2,1)S(1)}, bf16[256,1024]{1,0:T(8,128)(2,1)S(1)}, u32[]{:S(2)}, u32[]{:S(2)}) collective-permute-start(bf16[256,1024]{1,0:T(8,128)(2,1)S(1)} %get-tuple-element.121.refs_3_.refs_4_), channel_id=1, source_target_pairs={{0,4},{4,0},{8,12},{12,8},{1,5},{5,1},{9,13},{13,9},{2,6},{6,2},{1... | collective-permute-start | bytes 1572872 | tf_op jit(solution)/shard_map/ppermute | solution.py:35
  40.7 11.8 %collective-permute-start.12 = (bf16[64,512]{1,0:T(8,128)(2,1)S(1)}, bf16[64,512]{1,0:T(8,128)(2,1)S(1)}, u32[]{:S(2)}, u32[]{:S(2)}) collective-permute-start(bf16[64,512]{1,0:T(8,128)(2,1)S(1)} %get-tuple-element.120), channel_id=1, source_target_pairs={{0,2},{1,3},{2,0},{3,1},{4,6},{5,7},{6,4},{7,5},{8,10},{9,11},{10,... | collective-permute-start | bytes 196616 | tf_op jit(solution)/shard_map/ppermute | solution.py:35
  42.3 12.8 %collective-permute-start.13 = (bf16[256,1024]{1,0:T(8,128)(2,1)S(1)}, bf16[256,1024]{1,0:T(8,128)(2,1)S(1)}, u32[]{:S(2)}, u32[]{:S(2)}) collective-permute-start(bf16[256,1024]{1,0:T(8,128)(2,1)S(1)} %get-tuple-element.121.refs_3_.refs_4_), channel_id=1, source_target_pairs={{0,1},{1,0},{2,3},{3,2},{4,5},{5,4},{6,7},{7,6},{8,9},{9,8},{10,11... | collective-permute-start | bytes 1572872 | tf_op jit(solution)/shard_map/ppermute | solution.py:35
  52.6 2.5 %collective-permute-start.16 = (bf16[256,1024]{1,0:T(8,128)(2,1)S(1)}, bf16[256,1024]{1,0:T(8,128)(2,1)S(1)}, u32[]{:S(2)}, u32[]{:S(2)}) collective-permute-start(bf16[256,1024]{1,0:T(8,128)(2,1)S(1)} %get-tuple-element.124.refs_5_.refs_6_), channel_id=1, source_target_pairs={{0,1},{1,0},{2,3},{3,2},{4,5},{5,4},{6,7},{7,6},{8,9},{9,8},{10,11... | collective-permute-start | bytes 1572872 | tf_op jit(solution)/shard_map/ppermute | solution.py:35
  52.7 21.0 %collective-permute-start.21 = (bf16[256,1024]{1,0:T(8,128)(2,1)S(1)}, bf16[256,1024]{1,0:T(8,128)(2,1)S(1)}, u32[]{:S(2)}, u32[]{:S(2)}) collective-permute-start(bf16[256,1024]{1,0:T(8,128)(2,1)S(1)} %get-tuple-element.129.refs_3_.refs_6_), channel_id=1, source_target_pairs={{0,4},{4,0},{8,12},{12,8},{1,5},{5,1},{9,13},{13,9},{2,6},{6,2},{1... | collective-permute-start | bytes 1572872 | tf_op jit(solution)/shard_map/ppermute | solution.py:35
  55.6 18.1 %collective-permute-start.22 = (f32[2,8,64,128]{3,2,1,0:T(8,128)S(1)}, f32[2,8,64,128]{3,2,1,0:T(8,128)S(1)}, u32[]{:S(2)}, u32[]{:S(2)}) collective-permute-start(f32[2,8,64,128]{3,2,1,0:T(8,128)S(1)} %get-tuple-element.135), channel_id=1, source_target_pairs={{0,16},{16,0},{1,17},{17,1},{2,18},{18,2},{3,19},{19,3},{4,20},{20... | collective-permute-start | bytes 1572872 | tf_op jit(solution)/shard_map/ppermute | solution.py:35
  58.6 15.1 %collective-permute-start.17 = (bf16[64,2176]{1,0:T(8,128)(2,1)S(1)}, bf16[64,2176]{1,0:T(8,128)(2,1)S(1)}, u32[]{:S(2)}, u32[]{:S(2)}) collective-permute-start(bf16[64,2176]{1,0:T(8,128)(2,1)S(1)} %get-tuple-element.128), channel_id=1, source_target_pairs={{0,8},{4,12},{8,0},{12,4},{1,9},{5,13},{9,1},{13,5},{2,10},{6,14},... | collective-permute-start | bytes 835592 | tf_op jit(solution)/shard_map/ppermute | solution.py:35
  60.3 13.4 %collective-permute-start.19 = (bf16[16,4096]{1,0:T(8,128)(2,1)S(1)}, bf16[16,4096]{1,0:T(8,128)(2,1)S(1)}, u32[]{:S(2)}, u32[]{:S(2)}) collective-permute-start(bf16[16,4096]{1,0:T(8,128)(2,1)S(1)} %get-tuple-element.131), channel_id=1, source_target_pairs={{0,16},{16,0},{1,17},{17,1},{2,18},{18,2},{3,19},{19,3},{4,20},{20... | collective-permute-start | bytes 393224 | tf_op jit(solution)/shard_map/ppermute | solution.py:35
  60.3 13.3 %collective-permute-start.20 = (bf16[64,1024]{1,0:T(8,128)(2,1)S(1)}, bf16[64,1024]{1,0:T(8,128)(2,1)S(1)}, u32[]{:S(2)}, u32[]{:S(2)}) collective-permute-start(bf16[64,1024]{1,0:T(8,128)(2,1)S(1)} %get-tuple-element.133.refs_2_), channel_id=1, source_target_pairs={{0,1},{1,0},{2,3},{3,2},{4,5},{5,4},{6,7},{7,6},{8,9},{9,8},{10,11... | collective-permute-start | bytes 393224 | tf_op jit(solution)/shard_map/ppermute | solution.py:35
  73.7 4.8 %collective-permute-start.18 = (bf16[256,1024]{1,0:T(8,128)(2,1)S(1)}, bf16[256,1024]{1,0:T(8,128)(2,1)S(1)}, u32[]{:S(2)}, u32[]{:S(2)}) collective-permute-start(bf16[256,1024]{1,0:T(8,128)(2,1)S(1)} %get-tuple-element.129.refs_3_.refs_6_), channel_id=1, source_target_pairs={{0,1},{1,0},{2,3},{3,2},{4,5},{5,4},{6,7},{7,6},{8,9},{9,8},{10,11... | collective-permute-start | bytes 1572872 | tf_op jit(solution)/shard_map/ppermute | solution.py:35
  74.0 4.5 %collective-permute-start.23 = (bf16[256,1024]{1,0:T(8,128)(2,1)S(1)}, bf16[256,1024]{1,0:T(8,128)(2,1)S(1)}, u32[]{:S(2)}, u32[]{:S(2)}) collective-permute-start(bf16[256,1024]{1,0:T(8,128)(2,1)S(1)} %get-tuple-element.136.refs_5_.refs_8_), channel_id=1, source_target_pairs={{0,1},{1,0},{2,3},{3,2},{4,5},{5,4},{6,7},{7,6},{8,9},{9,8},{10,11... | collective-permute-start | bytes 1572872 | tf_op jit(solution)/shard_map/ppermute | solution.py:35
  74.6 9.5 %collective-permute-start.28 = (bf16[128,1024]{1,0:T(8,128)(2,1)S(1)}, bf16[128,1024]{1,0:T(8,128)(2,1)S(1)}, u32[]{:S(2)}, u32[]{:S(2)}) collective-permute-start(bf16[128,1024]{1,0:T(8,128)(2,1)S(1)} %get-tuple-element.140.refs_4_), channel_id=1, source_target_pairs={{0,16},{16,0},{1,17},{17,1},{2,18},{18,2},{3,19},{19,3},{4,20},{20... | collective-permute-start | bytes 786440 | tf_op jit(solution)/shard_map/ppermute | solution.py:35
  76.9 8.4 %collective-permute-start.25 = (bf16[128,1024]{1,0:T(8,128)(2,1)S(1)}, bf16[128,1024]{1,0:T(8,128)(2,1)S(1)}, u32[]{:S(2)}, u32[]{:S(2)}) collective-permute-start(bf16[128,1024]{1,0:T(8,128)(2,1)S(1)} %get-tuple-element.140.refs_4_), channel_id=1, source_target_pairs={{0,4},{4,0},{8,12},{12,8},{1,5},{5,1},{9,13},{13,9},{2,6},{6,2},{1... | collective-permute-start | bytes 786440 | tf_op jit(solution)/shard_map/ppermute | solution.py:35
  79.3 6.0 %collective-permute-start.24 = (bf16[64,1536]{1,0:T(8,128)(2,1)S(1)}, bf16[64,1536]{1,0:T(8,128)(2,1)S(1)}, u32[]{:S(2)}, u32[]{:S(2)}) collective-permute-start(bf16[64,1536]{1,0:T(8,128)(2,1)S(1)} %get-tuple-element.139), channel_id=1, source_target_pairs={{0,1},{1,0},{2,3},{3,2},{4,5},{5,4},{6,7},{7,6},{8,9},{9,8},{10,11... | collective-permute-start | bytes 589832 | tf_op jit(solution)/shard_map/ppermute | solution.py:35
  79.4 4.7 %collective-permute-start.26 = (bf16[16,2048]{1,0:T(8,128)(2,1)S(1)}, bf16[16,2048]{1,0:T(8,128)(2,1)S(1)}, u32[]{:S(2)}, u32[]{:S(2)}) collective-permute-start(bf16[16,2048]{1,0:T(8,128)(2,1)S(1)} %get-tuple-element.142), channel_id=1, source_target_pairs={{0,2},{1,3},{2,0},{3,1},{4,6},{5,7},{6,4},{7,5},{8,10},{9,11},{10,... | collective-permute-start | bytes 196616 | tf_op jit(solution)/shard_map/ppermute | solution.py:35
  81.0 4.3 %collective-permute-start.27 = (bf16[64,512]{1,0:T(8,128)(2,1)S(1)}, bf16[64,512]{1,0:T(8,128)(2,1)S(1)}, u32[]{:S(2)}, u32[]{:S(2)}) collective-permute-start(bf16[64,512]{1,0:T(8,128)(2,1)S(1)} %get-tuple-element.144), channel_id=1, source_target_pairs={{0,2},{1,3},{2,0},{3,1},{4,6},{5,7},{6,4},{7,5},{8,10},{9,11},{10,... | collective-permute-start | bytes 196616 | tf_op jit(solution)/shard_map/ppermute | solution.py:35
  85.9 15.9 %collective-permute-start.29 = (bf16[128,1280]{1,0:T(8,128)(2,1)S(1)}, bf16[128,1280]{1,0:T(8,128)(2,1)S(1)}, u32[]{:S(2)}, u32[]{:S(2)}) collective-permute-start(bf16[128,1280]{1,0:T(8,128)(2,1)S(1)} %get-tuple-element.146), channel_id=1, source_target_pairs={{0,4},{4,0},{8,12},{12,8},{1,5},{5,1},{9,13},{13,9},{2,6},{6,2},{1... | collective-permute-start | bytes 983048 | tf_op jit(solution)/shard_map/ppermute | solution.py:35
  87.5 14.3 %collective-permute-start.32 = (bf16[128,1280]{1,0:T(8,128)(2,1)S(1)}, bf16[128,1280]{1,0:T(8,128)(2,1)S(1)}, u32[]{:S(2)}, u32[]{:S(2)}) collective-permute-start(bf16[128,1280]{1,0:T(8,128)(2,1)S(1)} %get-tuple-element.152.refs_0_.refs_12_), channel_id=1, source_target_pairs={{0,16},{16,0},{1,17},{17,1},{2,18},{18,2},{3,19},{19,3},{4,20},{20... | collective-permute-start | bytes 983048 | tf_op jit(solution)/shard_map/ppermute | solution.py:35
  87.8 11.8 %collective-permute-start.30 = (bf16[64,2048]{1,0:T(8,128)(2,1)S(1)}, bf16[64,2048]{1,0:T(8,128)(2,1)S(1)}, u32[]{:S(2)}, u32[]{:S(2)}) collective-permute-start(bf16[64,2048]{1,0:T(8,128)(2,1)S(1)} %get-tuple-element.148), channel_id=1, source_target_pairs={{0,8},{4,12},{8,0},{12,4},{1,9},{5,13},{9,1},{13,5},{2,10},{6,14},... | collective-permute-start | bytes 786440 | tf_op jit(solution)/shard_map/ppermute | solution.py:35
  89.5 12.3 %collective-permute-start.31 = (bf16[128,1024]{1,0:T(8,128)(2,1)S(1)}, bf16[128,1024]{1,0:T(8,128)(2,1)S(1)}, u32[]{:S(2)}, u32[]{:S(2)}) collective-permute-start(bf16[128,1024]{1,0:T(8,128)(2,1)S(1)} %get-tuple-element.151.refs_5_), channel_id=1, source_target_pairs={{0,16},{16,0},{1,17},{17,1},{2,18},{18,2},{3,19},{19,3},{4,20},{20... | collective-permute-start | bytes 786440 | tf_op jit(solution)/shard_map/ppermute | solution.py:35
  102.6 4.6 %collective-permute-start.33 = (bf16[64,1536]{1,0:T(8,128)(2,1)S(1)}, bf16[64,1536]{1,0:T(8,128)(2,1)S(1)}, u32[]{:S(2)}, u32[]{:S(2)}) collective-permute-start(bf16[64,1536]{1,0:T(8,128)(2,1)S(1)} %get-tuple-element.154), channel_id=1, source_target_pairs={{0,1},{1,0},{2,3},{3,2},{4,5},{5,4},{6,7},{7,6},{8,9},{9,8},{10,11... | collective-permute-start | bytes 589832 | tf_op jit(solution)/shard_map/ppermute | solution.py:35
  102.7 4.5 %collective-permute-start.34 = (bf16[64,512]{1,0:T(8,128)(2,1)S(1)}, bf16[64,512]{1,0:T(8,128)(2,1)S(1)}, u32[]{:S(2)}, u32[]{:S(2)}) collective-permute-start(bf16[64,512]{1,0:T(8,128)(2,1)S(1)} %get-tuple-element.156), channel_id=1, source_target_pairs={{0,2},{1,3},{2,0},{3,1},{4,6},{5,7},{6,4},{7,5},{8,10},{9,11},{10,... | collective-permute-start | bytes 196616 | tf_op jit(solution)/shard_map/ppermute | solution.py:35
  107.8 17.8 %collective-permute-start.36 = (bf16[128,1536]{1,0:T(8,128)(2,1)S(1)}, bf16[128,1536]{1,0:T(8,128)(2,1)S(1)}, u32[]{:S(2)}, u32[]{:S(2)}) collective-permute-start(bf16[128,1536]{1,0:T(8,128)(2,1)S(1)} %get-tuple-element.160), channel_id=1, source_target_pairs={{0,16},{16,0},{1,17},{17,1},{2,18},{18,2},{3,19},{19,3},{4,20},{20... | collective-permute-start | bytes 1179656 | tf_op jit(solution)/shard_map/ppermute | solution.py:35
  108.4 17.1 %collective-permute-start.38 = (bf16[128,1280]{1,0:T(8,128)(2,1)S(1)}, bf16[128,1280]{1,0:T(8,128)(2,1)S(1)}, u32[]{:S(2)}, u32[]{:S(2)}) collective-permute-start(bf16[128,1280]{1,0:T(8,128)(2,1)S(1)} %get-tuple-element.168.refs_1_.refs_13_), channel_id=1, source_target_pairs={{0,16},{16,0},{1,17},{17,1},{2,18},{18,2},{3,19},{19,3},{4,20},{20... | collective-permute-start | bytes 983048 | tf_op jit(solution)/shard_map/ppermute | solution.py:35
  109.8 15.7 %collective-permute-start.35 = (bf16[128,1280]{1,0:T(8,128)(2,1)S(1)}, bf16[128,1280]{1,0:T(8,128)(2,1)S(1)}, u32[]{:S(2)}, u32[]{:S(2)}) collective-permute-start(bf16[128,1280]{1,0:T(8,128)(2,1)S(1)} %get-tuple-element.159), channel_id=1, source_target_pairs={{0,4},{4,0},{8,12},{12,8},{1,5},{5,1},{9,13},{13,9},{2,6},{6,2},{1... | collective-permute-start | bytes 983048 | tf_op jit(solution)/shard_map/ppermute | solution.py:35
  111.1 14.4 %collective-permute-start.37 = (bf16[64,2048]{1,0:T(8,128)(2,1)S(1)}, bf16[64,2048]{1,0:T(8,128)(2,1)S(1)}, u32[]{:S(2)}, u32[]{:S(2)}) collective-permute-start(bf16[64,2048]{1,0:T(8,128)(2,1)S(1)} %get-tuple-element.166), channel_id=1, source_target_pairs={{0,8},{4,12},{8,0},{12,4},{1,9},{5,13},{9,1},{13,5},{2,10},{6,14},... | collective-permute-start | bytes 786440 | tf_op jit(solution)/shard_map/ppermute | solution.py:35
  126.3 1.5 collective-permute-start.40
  127.9 9.8 %collective-permute-start.41 = (bf16[128,1280]{1,0:T(8,128)(2,1)S(1)}, bf16[128,1280]{1,0:T(8,128)(2,1)S(1)}, u32[]{:S(2)}, u32[]{:S(2)}) collective-permute-start(bf16[128,1280]{1,0:T(8,128)(2,1)S(1)} %get-tuple-element.176.refs_4_.refs_8_), channel_id=1, source_target_pairs={{0,16},{16,0},{1,17},{17,1},{2,18},{18,2},{3,19},{19,3},{4,20},{20... | collective-permute-start | bytes 983048 | tf_op jit(solution)/shard_map/ppermute | solution.py:35
  128.6 10.7 %collective-permute-start.47 = (bf16[128,1280]{1,0:T(8,128)(2,1)S(1)}, bf16[128,1280]{1,0:T(8,128)(2,1)S(1)}, u32[]{:S(2)}, u32[]{:S(2)}) collective-permute-start(bf16[128,1280]{1,0:T(8,128)(2,1)S(1)} %get-tuple-element.186), channel_id=1, source_target_pairs={{0,4},{4,0},{8,12},{12,8},{1,5},{5,1},{9,13},{13,9},{2,6},{6,2},{1... | collective-permute-start | bytes 983048 | tf_op jit(solution)/shard_map/ppermute | solution.py:35
  129.9 4.4 %collective-permute-start.39 = (bf16[64,640]{1,0:T(8,128)(2,1)S(1)}, bf16[64,640]{1,0:T(8,128)(2,1)S(1)}, u32[]{:S(2)}, u32[]{:S(2)}) collective-permute-start(bf16[64,640]{1,0:T(8,128)(2,1)S(1)} %get-tuple-element.171), channel_id=1, source_target_pairs={{0,2},{1,3},{2,0},{3,1},{4,6},{5,7},{6,4},{7,5},{8,10},{9,11},{10,... | collective-permute-start | bytes 245768 | tf_op jit(solution)/shard_map/ppermute | solution.py:35
  137.9 11.0 %collective-permute-start.42 = (bf16[128,1280]{1,0:T(8,128)(2,1)S(1)}, bf16[128,1280]{1,0:T(8,128)(2,1)S(1)}, u32[]{:S(2)}, u32[]{:S(2)}) collective-permute-start(bf16[128,1280]{1,0:T(8,128)(2,1)S(1)} %get-tuple-element.178), channel_id=1, source_target_pairs={{0,4},{4,0},{8,12},{12,8},{1,5},{5,1},{9,13},{13,9},{2,6},{6,2},{1... | collective-permute-start | bytes 983048 | tf_op jit(solution)/shard_map/ppermute | solution.py:35
  139.3 10.7 %collective-permute-start.48 = (bf16[128,1280]{1,0:T(8,128)(2,1)S(1)}, bf16[128,1280]{1,0:T(8,128)(2,1)S(1)}, u32[]{:S(2)}, u32[]{:S(2)}) collective-permute-start(bf16[128,1280]{1,0:T(8,128)(2,1)S(1)} %collective-permute-done.47.refs_5_.refs_9_), channel_id=1, source_target_pairs={{0,16},{16,0},{1,17},{17,1},{2,18},{18,2},{3,19},{19,3},{4,20},{20... | collective-permute-start | bytes 983048 | tf_op jit(solution)/shard_map/ppermute | solution.py:35
  141.2 7.1 %collective-permute-start.44 = (bf16[128,256]{1,0:T(8,128)(2,1)S(1)}, bf16[128,256]{1,0:T(8,128)(2,1)S(1)}, u32[]{:S(2)}, u32[]{:S(2)}) collective-permute-start(bf16[128,256]{1,0:T(8,128)(2,1)S(1)} %get-tuple-element.184), channel_id=1, source_target_pairs={{0,4},{4,0},{8,12},{12,8},{1,5},{5,1},{9,13},{13,9},{2,6},{6,2},{1... | collective-permute-start | bytes 196616 | tf_op jit(solution)/shard_map/ppermute | solution.py:35
  142.1 10.2 %collective-permute-start.45 = (bf16[128,256]{1,0:T(8,128)(2,1)S(1)}, bf16[128,256]{1,0:T(8,128)(2,1)S(1)}, u32[]{:S(2)}, u32[]{:S(2)}) collective-permute-start(bf16[128,256]{1,0:T(8,128)(2,1)S(1)} %get-tuple-element.183.refs_0_), channel_id=1, source_target_pairs={{0,16},{16,0},{1,17},{17,1},{2,18},{18,2},{3,19},{19,3},{4,20},{20... | collective-permute-start | bytes 196616 | tf_op jit(solution)/shard_map/ppermute | solution.py:35
  148.3 4.3 %collective-permute-start.46 = (bf16[128,256]{1,0:T(8,128)(2,1)S(1)}, bf16[128,256]{1,0:T(8,128)(2,1)S(1)}, u32[]{:S(2)}, u32[]{:S(2)}) collective-permute-start(bf16[128,256]{1,0:T(8,128)(2,1)S(1)} %collective-permute-done.44.refs_1_), channel_id=1, source_target_pairs={{0,16},{16,0},{1,17},{17,1},{2,18},{18,2},{3,19},{19,3},{4,20},{20... | collective-permute-start | bytes 196616 | tf_op jit(solution)/shard_map/ppermute | solution.py:35
  (6 other events, 31.6 us)

commit v5 on v4

--- a/solution.py
+++ b/solution.py
@@ -356,13 +356,16 @@
     to_solver, to_trainer = [(TRAINER, SOLVER)], [(SOLVER, TRAINER)]
     order = Order()
 
-    def keep_arrived(arrived, own, index, following, next_index):
+    def keep_arrived(arrived, own, index, following):
         def body(ins, outs, scratch):
             (sems,) = scratch
             solving = lax.axis_index("role") == SOLVER
-            if following is not None:
-                ahead = pltpu.make_async_copy(ins[2].at[next_index], outs[1], sems.at[0])
-                ahead.start()
+            ahead = [
+                pltpu.make_async_copy(ins[2].at[block], outs[1 + k], sems.at[1 + k])
+                for k, block in enumerate(following)
+            ]
+            for copy in ahead:
+                copy.start()
 
             @pl.when(solving)
             def _():
@@ -370,21 +373,20 @@
 
             @pl.when(jnp.logical_not(solving))
             def _():
-                mine = pltpu.make_async_copy(ins[1].at[index], outs[0], sems.at[1])
+                mine = pltpu.make_async_copy(ins[1].at[index], outs[0], sems.at[0])
                 mine.start()
                 mine.wait()
 
-            if following is not None:
-                ahead.wait()
-
-        more = [] if following is None else [following]
+            for copy in ahead:
+                copy.wait()
+
         return order.call(
             body,
             "held",
-            [struct(arrived.shape, BF16)] * (1 + len(more)),
-            [arrived, own] + more,
+            [struct(arrived.shape, BF16)] * (1 + len(following)),
+            [arrived, own] + ([mlp] if following else []),
             left=(1, 2),
-            scratch=[pltpu.SemaphoreType.DMA((2,))],
+            scratch=[pltpu.SemaphoreType.DMA((1 + len(following),))],
         )
 
     def relayed(blocks):
@@ -606,9 +608,10 @@
     splitting = split_patches(start_halves[0], arrived_start)
     order.wait_for([head_rows, tail_rows])
     order.run("split")
-    embed_kept, up_block = keep_arrived(arrived_embed, embed, 0, mlp, (0, 0))
+    embed_kept, up_block, down_block = keep_arrived(arrived_embed, embed, 0, ((0, 0), (0, 1)))
     embed_own, embed_bands = own_pieces(embed_kept)
     arrived_up = lax.ppermute(up_block, "role", to_solver)
+    arrived_down = lax.ppermute(down_block, "role", to_solver)
     ordering = order_rows(to_parts(splitting.results))
     edging = packed_edges(order, cells, head_rows, tail_rows, STEPS)
     order.run("order")
@@ -616,13 +619,18 @@
     (edges,) = edging.results
     from_left = lax.ppermute(edges, "mp", around("mp", 1))
     from_right = lax.ppermute(edges, "mp", around("mp", -1))
-    up_kept, down_block = keep_arrived(arrived_up, mlp, (0, 0), mlp, (0, 1))
+    (up_kept,) = keep_arrived(arrived_up, mlp, (0, 0), ())
     up_own, up_bands = own_pieces(up_kept)
-    arrived_down = lax.ppermute(down_block, "role", to_solver)
     relay = relayed(merged(embed_bands))
     order.wait_for([from_left, from_right] + input_parts[1:])
     order.run("relay")
     embed_held = held_matrix(embed_own, relay)
+    final_cells, *end_halves = stepped(
+        order, cells, head_rows, tail_rows, from_left, from_right, STEPS, 2
+    )
+    (down_kept,) = keep_arrived(arrived_down, mlp, (0, 1), ())
+    down_own, down_bands = own_pieces(down_kept)
+    up_relay = relayed(merged(up_bands))
 
     def embed_rows(ins, outs, _):
         parts, matrix = ins[: wide.size], ins[wide.size :]
@@ -647,15 +655,8 @@
     def core_slot(k):
         return slice((-k) % core.size * own_cols, ((-k) % core.size + 1) * own_cols)
 
-    final_cells, *end_halves = stepped(
-        order, cells, head_rows, tail_rows, from_left, from_right, STEPS, 2
-    )
     (arrived_end,) = role.from_others(end_halves[1])
-    relay = relayed(merged(up_bands))
-    order.wait_for(embed_others)
-    (down_kept,) = keep_arrived(arrived_down, mlp, (0, 1), None, ())
-    down_own, down_bands = own_pieces(down_kept)
-    up_held = held_matrix(up_own, relay)
+    up_held = held_matrix(up_own, up_relay)
     copying = relayed([final_cells])
 
     def added(mine, refs, cols):
@@ -850,7 +851,7 @@
     hidden_on.join()
     order.run("join")
     hidden_on.send()
-    order.wait_for(hidden_on.arrived)
+    hidden_kept_arrived = list(hidden_on.arrived)
     hidden_on.forward(False)
     residual_on.cut_crossed()
 
@@ -873,6 +874,7 @@
     )
     embed_sent_on = Gather(embed_sent, [embed_sent] * (core.size - 1), False, 1)
     embed_sent_on.join()
+    order.wait_for(hidden_kept_arrived)
     order.run("join")
     embed_sent_on.send()
     embed_sent_on.forward(False)

time: 155 us -> 153 us (0.987)
  starting transfers between devices: 59.6 us -> 58 us
    ppermute x41, waiting for transfers between devices: 62.2 us -> 59.3 us  [shifted(): return lax.ppermute(value, self.axis, pairs)]
    ppermute x1, waiting for transfers between devices: 1.67 us -> 4.09 us  [shards(): arrived_down = lax.ppermute(down_block, 'role', to_solver)]
    ppermute x41, starting transfers between devices: 45.4 us -> 43.9 us  [shifted(): return lax.ppermute(value, self.axis, pairs)]
  transfers between devices with their start and end apart: 49 -> 49, of which waited for: 21 -> 20; matrix products, arithmetic and copies ran while one was open for 0% -> 0% of each run, Pallas kernels for 11% -> 11%
where the time goes in v5:
time: 153 us; the launch traced here: 152 us
  waiting for transfers between devices  69.5 us (45%)
  starting transfers between devices  58 us (38%)
  Pallas kernels  22.5 us (15%)
    ppermute x41, waiting for transfers between devices, shifted(): return lax.ppermute(value, self.axis, pairs)  59.3 us
    ppermute x41, starting transfers between devices, shifted(): return lax.ppermute(value, self.axis, pairs)  43.9 us
    pallas_call x22, Pallas kernels, call(): pl.pallas_call(kernel, name=name, out_shape=outs + [struct(TOKEN, F32)],...  22.5 us
    ppermute x1, starting transfers between devices, shards(): arrived_start = lax.ppermute(start_halves[1], 'role', to_trainer)  4.88 us
    ppermute x1, waiting for transfers between devices, shards(): arrived_down = lax.ppermute(down_block, 'role', to_solver)  4.09 us
    ppermute x1, waiting for transfers between devices, shards(): arrived_up = lax.ppermute(up_block, 'role', to_solver)  3.48 us
  transfers between devices with their start and end apart: 49, of which 20 were waited for; matrix products, arithmetic and copies ran while one was open for 0% of the time, Pallas kernels for 11%

profile of v5, /device:TPU:0, one launch (start us, length us, event | category | flops | bytes accessed | tf_op | source)
XLA Modules:
  0.0 152.2 jit_solution(3499034587714484753)
XLA Ops:
  0.6 1.3 collective-permute-start.4
  3.0 1.7 %patches.1 = (bf16[16,4096]{1,0:T(8,128)(2,1)S(1)}, bf16[16,4096]{1,0:T(8,128)(2,1)S(1)}, f32[2,8,4,128]{3,2,1,0:T(4,128)S(1)}, f32[2,8,4,128]{3,2,1,0:T(4,128)S...) custom-call(f32[2,8,64,128]{3,2,1,0:T(8,128)S(1)} %bitcast.3), custom_call_target="tpu_custom_call" | custom-call | flops 1 | bytes 1 | tf_op jit(solution)/shard_map/patches/pallas_call | solution.py:131
  4.7 4.9 %collective-permute-start.2 = (bf16[16,4096]{1,0:T(8,128)(2,1)S(1)}, bf16[16,4096]{1,0:T(8,128)(2,1)S(1)}, u32[]{:S(2)}, u32[]{:S(2)}) collective-permute-start(bf16[16,4096]{1,0:T(8,128)(2,1)S(1)} %get-tuple-element.103), channel_id=1, source_target_pairs={{0,16},{1,17},{2,18},{3,19},{4,20},{5,21},{6,22},{7,23},{8,24},{9,... | collective-permute-start | bytes 393224 | tf_op jit(solution)/shard_map/ppermute | solution.py:605
  9.5 2.8 %collective-permute-start = (f32[2,8,4,128]{3,2,1,0:T(4,128)S(1)}, f32[2,8,4,128]{3,2,1,0:T(4,128)S(1)}, u32[]{:S(2)}, u32[]{:S(2)}) collective-permute-start(f32[2,8,4,128]{3,2,1,0:T(4,128)S(1)} %get-tuple-element.100), channel_id=1, source_target_pairs={{0,4},{4,8},{8,12},{12,0},{1,5},{5,9},{9,13},{13,1},{2,6},{6,10},{... | collective-permute-start | bytes 98312 | tf_op jit(solution)/shard_map/ppermute | solution.py:606
  12.3 2.1 %collective-permute-start.1 = (f32[2,8,4,128]{3,2,1,0:T(4,128)S(1)}, f32[2,8,4,128]{3,2,1,0:T(4,128)S(1)}, u32[]{:S(2)}, u32[]{:S(2)}) collective-permute-start(f32[2,8,4,128]{3,2,1,0:T(4,128)S(1)} %get-tuple-element.101), channel_id=1, source_target_pairs={{0,12},{4,0},{8,4},{12,8},{1,13},{5,1},{9,5},{13,9},{2,14},{6,2},{... | collective-permute-start | bytes 98312 | tf_op jit(solution)/shard_map/ppermute | solution.py:607
  14.4 2.1 %collective-permute-done.refs_3_.refs_1_ = f32[2,8,4,128]{3,2,1,0:T(4,128)S(1)} collective-permute-done((f32[2,8,4,128]{3,2,1,0:T(4,128)S(1)}, f32[2,8,4,128]{3,2,1,0:T(4,128)S(1)}, u32[]{:S(2)}, u32[]{:S(2)}) %collective-permute-start) | collective-permute-done | bytes 32800 | tf_op jit(solution)/shard_map/ppermute | solution.py:606
  17.0 1.2 held.3
  18.3 1.3 collective-permute-start.8
  19.6 2.5 %collective-permute-start.7 = (bf16[256,1024]{1,0:T(8,128)(2,1)S(1)}, bf16[256,1024]{1,0:T(8,128)(2,1)S(1)}, u32[]{:S(2)}, u32[]{:S(2)}) collective-permute-start(bf16[256,1024]{1,0:T(8,128)(2,1)S(1)} %get-tuple-element.110.refs_3_.refs_8_.refs_6_), channel_id=1, source_target_pairs={{0,4},{4,0},{8,12},{12,8},{1,5},{5,1},{9,13},{13,9},{2,6},{6,2},{1... | collective-permute-start | bytes 1572872 | tf_op jit(solution)/shard_map/ppermute | solution.py:35
  22.0 1.5 collective-permute-start.3
  23.5 2.7 %collective-permute-done.3.refs_1_ = bf16[16,2048]{1,0:T(8,128)(2,1)S(1)} collective-permute-done((bf16[16,2048]{1,0:T(8,128)(2,1)S(1)}, bf16[16,2048]{1,0:T(8,128)(2,1)S(1)}, u32[]{:S(2)}, u32[]{:S(2)}) %collective-permute-start.3) | collective-permute-done | bytes 65568 | tf_op jit(solution)/shard_map/ppermute | solution.py:35
  26.7 2.7 %collective-permute-start.9 = (bf16[32,2048]{1,0:T(8,128)(2,1)S(1)}, bf16[32,2048]{1,0:T(8,128)(2,1)S(1)}, u32[]{:S(2)}, u32[]{:S(2)}) collective-permute-start(bf16[32,2048]{1,0:T(8,128)(2,1)S(1)} %get-tuple-element.114.refs_1_), channel_id=1, source_target_pairs={{0,8},{4,12},{8,0},{12,4},{1,9},{5,13},{9,1},{13,5},{2,10},{6,14},... | collective-permute-start | bytes 393224 | tf_op jit(solution)/shard_map/ppermute | solution.py:35
  29.8 3.5 %collective-permute-done.8.refs_0_ = bf16[256,1024]{1,0:T(8,128)(2,1)S(1)} collective-permute-done((bf16[256,1024]{1,0:T(8,128)(2,1)S(1)}, bf16[256,1024]{1,0:T(8,128)(2,1)S(1)}, u32[]{:S(2)}, u32[]{:S(2)}) %collective-permute-start.8) | collective-permute-done | bytes 524320 | tf_op jit(solution)/shard_map/ppermute | solution.py:613
  33.4 1.3 collective-permute-start.13
  34.7 2.1 %collective-permute-start.10 = (bf16[256,1024]{1,0:T(8,128)(2,1)S(1)}, bf16[256,1024]{1,0:T(8,128)(2,1)S(1)}, u32[]{:S(2)}, u32[]{:S(2)}) collective-permute-start(bf16[256,1024]{1,0:T(8,128)(2,1)S(1)} %get-tuple-element.117.refs_3_.refs_4_), channel_id=1, source_target_pairs={{0,4},{4,0},{8,12},{12,8},{1,5},{5,1},{9,13},{13,9},{2,6},{6,2},{1... | collective-permute-start | bytes 1572872 | tf_op jit(solution)/shard_map/ppermute | solution.py:35
  37.4 8.1 %stencil.1 = (f32[2,8,64,128]{3,2,1,0:T(8,128)S(1)}, bf16[16,4096]{1,0:T(8,128)(2,1)S(1)}, bf16[16,4096]{1,0:T(8,128)(2,1)S(1)}, f32[8,128]{1,0:T(8,128)S(1)}) custom-call(f32[2,8,64,128]{3,2,1,0:T(8,128)S(1)} %get-tuple-element.99.refs_2_.refs_0_, f32[2,8,4,128]{3,2,1,0:T(4,128)S(1)} %collective-permute-done.refs_3_.refs_1_, ...), custom_call_target="tpu_custom_call" | custom-call | flops 1 | bytes 1 | tf_op jit(solution)/shard_map/stencil/pallas_call | solution.py:131
  45.5 4.1 %collective-permute-done.13.refs_0_ = bf16[256,1024]{1,0:T(8,128)(2,1)S(1)} collective-permute-done((bf16[256,1024]{1,0:T(8,128)(2,1)S(1)}, bf16[256,1024]{1,0:T(8,128)(2,1)S(1)}, u32[]{:S(2)}, u32[]{:S(2)}) %collective-permute-start.13) | collective-permute-done | bytes 524320 | tf_op jit(solution)/shard_map/ppermute | solution.py:614
  50.6 2.1 %collective-permute-start.14 = (bf16[64,512]{1,0:T(8,128)(2,1)S(1)}, bf16[64,512]{1,0:T(8,128)(2,1)S(1)}, u32[]{:S(2)}, u32[]{:S(2)}) collective-permute-start(bf16[64,512]{1,0:T(8,128)(2,1)S(1)} %get-tuple-element.123), channel_id=1, source_target_pairs={{0,2},{1,3},{2,0},{3,1},{4,6},{5,7},{6,4},{7,5},{8,10},{9,11},{10,... | collective-permute-start | bytes 196616 | tf_op jit(solution)/shard_map/ppermute | solution.py:35
  52.6 1.6 %collective-permute-start.21 = (bf16[256,1024]{1,0:T(8,128)(2,1)S(1)}, bf16[256,1024]{1,0:T(8,128)(2,1)S(1)}, u32[]{:S(2)}, u32[]{:S(2)}) collective-permute-start(bf16[256,1024]{1,0:T(8,128)(2,1)S(1)} %get-tuple-element.129.refs_3_.refs_6_), channel_id=1, source_target_pairs={{0,4},{4,0},{8,12},{12,8},{1,5},{5,1},{9,13},{13,9},{2,6},{6,2},{1... | collective-permute-start | bytes 1572872 | tf_op jit(solution)/shard_map/ppermute | solution.py:35
  54.2 1.1 collective-permute-done.14.refs_2_
  55.8 1.9 %collective-permute-start.22 = (f32[2,8,64,128]{3,2,1,0:T(8,128)S(1)}, f32[2,8,64,128]{3,2,1,0:T(8,128)S(1)}, u32[]{:S(2)}, u32[]{:S(2)}) collective-permute-start(f32[2,8,64,128]{3,2,1,0:T(8,128)S(1)} %get-tuple-element.135), channel_id=1, source_target_pairs={{0,16},{16,0},{1,17},{17,1},{2,18},{18,2},{3,19},{19,3},{4,20},{20... | collective-permute-start | bytes 1572872 | tf_op jit(solution)/shard_map/ppermute | solution.py:35
  57.8 2.8 %collective-permute-start.17 = (bf16[64,2176]{1,0:T(8,128)(2,1)S(1)}, bf16[64,2176]{1,0:T(8,128)(2,1)S(1)}, u32[]{:S(2)}, u32[]{:S(2)}) collective-permute-start(bf16[64,2176]{1,0:T(8,128)(2,1)S(1)} %get-tuple-element.128), channel_id=1, source_target_pairs={{0,8},{4,12},{8,0},{12,4},{1,9},{5,13},{9,1},{13,5},{2,10},{6,14},... | collective-permute-start | bytes 835592 | tf_op jit(solution)/shard_map/ppermute | solution.py:35
  60.8 11.6 %collective-permute-done.19.refs_1_ = bf16[16,4096]{1,0:T(8,128)(2,1)S(1)} collective-permute-done((bf16[16,4096]{1,0:T(8,128)(2,1)S(1)}, bf16[16,4096]{1,0:T(8,128)(2,1)S(1)}, u32[]{:S(2)}, u32[]{:S(2)}) %collective-permute-start.19) | collective-permute-done | bytes 131104 | tf_op jit(solution)/shard_map/ppermute | solution.py:35
  73.3 1.7 %collective-permute-start.28 = (bf16[128,1024]{1,0:T(8,128)(2,1)S(1)}, bf16[128,1024]{1,0:T(8,128)(2,1)S(1)}, u32[]{:S(2)}, u32[]{:S(2)}) collective-permute-start(bf16[128,1024]{1,0:T(8,128)(2,1)S(1)} %get-tuple-element.140.refs_4_), channel_id=1, source_target_pairs={{0,16},{16,0},{1,17},{17,1},{2,18},{18,2},{3,19},{19,3},{4,20},{20... | collective-permute-start | bytes 786440 | tf_op jit(solution)/shard_map/ppermute | solution.py:35
  75.0 2.4 %collective-permute-start.25 = (bf16[128,1024]{1,0:T(8,128)(2,1)S(1)}, bf16[128,1024]{1,0:T(8,128)(2,1)S(1)}, u32[]{:S(2)}, u32[]{:S(2)}) collective-permute-start(bf16[128,1024]{1,0:T(8,128)(2,1)S(1)} %get-tuple-element.140.refs_4_), channel_id=1, source_target_pairs={{0,4},{4,0},{8,12},{12,8},{1,5},{5,1},{9,13},{13,9},{2,6},{6,2},{1... | collective-permute-start | bytes 786440 | tf_op jit(solution)/shard_map/ppermute | solution.py:35
  79.2 1.2 collective-permute-start.27
  80.4 2.9 %collective-permute-done.26.refs_4_ = bf16[16,2048]{1,0:T(8,128)(2,1)S(1)} collective-permute-done((bf16[16,2048]{1,0:T(8,128)(2,1)S(1)}, bf16[16,2048]{1,0:T(8,128)(2,1)S(1)}, u32[]{:S(2)}, u32[]{:S(2)}) %collective-permute-start.26) | collective-permute-done | bytes 65568 | tf_op jit(solution)/shard_map/ppermute | solution.py:35
  84.8 1.6 %collective-permute-start.29 = (bf16[128,1280]{1,0:T(8,128)(2,1)S(1)}, bf16[128,1280]{1,0:T(8,128)(2,1)S(1)}, u32[]{:S(2)}, u32[]{:S(2)}) collective-permute-start(bf16[128,1280]{1,0:T(8,128)(2,1)S(1)} %get-tuple-element.146), channel_id=1, source_target_pairs={{0,4},{4,0},{8,12},{12,8},{1,5},{5,1},{9,13},{13,9},{2,6},{6,2},{1... | collective-permute-start | bytes 983048 | tf_op jit(solution)/shard_map/ppermute | solution.py:35
  86.7 1.8 %collective-permute-start.30 = (bf16[64,2048]{1,0:T(8,128)(2,1)S(1)}, bf16[64,2048]{1,0:T(8,128)(2,1)S(1)}, u32[]{:S(2)}, u32[]{:S(2)}) collective-permute-start(bf16[64,2048]{1,0:T(8,128)(2,1)S(1)} %get-tuple-element.148), channel_id=1, source_target_pairs={{0,8},{4,12},{8,0},{12,4},{1,9},{5,13},{9,1},{13,5},{2,10},{6,14},... | collective-permute-start | bytes 786440 | tf_op jit(solution)/shard_map/ppermute | solution.py:35
  88.6 1.5 collective-permute-start.31
  90.1 8.5 %collective-permute-done.30.refs_4_ = bf16[64,2048]{1,0:T(8,128)(2,1)S(1)} collective-permute-done((bf16[64,2048]{1,0:T(8,128)(2,1)S(1)}, bf16[64,2048]{1,0:T(8,128)(2,1)S(1)}, u32[]{:S(2)}, u32[]{:S(2)}) %collective-permute-start.30) | collective-permute-done | bytes 262176 | tf_op jit(solution)/shard_map/ppermute | solution.py:35
  98.5 2.2 %collective-permute-done.31.refs_12_.refs_7_ = bf16[128,1024]{1,0:T(8,128)(2,1)S(1)} collective-permute-done((bf16[128,1024]{1,0:T(8,128)(2,1)S(1)}, bf16[128,1024]{1,0:T(8,128)(2,1)S(1)}, u32[]{:S(2)}, u32[]{:S(2)}) %collective-permute-start.31) | collective-permute-done | bytes 262176 | tf_op jit(solution)/shard_map/ppermute | solution.py:35
  101.7 4.4 %collective-permute-done.34.refs_5_ = bf16[64,512]{1,0:T(8,128)(2,1)S(1)} collective-permute-done((bf16[64,512]{1,0:T(8,128)(2,1)S(1)}, bf16[64,512]{1,0:T(8,128)(2,1)S(1)}, u32[]{:S(2)}, u32[]{:S(2)}) %collective-permute-start.34) | collective-permute-done | bytes 65568 | tf_op jit(solution)/shard_map/ppermute | solution.py:35
  106.6 1.4 collective-permute-start.36
  109.6 1.7 %collective-permute-start.37 = (bf16[64,2048]{1,0:T(8,128)(2,1)S(1)}, bf16[64,2048]{1,0:T(8,128)(2,1)S(1)}, u32[]{:S(2)}, u32[]{:S(2)}) collective-permute-start(bf16[64,2048]{1,0:T(8,128)(2,1)S(1)} %get-tuple-element.166), channel_id=1, source_target_pairs={{0,8},{4,12},{8,0},{12,4},{1,9},{5,13},{9,1},{13,5},{2,10},{6,14},... | collective-permute-start | bytes 786440 | tf_op jit(solution)/shard_map/ppermute | solution.py:35
  111.3 13.1 %collective-permute-done.38.refs_10_.refs_3_.refs_15_ = bf16[128,1280]{1,0:T(8,128)(2,1)S(1)} collective-permute-done((bf16[128,1280]{1,0:T(8,128)(2,1)S(1)}, bf16[128,1280]{1,0:T(8,128)(2,1)S(1)}, u32[]{:S(2)}, u32[]{:S(2)}) %collective-permute-start.38) | collective-permute-done | bytes 327712 | tf_op jit(solution)/shard_map/ppermute | solution.py:35
  125.3 1.4 collective-permute-done.40.refs_1_
  128.2 1.4 collective-permute-start.39
  129.6 3.0 %collective-permute-done.39.refs_6_ = bf16[64,640]{1,0:T(8,128)(2,1)S(1)} collective-permute-done((bf16[64,640]{1,0:T(8,128)(2,1)S(1)}, bf16[64,640]{1,0:T(8,128)(2,1)S(1)}, u32[]{:S(2)}, u32[]{:S(2)}) %collective-permute-start.39) | collective-permute-done | bytes 81952 | tf_op jit(solution)/shard_map/ppermute | solution.py:35
  132.9 2.0 %collective-permute-start.41 = (bf16[128,1280]{1,0:T(8,128)(2,1)S(1)}, bf16[128,1280]{1,0:T(8,128)(2,1)S(1)}, u32[]{:S(2)}, u32[]{:S(2)}) collective-permute-start(bf16[128,1280]{1,0:T(8,128)(2,1)S(1)} %get-tuple-element.177), channel_id=1, source_target_pairs={{0,4},{4,0},{8,12},{12,8},{1,5},{5,1},{9,13},{13,9},{2,6},{6,2},{1... | collective-permute-start | bytes 983048 | tf_op jit(solution)/shard_map/ppermute | solution.py:35
  134.9 2.5 %collective-permute-done.47.refs_5_.refs_9_ = bf16[128,1280]{1,0:T(8,128)(2,1)S(1)} collective-permute-done((bf16[128,1280]{1,0:T(8,128)(2,1)S(1)}, bf16[128,1280]{1,0:T(8,128)(2,1)S(1)}, u32[]{:S(2)}, u32[]{:S(2)}) %collective-permute-start.47) | collective-permute-done | bytes 327712 | tf_op jit(solution)/shard_map/ppermute | solution.py:35
  137.4 1.3 collective-permute-start.48
  138.7 1.3 collective-permute-done.42.refs_1_
  140.1 1.5 %collective-permute-start.45 = (bf16[128,256]{1,0:T(8,128)(2,1)S(1)}, bf16[128,256]{1,0:T(8,128)(2,1)S(1)}, u32[]{:S(2)}, u32[]{:S(2)}) collective-permute-start(bf16[128,256]{1,0:T(8,128)(2,1)S(1)} %get-tuple-element.183.refs_0_), channel_id=1, source_target_pairs={{0,16},{16,0},{1,17},{17,1},{2,18},{18,2},{3,19},{19,3},{4,20},{20... | collective-permute-start | bytes 196616 | tf_op jit(solution)/shard_map/ppermute | solution.py:35
  141.6 3.4 %collective-permute-done.44.refs_1_ = bf16[128,256]{1,0:T(8,128)(2,1)S(1)} collective-permute-done((bf16[128,256]{1,0:T(8,128)(2,1)S(1)}, bf16[128,256]{1,0:T(8,128)(2,1)S(1)}, u32[]{:S(2)}, u32[]{:S(2)}) %collective-permute-start.44) | collective-permute-done | bytes 65568 | tf_op jit(solution)/shard_map/ppermute | solution.py:35
  145.0 1.3 collective-permute-start.46
  147.4 2.3 %update_mlp.1 = (f32[1,2,256,1024]{3,2,1,0:T(8,128)}, bf16[1,2,256,1024]{3,2,1,0:T(8,128)(2,1)}, f32[8,128]{1,0:T(8,128)S(1)}) custom-call(bf16[128,1280]{1,0:T(8,128)(2,1)S(1)} %get-tuple-element.152.refs_0_.refs_12_, bf16[128,1280]{1,0:T(8,128)(2,1)S(1)} %get-tuple-element.168.refs_1_.refs_13_, ...), custom_call_target="tpu_custom_call" | custom-call | flops 1 | bytes 1 | tf_op jit(solution)/shard_map/update_mlp/pallas_call | solution.py:131
  149.8 2.3 %update_embed.1 = (f32[1,256,1024]{2,1,0:T(8,128)}, bf16[1,256,1024]{2,1,0:T(8,128)(2,1)}, f32[8,128]{1,0:T(8,128)}) custom-call(bf16[128,256]{1,0:T(8,128)(2,1)S(1)} %get-tuple-element.183.refs_0_, bf16[128,256]{1,0:T(8,128)(2,1)S(1)} %collective-permute-done.44.refs_1_, bf16[128,256]{1,0:T(8,128)(2,1)S(1)} %collective-permute-done.45.refs_2_, ...), custom_call_target="tpu_custom_call" | custom-call | flops 1 | bytes 1 | tf_op jit(solution)/shard_map/update_embed/pallas_call | solution.py:131
  (82 shorter events, 16.1 us)
Async XLA Ops:
  0.6 16.4 %collective-permute-start.4 = (bf16[256,1024]{1,0:T(8,128)(2,1)}, bf16[256,1024]{1,0:T(8,128)(2,1)S(1)}, u32[]{:S(2)}, u32[]{:S(2)}) collective-permute-start(bf16[256,1024]{1,0:T(8,128)(2,1)} %bitcast.2), channel_id=1, source_target_pairs={{16,0},{17,1},{18,2},{19,3},{20,4},{21,5},{22,6},{23,7},{24,8},{25... | collective-permute-start | bytes 1572872 | tf_op jit(solution)/shard_map/ppermute | solution.py:597
  4.7 11.9 %collective-permute-start.2 = (bf16[16,4096]{1,0:T(8,128)(2,1)S(1)}, bf16[16,4096]{1,0:T(8,128)(2,1)S(1)}, u32[]{:S(2)}, u32[]{:S(2)}) collective-permute-start(bf16[16,4096]{1,0:T(8,128)(2,1)S(1)} %get-tuple-element.103), channel_id=1, source_target_pairs={{0,16},{1,17},{2,18},{3,19},{4,20},{5,21},{6,22},{7,23},{8,24},{9,... | collective-permute-start | bytes 393224 | tf_op jit(solution)/shard_map/ppermute | solution.py:605
  9.5 7.0 %collective-permute-start = (f32[2,8,4,128]{3,2,1,0:T(4,128)S(1)}, f32[2,8,4,128]{3,2,1,0:T(4,128)S(1)}, u32[]{:S(2)}, u32[]{:S(2)}) collective-permute-start(f32[2,8,4,128]{3,2,1,0:T(4,128)S(1)} %get-tuple-element.100), channel_id=1, source_target_pairs={{0,4},{4,8},{8,12},{12,0},{1,5},{5,9},{9,13},{13,1},{2,6},{6,10},{... | collective-permute-start | bytes 98312 | tf_op jit(solution)/shard_map/ppermute | solution.py:606
  12.3 4.3 %collective-permute-start.1 = (f32[2,8,4,128]{3,2,1,0:T(4,128)S(1)}, f32[2,8,4,128]{3,2,1,0:T(4,128)S(1)}, u32[]{:S(2)}, u32[]{:S(2)}) collective-permute-start(f32[2,8,4,128]{3,2,1,0:T(4,128)S(1)} %get-tuple-element.101), channel_id=1, source_target_pairs={{0,12},{4,0},{8,4},{12,8},{1,13},{5,1},{9,5},{13,9},{2,14},{6,2},{... | collective-permute-start | bytes 98312 | tf_op jit(solution)/shard_map/ppermute | solution.py:607
  18.3 15.0 %collective-permute-start.8 = (bf16[256,1024]{1,0:T(8,128)(2,1)S(1)}, bf16[256,1024]{1,0:T(8,128)(2,1)S(1)}, u32[]{:S(2)}, u32[]{:S(2)}) collective-permute-start(bf16[256,1024]{1,0:T(8,128)(2,1)S(1)} %get-tuple-element.111), channel_id=1, source_target_pairs={{16,0},{17,1},{18,2},{19,3},{20,4},{21,5},{22,6},{23,7},{24,8},{25... | collective-permute-start | bytes 1572872 | tf_op jit(solution)/shard_map/ppermute | solution.py:613
  19.6 17.2 %collective-permute-start.7 = (bf16[256,1024]{1,0:T(8,128)(2,1)S(1)}, bf16[256,1024]{1,0:T(8,128)(2,1)S(1)}, u32[]{:S(2)}, u32[]{:S(2)}) collective-permute-start(bf16[256,1024]{1,0:T(8,128)(2,1)S(1)} %get-tuple-element.110.refs_3_.refs_8_.refs_6_), channel_id=1, source_target_pairs={{0,4},{4,0},{8,12},{12,8},{1,5},{5,1},{9,13},{13,9},{2,6},{6,2},{1... | collective-permute-start | bytes 1572872 | tf_op jit(solution)/shard_map/ppermute | solution.py:35
  22.0 4.3 %collective-permute-start.3 = (bf16[16,2048]{1,0:T(8,128)(2,1)S(1)}, bf16[16,2048]{1,0:T(8,128)(2,1)S(1)}, u32[]{:S(2)}, u32[]{:S(2)}) collective-permute-start(bf16[16,2048]{1,0:T(8,128)(2,1)S(1)} %get-tuple-element.106), channel_id=1, source_target_pairs={{0,2},{1,3},{2,0},{3,1},{4,6},{5,7},{6,4},{7,5},{8,10},{9,11},{10,... | collective-permute-start | bytes 196616 | tf_op jit(solution)/shard_map/ppermute | solution.py:35
  26.7 10.1 %collective-permute-start.9 = (bf16[32,2048]{1,0:T(8,128)(2,1)S(1)}, bf16[32,2048]{1,0:T(8,128)(2,1)S(1)}, u32[]{:S(2)}, u32[]{:S(2)}) collective-permute-start(bf16[32,2048]{1,0:T(8,128)(2,1)S(1)} %get-tuple-element.114.refs_1_), channel_id=1, source_target_pairs={{0,8},{4,12},{8,0},{12,4},{1,9},{5,13},{9,1},{13,5},{2,10},{6,14},... | collective-permute-start | bytes 393224 | tf_op jit(solution)/shard_map/ppermute | solution.py:35
  29.3 4.1 %collective-permute-start.6 = (f32[72,128]{1,0:T(8,128)S(1)}, f32[72,128]{1,0:T(8,128)S(1)}, u32[]{:S(2)}, u32[]{:S(2)}) collective-permute-start(f32[72,128]{1,0:T(8,128)S(1)} %get-tuple-element.109), channel_id=1, source_target_pairs={{0,3},{1,0},{2,1},{3,2},{4,7},{5,4},{6,5},{7,6},{8,11},{9,8},{10,9... | collective-permute-start | bytes 110600 | tf_op jit(solution)/shard_map/ppermute | solution.py:621
  29.3 5.4 %collective-permute-start.5 = (f32[72,128]{1,0:T(8,128)S(1)}, f32[72,128]{1,0:T(8,128)S(1)}, u32[]{:S(2)}, u32[]{:S(2)}) collective-permute-start(f32[72,128]{1,0:T(8,128)S(1)} %get-tuple-element.109), channel_id=1, source_target_pairs={{0,1},{1,2},{2,3},{3,0},{4,5},{5,6},{6,7},{7,4},{8,9},{9,10},{10,1... | collective-permute-start | bytes 110600 | tf_op jit(solution)/shard_map/ppermute | solution.py:620
  33.3 16.4 %collective-permute-start.11 = (bf16[256,1024]{1,0:T(8,128)(2,1)S(1)}, bf16[256,1024]{1,0:T(8,128)(2,1)S(1)}, u32[]{:S(2)}, u32[]{:S(2)}) collective-permute-start(bf16[256,1024]{1,0:T(8,128)(2,1)S(1)} %get-tuple-element.110.refs_3_.refs_8_.refs_6_), channel_id=1, source_target_pairs={{0,1},{1,0},{2,3},{3,2},{4,5},{5,4},{6,7},{7,6},{8,9},{9,8},{10,11... | collective-permute-start | bytes 1572872 | tf_op jit(solution)/shard_map/ppermute | solution.py:35
  33.4 16.2 %collective-permute-start.13 = (bf16[256,1024]{1,0:T(8,128)(2,1)S(1)}, bf16[256,1024]{1,0:T(8,128)(2,1)S(1)}, u32[]{:S(2)}, u32[]{:S(2)}) collective-permute-start(bf16[256,1024]{1,0:T(8,128)(2,1)S(1)} %get-tuple-element.119), channel_id=1, source_target_pairs={{16,0},{17,1},{18,2},{19,3},{20,4},{21,5},{22,6},{23,7},{24,8},{25... | collective-permute-start | bytes 1572872 | tf_op jit(solution)/shard_map/ppermute | solution.py:614
  34.7 15.0 %collective-permute-start.10 = (bf16[256,1024]{1,0:T(8,128)(2,1)S(1)}, bf16[256,1024]{1,0:T(8,128)(2,1)S(1)}, u32[]{:S(2)}, u32[]{:S(2)}) collective-permute-start(bf16[256,1024]{1,0:T(8,128)(2,1)S(1)} %get-tuple-element.117.refs_3_.refs_4_), channel_id=1, source_target_pairs={{0,4},{4,0},{8,12},{12,8},{1,5},{5,1},{9,13},{13,9},{2,6},{6,2},{1... | collective-permute-start | bytes 1572872 | tf_op jit(solution)/shard_map/ppermute | solution.py:35
  36.8 12.8 %collective-permute-start.12 = (bf16[256,1024]{1,0:T(8,128)(2,1)S(1)}, bf16[256,1024]{1,0:T(8,128)(2,1)S(1)}, u32[]{:S(2)}, u32[]{:S(2)}) collective-permute-start(bf16[256,1024]{1,0:T(8,128)(2,1)S(1)} %get-tuple-element.118.refs_5_.refs_10_.refs_8_), channel_id=1, source_target_pairs={{0,1},{1,0},{2,3},{3,2},{4,5},{5,4},{6,7},{7,6},{8,9},{9,8},{10,11... | collective-permute-start | bytes 1572872 | tf_op jit(solution)/shard_map/ppermute | solution.py:35
  37.1 17.1 %collective-permute-start.15 = (bf16[256,1024]{1,0:T(8,128)(2,1)S(1)}, bf16[256,1024]{1,0:T(8,128)(2,1)S(1)}, u32[]{:S(2)}, u32[]{:S(2)}) collective-permute-start(bf16[256,1024]{1,0:T(8,128)(2,1)S(1)} %get-tuple-element.117.refs_3_.refs_4_), channel_id=1, source_target_pairs={{0,1},{1,0},{2,3},{3,2},{4,5},{5,4},{6,7},{7,6},{8,9},{9,8},{10,11... | collective-permute-start | bytes 1572872 | tf_op jit(solution)/shard_map/ppermute | solution.py:35
  50.5 4.8 %collective-permute-start.16 = (bf16[256,1024]{1,0:T(8,128)(2,1)S(1)}, bf16[256,1024]{1,0:T(8,128)(2,1)S(1)}, u32[]{:S(2)}, u32[]{:S(2)}) collective-permute-start(bf16[256,1024]{1,0:T(8,128)(2,1)S(1)} %get-tuple-element.124.refs_5_.refs_6_), channel_id=1, source_target_pairs={{0,1},{1,0},{2,3},{3,2},{4,5},{5,4},{6,7},{7,6},{8,9},{9,8},{10,11... | collective-permute-start | bytes 1572872 | tf_op jit(solution)/shard_map/ppermute | solution.py:35
  50.6 4.7 %collective-permute-start.14 = (bf16[64,512]{1,0:T(8,128)(2,1)S(1)}, bf16[64,512]{1,0:T(8,128)(2,1)S(1)}, u32[]{:S(2)}, u32[]{:S(2)}) collective-permute-start(bf16[64,512]{1,0:T(8,128)(2,1)S(1)} %get-tuple-element.123), channel_id=1, source_target_pairs={{0,2},{1,3},{2,0},{3,1},{4,6},{5,7},{6,4},{7,5},{8,10},{9,11},{10,... | collective-permute-start | bytes 196616 | tf_op jit(solution)/shard_map/ppermute | solution.py:35
  52.6 20.0 %collective-permute-start.21 = (bf16[256,1024]{1,0:T(8,128)(2,1)S(1)}, bf16[256,1024]{1,0:T(8,128)(2,1)S(1)}, u32[]{:S(2)}, u32[]{:S(2)}) collective-permute-start(bf16[256,1024]{1,0:T(8,128)(2,1)S(1)} %get-tuple-element.129.refs_3_.refs_6_), channel_id=1, source_target_pairs={{0,4},{4,0},{8,12},{12,8},{1,5},{5,1},{9,13},{13,9},{2,6},{6,2},{1... | collective-permute-start | bytes 1572872 | tf_op jit(solution)/shard_map/ppermute | solution.py:35
  55.8 16.7 %collective-permute-start.22 = (f32[2,8,64,128]{3,2,1,0:T(8,128)S(1)}, f32[2,8,64,128]{3,2,1,0:T(8,128)S(1)}, u32[]{:S(2)}, u32[]{:S(2)}) collective-permute-start(f32[2,8,64,128]{3,2,1,0:T(8,128)S(1)} %get-tuple-element.135), channel_id=1, source_target_pairs={{0,16},{16,0},{1,17},{17,1},{2,18},{18,2},{3,19},{19,3},{4,20},{20... | collective-permute-start | bytes 1572872 | tf_op jit(solution)/shard_map/ppermute | solution.py:35
  57.8 14.8 %collective-permute-start.17 = (bf16[64,2176]{1,0:T(8,128)(2,1)S(1)}, bf16[64,2176]{1,0:T(8,128)(2,1)S(1)}, u32[]{:S(2)}, u32[]{:S(2)}) collective-permute-start(bf16[64,2176]{1,0:T(8,128)(2,1)S(1)} %get-tuple-element.128), channel_id=1, source_target_pairs={{0,8},{4,12},{8,0},{12,4},{1,9},{5,13},{9,1},{13,5},{2,10},{6,14},... | collective-permute-start | bytes 835592 | tf_op jit(solution)/shard_map/ppermute | solution.py:35
  60.5 11.8 %collective-permute-start.19 = (bf16[16,4096]{1,0:T(8,128)(2,1)S(1)}, bf16[16,4096]{1,0:T(8,128)(2,1)S(1)}, u32[]{:S(2)}, u32[]{:S(2)}) collective-permute-start(bf16[16,4096]{1,0:T(8,128)(2,1)S(1)} %get-tuple-element.131), channel_id=1, source_target_pairs={{0,16},{16,0},{1,17},{17,1},{2,18},{18,2},{3,19},{19,3},{4,20},{20... | collective-permute-start | bytes 393224 | tf_op jit(solution)/shard_map/ppermute | solution.py:35
  60.8 11.8 %collective-permute-start.20 = (bf16[64,1024]{1,0:T(8,128)(2,1)S(1)}, bf16[64,1024]{1,0:T(8,128)(2,1)S(1)}, u32[]{:S(2)}, u32[]{:S(2)}) collective-permute-start(bf16[64,1024]{1,0:T(8,128)(2,1)S(1)} %get-tuple-element.133.refs_2_), channel_id=1, source_target_pairs={{0,1},{1,0},{2,3},{3,2},{4,5},{5,4},{6,7},{7,6},{8,9},{9,8},{10,11... | collective-permute-start | bytes 393224 | tf_op jit(solution)/shard_map/ppermute | solution.py:35
  72.3 5.0 %collective-permute-start.18 = (bf16[256,1024]{1,0:T(8,128)(2,1)S(1)}, bf16[256,1024]{1,0:T(8,128)(2,1)S(1)}, u32[]{:S(2)}, u32[]{:S(2)}) collective-permute-start(bf16[256,1024]{1,0:T(8,128)(2,1)S(1)} %get-tuple-element.129.refs_3_.refs_6_), channel_id=1, source_target_pairs={{0,1},{1,0},{2,3},{3,2},{4,5},{5,4},{6,7},{7,6},{8,9},{9,8},{10,11... | collective-permute-start | bytes 1572872 | tf_op jit(solution)/shard_map/ppermute | solution.py:35
  72.9 4.5 %collective-permute-start.23 = (bf16[256,1024]{1,0:T(8,128)(2,1)S(1)}, bf16[256,1024]{1,0:T(8,128)(2,1)S(1)}, u32[]{:S(2)}, u32[]{:S(2)}) collective-permute-start(bf16[256,1024]{1,0:T(8,128)(2,1)S(1)} %get-tuple-element.136.refs_5_.refs_8_), channel_id=1, source_target_pairs={{0,1},{1,0},{2,3},{3,2},{4,5},{5,4},{6,7},{7,6},{8,9},{9,8},{10,11... | collective-permute-start | bytes 1572872 | tf_op jit(solution)/shard_map/ppermute | solution.py:35
  73.3 10.0 %collective-permute-start.28 = (bf16[128,1024]{1,0:T(8,128)(2,1)S(1)}, bf16[128,1024]{1,0:T(8,128)(2,1)S(1)}, u32[]{:S(2)}, u32[]{:S(2)}) collective-permute-start(bf16[128,1024]{1,0:T(8,128)(2,1)S(1)} %get-tuple-element.140.refs_4_), channel_id=1, source_target_pairs={{0,16},{16,0},{1,17},{17,1},{2,18},{18,2},{3,19},{19,3},{4,20},{20... | collective-permute-start | bytes 786440 | tf_op jit(solution)/shard_map/ppermute | solution.py:35
  75.0 9.0 %collective-permute-start.25 = (bf16[128,1024]{1,0:T(8,128)(2,1)S(1)}, bf16[128,1024]{1,0:T(8,128)(2,1)S(1)}, u32[]{:S(2)}, u32[]{:S(2)}) collective-permute-start(bf16[128,1024]{1,0:T(8,128)(2,1)S(1)} %get-tuple-element.140.refs_4_), channel_id=1, source_target_pairs={{0,4},{4,0},{8,12},{12,8},{1,5},{5,1},{9,13},{13,9},{2,6},{6,2},{1... | collective-permute-start | bytes 786440 | tf_op jit(solution)/shard_map/ppermute | solution.py:35
  78.2 6.0 %collective-permute-start.24 = (bf16[64,1536]{1,0:T(8,128)(2,1)S(1)}, bf16[64,1536]{1,0:T(8,128)(2,1)S(1)}, u32[]{:S(2)}, u32[]{:S(2)}) collective-permute-start(bf16[64,1536]{1,0:T(8,128)(2,1)S(1)} %get-tuple-element.139), channel_id=1, source_target_pairs={{0,1},{1,0},{2,3},{3,2},{4,5},{5,4},{6,7},{7,6},{8,9},{9,8},{10,11... | collective-permute-start | bytes 589832 | tf_op jit(solution)/shard_map/ppermute | solution.py:35
  78.3 5.0 %collective-permute-start.26 = (bf16[16,2048]{1,0:T(8,128)(2,1)S(1)}, bf16[16,2048]{1,0:T(8,128)(2,1)S(1)}, u32[]{:S(2)}, u32[]{:S(2)}) collective-permute-start(bf16[16,2048]{1,0:T(8,128)(2,1)S(1)} %get-tuple-element.142), channel_id=1, source_target_pairs={{0,2},{1,3},{2,0},{3,1},{4,6},{5,7},{6,4},{7,5},{8,10},{9,11},{10,... | collective-permute-start | bytes 196616 | tf_op jit(solution)/shard_map/ppermute | solution.py:35
  79.2 5.0 %collective-permute-start.27 = (bf16[64,512]{1,0:T(8,128)(2,1)S(1)}, bf16[64,512]{1,0:T(8,128)(2,1)S(1)}, u32[]{:S(2)}, u32[]{:S(2)}) collective-permute-start(bf16[64,512]{1,0:T(8,128)(2,1)S(1)} %get-tuple-element.144), channel_id=1, source_target_pairs={{0,2},{1,3},{2,0},{3,1},{4,6},{5,7},{6,4},{7,5},{8,10},{9,11},{10,... | collective-permute-start | bytes 196616 | tf_op jit(solution)/shard_map/ppermute | solution.py:35
  84.8 15.9 %collective-permute-start.29 = (bf16[128,1280]{1,0:T(8,128)(2,1)S(1)}, bf16[128,1280]{1,0:T(8,128)(2,1)S(1)}, u32[]{:S(2)}, u32[]{:S(2)}) collective-permute-start(bf16[128,1280]{1,0:T(8,128)(2,1)S(1)} %get-tuple-element.146), channel_id=1, source_target_pairs={{0,4},{4,0},{8,12},{12,8},{1,5},{5,1},{9,13},{13,9},{2,6},{6,2},{1... | collective-permute-start | bytes 983048 | tf_op jit(solution)/shard_map/ppermute | solution.py:35
  86.4 14.3 %collective-permute-start.32 = (bf16[128,1280]{1,0:T(8,128)(2,1)S(1)}, bf16[128,1280]{1,0:T(8,128)(2,1)S(1)}, u32[]{:S(2)}, u32[]{:S(2)}) collective-permute-start(bf16[128,1280]{1,0:T(8,128)(2,1)S(1)} %get-tuple-element.152.refs_0_.refs_12_), channel_id=1, source_target_pairs={{0,16},{16,0},{1,17},{17,1},{2,18},{18,2},{3,19},{19,3},{4,20},{20... | collective-permute-start | bytes 983048 | tf_op jit(solution)/shard_map/ppermute | solution.py:35
  86.7 11.8 %collective-permute-start.30 = (bf16[64,2048]{1,0:T(8,128)(2,1)S(1)}, bf16[64,2048]{1,0:T(8,128)(2,1)S(1)}, u32[]{:S(2)}, u32[]{:S(2)}) collective-permute-start(bf16[64,2048]{1,0:T(8,128)(2,1)S(1)} %get-tuple-element.148), channel_id=1, source_target_pairs={{0,8},{4,12},{8,0},{12,4},{1,9},{5,13},{9,1},{13,5},{2,10},{6,14},... | collective-permute-start | bytes 786440 | tf_op jit(solution)/shard_map/ppermute | solution.py:35
  88.6 12.2 %collective-permute-start.31 = (bf16[128,1024]{1,0:T(8,128)(2,1)S(1)}, bf16[128,1024]{1,0:T(8,128)(2,1)S(1)}, u32[]{:S(2)}, u32[]{:S(2)}) collective-permute-start(bf16[128,1024]{1,0:T(8,128)(2,1)S(1)} %get-tuple-element.151.refs_5_), channel_id=1, source_target_pairs={{0,16},{16,0},{1,17},{17,1},{2,18},{18,2},{3,19},{19,3},{4,20},{20... | collective-permute-start | bytes 786440 | tf_op jit(solution)/shard_map/ppermute | solution.py:35
  101.5 4.6 %collective-permute-start.33 = (bf16[64,1536]{1,0:T(8,128)(2,1)S(1)}, bf16[64,1536]{1,0:T(8,128)(2,1)S(1)}, u32[]{:S(2)}, u32[]{:S(2)}) collective-permute-start(bf16[64,1536]{1,0:T(8,128)(2,1)S(1)} %get-tuple-element.154), channel_id=1, source_target_pairs={{0,1},{1,0},{2,3},{3,2},{4,5},{5,4},{6,7},{7,6},{8,9},{9,8},{10,11... | collective-permute-start | bytes 589832 | tf_op jit(solution)/shard_map/ppermute | solution.py:35
  101.6 4.5 %collective-permute-start.34 = (bf16[64,512]{1,0:T(8,128)(2,1)S(1)}, bf16[64,512]{1,0:T(8,128)(2,1)S(1)}, u32[]{:S(2)}, u32[]{:S(2)}) collective-permute-start(bf16[64,512]{1,0:T(8,128)(2,1)S(1)} %get-tuple-element.156), channel_id=1, source_target_pairs={{0,2},{1,3},{2,0},{3,1},{4,6},{5,7},{6,4},{7,5},{8,10},{9,11},{10,... | collective-permute-start | bytes 196616 | tf_op jit(solution)/shard_map/ppermute | solution.py:35
  106.6 17.8 %collective-permute-start.36 = (bf16[128,1536]{1,0:T(8,128)(2,1)S(1)}, bf16[128,1536]{1,0:T(8,128)(2,1)S(1)}, u32[]{:S(2)}, u32[]{:S(2)}) collective-permute-start(bf16[128,1536]{1,0:T(8,128)(2,1)S(1)} %get-tuple-element.160), channel_id=1, source_target_pairs={{0,16},{16,0},{1,17},{17,1},{2,18},{18,2},{3,19},{19,3},{4,20},{20... | collective-permute-start | bytes 1179656 | tf_op jit(solution)/shard_map/ppermute | solution.py:35
  108.0 16.4 %collective-permute-start.38 = (bf16[128,1280]{1,0:T(8,128)(2,1)S(1)}, bf16[128,1280]{1,0:T(8,128)(2,1)S(1)}, u32[]{:S(2)}, u32[]{:S(2)}) collective-permute-start(bf16[128,1280]{1,0:T(8,128)(2,1)S(1)} %get-tuple-element.168.refs_1_.refs_13_), channel_id=1, source_target_pairs={{0,16},{16,0},{1,17},{17,1},{2,18},{18,2},{3,19},{19,3},{4,20},{20... | collective-permute-start | bytes 983048 | tf_op jit(solution)/shard_map/ppermute | solution.py:35
  108.7 15.7 %collective-permute-start.35 = (bf16[128,1280]{1,0:T(8,128)(2,1)S(1)}, bf16[128,1280]{1,0:T(8,128)(2,1)S(1)}, u32[]{:S(2)}, u32[]{:S(2)}) collective-permute-start(bf16[128,1280]{1,0:T(8,128)(2,1)S(1)} %get-tuple-element.159), channel_id=1, source_target_pairs={{0,4},{4,0},{8,12},{12,8},{1,5},{5,1},{9,13},{13,9},{2,6},{6,2},{1... | collective-permute-start | bytes 983048 | tf_op jit(solution)/shard_map/ppermute | solution.py:35
  109.6 14.9 %collective-permute-start.37 = (bf16[64,2048]{1,0:T(8,128)(2,1)S(1)}, bf16[64,2048]{1,0:T(8,128)(2,1)S(1)}, u32[]{:S(2)}, u32[]{:S(2)}) collective-permute-start(bf16[64,2048]{1,0:T(8,128)(2,1)S(1)} %get-tuple-element.166), channel_id=1, source_target_pairs={{0,8},{4,12},{8,0},{12,4},{1,9},{5,13},{9,1},{13,5},{2,10},{6,14},... | collective-permute-start | bytes 786440 | tf_op jit(solution)/shard_map/ppermute | solution.py:35
  125.2 1.5 collective-permute-start.40
  126.8 10.6 %collective-permute-start.47 = (bf16[128,1280]{1,0:T(8,128)(2,1)S(1)}, bf16[128,1280]{1,0:T(8,128)(2,1)S(1)}, u32[]{:S(2)}, u32[]{:S(2)}) collective-permute-start(bf16[128,1280]{1,0:T(8,128)(2,1)S(1)} %get-tuple-element.186), channel_id=1, source_target_pairs={{0,4},{4,0},{8,12},{12,8},{1,5},{5,1},{9,13},{13,9},{2,6},{6,2},{1... | collective-permute-start | bytes 983048 | tf_op jit(solution)/shard_map/ppermute | solution.py:35
  127.7 12.3 %collective-permute-start.43 = (bf16[128,1280]{1,0:T(8,128)(2,1)S(1)}, bf16[128,1280]{1,0:T(8,128)(2,1)S(1)}, u32[]{:S(2)}, u32[]{:S(2)}) collective-permute-start(bf16[128,1280]{1,0:T(8,128)(2,1)S(1)} %get-tuple-element.180.refs_4_.refs_8_), channel_id=1, source_target_pairs={{0,16},{16,0},{1,17},{17,1},{2,18},{18,2},{3,19},{19,3},{4,20},{20... | collective-permute-start | bytes 983048 | tf_op jit(solution)/shard_map/ppermute | solution.py:35
  128.2 4.4 %collective-permute-start.39 = (bf16[64,640]{1,0:T(8,128)(2,1)S(1)}, bf16[64,640]{1,0:T(8,128)(2,1)S(1)}, u32[]{:S(2)}, u32[]{:S(2)}) collective-permute-start(bf16[64,640]{1,0:T(8,128)(2,1)S(1)} %get-tuple-element.171), channel_id=1, source_target_pairs={{0,2},{1,3},{2,0},{3,1},{4,6},{5,7},{6,4},{7,5},{8,10},{9,11},{10,... | collective-permute-start | bytes 245768 | tf_op jit(solution)/shard_map/ppermute | solution.py:35
  132.9 13.5 %collective-permute-start.41 = (bf16[128,1280]{1,0:T(8,128)(2,1)S(1)}, bf16[128,1280]{1,0:T(8,128)(2,1)S(1)}, u32[]{:S(2)}, u32[]{:S(2)}) collective-permute-start(bf16[128,1280]{1,0:T(8,128)(2,1)S(1)} %get-tuple-element.177), channel_id=1, source_target_pairs={{0,4},{4,0},{8,12},{12,8},{1,5},{5,1},{9,13},{13,9},{2,6},{6,2},{1... | collective-permute-start | bytes 983048 | tf_op jit(solution)/shard_map/ppermute | solution.py:35
  137.4 10.0 %collective-permute-start.48 = (bf16[128,1280]{1,0:T(8,128)(2,1)S(1)}, bf16[128,1280]{1,0:T(8,128)(2,1)S(1)}, u32[]{:S(2)}, u32[]{:S(2)}) collective-permute-start(bf16[128,1280]{1,0:T(8,128)(2,1)S(1)} %collective-permute-done.47.refs_5_.refs_9_), channel_id=1, source_target_pairs={{0,16},{16,0},{1,17},{17,1},{2,18},{18,2},{3,19},{19,3},{4,20},{20... | collective-permute-start | bytes 983048 | tf_op jit(solution)/shard_map/ppermute | solution.py:35
  140.0 5.1 %collective-permute-start.44 = (bf16[128,256]{1,0:T(8,128)(2,1)S(1)}, bf16[128,256]{1,0:T(8,128)(2,1)S(1)}, u32[]{:S(2)}, u32[]{:S(2)}) collective-permute-start(bf16[128,256]{1,0:T(8,128)(2,1)S(1)} %get-tuple-element.184), channel_id=1, source_target_pairs={{0,4},{4,0},{8,12},{12,8},{1,5},{5,1},{9,13},{13,9},{2,6},{6,2},{1... | collective-permute-start | bytes 196616 | tf_op jit(solution)/shard_map/ppermute | solution.py:35
  140.1 9.7 %collective-permute-start.45 = (bf16[128,256]{1,0:T(8,128)(2,1)S(1)}, bf16[128,256]{1,0:T(8,128)(2,1)S(1)}, u32[]{:S(2)}, u32[]{:S(2)}) collective-permute-start(bf16[128,256]{1,0:T(8,128)(2,1)S(1)} %get-tuple-element.183.refs_0_), channel_id=1, source_target_pairs={{0,16},{16,0},{1,17},{17,1},{2,18},{18,2},{3,19},{19,3},{4,20},{20... | collective-permute-start | bytes 196616 | tf_op jit(solution)/shard_map/ppermute | solution.py:35
  145.0 4.7 %collective-permute-start.46 = (bf16[128,256]{1,0:T(8,128)(2,1)S(1)}, bf16[128,256]{1,0:T(8,128)(2,1)S(1)}, u32[]{:S(2)}, u32[]{:S(2)}) collective-permute-start(bf16[128,256]{1,0:T(8,128)(2,1)S(1)} %collective-permute-done.44.refs_1_), channel_id=1, source_target_pairs={{0,16},{16,0},{1,17},{17,1},{2,18},{18,2},{3,19},{19,3},{4,20},{20... | collective-permute-start | bytes 196616 | tf_op jit(solution)/shard_map/ppermute | solution.py:35
  (6 other events, 36.1 us)

commit v6 on v5

--- a/solution.py
+++ b/solution.py
@@ -762,7 +762,7 @@
     inputs_on.forward()
     active_on.send()
     active_on.relay()
-    order.wait_for(inputs_on.arrived + active_on.arrived)
+    order.wait_for(active_on.arrived)
 
     def residual_rows(ins, outs, _):
         inputs, ins = ins[: core.size], ins[core.size :]
@@ -790,6 +790,7 @@
     active_on.forward()
     residual_on = Gather(residual_packs[0], residual_packs[1:], True, 1)
     residual_on.join_for_role()
+    order.wait_for(inputs_on.arrived)
 
     def hidden_rows(ins, outs, _):
         others, matrix = ins[1 : part.size], ins[part.size :]

time: 153 us -> 152 us (level)
  waiting for transfers between devices: 69.5 us -> 67.6 us
  starting transfers between devices: 58 us -> 59.6 us
    ppermute x1, starting transfers between devices: 0.01 us -> 1.74 us  [shards(): from_right = lax.ppermute(edges, 'mp', around('mp', -1))]
    ppermute x1, waiting for transfers between devices: 4.09 us -> 2.51 us  [shards(): arrived_down = lax.ppermute(down_block, 'role', to_solver)]
  transfers between devices with their start and end apart: 49 -> 49, of which waited for: 20 -> 22; matrix products, arithmetic and copies ran while one was open for 0% -> 0% of each run, Pallas kernels for 11% -> 11%
where the time goes in v6:
time: 152 us
  waiting for transfers between devices  67.6 us (44%)
  starting transfers between devices  59.6 us (39%)
  Pallas kernels  22.5 us (15%)
    ppermute x41, waiting for transfers between devices, shifted(): return lax.ppermute(value, self.axis, pairs)  60.3 us
    ppermute x41, starting transfers between devices, shifted(): return lax.ppermute(value, self.axis, pairs)  44.2 us
    pallas_call x22, Pallas kernels, call(): pl.pallas_call(kernel, name=name, out_shape=outs + [struct(TOKEN, F32)],...  22.5 us
    ppermute x1, starting transfers between devices, shards(): arrived_start = lax.ppermute(start_halves[1], 'role', to_trainer)  4.88 us
  transfers between devices with their start and end apart: 49, of which 22 were waited for; matrix products, arithmetic and copies ran while one was open for 0% of the time, Pallas kernels for 11%

profile of v6, /device:TPU:0, one launch (start us, length us, event | category | flops | bytes accessed | tf_op | source)
XLA Modules:
  0.0 151.9 jit_solution(12180305165213015659)
XLA Ops:
  0.6 1.3 collective-permute-start.4
  3.0 1.7 %patches.1 = (bf16[16,4096]{1,0:T(8,128)(2,1)S(1)}, bf16[16,4096]{1,0:T(8,128)(2,1)S(1)}, f32[2,8,4,128]{3,2,1,0:T(4,128)S(1)}, f32[2,8,4,128]{3,2,1,0:T(4,128)S...) custom-call(f32[2,8,64,128]{3,2,1,0:T(8,128)S(1)} %bitcast.3), custom_call_target="tpu_custom_call" | custom-call | flops 1 | bytes 1 | tf_op jit(solution)/shard_map/patches/pallas_call | solution.py:131
  4.7 4.9 %collective-permute-start.2 = (bf16[16,4096]{1,0:T(8,128)(2,1)S(1)}, bf16[16,4096]{1,0:T(8,128)(2,1)S(1)}, u32[]{:S(2)}, u32[]{:S(2)}) collective-permute-start(bf16[16,4096]{1,0:T(8,128)(2,1)S(1)} %get-tuple-element.103), channel_id=1, source_target_pairs={{0,16},{1,17},{2,18},{3,19},{4,20},{5,21},{6,22},{7,23},{8,24},{9,... | collective-permute-start | bytes 393224 | tf_op jit(solution)/shard_map/ppermute | solution.py:605
  9.5 2.8 %collective-permute-start = (f32[2,8,4,128]{3,2,1,0:T(4,128)S(1)}, f32[2,8,4,128]{3,2,1,0:T(4,128)S(1)}, u32[]{:S(2)}, u32[]{:S(2)}) collective-permute-start(f32[2,8,4,128]{3,2,1,0:T(4,128)S(1)} %get-tuple-element.100), channel_id=1, source_target_pairs={{0,4},{4,8},{8,12},{12,0},{1,5},{5,9},{9,13},{13,1},{2,6},{6,10},{... | collective-permute-start | bytes 98312 | tf_op jit(solution)/shard_map/ppermute | solution.py:606
  12.3 2.1 %collective-permute-start.1 = (f32[2,8,4,128]{3,2,1,0:T(4,128)S(1)}, f32[2,8,4,128]{3,2,1,0:T(4,128)S(1)}, u32[]{:S(2)}, u32[]{:S(2)}) collective-permute-start(f32[2,8,4,128]{3,2,1,0:T(4,128)S(1)} %get-tuple-element.101), channel_id=1, source_target_pairs={{0,12},{4,0},{8,4},{12,8},{1,13},{5,1},{9,5},{13,9},{2,14},{6,2},{... | collective-permute-start | bytes 98312 | tf_op jit(solution)/shard_map/ppermute | solution.py:607
  14.4 2.1 %collective-permute-done.refs_3_.refs_1_ = f32[2,8,4,128]{3,2,1,0:T(4,128)S(1)} collective-permute-done((f32[2,8,4,128]{3,2,1,0:T(4,128)S(1)}, f32[2,8,4,128]{3,2,1,0:T(4,128)S(1)}, u32[]{:S(2)}, u32[]{:S(2)}) %collective-permute-start) | collective-permute-done | bytes 32800 | tf_op jit(solution)/shard_map/ppermute | solution.py:606
  17.0 1.2 held.3
  18.3 1.3 collective-permute-start.8
  19.6 2.5 %collective-permute-start.7 = (bf16[256,1024]{1,0:T(8,128)(2,1)S(1)}, bf16[256,1024]{1,0:T(8,128)(2,1)S(1)}, u32[]{:S(2)}, u32[]{:S(2)}) collective-permute-start(bf16[256,1024]{1,0:T(8,128)(2,1)S(1)} %get-tuple-element.110.refs_3_.refs_8_.refs_6_), channel_id=1, source_target_pairs={{0,4},{4,0},{8,12},{12,8},{1,5},{5,1},{9,13},{13,9},{2,6},{6,2},{1... | collective-permute-start | bytes 1572872 | tf_op jit(solution)/shard_map/ppermute | solution.py:35
  22.0 1.5 %collective-permute-start.3 = (bf16[16,2048]{1,0:T(8,128)(2,1)S(1)}, bf16[16,2048]{1,0:T(8,128)(2,1)S(1)}, u32[]{:S(2)}, u32[]{:S(2)}) collective-permute-start(bf16[16,2048]{1,0:T(8,128)(2,1)S(1)} %get-tuple-element.106), channel_id=1, source_target_pairs={{0,2},{1,3},{2,0},{3,1},{4,6},{5,7},{6,4},{7,5},{8,10},{9,11},{10,... | collective-permute-start | bytes 196616 | tf_op jit(solution)/shard_map/ppermute | solution.py:35
  23.5 2.7 %collective-permute-done.3.refs_1_ = bf16[16,2048]{1,0:T(8,128)(2,1)S(1)} collective-permute-done((bf16[16,2048]{1,0:T(8,128)(2,1)S(1)}, bf16[16,2048]{1,0:T(8,128)(2,1)S(1)}, u32[]{:S(2)}, u32[]{:S(2)}) %collective-permute-start.3) | collective-permute-done | bytes 65568 | tf_op jit(solution)/shard_map/ppermute | solution.py:35
  26.7 2.7 %collective-permute-start.9 = (bf16[32,2048]{1,0:T(8,128)(2,1)S(1)}, bf16[32,2048]{1,0:T(8,128)(2,1)S(1)}, u32[]{:S(2)}, u32[]{:S(2)}) collective-permute-start(bf16[32,2048]{1,0:T(8,128)(2,1)S(1)} %get-tuple-element.114.refs_1_), channel_id=1, source_target_pairs={{0,8},{4,12},{8,0},{12,4},{1,9},{5,13},{9,1},{13,5},{2,10},{6,14},... | collective-permute-start | bytes 393224 | tf_op jit(solution)/shard_map/ppermute | solution.py:35
  29.3 1.7 %collective-permute-start.6 = (f32[72,128]{1,0:T(8,128)S(1)}, f32[72,128]{1,0:T(8,128)S(1)}, u32[]{:S(2)}, u32[]{:S(2)}) collective-permute-start(f32[72,128]{1,0:T(8,128)S(1)} %get-tuple-element.109), channel_id=1, source_target_pairs={{0,3},{1,0},{2,1},{3,2},{4,7},{5,4},{6,5},{7,6},{8,11},{9,8},{10,9... | collective-permute-start | bytes 110600 | tf_op jit(solution)/shard_map/ppermute | solution.py:621
  31.1 2.2 %collective-permute-done.8.refs_0_ = bf16[256,1024]{1,0:T(8,128)(2,1)S(1)} collective-permute-done((bf16[256,1024]{1,0:T(8,128)(2,1)S(1)}, bf16[256,1024]{1,0:T(8,128)(2,1)S(1)}, u32[]{:S(2)}, u32[]{:S(2)}) %collective-permute-start.8) | collective-permute-done | bytes 524320 | tf_op jit(solution)/shard_map/ppermute | solution.py:613
  33.4 1.3 collective-permute-start.13
  36.0 2.8 %collective-permute-start.10 = (bf16[256,1024]{1,0:T(8,128)(2,1)S(1)}, bf16[256,1024]{1,0:T(8,128)(2,1)S(1)}, u32[]{:S(2)}, u32[]{:S(2)}) collective-permute-start(bf16[256,1024]{1,0:T(8,128)(2,1)S(1)} %get-tuple-element.117.refs_3_.refs_4_), channel_id=1, source_target_pairs={{0,4},{4,0},{8,12},{12,8},{1,5},{5,1},{9,13},{13,9},{2,6},{6,2},{1... | collective-permute-start | bytes 1572872 | tf_op jit(solution)/shard_map/ppermute | solution.py:35
  39.0 8.1 %stencil.1 = (f32[2,8,64,128]{3,2,1,0:T(8,128)S(1)}, bf16[16,4096]{1,0:T(8,128)(2,1)S(1)}, bf16[16,4096]{1,0:T(8,128)(2,1)S(1)}, f32[8,128]{1,0:T(8,128)S(1)}) custom-call(f32[2,8,64,128]{3,2,1,0:T(8,128)S(1)} %get-tuple-element.99.refs_2_.refs_0_, f32[2,8,4,128]{3,2,1,0:T(4,128)S(1)} %collective-permute-done.refs_3_.refs_1_, ...), custom_call_target="tpu_custom_call" | custom-call | flops 1 | bytes 1 | tf_op jit(solution)/shard_map/stencil/pallas_call | solution.py:131
  47.1 2.5 %collective-permute-done.13.refs_0_ = bf16[256,1024]{1,0:T(8,128)(2,1)S(1)} collective-permute-done((bf16[256,1024]{1,0:T(8,128)(2,1)S(1)}, bf16[256,1024]{1,0:T(8,128)(2,1)S(1)}, u32[]{:S(2)}, u32[]{:S(2)}) %collective-permute-start.13) | collective-permute-done | bytes 524320 | tf_op jit(solution)/shard_map/ppermute | solution.py:614
  49.7 1.7 %collective-permute-done.10.refs_0_ = bf16[256,1024]{1,0:T(8,128)(2,1)S(1)} collective-permute-done((bf16[256,1024]{1,0:T(8,128)(2,1)S(1)}, bf16[256,1024]{1,0:T(8,128)(2,1)S(1)}, u32[]{:S(2)}, u32[]{:S(2)}) %collective-permute-start.10) | collective-permute-done | bytes 524320 | tf_op jit(solution)/shard_map/ppermute | solution.py:35
  52.2 1.6 %collective-permute-start.14 = (bf16[64,512]{1,0:T(8,128)(2,1)S(1)}, bf16[64,512]{1,0:T(8,128)(2,1)S(1)}, u32[]{:S(2)}, u32[]{:S(2)}) collective-permute-start(bf16[64,512]{1,0:T(8,128)(2,1)S(1)} %get-tuple-element.123), channel_id=1, source_target_pairs={{0,2},{1,3},{2,0},{3,1},{4,6},{5,7},{6,4},{7,5},{8,10},{9,11},{10,... | collective-permute-start | bytes 196616 | tf_op jit(solution)/shard_map/ppermute | solution.py:35
  53.8 1.8 %collective-permute-start.21 = (bf16[256,1024]{1,0:T(8,128)(2,1)S(1)}, bf16[256,1024]{1,0:T(8,128)(2,1)S(1)}, u32[]{:S(2)}, u32[]{:S(2)}) collective-permute-start(bf16[256,1024]{1,0:T(8,128)(2,1)S(1)} %get-tuple-element.129.refs_3_.refs_6_), channel_id=1, source_target_pairs={{0,4},{4,0},{8,12},{12,8},{1,5},{5,1},{9,13},{13,9},{2,6},{6,2},{1... | collective-permute-start | bytes 1572872 | tf_op jit(solution)/shard_map/ppermute | solution.py:35
  55.6 1.2 collective-permute-done.14.refs_2_
  57.3 2.5 %collective-permute-start.22 = (f32[2,8,64,128]{3,2,1,0:T(8,128)S(1)}, f32[2,8,64,128]{3,2,1,0:T(8,128)S(1)}, u32[]{:S(2)}, u32[]{:S(2)}) collective-permute-start(f32[2,8,64,128]{3,2,1,0:T(8,128)S(1)} %get-tuple-element.135), channel_id=1, source_target_pairs={{0,16},{16,0},{1,17},{17,1},{2,18},{18,2},{3,19},{19,3},{4,20},{20... | collective-permute-start | bytes 1572872 | tf_op jit(solution)/shard_map/ppermute | solution.py:35
  59.7 1.7 %collective-permute-start.17 = (bf16[64,2176]{1,0:T(8,128)(2,1)S(1)}, bf16[64,2176]{1,0:T(8,128)(2,1)S(1)}, u32[]{:S(2)}, u32[]{:S(2)}) collective-permute-start(bf16[64,2176]{1,0:T(8,128)(2,1)S(1)} %get-tuple-element.128), channel_id=1, source_target_pairs={{0,8},{4,12},{8,0},{12,4},{1,9},{5,13},{9,1},{13,5},{2,10},{6,14},... | collective-permute-start | bytes 835592 | tf_op jit(solution)/shard_map/ppermute | solution.py:35
  61.4 12.8 %collective-permute-done.19.refs_1_ = bf16[16,4096]{1,0:T(8,128)(2,1)S(1)} collective-permute-done((bf16[16,4096]{1,0:T(8,128)(2,1)S(1)}, bf16[16,4096]{1,0:T(8,128)(2,1)S(1)}, u32[]{:S(2)}, u32[]{:S(2)}) %collective-permute-start.19) | collective-permute-done | bytes 131104 | tf_op jit(solution)/shard_map/ppermute | solution.py:35
  75.2 1.8 %collective-permute-start.25 = (bf16[128,1024]{1,0:T(8,128)(2,1)S(1)}, bf16[128,1024]{1,0:T(8,128)(2,1)S(1)}, u32[]{:S(2)}, u32[]{:S(2)}) collective-permute-start(bf16[128,1024]{1,0:T(8,128)(2,1)S(1)} %get-tuple-element.140.refs_4_), channel_id=1, source_target_pairs={{0,4},{4,0},{8,12},{12,8},{1,5},{5,1},{9,13},{13,9},{2,6},{6,2},{1... | collective-permute-start | bytes 786440 | tf_op jit(solution)/shard_map/ppermute | solution.py:35
  76.9 1.7 %collective-permute-start.28 = (bf16[128,1024]{1,0:T(8,128)(2,1)S(1)}, bf16[128,1024]{1,0:T(8,128)(2,1)S(1)}, u32[]{:S(2)}, u32[]{:S(2)}) collective-permute-start(bf16[128,1024]{1,0:T(8,128)(2,1)S(1)} %get-tuple-element.140.refs_4_), channel_id=1, source_target_pairs={{0,16},{16,0},{1,17},{17,1},{2,18},{18,2},{3,19},{19,3},{4,20},{20... | collective-permute-start | bytes 786440 | tf_op jit(solution)/shard_map/ppermute | solution.py:35
  79.6 1.6 %collective-permute-start.26 = (bf16[16,2048]{1,0:T(8,128)(2,1)S(1)}, bf16[16,2048]{1,0:T(8,128)(2,1)S(1)}, u32[]{:S(2)}, u32[]{:S(2)}) collective-permute-start(bf16[16,2048]{1,0:T(8,128)(2,1)S(1)} %get-tuple-element.142), channel_id=1, source_target_pairs={{0,2},{1,3},{2,0},{3,1},{4,6},{5,7},{6,4},{7,5},{8,10},{9,11},{10,... | collective-permute-start | bytes 196616 | tf_op jit(solution)/shard_map/ppermute | solution.py:35
  81.7 2.6 %collective-permute-done.26.refs_4_ = bf16[16,2048]{1,0:T(8,128)(2,1)S(1)} collective-permute-done((bf16[16,2048]{1,0:T(8,128)(2,1)S(1)}, bf16[16,2048]{1,0:T(8,128)(2,1)S(1)}, u32[]{:S(2)}, u32[]{:S(2)}) %collective-permute-start.26) | collective-permute-done | bytes 65568 | tf_op jit(solution)/shard_map/ppermute | solution.py:35
  86.4 1.5 collective-permute-start.31
  87.9 2.4 %collective-permute-start.30 = (bf16[64,2048]{1,0:T(8,128)(2,1)S(1)}, bf16[64,2048]{1,0:T(8,128)(2,1)S(1)}, u32[]{:S(2)}, u32[]{:S(2)}) collective-permute-start(bf16[64,2048]{1,0:T(8,128)(2,1)S(1)} %get-tuple-element.148), channel_id=1, source_target_pairs={{0,8},{4,12},{8,0},{12,4},{1,9},{5,13},{9,1},{13,5},{2,10},{6,14},... | collective-permute-start | bytes 786440 | tf_op jit(solution)/shard_map/ppermute | solution.py:35
  90.7 8.0 %collective-permute-done.30.refs_4_ = bf16[64,2048]{1,0:T(8,128)(2,1)S(1)} collective-permute-done((bf16[64,2048]{1,0:T(8,128)(2,1)S(1)}, bf16[64,2048]{1,0:T(8,128)(2,1)S(1)}, u32[]{:S(2)}, u32[]{:S(2)}) %collective-permute-start.30) | collective-permute-done | bytes 262176 | tf_op jit(solution)/shard_map/ppermute | solution.py:35
  98.7 2.1 %collective-permute-done.29.refs_0_ = bf16[128,1280]{1,0:T(8,128)(2,1)S(1)} collective-permute-done((bf16[128,1280]{1,0:T(8,128)(2,1)S(1)}, bf16[128,1280]{1,0:T(8,128)(2,1)S(1)}, u32[]{:S(2)}, u32[]{:S(2)}) %collective-permute-start.29) | collective-permute-done | bytes 327712 | tf_op jit(solution)/shard_map/ppermute | solution.py:35
  101.7 1.8 %collective-permute-start.33 = (bf16[64,512]{1,0:T(8,128)(2,1)S(1)}, bf16[64,512]{1,0:T(8,128)(2,1)S(1)}, u32[]{:S(2)}, u32[]{:S(2)}) collective-permute-start(bf16[64,512]{1,0:T(8,128)(2,1)S(1)} %get-tuple-element.155), channel_id=1, source_target_pairs={{0,2},{1,3},{2,0},{3,1},{4,6},{5,7},{6,4},{7,5},{8,10},{9,11},{10,... | collective-permute-start | bytes 196616 | tf_op jit(solution)/shard_map/ppermute | solution.py:35
  103.5 2.8 %collective-permute-done.33.refs_5_ = bf16[64,512]{1,0:T(8,128)(2,1)S(1)} collective-permute-done((bf16[64,512]{1,0:T(8,128)(2,1)S(1)}, bf16[64,512]{1,0:T(8,128)(2,1)S(1)}, u32[]{:S(2)}, u32[]{:S(2)}) %collective-permute-start.33) | collective-permute-done | bytes 65568 | tf_op jit(solution)/shard_map/ppermute | solution.py:35
  107.5 1.4 collective-permute-start.38
  108.9 1.6 %collective-permute-start.35 = (bf16[128,1280]{1,0:T(8,128)(2,1)S(1)}, bf16[128,1280]{1,0:T(8,128)(2,1)S(1)}, u32[]{:S(2)}, u32[]{:S(2)}) collective-permute-start(bf16[128,1280]{1,0:T(8,128)(2,1)S(1)} %get-tuple-element.159), channel_id=1, source_target_pairs={{0,4},{4,0},{8,12},{12,8},{1,5},{5,1},{9,13},{13,9},{2,6},{6,2},{1... | collective-permute-start | bytes 983048 | tf_op jit(solution)/shard_map/ppermute | solution.py:35
  110.5 2.0 %collective-permute-start.37 = (bf16[64,2048]{1,0:T(8,128)(2,1)S(1)}, bf16[64,2048]{1,0:T(8,128)(2,1)S(1)}, u32[]{:S(2)}, u32[]{:S(2)}) collective-permute-start(bf16[64,2048]{1,0:T(8,128)(2,1)S(1)} %get-tuple-element.166), channel_id=1, source_target_pairs={{0,8},{4,12},{8,0},{12,4},{1,9},{5,13},{9,1},{13,5},{2,10},{6,14},... | collective-permute-start | bytes 786440 | tf_op jit(solution)/shard_map/ppermute | solution.py:35
  112.5 12.1 %collective-permute-done.38.refs_10_.refs_3_.refs_15_ = bf16[128,1280]{1,0:T(8,128)(2,1)S(1)} collective-permute-done((bf16[128,1280]{1,0:T(8,128)(2,1)S(1)}, bf16[128,1280]{1,0:T(8,128)(2,1)S(1)}, u32[]{:S(2)}, u32[]{:S(2)}) %collective-permute-start.38) | collective-permute-done | bytes 327712 | tf_op jit(solution)/shard_map/ppermute | solution.py:35
  125.5 1.4 collective-permute-done.40.refs_1_
  126.9 1.7 %collective-permute-start.47 = (bf16[128,1280]{1,0:T(8,128)(2,1)S(1)}, bf16[128,1280]{1,0:T(8,128)(2,1)S(1)}, u32[]{:S(2)}, u32[]{:S(2)}) collective-permute-start(bf16[128,1280]{1,0:T(8,128)(2,1)S(1)} %get-tuple-element.186), channel_id=1, source_target_pairs={{0,4},{4,0},{8,12},{12,8},{1,5},{5,1},{9,13},{13,9},{2,6},{6,2},{1... | collective-permute-start | bytes 983048 | tf_op jit(solution)/shard_map/ppermute | solution.py:35
  130.7 3.3 %collective-permute-done.39.refs_6_ = bf16[64,640]{1,0:T(8,128)(2,1)S(1)} collective-permute-done((bf16[64,640]{1,0:T(8,128)(2,1)S(1)}, bf16[64,640]{1,0:T(8,128)(2,1)S(1)}, u32[]{:S(2)}, u32[]{:S(2)}) %collective-permute-start.39) | collective-permute-done | bytes 81952 | tf_op jit(solution)/shard_map/ppermute | solution.py:35
  134.4 3.2 %collective-permute-done.47.refs_5_.refs_9_ = bf16[128,1280]{1,0:T(8,128)(2,1)S(1)} collective-permute-done((bf16[128,1280]{1,0:T(8,128)(2,1)S(1)}, bf16[128,1280]{1,0:T(8,128)(2,1)S(1)}, u32[]{:S(2)}, u32[]{:S(2)}) %collective-permute-start.47) | collective-permute-done | bytes 327712 | tf_op jit(solution)/shard_map/ppermute | solution.py:35
  138.2 1.3 collective-permute-done.42.refs_1_
  139.4 2.0 %collective-permute-start.44 = (bf16[128,256]{1,0:T(8,128)(2,1)S(1)}, bf16[128,256]{1,0:T(8,128)(2,1)S(1)}, u32[]{:S(2)}, u32[]{:S(2)}) collective-permute-start(bf16[128,256]{1,0:T(8,128)(2,1)S(1)} %get-tuple-element.184), channel_id=1, source_target_pairs={{0,4},{4,0},{8,12},{12,8},{1,5},{5,1},{9,13},{13,9},{2,6},{6,2},{1... | collective-permute-start | bytes 196616 | tf_op jit(solution)/shard_map/ppermute | solution.py:35
  142.5 2.7 %collective-permute-done.44.refs_1_ = bf16[128,256]{1,0:T(8,128)(2,1)S(1)} collective-permute-done((bf16[128,256]{1,0:T(8,128)(2,1)S(1)}, bf16[128,256]{1,0:T(8,128)(2,1)S(1)}, u32[]{:S(2)}, u32[]{:S(2)}) %collective-permute-start.44) | collective-permute-done | bytes 65568 | tf_op jit(solution)/shard_map/ppermute | solution.py:35
  147.1 2.3 %update_mlp.1 = (f32[1,2,256,1024]{3,2,1,0:T(8,128)}, bf16[1,2,256,1024]{3,2,1,0:T(8,128)(2,1)}, f32[8,128]{1,0:T(8,128)S(1)}) custom-call(bf16[128,1280]{1,0:T(8,128)(2,1)S(1)} %get-tuple-element.151.refs_0_.refs_12_, bf16[128,1280]{1,0:T(8,128)(2,1)S(1)} %get-tuple-element.168.refs_1_.refs_13_, ...), custom_call_target="tpu_custom_call" | custom-call | flops 1 | bytes 1 | tf_op jit(solution)/shard_map/update_mlp/pallas_call | solution.py:131
  149.5 2.3 %update_embed.1 = (f32[1,256,1024]{2,1,0:T(8,128)}, bf16[1,256,1024]{2,1,0:T(8,128)(2,1)}, f32[8,128]{1,0:T(8,128)}) custom-call(bf16[128,256]{1,0:T(8,128)(2,1)S(1)} %get-tuple-element.183.refs_0_, bf16[128,256]{1,0:T(8,128)(2,1)S(1)} %collective-permute-done.44.refs_1_, bf16[128,256]{1,0:T(8,128)(2,1)S(1)} %collective-permute-done.45.refs_2_, ...), custom_call_target="tpu_custom_call" | custom-call | flops 1 | bytes 1 | tf_op jit(solution)/shard_map/update_embed/pallas_call | solution.py:131
  (82 shorter events, 18.8 us)
Async XLA Ops:
  0.6 16.4 %collective-permute-start.4 = (bf16[256,1024]{1,0:T(8,128)(2,1)}, bf16[256,1024]{1,0:T(8,128)(2,1)S(1)}, u32[]{:S(2)}, u32[]{:S(2)}) collective-permute-start(bf16[256,1024]{1,0:T(8,128)(2,1)} %bitcast.2), channel_id=1, source_target_pairs={{16,0},{17,1},{18,2},{19,3},{20,4},{21,5},{22,6},{23,7},{24,8},{25... | collective-permute-start | bytes 1572872 | tf_op jit(solution)/shard_map/ppermute | solution.py:597
  4.7 11.9 %collective-permute-start.2 = (bf16[16,4096]{1,0:T(8,128)(2,1)S(1)}, bf16[16,4096]{1,0:T(8,128)(2,1)S(1)}, u32[]{:S(2)}, u32[]{:S(2)}) collective-permute-start(bf16[16,4096]{1,0:T(8,128)(2,1)S(1)} %get-tuple-element.103), channel_id=1, source_target_pairs={{0,16},{1,17},{2,18},{3,19},{4,20},{5,21},{6,22},{7,23},{8,24},{9,... | collective-permute-start | bytes 393224 | tf_op jit(solution)/shard_map/ppermute | solution.py:605
  9.5 7.0 %collective-permute-start = (f32[2,8,4,128]{3,2,1,0:T(4,128)S(1)}, f32[2,8,4,128]{3,2,1,0:T(4,128)S(1)}, u32[]{:S(2)}, u32[]{:S(2)}) collective-permute-start(f32[2,8,4,128]{3,2,1,0:T(4,128)S(1)} %get-tuple-element.100), channel_id=1, source_target_pairs={{0,4},{4,8},{8,12},{12,0},{1,5},{5,9},{9,13},{13,1},{2,6},{6,10},{... | collective-permute-start | bytes 98312 | tf_op jit(solution)/shard_map/ppermute | solution.py:606
  12.3 4.3 %collective-permute-start.1 = (f32[2,8,4,128]{3,2,1,0:T(4,128)S(1)}, f32[2,8,4,128]{3,2,1,0:T(4,128)S(1)}, u32[]{:S(2)}, u32[]{:S(2)}) collective-permute-start(f32[2,8,4,128]{3,2,1,0:T(4,128)S(1)} %get-tuple-element.101), channel_id=1, source_target_pairs={{0,12},{4,0},{8,4},{12,8},{1,13},{5,1},{9,5},{13,9},{2,14},{6,2},{... | collective-permute-start | bytes 98312 | tf_op jit(solution)/shard_map/ppermute | solution.py:607
  18.3 15.0 %collective-permute-start.8 = (bf16[256,1024]{1,0:T(8,128)(2,1)S(1)}, bf16[256,1024]{1,0:T(8,128)(2,1)S(1)}, u32[]{:S(2)}, u32[]{:S(2)}) collective-permute-start(bf16[256,1024]{1,0:T(8,128)(2,1)S(1)} %get-tuple-element.111), channel_id=1, source_target_pairs={{16,0},{17,1},{18,2},{19,3},{20,4},{21,5},{22,6},{23,7},{24,8},{25... | collective-permute-start | bytes 1572872 | tf_op jit(solution)/shard_map/ppermute | solution.py:613
  19.6 16.3 %collective-permute-start.7 = (bf16[256,1024]{1,0:T(8,128)(2,1)S(1)}, bf16[256,1024]{1,0:T(8,128)(2,1)S(1)}, u32[]{:S(2)}, u32[]{:S(2)}) collective-permute-start(bf16[256,1024]{1,0:T(8,128)(2,1)S(1)} %get-tuple-element.110.refs_3_.refs_8_.refs_6_), channel_id=1, source_target_pairs={{0,4},{4,0},{8,12},{12,8},{1,5},{5,1},{9,13},{13,9},{2,6},{6,2},{1... | collective-permute-start | bytes 1572872 | tf_op jit(solution)/shard_map/ppermute | solution.py:35
  22.0 4.3 %collective-permute-start.3 = (bf16[16,2048]{1,0:T(8,128)(2,1)S(1)}, bf16[16,2048]{1,0:T(8,128)(2,1)S(1)}, u32[]{:S(2)}, u32[]{:S(2)}) collective-permute-start(bf16[16,2048]{1,0:T(8,128)(2,1)S(1)} %get-tuple-element.106), channel_id=1, source_target_pairs={{0,2},{1,3},{2,0},{3,1},{4,6},{5,7},{6,4},{7,5},{8,10},{9,11},{10,... | collective-permute-start | bytes 196616 | tf_op jit(solution)/shard_map/ppermute | solution.py:35
  26.7 8.5 %collective-permute-start.9 = (bf16[32,2048]{1,0:T(8,128)(2,1)S(1)}, bf16[32,2048]{1,0:T(8,128)(2,1)S(1)}, u32[]{:S(2)}, u32[]{:S(2)}) collective-permute-start(bf16[32,2048]{1,0:T(8,128)(2,1)S(1)} %get-tuple-element.114.refs_1_), channel_id=1, source_target_pairs={{0,8},{4,12},{8,0},{12,4},{1,9},{5,13},{9,1},{13,5},{2,10},{6,14},... | collective-permute-start | bytes 393224 | tf_op jit(solution)/shard_map/ppermute | solution.py:35
  29.3 4.1 %collective-permute-start.5 = (f32[72,128]{1,0:T(8,128)S(1)}, f32[72,128]{1,0:T(8,128)S(1)}, u32[]{:S(2)}, u32[]{:S(2)}) collective-permute-start(f32[72,128]{1,0:T(8,128)S(1)} %get-tuple-element.109), channel_id=1, source_target_pairs={{0,1},{1,2},{2,3},{3,0},{4,5},{5,6},{6,7},{7,4},{8,9},{9,10},{10,1... | collective-permute-start | bytes 110600 | tf_op jit(solution)/shard_map/ppermute | solution.py:620
  29.3 5.4 %collective-permute-start.6 = (f32[72,128]{1,0:T(8,128)S(1)}, f32[72,128]{1,0:T(8,128)S(1)}, u32[]{:S(2)}, u32[]{:S(2)}) collective-permute-start(f32[72,128]{1,0:T(8,128)S(1)} %get-tuple-element.109), channel_id=1, source_target_pairs={{0,3},{1,0},{2,1},{3,2},{4,7},{5,4},{6,5},{7,6},{8,11},{9,8},{10,9... | collective-permute-start | bytes 110600 | tf_op jit(solution)/shard_map/ppermute | solution.py:621
  33.3 16.4 %collective-permute-start.11 = (bf16[256,1024]{1,0:T(8,128)(2,1)S(1)}, bf16[256,1024]{1,0:T(8,128)(2,1)S(1)}, u32[]{:S(2)}, u32[]{:S(2)}) collective-permute-start(bf16[256,1024]{1,0:T(8,128)(2,1)S(1)} %get-tuple-element.110.refs_3_.refs_8_.refs_6_), channel_id=1, source_target_pairs={{0,1},{1,0},{2,3},{3,2},{4,5},{5,4},{6,7},{7,6},{8,9},{9,8},{10,11... | collective-permute-start | bytes 1572872 | tf_op jit(solution)/shard_map/ppermute | solution.py:35
  33.4 16.2 %collective-permute-start.13 = (bf16[256,1024]{1,0:T(8,128)(2,1)S(1)}, bf16[256,1024]{1,0:T(8,128)(2,1)S(1)}, u32[]{:S(2)}, u32[]{:S(2)}) collective-permute-start(bf16[256,1024]{1,0:T(8,128)(2,1)S(1)} %get-tuple-element.119), channel_id=1, source_target_pairs={{16,0},{17,1},{18,2},{19,3},{20,4},{21,5},{22,6},{23,7},{24,8},{25... | collective-permute-start | bytes 1572872 | tf_op jit(solution)/shard_map/ppermute | solution.py:614
  35.9 13.7 %collective-permute-start.12 = (bf16[256,1024]{1,0:T(8,128)(2,1)S(1)}, bf16[256,1024]{1,0:T(8,128)(2,1)S(1)}, u32[]{:S(2)}, u32[]{:S(2)}) collective-permute-start(bf16[256,1024]{1,0:T(8,128)(2,1)S(1)} %get-tuple-element.118.refs_5_.refs_10_.refs_8_), channel_id=1, source_target_pairs={{0,1},{1,0},{2,3},{3,2},{4,5},{5,4},{6,7},{7,6},{8,9},{9,8},{10,11... | collective-permute-start | bytes 1572872 | tf_op jit(solution)/shard_map/ppermute | solution.py:35
  36.0 15.3 %collective-permute-start.10 = (bf16[256,1024]{1,0:T(8,128)(2,1)S(1)}, bf16[256,1024]{1,0:T(8,128)(2,1)S(1)}, u32[]{:S(2)}, u32[]{:S(2)}) collective-permute-start(bf16[256,1024]{1,0:T(8,128)(2,1)S(1)} %get-tuple-element.117.refs_3_.refs_4_), channel_id=1, source_target_pairs={{0,4},{4,0},{8,12},{12,8},{1,5},{5,1},{9,13},{13,9},{2,6},{6,2},{1... | collective-permute-start | bytes 1572872 | tf_op jit(solution)/shard_map/ppermute | solution.py:35
  38.8 16.7 %collective-permute-start.15 = (bf16[256,1024]{1,0:T(8,128)(2,1)S(1)}, bf16[256,1024]{1,0:T(8,128)(2,1)S(1)}, u32[]{:S(2)}, u32[]{:S(2)}) collective-permute-start(bf16[256,1024]{1,0:T(8,128)(2,1)S(1)} %get-tuple-element.117.refs_3_.refs_4_), channel_id=1, source_target_pairs={{0,1},{1,0},{2,3},{3,2},{4,5},{5,4},{6,7},{7,6},{8,9},{9,8},{10,11... | collective-permute-start | bytes 1572872 | tf_op jit(solution)/shard_map/ppermute | solution.py:35
  52.1 4.6 %collective-permute-start.16 = (bf16[256,1024]{1,0:T(8,128)(2,1)S(1)}, bf16[256,1024]{1,0:T(8,128)(2,1)S(1)}, u32[]{:S(2)}, u32[]{:S(2)}) collective-permute-start(bf16[256,1024]{1,0:T(8,128)(2,1)S(1)} %get-tuple-element.124.refs_5_.refs_6_), channel_id=1, source_target_pairs={{0,1},{1,0},{2,3},{3,2},{4,5},{5,4},{6,7},{7,6},{8,9},{9,8},{10,11... | collective-permute-start | bytes 1572872 | tf_op jit(solution)/shard_map/ppermute | solution.py:35
  52.2 4.5 %collective-permute-start.14 = (bf16[64,512]{1,0:T(8,128)(2,1)S(1)}, bf16[64,512]{1,0:T(8,128)(2,1)S(1)}, u32[]{:S(2)}, u32[]{:S(2)}) collective-permute-start(bf16[64,512]{1,0:T(8,128)(2,1)S(1)} %get-tuple-element.123), channel_id=1, source_target_pairs={{0,2},{1,3},{2,0},{3,1},{4,6},{5,7},{6,4},{7,5},{8,10},{9,11},{10,... | collective-permute-start | bytes 196616 | tf_op jit(solution)/shard_map/ppermute | solution.py:35
  53.8 20.5 %collective-permute-start.21 = (bf16[256,1024]{1,0:T(8,128)(2,1)S(1)}, bf16[256,1024]{1,0:T(8,128)(2,1)S(1)}, u32[]{:S(2)}, u32[]{:S(2)}) collective-permute-start(bf16[256,1024]{1,0:T(8,128)(2,1)S(1)} %get-tuple-element.129.refs_3_.refs_6_), channel_id=1, source_target_pairs={{0,4},{4,0},{8,12},{12,8},{1,5},{5,1},{9,13},{13,9},{2,6},{6,2},{1... | collective-permute-start | bytes 1572872 | tf_op jit(solution)/shard_map/ppermute | solution.py:35
  57.3 17.0 %collective-permute-start.22 = (f32[2,8,64,128]{3,2,1,0:T(8,128)S(1)}, f32[2,8,64,128]{3,2,1,0:T(8,128)S(1)}, u32[]{:S(2)}, u32[]{:S(2)}) collective-permute-start(f32[2,8,64,128]{3,2,1,0:T(8,128)S(1)} %get-tuple-element.135), channel_id=1, source_target_pairs={{0,16},{16,0},{1,17},{17,1},{2,18},{18,2},{3,19},{19,3},{4,20},{20... | collective-permute-start | bytes 1572872 | tf_op jit(solution)/shard_map/ppermute | solution.py:35
  59.7 14.6 %collective-permute-start.17 = (bf16[64,2176]{1,0:T(8,128)(2,1)S(1)}, bf16[64,2176]{1,0:T(8,128)(2,1)S(1)}, u32[]{:S(2)}, u32[]{:S(2)}) collective-permute-start(bf16[64,2176]{1,0:T(8,128)(2,1)S(1)} %get-tuple-element.128), channel_id=1, source_target_pairs={{0,8},{4,12},{8,0},{12,4},{1,9},{5,13},{9,1},{13,5},{2,10},{6,14},... | collective-permute-start | bytes 835592 | tf_op jit(solution)/shard_map/ppermute | solution.py:35
  61.4 12.9 %collective-permute-start.19 = (bf16[16,4096]{1,0:T(8,128)(2,1)S(1)}, bf16[16,4096]{1,0:T(8,128)(2,1)S(1)}, u32[]{:S(2)}, u32[]{:S(2)}) collective-permute-start(bf16[16,4096]{1,0:T(8,128)(2,1)S(1)} %get-tuple-element.131), channel_id=1, source_target_pairs={{0,16},{16,0},{1,17},{17,1},{2,18},{18,2},{3,19},{19,3},{4,20},{20... | collective-permute-start | bytes 393224 | tf_op jit(solution)/shard_map/ppermute | solution.py:35
  61.4 12.8 %collective-permute-start.20 = (bf16[64,1024]{1,0:T(8,128)(2,1)S(1)}, bf16[64,1024]{1,0:T(8,128)(2,1)S(1)}, u32[]{:S(2)}, u32[]{:S(2)}) collective-permute-start(bf16[64,1024]{1,0:T(8,128)(2,1)S(1)} %get-tuple-element.133.refs_2_), channel_id=1, source_target_pairs={{0,1},{1,0},{2,3},{3,2},{4,5},{5,4},{6,7},{7,6},{8,9},{9,8},{10,11... | collective-permute-start | bytes 393224 | tf_op jit(solution)/shard_map/ppermute | solution.py:35
  74.3 4.4 %collective-permute-start.18 = (bf16[256,1024]{1,0:T(8,128)(2,1)S(1)}, bf16[256,1024]{1,0:T(8,128)(2,1)S(1)}, u32[]{:S(2)}, u32[]{:S(2)}) collective-permute-start(bf16[256,1024]{1,0:T(8,128)(2,1)S(1)} %get-tuple-element.129.refs_3_.refs_6_), channel_id=1, source_target_pairs={{0,1},{1,0},{2,3},{3,2},{4,5},{5,4},{6,7},{7,6},{8,9},{9,8},{10,11... | collective-permute-start | bytes 1572872 | tf_op jit(solution)/shard_map/ppermute | solution.py:35
  74.6 4.1 %collective-permute-start.23 = (bf16[256,1024]{1,0:T(8,128)(2,1)S(1)}, bf16[256,1024]{1,0:T(8,128)(2,1)S(1)}, u32[]{:S(2)}, u32[]{:S(2)}) collective-permute-start(bf16[256,1024]{1,0:T(8,128)(2,1)S(1)} %get-tuple-element.136.refs_5_.refs_8_), channel_id=1, source_target_pairs={{0,1},{1,0},{2,3},{3,2},{4,5},{5,4},{6,7},{7,6},{8,9},{9,8},{10,11... | collective-permute-start | bytes 1572872 | tf_op jit(solution)/shard_map/ppermute | solution.py:35
  75.2 9.1 %collective-permute-start.25 = (bf16[128,1024]{1,0:T(8,128)(2,1)S(1)}, bf16[128,1024]{1,0:T(8,128)(2,1)S(1)}, u32[]{:S(2)}, u32[]{:S(2)}) collective-permute-start(bf16[128,1024]{1,0:T(8,128)(2,1)S(1)} %get-tuple-element.140.refs_4_), channel_id=1, source_target_pairs={{0,4},{4,0},{8,12},{12,8},{1,5},{5,1},{9,13},{13,9},{2,6},{6,2},{1... | collective-permute-start | bytes 786440 | tf_op jit(solution)/shard_map/ppermute | solution.py:35
  76.9 8.0 %collective-permute-start.28 = (bf16[128,1024]{1,0:T(8,128)(2,1)S(1)}, bf16[128,1024]{1,0:T(8,128)(2,1)S(1)}, u32[]{:S(2)}, u32[]{:S(2)}) collective-permute-start(bf16[128,1024]{1,0:T(8,128)(2,1)S(1)} %get-tuple-element.140.refs_4_), channel_id=1, source_target_pairs={{0,16},{16,0},{1,17},{17,1},{2,18},{18,2},{3,19},{19,3},{4,20},{20... | collective-permute-start | bytes 786440 | tf_op jit(solution)/shard_map/ppermute | solution.py:35
  79.5 6.0 %collective-permute-start.24 = (bf16[64,1536]{1,0:T(8,128)(2,1)S(1)}, bf16[64,1536]{1,0:T(8,128)(2,1)S(1)}, u32[]{:S(2)}, u32[]{:S(2)}) collective-permute-start(bf16[64,1536]{1,0:T(8,128)(2,1)S(1)} %get-tuple-element.139), channel_id=1, source_target_pairs={{0,1},{1,0},{2,3},{3,2},{4,5},{5,4},{6,7},{7,6},{8,9},{9,8},{10,11... | collective-permute-start | bytes 589832 | tf_op jit(solution)/shard_map/ppermute | solution.py:35
  79.6 4.7 %collective-permute-start.26 = (bf16[16,2048]{1,0:T(8,128)(2,1)S(1)}, bf16[16,2048]{1,0:T(8,128)(2,1)S(1)}, u32[]{:S(2)}, u32[]{:S(2)}) collective-permute-start(bf16[16,2048]{1,0:T(8,128)(2,1)S(1)} %get-tuple-element.142), channel_id=1, source_target_pairs={{0,2},{1,3},{2,0},{3,1},{4,6},{5,7},{6,4},{7,5},{8,10},{9,11},{10,... | collective-permute-start | bytes 196616 | tf_op jit(solution)/shard_map/ppermute | solution.py:35
  81.2 4.3 %collective-permute-start.27 = (bf16[64,512]{1,0:T(8,128)(2,1)S(1)}, bf16[64,512]{1,0:T(8,128)(2,1)S(1)}, u32[]{:S(2)}, u32[]{:S(2)}) collective-permute-start(bf16[64,512]{1,0:T(8,128)(2,1)S(1)} %get-tuple-element.144), channel_id=1, source_target_pairs={{0,2},{1,3},{2,0},{3,1},{4,6},{5,7},{6,4},{7,5},{8,10},{9,11},{10,... | collective-permute-start | bytes 196616 | tf_op jit(solution)/shard_map/ppermute | solution.py:35
  86.1 14.8 %collective-permute-start.29 = (bf16[128,1280]{1,0:T(8,128)(2,1)S(1)}, bf16[128,1280]{1,0:T(8,128)(2,1)S(1)}, u32[]{:S(2)}, u32[]{:S(2)}) collective-permute-start(bf16[128,1280]{1,0:T(8,128)(2,1)S(1)} %get-tuple-element.146), channel_id=1, source_target_pairs={{0,4},{4,0},{8,12},{12,8},{1,5},{5,1},{9,13},{13,9},{2,6},{6,2},{1... | collective-permute-start | bytes 983048 | tf_op jit(solution)/shard_map/ppermute | solution.py:35
  86.4 14.5 %collective-permute-start.31 = (bf16[128,1280]{1,0:T(8,128)(2,1)S(1)}, bf16[128,1280]{1,0:T(8,128)(2,1)S(1)}, u32[]{:S(2)}, u32[]{:S(2)}) collective-permute-start(bf16[128,1280]{1,0:T(8,128)(2,1)S(1)} %get-tuple-element.151.refs_0_.refs_12_), channel_id=1, source_target_pairs={{0,16},{16,0},{1,17},{17,1},{2,18},{18,2},{3,19},{19,3},{4,20},{20... | collective-permute-start | bytes 983048 | tf_op jit(solution)/shard_map/ppermute | solution.py:35
  87.9 10.8 %collective-permute-start.30 = (bf16[64,2048]{1,0:T(8,128)(2,1)S(1)}, bf16[64,2048]{1,0:T(8,128)(2,1)S(1)}, u32[]{:S(2)}, u32[]{:S(2)}) collective-permute-start(bf16[64,2048]{1,0:T(8,128)(2,1)S(1)} %get-tuple-element.148), channel_id=1, source_target_pairs={{0,8},{4,12},{8,0},{12,4},{1,9},{5,13},{9,1},{13,5},{2,10},{6,14},... | collective-permute-start | bytes 786440 | tf_op jit(solution)/shard_map/ppermute | solution.py:35
  90.3 13.2 %collective-permute-start.34 = (bf16[128,1024]{1,0:T(8,128)(2,1)S(1)}, bf16[128,1024]{1,0:T(8,128)(2,1)S(1)}, u32[]{:S(2)}, u32[]{:S(2)}) collective-permute-start(bf16[128,1024]{1,0:T(8,128)(2,1)S(1)} %get-tuple-element.157.refs_5_), channel_id=1, source_target_pairs={{0,16},{16,0},{1,17},{17,1},{2,18},{18,2},{3,19},{19,3},{4,20},{20... | collective-permute-start | bytes 786440 | tf_op jit(solution)/shard_map/ppermute | solution.py:35
  101.7 4.6 %collective-permute-start.32 = (bf16[64,1536]{1,0:T(8,128)(2,1)S(1)}, bf16[64,1536]{1,0:T(8,128)(2,1)S(1)}, u32[]{:S(2)}, u32[]{:S(2)}) collective-permute-start(bf16[64,1536]{1,0:T(8,128)(2,1)S(1)} %get-tuple-element.153), channel_id=1, source_target_pairs={{0,1},{1,0},{2,3},{3,2},{4,5},{5,4},{6,7},{7,6},{8,9},{9,8},{10,11... | collective-permute-start | bytes 589832 | tf_op jit(solution)/shard_map/ppermute | solution.py:35
  101.7 4.5 %collective-permute-start.33 = (bf16[64,512]{1,0:T(8,128)(2,1)S(1)}, bf16[64,512]{1,0:T(8,128)(2,1)S(1)}, u32[]{:S(2)}, u32[]{:S(2)}) collective-permute-start(bf16[64,512]{1,0:T(8,128)(2,1)S(1)} %get-tuple-element.155), channel_id=1, source_target_pairs={{0,2},{1,3},{2,0},{3,1},{4,6},{5,7},{6,4},{7,5},{8,10},{9,11},{10,... | collective-permute-start | bytes 196616 | tf_op jit(solution)/shard_map/ppermute | solution.py:35
  106.8 17.8 %collective-permute-start.36 = (bf16[128,1536]{1,0:T(8,128)(2,1)S(1)}, bf16[128,1536]{1,0:T(8,128)(2,1)S(1)}, u32[]{:S(2)}, u32[]{:S(2)}) collective-permute-start(bf16[128,1536]{1,0:T(8,128)(2,1)S(1)} %get-tuple-element.160), channel_id=1, source_target_pairs={{0,16},{16,0},{1,17},{17,1},{2,18},{18,2},{3,19},{19,3},{4,20},{20... | collective-permute-start | bytes 1179656 | tf_op jit(solution)/shard_map/ppermute | solution.py:35
  107.5 17.1 %collective-permute-start.38 = (bf16[128,1280]{1,0:T(8,128)(2,1)S(1)}, bf16[128,1280]{1,0:T(8,128)(2,1)S(1)}, u32[]{:S(2)}, u32[]{:S(2)}) collective-permute-start(bf16[128,1280]{1,0:T(8,128)(2,1)S(1)} %get-tuple-element.168.refs_1_.refs_13_), channel_id=1, source_target_pairs={{0,16},{16,0},{1,17},{17,1},{2,18},{18,2},{3,19},{19,3},{4,20},{20... | collective-permute-start | bytes 983048 | tf_op jit(solution)/shard_map/ppermute | solution.py:35
  108.9 15.7 %collective-permute-start.35 = (bf16[128,1280]{1,0:T(8,128)(2,1)S(1)}, bf16[128,1280]{1,0:T(8,128)(2,1)S(1)}, u32[]{:S(2)}, u32[]{:S(2)}) collective-permute-start(bf16[128,1280]{1,0:T(8,128)(2,1)S(1)} %get-tuple-element.159), channel_id=1, source_target_pairs={{0,4},{4,0},{8,12},{12,8},{1,5},{5,1},{9,13},{13,9},{2,6},{6,2},{1... | collective-permute-start | bytes 983048 | tf_op jit(solution)/shard_map/ppermute | solution.py:35
  110.5 14.1 %collective-permute-start.37 = (bf16[64,2048]{1,0:T(8,128)(2,1)S(1)}, bf16[64,2048]{1,0:T(8,128)(2,1)S(1)}, u32[]{:S(2)}, u32[]{:S(2)}) collective-permute-start(bf16[64,2048]{1,0:T(8,128)(2,1)S(1)} %get-tuple-element.166), channel_id=1, source_target_pairs={{0,8},{4,12},{8,0},{12,4},{1,9},{5,13},{9,1},{13,5},{2,10},{6,14},... | collective-permute-start | bytes 786440 | tf_op jit(solution)/shard_map/ppermute | solution.py:35
  125.4 1.5 collective-permute-start.40
  126.9 10.6 %collective-permute-start.47 = (bf16[128,1280]{1,0:T(8,128)(2,1)S(1)}, bf16[128,1280]{1,0:T(8,128)(2,1)S(1)}, u32[]{:S(2)}, u32[]{:S(2)}) collective-permute-start(bf16[128,1280]{1,0:T(8,128)(2,1)S(1)} %get-tuple-element.186), channel_id=1, source_target_pairs={{0,4},{4,0},{8,12},{12,8},{1,5},{5,1},{9,13},{13,9},{2,6},{6,2},{1... | collective-permute-start | bytes 983048 | tf_op jit(solution)/shard_map/ppermute | solution.py:35
  128.6 10.8 %collective-permute-start.43 = (bf16[128,1280]{1,0:T(8,128)(2,1)S(1)}, bf16[128,1280]{1,0:T(8,128)(2,1)S(1)}, u32[]{:S(2)}, u32[]{:S(2)}) collective-permute-start(bf16[128,1280]{1,0:T(8,128)(2,1)S(1)} %get-tuple-element.180.refs_4_.refs_8_), channel_id=1, source_target_pairs={{0,16},{16,0},{1,17},{17,1},{2,18},{18,2},{3,19},{19,3},{4,20},{20... | collective-permute-start | bytes 983048 | tf_op jit(solution)/shard_map/ppermute | solution.py:35
  129.6 4.4 %collective-permute-start.39 = (bf16[64,640]{1,0:T(8,128)(2,1)S(1)}, bf16[64,640]{1,0:T(8,128)(2,1)S(1)}, u32[]{:S(2)}, u32[]{:S(2)}) collective-permute-start(bf16[64,640]{1,0:T(8,128)(2,1)S(1)} %get-tuple-element.171), channel_id=1, source_target_pairs={{0,2},{1,3},{2,0},{3,1},{4,6},{5,7},{6,4},{7,5},{8,10},{9,11},{10,... | collective-permute-start | bytes 245768 | tf_op jit(solution)/shard_map/ppermute | solution.py:35
  134.2 11.8 %collective-permute-start.41 = (bf16[128,1280]{1,0:T(8,128)(2,1)S(1)}, bf16[128,1280]{1,0:T(8,128)(2,1)S(1)}, u32[]{:S(2)}, u32[]{:S(2)}) collective-permute-start(bf16[128,1280]{1,0:T(8,128)(2,1)S(1)} %get-tuple-element.177), channel_id=1, source_target_pairs={{0,4},{4,0},{8,12},{12,8},{1,5},{5,1},{9,13},{13,9},{2,6},{6,2},{1... | collective-permute-start | bytes 983048 | tf_op jit(solution)/shard_map/ppermute | solution.py:35
  137.6 9.5 %collective-permute-start.48 = (bf16[128,1280]{1,0:T(8,128)(2,1)S(1)}, bf16[128,1280]{1,0:T(8,128)(2,1)S(1)}, u32[]{:S(2)}, u32[]{:S(2)}) collective-permute-start(bf16[128,1280]{1,0:T(8,128)(2,1)S(1)} %collective-permute-done.47.refs_5_.refs_9_), channel_id=1, source_target_pairs={{0,16},{16,0},{1,17},{17,1},{2,18},{18,2},{3,19},{19,3},{4,20},{20... | collective-permute-start | bytes 983048 | tf_op jit(solution)/shard_map/ppermute | solution.py:35
  139.4 5.8 %collective-permute-start.44 = (bf16[128,256]{1,0:T(8,128)(2,1)S(1)}, bf16[128,256]{1,0:T(8,128)(2,1)S(1)}, u32[]{:S(2)}, u32[]{:S(2)}) collective-permute-start(bf16[128,256]{1,0:T(8,128)(2,1)S(1)} %get-tuple-element.184), channel_id=1, source_target_pairs={{0,4},{4,0},{8,12},{12,8},{1,5},{5,1},{9,13},{13,9},{2,6},{6,2},{1... | collective-permute-start | bytes 196616 | tf_op jit(solution)/shard_map/ppermute | solution.py:35
  141.5 7.9 %collective-permute-start.45 = (bf16[128,256]{1,0:T(8,128)(2,1)S(1)}, bf16[128,256]{1,0:T(8,128)(2,1)S(1)}, u32[]{:S(2)}, u32[]{:S(2)}) collective-permute-start(bf16[128,256]{1,0:T(8,128)(2,1)S(1)} %get-tuple-element.183.refs_0_), channel_id=1, source_target_pairs={{0,16},{16,0},{1,17},{17,1},{2,18},{18,2},{3,19},{19,3},{4,20},{20... | collective-permute-start | bytes 196616 | tf_op jit(solution)/shard_map/ppermute | solution.py:35
  145.2 4.3 %collective-permute-start.46 = (bf16[128,256]{1,0:T(8,128)(2,1)S(1)}, bf16[128,256]{1,0:T(8,128)(2,1)S(1)}, u32[]{:S(2)}, u32[]{:S(2)}) collective-permute-start(bf16[128,256]{1,0:T(8,128)(2,1)S(1)} %collective-permute-done.44.refs_1_), channel_id=1, source_target_pairs={{0,16},{16,0},{1,17},{17,1},{2,18},{18,2},{3,19},{19,3},{4,20},{20... | collective-permute-start | bytes 196616 | tf_op jit(solution)/shard_map/ppermute | solution.py:35
  (6 other events, 32.7 us)
